TPU v7x, 32 devices: a whole 2x2x4 slice. The times are simulated.
32 devices in a mesh: gx: 8 (over y, x, core), gy: 4 (over z).
Axes of the slice: x: 2, y: 2, z: 4, core: 2. Of those that a mesh axis runs over, the one named last changes fastest.
Arguments:
- velocity: float32 [3, 512, 128, 128], P(None, 'gx', 'gy'), may hold values from -6 to 6
- host_cell: int32 [3, 16384], P(None, ('gx', 'gy')), may hold values from 0 to 126, as said below
- host_frac: float32 [3, 16384], P(None, ('gx', 'gy')), may hold values from 0 to 1
- host_dst: int32 [16384], P(('gx', 'gy')), may hold values from -1 to 8191, as said below
- owner_src: int32 [8192], P(('gx', 'gy')), may hold values from 0 to 16383, as said below
- rotor_speed: float32 [32], P(('gx', 'gy')), may hold values from 1.5 to 4
- blade_radius: float32 [8192], P(('gx', 'gy')), may hold values from 0.1 to 1
- blade_chord: float32 [8192], P(('gx', 'gy')), may hold values from 0.2 to 0.8
- blade_twist: float32 [8192], P(('gx', 'gy')), may hold values from -0.4 to 0.4
- blade_angle: float32 [8192], P(('gx', 'gy')), may hold values from -3.140625 to 3.140625
Outputs:
- velocity_next: float32 [3, 512, 128, 128], P(None, 'gx', 'gy')
- point_force: float32 [3, 8192], P(None, ('gx', 'gy'))
Inputs may be any that keep to these rules, and one draw needn't show every extreme that they name: `host_cell`: row 0 of a slot is its anchor cell streamwise inside its brick (below 64), row 1 spanwise (below 32), row 2 vertically (below 127). `host_dst`: each point number appears in exactly one slot; all other slots hold -1. The points of one turbine lie in slots of two bricks whose streamwise indices differ in the lowest bit (same spanwise index); those two bricks hold the points of two turbines. A brick may use all of its 512 slots, and some brick does. host_dst[owner_src[r]] = r for every point r.
All inputs are finite; a program needn't handle non-finite values.
Results may differ from a plain program's by a relative error of at most 0.00011.
Values sent between devices are 32-bit elements; how exact they have to be, the bound alone decides.
No kernel may reach another device: no remote copies, remote signals or barrier semaphores. Data moves between devices by JAX's collectives and lax.ppermute only.
A program may use at most 128 MiB of HBM per device.

v0:
```python
import jax
import jax.numpy as jnp
from jax import lax
from jax.sharding import PartitionSpec as P

CX = 64
CY = 32
CZ = 128
P_SIZE = 256
HOST = 512


DT_STEP = 0.2
NU_VISC = 0.5
EPS_SQ = 1.44
CORE_SQ = 0.01


def with_halo(block, sides, width):
    for axis, dim in sides:
        count = lax.axis_size(axis)
        forward = [(i, i + 1) for i in range(count - 1)]
        backward = [(target, source) for source, target in forward]
        low = lax.ppermute(
            lax.slice_in_dim(block, block.shape[dim] - width, None, axis=dim), axis, forward
        )
        high = lax.ppermute(lax.slice_in_dim(block, 0, width, axis=dim), axis, backward)
        block = jnp.concatenate([low, block, high], axis=dim)
    return block


def offset_weights(fraction):
    offsets = jnp.arange(-1, 3).astype(jnp.float32)
    kernel_raw = jnp.exp(-((offsets[:, None] - fraction[None, :]) ** 2) / EPS_SQ)
    return kernel_raw / jnp.sum(kernel_raw, axis=0, keepdims=True)


def attack(axial_flow, tangent, pitch_twist):
    rel_speed = jnp.sqrt(axial_flow * axial_flow + tangent * tangent + 1.0)
    cos_phi = tangent / rel_speed
    sin_phi = axial_flow / rel_speed
    sin_alpha = sin_phi * jnp.cos(pitch_twist) - cos_phi * jnp.sin(pitch_twist)
    cos_alpha = cos_phi * jnp.cos(pitch_twist) + sin_phi * jnp.sin(pitch_twist)
    lift_coef = 2.0 * jnp.pi * sin_alpha * cos_alpha / (1.0 + 4.0 * sin_alpha * sin_alpha)
    drag_coef = 0.02 + 0.8 * sin_alpha * sin_alpha
    return (rel_speed, cos_phi, sin_phi, lift_coef, drag_coef)


def blade_loads(sampled, spin_rate, radius, blade_chord, pitch_twist, azimuth):
    cos_angle = jnp.cos(azimuth)
    sin_angle = jnp.sin(azimuth)
    axial_flow = sampled[0]
    tangent = spin_rate * radius - (cos_angle * sampled[2] - sin_angle * sampled[1])
    rel_speed, cos_phi, sin_phi, lift_coef, drag_coef = attack(axial_flow, tangent, pitch_twist)
    circulation = 0.5 * blade_chord * rel_speed * lift_coef
    spacing = radius[:, :, None] - radius[:, None, :]
    alignment = (
        cos_angle[:, :, None] * cos_angle[:, None, :]
        + sin_angle[:, :, None] * sin_angle[:, None, :]
    )
    kernel = spacing / (spacing * spacing + CORE_SQ) * alignment / (4.0 * jnp.pi)
    induced = jnp.einsum("tij,tj->ti", kernel, circulation, precision=lax.Precision.HIGHEST)
    rel_speed, cos_phi, sin_phi, lift_coef, drag_coef = attack(
        axial_flow + induced, tangent, pitch_twist
    )
    dynamic = 0.5 * blade_chord * rel_speed * rel_speed
    lift_force = dynamic * lift_coef
    drag_force = dynamic * drag_coef
    thrust_part = lift_force * cos_phi + drag_force * sin_phi
    torque_part = lift_force * sin_phi - drag_force * cos_phi
    return jnp.stack([-thrust_part, torque_part * sin_angle, -torque_part * cos_angle])


def advance(velocity_pad, force_field):
    center = velocity_pad[:, 1:-1, 1:-1, 1:-1]
    outputs = []
    for component in range(3):
        one_field = velocity_pad[component]
        plus_x = one_field[2:, 1:-1, 1:-1]
        minus_x = one_field[:-2, 1:-1, 1:-1]
        plus_y = one_field[1:-1, 2:, 1:-1]
        minus_y = one_field[1:-1, :-2, 1:-1]
        plus_z = one_field[1:-1, 1:-1, 2:]
        minus_z = one_field[1:-1, 1:-1, :-2]
        middle = one_field[1:-1, 1:-1, 1:-1]
        transport = (
            center[0] * (plus_x - minus_x) * 0.5
            + center[1] * (plus_y - minus_y) * 0.5
            + center[2] * (plus_z - minus_z) * 0.5
        )
        diffusion = plus_x + minus_x + plus_y + minus_y + plus_z + minus_z - 6.0 * middle
        outputs.append(
            middle + DT_STEP * (-transport + NU_VISC * diffusion + force_field[component])
        )
    return jnp.stack(outputs)


def profile(anchor, weights, cell_count, margin):
    relative = (
        jnp.arange(cell_count + 2 * margin, dtype=jnp.int32)[None, :] - margin - anchor[:, None]
    )
    result = jnp.zeros(relative.shape, jnp.float32)
    for offset in range(4):
        result = result + jnp.where(relative == offset - 1, weights[offset][:, None], 0.0)
    return result


def fold_rims(array_in, axis_dim, cell_count):
    interior = lax.slice_in_dim(array_in, 4, 4 + cell_count, axis=axis_dim)
    lower_rim = lax.slice_in_dim(array_in, 0, 2, axis=axis_dim)
    upper_rim = lax.slice_in_dim(array_in, cell_count + 6, cell_count + 8, axis=axis_dim)
    first_cells = lax.slice_in_dim(interior, 0, 2, axis=axis_dim) + lower_rim
    interior = lax.dynamic_update_slice_in_dim(interior, first_cells, 0, axis_dim)
    last_cells = lax.slice_in_dim(interior, cell_count - 2, cell_count, axis=axis_dim) + upper_rim
    return lax.dynamic_update_slice_in_dim(interior, last_cells, cell_count - 2, axis_dim)


def per_device(
    velocity,
    host_cell,
    host_frac,
    host_dst,
    owner_src,
    rotor_speed,
    blade_radius,
    blade_chord,
    blade_twist,
    blade_angle,
):
    extended = with_halo(velocity, (("gx", 1), ("gy", 2)), 1)
    flat_field = extended.reshape(3, -1)
    cell_x = host_cell[0]
    cell_y = host_cell[1]
    cell_z = host_cell[2]
    corner_index = []
    corner_weight = []
    for step_x in range(2):
        weight_x = host_frac[0] if step_x else 1.0 - host_frac[0]
        for step_y in range(2):
            weight_y = host_frac[1] if step_y else 1.0 - host_frac[1]
            for step_z in range(2):
                weight_z = host_frac[2] if step_z else 1.0 - host_frac[2]
                corner_weight.append(weight_x * weight_y * weight_z)
                corner_index.append(
                    ((cell_x + 1 + step_x) * (CY + 2) + cell_y + 1 + step_y) * CZ + cell_z + step_z
                )
    corner_values = jnp.take(flat_field, jnp.concatenate(corner_index), axis=1).reshape(3, 8, HOST)
    sampled = jnp.zeros((3, HOST), jnp.float32)
    for corner in range(8):
        sampled = sampled + corner_weight[corner] * corner_values[:, corner]
    shard_part = lax.all_gather(sampled, ("gx", "gy"), axis=1, tiled=True)
    piece_len = shard_part.shape[1]
    position = owner_src
    inside = (position >= 0) & (position < piece_len)
    picked = jnp.take(shard_part, jnp.clip(position, 0, piece_len - 1), axis=1)
    owned_rows = jnp.where(inside[None, :], picked, 0.0)
    point_force = blade_loads(
        owned_rows.reshape(3, 1, P_SIZE),
        rotor_speed[:, None],
        blade_radius.reshape(1, P_SIZE),
        blade_chord.reshape(1, P_SIZE),
        blade_twist.reshape(1, P_SIZE),
        blade_angle.reshape(1, P_SIZE),
    )
    point_force = point_force.reshape(3, P_SIZE)
    shard_part = lax.all_gather(point_force, ("gx", "gy"), axis=1, tiled=True)
    piece_len = shard_part.shape[1]
    position = host_dst
    inside = (host_dst >= 0) & (position >= 0) & (position < piece_len)
    picked = jnp.take(shard_part, jnp.clip(position, 0, piece_len - 1), axis=1)
    host_force = jnp.where(inside[None, :], picked, 0.0)
    profile_x = profile(cell_x, offset_weights(host_frac[0]), CX, 2)
    profile_y = profile(cell_y, offset_weights(host_frac[1]), CY, 2)
    profile_z = profile(cell_z, offset_weights(host_frac[2]), CZ, 0)
    plane_weights = (profile_x[:, :, None] * profile_y[:, None, :]).reshape(HOST, -1)
    components = []
    for component in range(3):
        line_loads = host_force[component][:, None] * profile_z
        spread = lax.dot_general(
            plane_weights,
            line_loads,
            (((0,), (0,)), ((), ())),
            precision=lax.Precision.HIGHEST,
            preferred_element_type=jnp.float32,
        )
        components.append(spread.reshape(CX + 4, CY + 4, CZ))
    partial_value = jnp.stack(components)
    widened = with_halo(partial_value, (("gx", 1),), 2)
    folded = fold_rims(widened, 1, CX)
    widened = with_halo(folded, (("gy", 2),), 2)
    force_field = fold_rims(widened, 2, CY)
    velocity_pad = jnp.pad(extended, ((0, 0), (0, 0), (0, 0), (1, 1)))
    velocity_next = advance(velocity_pad, force_field)
    return (velocity_next, point_force)


def solution(mesh):
    return jax.shard_map(
        per_device,
        mesh=mesh,
        in_specs=(
            P(None, "gx", "gy", None),
            P(None, ("gx", "gy")),
            P(None, ("gx", "gy")),
            P(("gx", "gy")),
            P(("gx", "gy")),
            P(("gx", "gy")),
            P(("gx", "gy")),
            P(("gx", "gy")),
            P(("gx", "gy")),
            P(("gx", "gy")),
        ),
        out_specs=(P(None, "gx", "gy", None), P(None, ("gx", "gy"))),
        check_vma=False,
    )
```

profile of v0, /device:TPU:0, one launch (start us, length us, event | category | flops | bytes accessed | tf_op | source)
XLA Modules:
  0.0 491.6 jit_solution(1830016694026308460)
XLA Ops:
  1.5 2.3 collective-permute-start
  3.8 1.3 collective-permute-start.1
  13.3 3.2 broadcast_multiply_fusion
  17.1 6.6 %mul.709 = f32[512,2448]{0,1:T(8,128)} reshape(f32[512,68,36]{0,2,1:T(8,128)} %broadcast_multiply_fusion) | data formatting | bytes 10027008 | tf_op jit(solution)/shard_map/mul | solution.py:175
  23.7 6.7 %reshape.1004 = f32[68,36,512]{2,1,0:T(8,128)} reshape(f32[2448,512]{1,0:T(8,128)} %bitcast.259) | data formatting | bytes 10027008 | tf_op jit(solution)/shard_map/reshape.275
  30.9 4.3 collective-permute-start.2
  35.2 1.3 collective-permute-start.3
  36.5 0.9 collective-permute-done.2
  37.4 4.3 collective-permute-done.3
  41.8 2.6 pad_maximum_fusion.1
  44.3 6.2 %reshape.1005 = f32[3,287232]{1,0:T(4,128)} reshape(f32[3,66,34,128]{3,2,1,0:T(8,128)} %pad_maximum_fusion.1) | data formatting | bytes 6893568 | tf_op jit(solution)/shard_map/reshape | solution.py:131
  50.5 46.6 %gather_fusion = f32[4096,3]{0,1:T(4,128)S(1)} fusion(f32[3,287232]{1,0:T(4,128)} %reshape.1005, s32[4096]{0:T(1024)S(1)} %broadcast_clamp_fusion), kind=kCustom, calls=%fused_computation | custom fusion | bytes 114688 | tf_op jit(solution)/shard_map/jit(_take)/gather | solution.py:147
  99.2 211.9 %all_gather.6 = f32[3,16384]{0,1:T(8,128)} all-gather(f32[3,512]{0,1:T(8,128)S(1)} %fusion.35), channel_id=1, replica_groups=mesh['gx'=8,'gy'=4] {'gx','gy'}, dimensions={1}, use_global_device_ids=true | all-gather | bytes 202752 | tf_op jit(solution)/shard_map/all_gather | solution.py:151
  311.2 4.1 gather_fusion.1
  316.7 121.0 %all-gather = f32[3,1,8192]{0,2,1:T(8,128)} all-gather(f32[3,1,256]{0,2,1:T(8,128)S(1)} %copy.110), channel_id=2, replica_groups=mesh['gx'=8,'gy'=4] {'gx','gy'}, dimensions={2}, use_global_device_ids=true | all-gather | bytes 101376 | tf_op jit(solution)/shard_map/all_gather | solution.py:166
  437.7 3.2 gather_fusion.2
  441.6 7.6 %convolution_bitcast_fusion.2 = f32[1,68,36,128]{3,2,1,0:T(8,128)S(1)} fusion(f32[68,36,512]{2,1,0:T(8,128)} %reshape.1004, f32[512]{0:T(512)S(1)} %bitcast.284, f32[512]{0:T(512)S(1)} %bitcast.287, f32[512]{0:T(512)S(1)} %bitcast.290, f32[512]{0:T(512)S(1)} %bitcast.281, s32[512]{0:T(512)S(1)} %bitcast.267, f32[512]{0:T(512)S(1)} %get-tuple-element.6), kind=kOutput, calls=%fused_computation.15 | convolution fusion | flops 1926037504 | bytes 6279168 | tf_op jit(solution)/shard_map/dot_general | solution.py:179
  449.2 4.7 convolution_bitcast_fusion.1
  453.9 4.7 convolution_bitcast_fusion
  458.7 1.3 collective-permute-start.4
  460.5 1.6 collective-permute-start.5
  462.1 1.9 collective-permute-done.5
  464.2 1.5 collective-permute-start.6
  465.7 2.2 fusion
  467.9 2.2 slice.380
  470.1 1.3 collective-permute-start.7
  472.2 6.7 %collective-permute-done.7 = f32[3,64,2,128]{3,2,1,0:T(2,128)S(1)} collective-permute-done((f32[3,64,2,128]{3,2,1,0:T(2,128)S(1)}, f32[3,64,2,128]{3,2,1,0:T(2,128)S(1)}, u32[]{:S(2)}, u32[]{:S(2)}) %collective-permute-start.7) | collective-permute-done | bytes 196640 | tf_op jit(solution)/shard_map/ppermute | solution.py:27
  478.9 1.9 fusion.60
  480.9 2.9 fusion.14
  483.8 2.9 fusion.10
  486.7 2.9 fusion.6
  489.6 2.0 pad_maximum_fusion.2
  (87 shorter events, 15.0 us)
Async XLA Ops:
  1.5 28.9 %collective-permute-start = (f32[3,1,32,128]{3,2,1,0:T(8,128)S(1)}, f32[3,1,32,128]{3,2,1,0:T(8,128)S(1)}, u32[]{:S(2)}, u32[]{:S(2)}) collective-permute-start(f32[3,1,32,128]{3,2,1,0:T(8,128)S(1)} %get-tuple-element.39), channel_id=1, source_target_pairs={{0,4},{4,8},{8,12},{12,16},{16,20},{20,24},{24,28},{1,5},{5,9},{9,... | collective-permute-start | bytes 147464 | tf_op jit(solution)/shard_map/ppermute | solution.py:24
  3.8 26.9 %collective-permute-start.1 = (f32[3,1,32,128]{3,2,1,0:T(8,128)S(1)}, f32[3,1,32,128]{3,2,1,0:T(8,128)S(1)}, u32[]{:S(2)}, u32[]{:S(2)}) collective-permute-start(f32[3,1,32,128]{3,2,1,0:T(8,128)S(1)} %get-tuple-element.38), channel_id=1, source_target_pairs={{4,0},{8,4},{12,8},{16,12},{20,16},{24,20},{28,24},{5,1},{9,5},{13... | collective-permute-start | bytes 147464 | tf_op jit(solution)/shard_map/ppermute | solution.py:27
  23.7 6.7 %copy-start = (f32[3,64,32,128]{3,2,1,0:T(8,128)S(1)}, f32[3,64,32,128]{3,2,1,0:T(8,128)}, u32[]{:S(2)}) copy-start(f32[3,64,32,128]{3,2,1,0:T(8,128)} %param.10) | copy-start | bytes 9437188
  30.9 6.5 %collective-permute-start.2 = (f32[3,66,1,128]{3,2,1,0:T(1,128)S(1)}, f32[3,66,1,128]{3,2,1,0:T(1,128)S(1)}, u32[]{:S(2)}, u32[]{:S(2)}) collective-permute-start(f32[3,66,1,128]{3,2,1,0:T(1,128)S(1)} %get-tuple-element.36), channel_id=1, source_target_pairs={{0,1},{1,2},{2,3},{4,5},{5,6},{6,7},{8,9},{9,10},{10,11},{12,13},{... | collective-permute-start | bytes 304136 | tf_op jit(solution)/shard_map/ppermute | solution.py:24
  35.2 6.5 %collective-permute-start.3 = (f32[3,66,1,128]{3,2,1,0:T(1,128)S(1)}, f32[3,66,1,128]{3,2,1,0:T(1,128)S(1)}, u32[]{:S(2)}, u32[]{:S(2)}) collective-permute-start(f32[3,66,1,128]{3,2,1,0:T(1,128)S(1)} %get-tuple-element.37), channel_id=1, source_target_pairs={{1,0},{2,1},{3,2},{5,4},{6,5},{7,6},{9,8},{10,9},{11,10},{13,12},{... | collective-permute-start | bytes 304136 | tf_op jit(solution)/shard_map/ppermute | solution.py:27
  99.2 216.1 %copy-start.3 = (f32[256]{0:T(256)S(1)}, f32[256]{0:T(256)}, u32[]{:S(2)}) copy-start(f32[256]{0:T(256)} %param.16) | copy-start | bytes 3076
  315.4 133.8 %slice-start = ((s8[5570560]{0:T(1024)(128)(4,1)}), s8[1376256]{0:T(1024)(128)(4,1)S(1)}, s32[]{:S(2)}) async-start(s8[5570560]{0:T(1024)(128)(4,1)} %bitcast.257), calls=%async_computation | async-start | bytes 2752512
  441.1 8.0 %slice-start.1 = ((s8[5570560]{0:T(1024)(128)(4,1)}), s8[4194304]{0:T(1024)(128)(4,1)S(1)}, s32[]{:S(2)}) async-start(s8[5570560]{0:T(1024)(128)(4,1)} %bitcast.257), calls=%async_computation.1 | async-start | bytes 8388608
  458.7 3.4 collective-permute-start.4
  460.5 5.2 %copy-start.2 = (f32[3,66,34,128]{3,2,1,0:T(8,128)S(1)}, f32[3,66,34,128]{3,2,1,0:T(8,128)}, u32[]{:S(2)}) copy-start(f32[3,66,34,128]{3,2,1,0:T(8,128)} %pad_maximum_fusion.1) | copy-start | bytes 10340356
  460.5 3.5 collective-permute-start.5
  464.2 7.2 %collective-permute-start.6 = (f32[3,64,2,128]{3,2,1,0:T(2,128)S(1)}, f32[3,64,2,128]{3,2,1,0:T(2,128)S(1)}, u32[]{:S(2)}, u32[]{:S(2)}) collective-permute-start(f32[3,64,2,128]{3,2,1,0:T(2,128)S(1)} %get-tuple-element.35), channel_id=1, source_target_pairs={{0,1},{1,2},{2,3},{4,5},{5,6},{6,7},{8,9},{9,10},{10,11},{12,13},{... | collective-permute-start | bytes 589832 | tf_op jit(solution)/shard_map/ppermute | solution.py:24
  467.9 13.0 %copy-start.1 = (f32[3,64,32,128]{3,2,1,0:T(8,128)S(1)}, f32[3,64,32,128]{3,2,1,0:T(8,128)}, u32[]{:S(2)}) copy-start(f32[3,64,32,128]{3,2,1,0:T(8,128)} %param.10) | copy-start | bytes 9437188
  470.1 8.8 %collective-permute-start.7 = (f32[3,64,2,128]{3,2,1,0:T(2,128)S(1)}, f32[3,64,2,128]{3,2,1,0:T(2,128)S(1)}, u32[]{:S(2)}, u32[]{:S(2)}) collective-permute-start(f32[3,64,2,128]{3,2,1,0:T(2,128)S(1)} %get-tuple-element.34), channel_id=1, source_target_pairs={{1,0},{2,1},{3,2},{5,4},{6,5},{7,6},{9,8},{10,9},{11,10},{13,12},{... | collective-permute-start | bytes 589832 | tf_op jit(solution)/shard_map/ppermute | solution.py:27
where the time goes:
time: 496 us; the launch traced here: 492 us
  blocking collectives  333 us (67%)
  local copies, waits for them, and re-layouts  83.7 us (17%)
  other arithmetic  26.9 us (5%)
  matrix products  17.5 us (4%)
  starting transfers between devices  14.9 us (3%)
  waiting for transfers between devices  13.9 us (3%)
    all_gather x1, blocking collectives, per_device(): shard_part = lax.all_gather(sampled, ('gx', 'gy'), axis=1, tiled=True)  212 us
    all_gather x1, blocking collectives, per_device(): shard_part = lax.all_gather(point_force, ('gx', 'gy'), axis=1, tiled=True)  121 us
    gather x2, local copies, waits for them, and re-layouts, per_device(): jnp.take(flat_field, jnp.concatenate(corner_index), axis=1)  47.2 us
    dot_general x3, matrix products, per_device(): lax.dot_general(plane_weights, line_loads, (((0,), (0,)), ((), ())), prec...  17 us
    ppermute x4, waiting for transfers between devices, with_halo(): lax.ppermute(lax.slice_in_dim(block, 0, width, axis=dim), axis, backward)  13 us
    another operation x4, other arithmetic, advance(): return jnp.stack(outputs)  10.7 us
  transfers between devices with their start and end apart: 8, of which 4 were waited for; matrix products, arithmetic and copies ran while one was open for 6% of the time, Pallas kernels for 0%

commit v1 on v0

v1 whole, which is shorter than its diff:
```python
import math

import jax
import jax.numpy as jnp
from jax import lax
from jax.experimental import pallas as pl
from jax.experimental.pallas import tpu as pltpu
from jax.sharding import PartitionSpec as P

CX = 64
CY = 32
CZ = 128
P_SIZE = 256
HOST = 512
PTS = 2 * P_SIZE

DT_STEP = 0.2
NU_VISC = 0.5
EPS_SQ = 1.44
CORE_SQ = 0.01

ROWS = 16
YROWS = 72
FACE_X = 3 * CY
FACE_Y = 3 * YROWS
RIM_Y = 2 * 3 * YROWS
RIM_X = 2 * 3 * CY

F32 = jnp.float32
BF16 = jnp.bfloat16
VM = pl.BlockSpec(memory_space=pltpu.MemorySpace.VMEM)
SM = pl.BlockSpec(memory_space=pltpu.MemorySpace.SMEM)
PARAMS = pltpu.CompilerParams(vmem_limit_bytes=48 * 1024 * 1024)

S_PX, S_PY, S_OKD, S_BRICK, S_B0, S_B1, S_KEY = range(7)


def call(body, outs, n_in, name, scratch=()):
    return pl.pallas_call(
        body,
        out_shape=[jax.ShapeDtypeStruct(s, F32) for s in outs],
        in_specs=[SM] + [VM] * (n_in - 1),
        out_specs=[VM] * len(outs),
        scratch_shapes=list(scratch),
        compiler_params=PARAMS,
        name=name,
    )


def split(value):
    high = value.astype(BF16)
    low = (value - high.astype(F32)).astype(BF16)
    return high, low


def dot3(a_high, a_low, b_high, b_low):
    def one(a, b):
        return jnp.dot(a, b, preferred_element_type=F32)

    return one(a_high, b_high) + (one(a_high, b_low) + one(a_low, b_high))


def stencil_body(scal, v_ref, out_ref, ylo_ref, yhi_ref):
    row = lax.broadcasted_iota(jnp.int32, (CY, CZ), 0)
    lane = lax.broadcasted_iota(jnp.int32, (CY, CZ), 1)

    def step(x, carry):
        has_plus = jnp.where(x < CX - 1, 1.0, 0.0)
        has_minus = jnp.where(x > 0, 1.0, 0.0)
        up = jnp.minimum(x + 1, CX - 1)
        down = jnp.maximum(x - 1, 0)
        v0 = v_ref[0, x]
        v1 = v_ref[1, x]
        v2 = v_ref[2, x]
        for c in range(3):
            mid = (v0, v1, v2)[c]
            xp = v_ref[c, up] * has_plus
            xm = v_ref[c, down] * has_minus
            yp = jnp.where(row == CY - 1, 0.0, pltpu.roll(mid, CY - 1, 0))
            ym = jnp.where(row == 0, 0.0, pltpu.roll(mid, 1, 0))
            zp = jnp.where(lane == CZ - 1, 0.0, pltpu.roll(mid, CZ - 1, 1))
            zm = jnp.where(lane == 0, 0.0, pltpu.roll(mid, 1, 1))
            transport = v0 * (xp - xm) * 0.5 + v1 * (yp - ym) * 0.5 + v2 * (zp - zm) * 0.5
            diffusion = xp + xm + yp + ym + zp + zm - 6.0 * mid
            out_ref[c, x] = mid + DT_STEP * (NU_VISC * diffusion - transport)
            ylo_ref[c, pl.ds(x, 1)] = mid[0:1]
            yhi_ref[c, pl.ds(x, 1)] = mid[CY - 1 : CY]
        return carry

    lax.fori_loop(0, CX, step, 0)


def ypack_body(n_gx, scal, ylo_ref, yhi_ref, face_a, face_b, own_ref, *rest):
    gathered, (pay_c, pay_d, blk_ref) = rest[:n_gx], rest[n_gx:]
    even_x = scal[S_PX] == 0
    even_y = scal[S_PY] == 0
    tail = jnp.zeros((YROWS - CX - 1, CZ), F32)
    for c in range(3):
        x_high = jnp.where(even_x, face_a[c * CY : c * CY + 1], face_b[c * CY : c * CY + 1])
        low = jnp.concatenate([ylo_ref[c], x_high, tail], axis=0)
        high = jnp.concatenate([yhi_ref[c], x_high, tail], axis=0)
        pay_c[c * YROWS : (c + 1) * YROWS] = jnp.where(even_y, high, low)
        pay_d[c * YROWS : (c + 1) * YROWS] = jnp.where(even_y, low, high)
    pieces = [own_ref[...], face_a[FACE_X : FACE_X + ROWS]] + [g[...] for g in gathered]
    blocks = jnp.concatenate(pieces, axis=0)
    blk_ref[...] = blocks
    pay_c[FACE_Y:] = blocks
    pay_d[FACE_Y:] = blocks


def sample_body(n_blk, scal, v_ref, cell_ref, frac_ref, face_a, face_b, rec_c, rec_d, blk_ref, *rest):
    others, (samp_ref, sel_ref, pts_ref) = rest[:n_blk], rest[n_blk:]
    b0, b1, brick = scal[S_B0], scal[S_B1], scal[S_BRICK]
    sources = [(blk_ref, 0), (rec_c, FACE_Y)]
    if rec_d.shape[0] > FACE_Y:
        sources.append((rec_d, FACE_Y))
    sources += [(o, 0) for o in others]
    keys, members, values = [], [], []
    for ref, first in sources:
        for k in range((ref.shape[0] - first) // ROWS):
            value = ref[first + k * ROWS : first + (k + 1) * ROWS]
            key = value[14:15, 0:1]
            home = key.astype(jnp.int32) // HOST
            keys.append(key)
            members.append((home == b0) | (home == b1))
            values.append(value)
    low_key = functools_min([jnp.where(m, k, 1e9) for k, m in zip(keys, members)], jnp.minimum)
    high_key = functools_min([jnp.where(m, k, -1.0) for k, m in zip(keys, members)], jnp.maximum)
    turbine_a = jnp.zeros((ROWS, CZ), F32)
    turbine_b = jnp.zeros((ROWS, CZ), F32)
    for key, value in zip(keys, values):
        turbine_a = jnp.where(key == low_key, value, turbine_a)
        turbine_b = jnp.where(key == high_key, value, turbine_b)
    sel = jnp.concatenate([turbine_a, turbine_b], axis=0)
    sel_ref[...] = sel
    turned = jnp.concatenate([sel, jnp.zeros((CZ - 2 * ROWS, CZ), F32)], axis=0).T

    def column(k):
        picks = (2 * k, 2 * k + 1, ROWS + 2 * k, ROWS + 2 * k + 1)
        return jnp.concatenate([turned[:, j : j + 1] for j in picks], axis=0)

    slot = column(7).astype(jnp.int32)
    mine = (slot // HOST) == brick
    local = jnp.where(mine, slot % HOST, -1)
    lane_s = lax.broadcasted_iota(jnp.int32, (PTS, HOST), 1)
    hit = lane_s == local
    code = ((cell_ref[0:1] * CY + cell_ref[1:2]) * CZ + cell_ref[2:3]).astype(F32)

    def pull(row):
        return jnp.sum(jnp.where(hit, row, 0.0), axis=1, keepdims=True)

    code_col = pull(code).astype(jnp.int32)
    fx, fy, fz = pull(frac_ref[0:1]), pull(frac_ref[1:2]), pull(frac_ref[2:3])
    x_col = jnp.where(mine, code_col // (CY * CZ), -100)
    y_col = (code_col // CZ) % CY
    z_col = code_col % CZ
    lane = lax.broadcasted_iota(jnp.int32, (PTS, CZ), 1)
    columns = (x_col.astype(F32), y_col.astype(F32), z_col.astype(F32), fx, fy, fz, column(0))
    table = jnp.zeros((PTS, CZ), F32)
    for k, col in enumerate(columns):
        table = jnp.where(lane == k, col, table)
    pts_ref[...] = table

    def weight(coord, base, frac):
        return jnp.where(coord == base, 1.0 - frac, jnp.where(coord == base + 1, frac, 0.0))

    wy = weight(lane % CY, y_col, fy)
    x_lane = lane // CY - x_col
    acc = None
    per = 4
    for j in range(CX * CY // (CZ * per)):
        parts = []
        for i in range(per):
            shift = (CZ // CY) * (j * per + i)
            wx = jnp.where(x_lane == -shift, 1.0 - fx, jnp.where(x_lane == 1 - shift, fx, 0.0))
            parts.append(wx * wy)
        w_high, w_low = split(jnp.concatenate(parts, axis=1))
        nx = CZ * per // CY
        rows = [v_ref[c, j * nx : (j + 1) * nx].reshape(nx * CY, CZ) for c in range(3)]
        f_high, f_low = split(jnp.concatenate(rows, axis=1))
        part = dot3(w_high, w_low, f_high, f_low)
        acc = part if acc is None else acc + part
    edge_x = jnp.where(lane < CY, CX, lane - CY)
    edge_y = jnp.where(lane < CY, lane, CY)
    edge_w = jnp.where(lane < CY + YROWS, weight(edge_x, x_col, fx) * weight(edge_y, y_col, fy), 0.0)
    even_x = scal[S_PX] == 0
    even_y = scal[S_PY] == 0
    ok_d = scal[S_OKD] == 1
    rows = []
    for c in range(3):
        plane = jnp.where(even_x, face_a[c * CY : (c + 1) * CY], face_b[c * CY : (c + 1) * CY])
        from_d = jnp.where(ok_d, rec_d[c * YROWS : (c + 1) * YROWS], 0.0)
        line = jnp.where(even_y, rec_c[c * YROWS : (c + 1) * YROWS], from_d)
        rows.append(jnp.concatenate([plane, line, jnp.zeros((CZ - CY - YROWS, CZ), F32)], axis=0))
    w_high, w_low = split(edge_w)
    f_high, f_low = split(jnp.concatenate(rows, axis=1))
    acc = acc + dot3(w_high, w_low, f_high, f_low)
    wz = weight(lane, z_col, fz)
    out = jnp.zeros((PTS, CZ), F32)
    for c in range(3):
        value = jnp.sum(acc[:, c * CZ : (c + 1) * CZ] * wz, axis=1, keepdims=True)
        out = jnp.where(lane == c, value, out)
    samp_ref[...] = out.T[0:8]


def functools_min(items, op):
    result = items[0]
    for item in items[1:]:
        result = op(result, item)
    return result


def weights_body(scal, pts_ref, gx_ref, gy_ref, pz_ref):
    table = pts_ref[...].T

    def offsets(frac):
        raw = [jnp.exp(-((o - frac) ** 2) / EPS_SQ) for o in (-1.0, 0.0, 1.0, 2.0)]
        total = (raw[0] + raw[1]) + (raw[2] + raw[3])
        return [value / total for value in raw]

    def profile(rows, inner, base, frac):
        index = lax.broadcasted_iota(jnp.int32, (rows, PTS), 0)
        late = index - inner
        index = jnp.where(index < inner, index, jnp.where(late < 2, late - 2, late - 2 + inner))
        rel = index - base.astype(jnp.int32)
        result = jnp.zeros((rows, PTS), F32)
        for k, w in enumerate(offsets(frac)):
            result = jnp.where(rel == k - 1, w, result)
        return result

    gx_ref[...] = profile(YROWS, CX, table[0:1], table[3:4])
    gy_ref[...] = profile(CY + 8, CY, table[1:2], table[4:5])
    wz = offsets(table[5:6])
    stack = jnp.concatenate(wz + [jnp.zeros((CZ - 4, PTS), F32)], axis=0).T
    z_rel = lax.broadcasted_iota(jnp.int32, (PTS, CZ), 1) - pts_ref[:, 2:3].astype(jnp.int32)
    pz = jnp.zeros((PTS, CZ), F32)
    for k in range(4):
        pz = jnp.where(z_rel == k - 1, stack[:, k : k + 1], pz)
    pz_ref[...] = pz


def attack(axial_flow, tangent, cos_twist, sin_twist):
    rel_speed = jnp.sqrt(axial_flow * axial_flow + tangent * tangent + 1.0)
    cos_phi = tangent / rel_speed
    sin_phi = axial_flow / rel_speed
    sin_alpha = sin_phi * cos_twist - cos_phi * sin_twist
    cos_alpha = cos_phi * cos_twist + sin_phi * sin_twist
    lift_coef = 2.0 * jnp.pi * sin_alpha * cos_alpha / (1.0 + 4.0 * sin_alpha * sin_alpha)
    drag_coef = 0.02 + 0.8 * sin_alpha * sin_alpha
    return rel_speed, cos_phi, sin_phi, lift_coef, drag_coef


def loads_body(scal, samp_ref, other_ref, sel_ref, pts_ref, gx_ref, gy_ref, pz_ref, lh_ref, pay_c, pay_d, ret_ref, xrim_ref):
    def row(k):
        picks = (2 * k, 2 * k + 1, ROWS + 2 * k, ROWS + 2 * k + 1)
        return jnp.concatenate([sel_ref[j : j + 1] for j in picks], axis=1)

    radius, chord, spin, cos_t, sin_t, cos_a, sin_a = [row(k) for k in range(7)]
    flow = samp_ref[...] + other_ref[...]
    axial = flow[0:1]
    tangent = spin - (cos_a * flow[2:3] - sin_a * flow[1:2])
    rel_speed, cos_phi, sin_phi, lift_coef, drag_coef = attack(axial, tangent, cos_t, sin_t)
    circ = 0.5 * chord * rel_speed * lift_coef
    parts = []
    for t in range(2):
        seg = slice(t * P_SIZE, (t + 1) * P_SIZE)
        spacing = radius[:, seg] - pts_ref[seg, 6:7]
        kernel = spacing / (spacing * spacing + CORE_SQ)
        lhs = jnp.concatenate([cos_a[:, seg] * circ[:, seg], sin_a[:, seg] * circ[:, seg], jnp.zeros((6, P_SIZE), F32)], axis=0)
        both = jnp.dot(lhs, kernel, preferred_element_type=F32, precision=lax.Precision.HIGHEST)
        parts.append((cos_a[:, seg] * both[0:1] + sin_a[:, seg] * both[1:2]) / (4.0 * math.pi))
    induced = jnp.concatenate(parts, axis=1)
    rel_speed, cos_phi, sin_phi, lift_coef, drag_coef = attack(axial + induced, tangent, cos_t, sin_t)
    dynamic = 0.5 * chord * rel_speed * rel_speed
    lift = dynamic * lift_coef
    drag = dynamic * drag_coef
    thrust = lift * cos_phi + drag * sin_phi
    torque = lift * sin_phi - drag * cos_phi
    force = [-thrust, torque * sin_a, -torque * cos_a]
    pieces = []
    for t in range(2):
        for c in range(3):
            for h in range(2):
                at = t * P_SIZE + h * CZ
                pieces.append(force[c][:, at : at + CZ])
        key = sel_ref[t * ROWS + 14 : t * ROWS + 15, 0:1]
        pieces.append(jnp.broadcast_to(key, (2, CZ)))
    blocks = jnp.concatenate(pieces, axis=0)
    ret_ref[...] = blocks
    pay_c[RIM_Y:] = blocks
    pay_d[RIM_Y:] = blocks
    cols = jnp.concatenate(force + [jnp.zeros((CZ - 3, PTS), F32)], axis=0).T
    pz = pz_ref[...] * DT_STEP
    lines = jnp.concatenate([cols[:, c : c + 1] * pz for c in range(3)], axis=1)
    l_high, l_low = split(lines)
    lh_ref[...] = lines
    gx = gx_ref[...]
    gy = gy_ref[...]
    planes = [gx * gy[CY + k : CY + k + 1] for k in range(4)]
    planes += [gx[CX + k : CX + k + 1] * gy[0:CY] for k in range(4)]
    w_high, w_low = split(jnp.concatenate(planes, axis=0))
    rim = dot3(w_high, w_low, l_high, l_low)
    even_y = scal[S_PY] == 0
    for k in range(2):
        for c in range(3):
            low = rim[k * YROWS : (k + 1) * YROWS, c * CZ : (c + 1) * CZ]
            high = rim[(k + 2) * YROWS : (k + 3) * YROWS, c * CZ : (c + 1) * CZ]
            at = (k * 3 + c) * YROWS
            pay_c[at : at + YROWS] = jnp.where(even_y, high, low)
            pay_d[at : at + YROWS] = jnp.where(even_y, low, high)
    first = 4 * YROWS
    for k in range(4):
        for c in range(3):
            at = (k * 3 + c) * CY
            xrim_ref[at : at + CY] = rim[first + k * CY : first + (k + 1) * CY, c * CZ : (c + 1) * CZ]


SPREAD_X = 16


def spread_body(lines_ref, gx_ref, gy_ref, base_ref, out_ref, lh, ll):
    @pl.when(pl.program_id(0) == 0)
    def _():
        high, low = split(lines_ref[...])
        lh[...] = high
        ll[...] = low

    first = pl.multiple_of(pl.program_id(0) * SPREAD_X, SPREAD_X)
    gx = gx_ref[pl.ds(first, SPREAD_X)]
    gy = gy_ref[0:CY]
    planes = jnp.concatenate([gx[i : i + 1] * gy for i in range(SPREAD_X)], axis=0)
    w_high, w_low = split(planes)
    value = dot3(w_high, w_low, lh[...], ll[...])
    for c in range(3):
        out_ref[c] = base_ref[c] + value[:, c * CZ : (c + 1) * CZ].reshape(SPREAD_X, CY, CZ)


def spread(lines, gx, gy, base):
    whole = lambda i: (0, 0)
    block = pl.BlockSpec((3, SPREAD_X, CY, CZ), lambda i: (0, i, 0, 0))
    return pl.pallas_call(
        spread_body,
        out_shape=jax.ShapeDtypeStruct(base.shape, F32),
        grid=(CX // SPREAD_X,),
        in_specs=[
            pl.BlockSpec(lines.shape, whole),
            pl.BlockSpec(gx.shape, whole),
            pl.BlockSpec(gy.shape, whole),
            block,
        ],
        out_specs=block,
        scratch_shapes=[pltpu.VMEM((PTS, 3 * CZ), BF16)] * 2,
        compiler_params=PARAMS,
        name="spread",
    )(lines, gx, gy, base)


def xpack_body(scal, xrim_ref, rec_c, rec_d, pay_a, pay_b):
    even_x = scal[S_PX] == 0
    even_y = scal[S_PY] == 0
    ok_d = scal[S_OKD] == 1
    zero = jnp.zeros((CY - 4, CZ), F32)
    for k in range(2):
        sides = []
        for s in range(2):
            sides.append([])
            for c in range(3):
                near, far = [], []
                for y in range(2):
                    at = (y * 3 + c) * YROWS + CX + 2 * s + k
                    from_c = rec_c[at : at + 1]
                    from_d = jnp.where(ok_d, rec_d[at : at + 1], 0.0)
                    near.append(jnp.where(even_y, from_d, from_c))
                    far.append(jnp.where(even_y, from_c, from_d))
                at = ((2 * s + k) * 3 + c) * CY
                sides[s].append(xrim_ref[at : at + CY] + jnp.concatenate(near + [zero] + far, axis=0))
        for c in range(3):
            at = (k * 3 + c) * CY
            pay_a[at : at + CY] = jnp.where(even_x, sides[1][c], sides[0][c])
            pay_b[at : at + CY] = jnp.where(even_x, sides[0][c], sides[1][c])


def final_body(n_ret, scal, main_ref, v_ref, face_a, face_b, yc_ref, yd_ref, rim_a, rim_b, rim_c, rim_d, *rest):
    rets, (out_ref, pf_ref) = rest[:n_ret], rest[n_ret:]
    even_x = scal[S_PX] == 0
    even_y = scal[S_PY] == 0
    ok_d = scal[S_OKD] == 1
    coef = DT_STEP * 0.5
    out_ref[...] = main_ref[...]
    for c in range(3):
        rows = slice(c * CY, (c + 1) * CY)
        a, b = face_a[rows], face_b[rows]
        x_low = jnp.where(even_x, b, a)
        x_high = jnp.where(even_x, a, b)
        out_ref[c, 0] += coef * x_low * (2.0 * NU_VISC + v_ref[0, 0])
        out_ref[c, CX - 1] += coef * x_high * (2.0 * NU_VISC - v_ref[0, CX - 1])
        for k in range(2):
            rows = slice((k * 3 + c) * CY, (k * 3 + c + 1) * CY)
            a, b = rim_a[rows], rim_b[rows]
            out_ref[c, k] += jnp.where(even_x, b, a)
            out_ref[c, CX - 2 + k] += jnp.where(even_x, a, b)
        rows = slice(c * YROWS, c * YROWS + CX)
        a, b = yc_ref[rows], jnp.where(ok_d, yd_ref[rows], 0.0)
        y_low = jnp.where(even_y, b, a)
        y_high = jnp.where(even_y, a, b)
        out_ref[c, :, 0, :] += coef * y_low * (2.0 * NU_VISC + v_ref[1, :, 0, :])
        out_ref[c, :, CY - 1, :] += coef * y_high * (2.0 * NU_VISC - v_ref[1, :, CY - 1, :])
        for k in range(2):
            at = (k * 3 + c) * YROWS
            a, b = rim_c[at : at + CX], jnp.where(ok_d, rim_d[at : at + CX], 0.0)
            out_ref[c, :, k, :] += jnp.where(even_y, b, a)
            out_ref[c, :, CY - 2 + k, :] += jnp.where(even_y, a, b)
    mine = scal[S_KEY].astype(F32)
    found = jnp.zeros((8, CZ), F32)
    for ref in rets:
        for k in range(ref.shape[0] // 8):
            value = ref[8 * k : 8 * k + 8]
            found = jnp.where(value[6:7, 0:1] == mine, value, found)
    for c in range(3):
        pf_ref[c : c + 1] = jnp.concatenate([found[2 * c : 2 * c + 1], found[2 * c + 1 : 2 * c + 2]], axis=1)


def per_device(
    velocity,
    host_cell,
    host_frac,
    host_dst,
    owner_src,
    rotor_speed,
    blade_radius,
    blade_chord,
    blade_twist,
    blade_angle,
):
    nx, ny = lax.axis_size("gx"), lax.axis_size("gy")
    ix, iy = lax.axis_index("gx"), lax.axis_index("gy")
    px, py = ix % 2, iy % 2
    merged = ny == 4

    def flip(n, bits):
        return [(i, i ^ bits) for i in range(n)]

    def odd_pairs(n):
        up = [(i, i + 1) for i in range(1, n - 1, 2)]
        return up + [(t, s) for s, t in up]

    ok_d = jnp.where(py == 0, iy > 0, iy < ny - 1).astype(jnp.int32)
    low_brick = (ix - px) * ny + iy
    scal = jnp.stack([px, py, ok_d, ix * ny + iy, low_brick, low_brick + ny, owner_src[0]]).astype(jnp.int32)

    block = jnp.concatenate(
        [
            value.reshape(2, CZ)
            for value in (
                blade_radius,
                blade_chord,
                rotor_speed * blade_radius,
                jnp.cos(blade_twist),
                jnp.sin(blade_twist),
                jnp.cos(blade_angle),
                jnp.sin(blade_angle),
                owner_src.astype(F32),
            )
        ],
        axis=0,
    )
    edge_a = lax.dynamic_slice_in_dim(velocity, (CX - 1) * (1 - px), 1, axis=1).reshape(FACE_X, CZ)
    edge_b = lax.dynamic_slice_in_dim(velocity, (CX - 1) * px, 1, axis=1).reshape(FACE_X, CZ)
    face_a = lax.ppermute(jnp.concatenate([edge_a, block], axis=0), "gx", flip(nx, 1))
    face_b = lax.ppermute(edge_b, "gx", odd_pairs(nx))
    base, ylo, yhi = call(stencil_body, [velocity.shape, (3, CX, CZ), (3, CX, CZ)], 2, "stencil")(scal, velocity)
    pair = jnp.concatenate([block, face_a[FACE_X:]], axis=0)
    gathered = [lax.ppermute(pair, "gx", flip(nx, 2 * o)) for o in range(1, nx // 2)]
    n_rows = nx * ROWS
    pay_c, pay_d, blocks = call(
        lambda *refs: ypack_body(len(gathered), *refs),
        [(FACE_Y + n_rows, CZ), (FACE_Y + n_rows, CZ), (n_rows, CZ)],
        6 + len(gathered),
        "ypack",
    )(scal, ylo, yhi, face_a, face_b, block, *gathered)
    rec_c = lax.ppermute(pay_c, "gy", flip(ny, 1))
    if merged:
        rec_d = lax.ppermute(pay_d, "gy", flip(ny, 3))
    else:
        rec_d = lax.ppermute(pay_d[:FACE_Y], "gy", odd_pairs(ny))
    bits = [o for o in range(2, ny) if not (merged and o == 3)]
    others = [lax.ppermute(blocks, "gy", flip(ny, o)) for o in bits]
    samp, sel, pts = call(
        lambda *refs: sample_body(len(others), *refs),
        [(8, PTS), (2 * ROWS, CZ), (PTS, CZ)],
        9 + len(others),
        "sample",
    )(scal, velocity, host_cell, host_frac, face_a, face_b, rec_c, rec_d, blocks, *others)
    other = lax.ppermute(samp, "gx", flip(nx, 1))
    gx, gy, pz = call(weights_body, [(YROWS, PTS), (CY + 8, PTS), (PTS, CZ)], 2, "weights")(scal, pts)
    lines, pay_c, pay_d, ret, xrim = call(
        loads_body,
        [(PTS, 3 * CZ), (RIM_Y + ROWS, CZ), (RIM_Y + ROWS, CZ), (ROWS, CZ), (2 * RIM_X, CZ)],
        8,
        "loads",
    )(scal, samp, other, sel, pts, gx, gy, pz)
    rim_c = lax.ppermute(pay_c, "gy", flip(ny, 1))
    if merged:
        rim_d = lax.ppermute(pay_d, "gy", flip(ny, 3))
        back = [ret, rim_c[RIM_Y:], rim_d[RIM_Y:]]
    else:
        rim_d = lax.ppermute(pay_d[:RIM_Y], "gy", odd_pairs(ny))
        back = [ret, rim_c[RIM_Y:]]
    back += [lax.ppermute(ret, "gy", flip(ny, o)) for o in bits]
    back = jnp.concatenate(back, axis=0)
    main = spread(lines, gx, gy, base)
    pay_a, pay_b = call(xpack_body, [(RIM_X, CZ)] * 2, 4, "xpack")(scal, xrim, rim_c, rim_d)
    rim_a = lax.ppermute(pay_a, "gx", flip(nx, 1))
    rim_b = lax.ppermute(pay_b, "gx", odd_pairs(nx))
    rets = [back] + [lax.ppermute(back, "gx", flip(nx, 2 * o)) for o in range(1, nx // 2)]
    return tuple(
        call(lambda *refs: final_body(len(rets), *refs), [velocity.shape, (3, P_SIZE)], 11 + len(rets), "final")(
            scal, main, velocity, face_a, face_b, rec_c, rec_d, rim_a, rim_b, rim_c, rim_d, *rets
        )
    )


def solution(mesh):
    return jax.shard_map(
        per_device,
        mesh=mesh,
        in_specs=(
            P(None, "gx", "gy", None),
            P(None, ("gx", "gy")),
            P(None, ("gx", "gy")),
            P(("gx", "gy")),
            P(("gx", "gy")),
            P(("gx", "gy")),
            P(("gx", "gy")),
            P(("gx", "gy")),
            P(("gx", "gy")),
            P(("gx", "gy")),
        ),
        out_specs=(P(None, "gx", "gy", None), P(None, ("gx", "gy"))),
        check_vma=False,
    )
```

time: 496 us -> 84.6 us (0.17)
  blocking collectives: 333 us -> 0 us
  local copies, waits for them, and re-layouts: 83.7 us -> 7.3 us
  Pallas kernels: 0 us -> 30 us
  other arithmetic: 26.9 us -> 1.51 us
  matrix products: 17.5 us -> 0 us
  waiting for transfers between devices: 13.9 us -> 21.5 us
  starting transfers between devices: 14.9 us -> 22.2 us
    all_gather x2 -> x0, blocking collectives: 333 us -> none  [the longest x1 212 us: per_device(): shard_part = lax.all_gather(sampled, ('gx', 'gy'), axis=1, tiled=True)]
    gather x5 -> x0, local copies, waits for them, and re-layouts: 54.6 us -> none  [the longest x2 47.2 us: per_device(): jnp.take(flat_field, jnp.concatenate(corner_index), axis=1)]
    pallas_call x0 -> x8, Pallas kernels: none -> 30 us  [the longest x1 8.44 us: per_device(): call(stencil_body, [velocity.shape, (3, CX, CZ), (3, CX, CZ)], 2, 'stencil')]
    dot_general x4 -> x0, matrix products: 17.5 us -> none  [the longest x3 17 us: per_device(): lax.dot_general(plane_weights, line_loads, (((0,), (0,)), ((), ())), prec...]
    another operation x9 -> x0, other arithmetic: 11 us -> none  [the longest x4 10.7 us: advance(): return jnp.stack(outputs)]
    ppermute x8 -> x17, waiting for transfers between devices: 13.9 us -> 21.5 us  [the longest x1 10.7 us: per_device(): others = [lax.ppermute(blocks, 'gy', flip(ny, o)) for o in bits]]
    ppermute x8 -> x17, starting transfers between devices: 14.9 us -> 22.2 us  [the longest x3 6.62 us: per_device(): lax.ppermute(pair, 'gx', flip(nx, 2 * o))]
    mul x1 -> x0, local copies, waits for them, and re-layouts: 6.59 us -> none  [per_device(): profile_x[:, :, None] * profile_y[:, None, :]]
  transfers between devices with their start and end apart: 8 -> 17, of which waited for: 4 -> 4; matrix products, arithmetic and copies ran while one was open for 6% -> 4% of each run, Pallas kernels for 0% -> 19%
where the time goes in v1:
time: 84.6 us; the launch traced here: 84.2 us
  Pallas kernels  30 us (35%)
  starting transfers between devices  22.2 us (26%)
  waiting for transfers between devices  21.5 us (25%)
  local copies, waits for them, and re-layouts  7.3 us (9%)
  between operations  1.71 us (2%)
  other arithmetic  1.51 us (2%)
    ppermute x1, waiting for transfers between devices, per_device(): others = [lax.ppermute(blocks, 'gy', flip(ny, o)) for o in bits]  10.7 us
    pallas_call x1, Pallas kernels, per_device(): call(stencil_body, [velocity.shape, (3, CX, CZ), (3, CX, CZ)], 2, 'stencil')  8.44 us
    ppermute x3, starting transfers between devices, per_device(): lax.ppermute(pair, 'gx', flip(nx, 2 * o))  6.62 us
    pallas_call x1, Pallas kernels, per_device(): call(lambda *refs: sample_body(len(others), *refs), [(8, PTS), (2 * ROWS,...  6.04 us
    ppermute x1, waiting for transfers between devices, per_device(): rim_d = lax.ppermute(pay_d, 'gy', flip(ny, 3))  6 us
    ppermute x3, starting transfers between devices, per_device(): lax.ppermute(back, 'gx', flip(nx, 2 * o))  5.83 us
    pallas_call x1, Pallas kernels, spread(): pl.pallas_call(spread_body, out_shape=jax.ShapeDtypeStruct(base.shape, F3...  5.56 us
    pallas_call x1, Pallas kernels, per_device(): call(lambda *refs: final_body(len(rets), *refs), [velocity.shape, (3, P_S...  5.22 us
  transfers between devices with their start and end apart: 17, of which 4 were waited for; matrix products, arithmetic and copies ran while one was open for 4% of the time, Pallas kernels for 19%

profile of v1, /device:TPU:0, one launch (start us, length us, event | category | flops | bytes accessed | tf_op | source)
XLA Modules:
  0.0 84.2 jit_solution(1350083205682688570)
XLA Ops:
  1.5 0.8 convert_bitcast_fusion
  2.3 0.7 multiply_bitcast_fusion
  3.0 0.7 sine_bitcast_fusion
  3.7 0.8 %constant_dynamic-slice_fusion = (f32[3,1,32,128]{3,2,1,0:T(8,128)S(1)}, f32[3,1,32,128]{3,2,1,0:T(8,128)S(1)}) fusion(f32[3,64,32,128]{3,2,1,0:T(8,128)} %refs_2_.3, s32[]{:T(128)S(6)} %select_n.25, s32[]{:T(128)S(6)} %select_n.24), kind=kLoop, calls=%fused_computation.7 | loop fusion | bytes 196616 | tf_op jit(solution)/shard_map/dynamic_slice | solution.py:468
  4.6 0.7 concatenate.14
  5.3 0.5 collective-permute-start
  5.8 0.7 collective-permute-start.1
  6.7 0.7 concatenate.16
  7.5 5.2 %collective-permute-start.4 = (f32[32,128]{1,0:T(8,128)S(1)}, f32[32,128]{1,0:T(8,128)S(1)}, u32[]{:S(2)}, u32[]{:S(2)}) collective-permute-start(f32[32,128]{1,0:T(8,128)S(1)} %concatenate.16), channel_id=1, source_target_pairs={{0,24},{4,28},{8,16},{12,20},{16,8},{20,12},{24,0},{28,4},{1,25},{... | collective-permute-start | bytes 49160 | tf_op jit(solution)/shard_map/ppermute | solution.py:473
  12.7 1.4 %collective-permute-start.2 = (f32[32,128]{1,0:T(8,128)S(1)}, f32[32,128]{1,0:T(8,128)S(1)}, u32[]{:S(2)}, u32[]{:S(2)}) collective-permute-start(f32[32,128]{1,0:T(8,128)S(1)} %concatenate.16), channel_id=1, source_target_pairs={{0,8},{4,12},{8,0},{12,4},{16,24},{20,28},{24,16},{28,20},{1,9},{5... | collective-permute-start | bytes 49160 | tf_op jit(solution)/shard_map/ppermute | solution.py:473
  14.1 1.2 %slice.12 = s32[1]{0:T(128)} slice(s32[256]{0:T(256)} %param.13), slice={[0:1]} | slice | bytes 8 | tf_op jit(solution)/shard_map/slice | solution.py:449
  15.3 0.7 concatenate.15.refs_5_
  16.0 0.7 stack.31.scal.refs_0_
  16.7 8.4 %stencil.1 = (f32[3,64,32,128]{3,2,1,0:T(8,128)S(1)}, f32[3,64,128]{2,1,0:T(8,128)S(1)}, f32[3,64,128]{2,1,0:T(8,128)S(1)}) custom-call(s32[7]{0:T(128)S(1)} %stack.31.scal.refs_0_, f32[3,64,32,128]{3,2,1,0:T(8,128)} %refs_2_.3), custom_call_target="tpu_custom_call" | custom-call | tf_op jit(solution)/shard_map/stencil/pallas_call | solution.py:471
  25.1 1.7 %copy-done.1 = f32[3,64,32,128]{3,2,1,0:T(8,128)} copy-done((f32[3,64,32,128]{3,2,1,0:T(8,128)}, f32[3,64,32,128]{3,2,1,0:T(8,128)S(1)}, u32[]{:S(2)}) %copy-start.1) | copy-done | bytes 3145752
  26.8 0.6 ypack.1
  27.4 1.6 %collective-permute-start.5 = (f32[344,128]{1,0:T(8,128)S(1)}, f32[344,128]{1,0:T(8,128)S(1)}, u32[]{:S(2)}, u32[]{:S(2)}) collective-permute-start(f32[344,128]{1,0:T(8,128)S(1)} %get-tuple-element.23), channel_id=1, source_target_pairs={{0,1},{1,0},{2,3},{3,2},{4,5},{5,4},{6,7},{7,6},{8,9},{9,8},{10,11... | collective-permute-start | bytes 528392 | tf_op jit(solution)/shard_map/ppermute | solution.py:481
  29.0 2.5 %collective-permute-start.6 = (f32[344,128]{1,0:T(8,128)S(1)}, f32[344,128]{1,0:T(8,128)S(1)}, u32[]{:S(2)}, u32[]{:S(2)}) collective-permute-start(f32[344,128]{1,0:T(8,128)S(1)} %get-tuple-element.24), channel_id=1, source_target_pairs={{0,3},{1,2},{2,1},{3,0},{4,7},{5,6},{6,5},{7,4},{8,11},{9,10},{10,... | collective-permute-start | bytes 528392 | tf_op jit(solution)/shard_map/ppermute | solution.py:483
  31.6 10.7 %collective-permute-done.7.refs_9_ = f32[128,128]{1,0:T(8,128)S(1)} collective-permute-done((f32[128,128]{1,0:T(8,128)S(1)}, f32[128,128]{1,0:T(8,128)S(1)}, u32[]{:S(2)}, u32[]{:S(2)}) %collective-permute-start.7) | collective-permute-done | bytes 65568 | tf_op jit(solution)/shard_map/ppermute | solution.py:487
  42.3 6.0 %sample.1 = (f32[8,512]{1,0:T(8,128)S(1)}, f32[32,128]{1,0:T(8,128)S(1)}, f32[512,128]{1,0:T(8,128)S(1)}) custom-call(s32[7]{0:T(128)S(1)} %stack.31.scal.refs_0_, f32[3,64,32,128]{3,2,1,0:T(8,128)S(1)} %copy-done, s32[3,512]{1,0:T(4,128)S(1)} %copy-done.2, f32[3,512]{1,0:T(4,128)S(1)} %copy-done.3, f32[112,128]{1,0:T(8,128)S(1)} %collective-permute-done.refs_3_.refs_4_, ...), custom_call_target="tpu_custom_call" | custom-call | tf_op jit(solution)/shard_map/sample/pallas_call | solution.py:488
  48.4 1.2 %weights.1 = (f32[72,512]{1,0:T(8,128)S(1)}, f32[40,512]{1,0:T(8,128)S(1)}, f32[512,128]{1,0:T(8,128)S(1)}) custom-call(s32[7]{0:T(128)S(1)} %stack.31.scal.refs_0_, f32[512,128]{1,0:T(8,128)S(1)} %get-tuple-element.28.pts_ref), custom_call_target="tpu_custom_call" | custom-call | tf_op jit(solution)/shard_map/weights/pallas_call | solution.py:495
  49.6 2.4 %loads.1 = (f32[512,384]{1,0:T(8,128)S(1)}, f32[448,128]{1,0:T(8,128)S(1)}, f32[448,128]{1,0:T(8,128)S(1)}, f32[16,128]{1,0:T(8,128)S(1)}, f32[384,128]{1,0:T(8,128)S(1)}) custom-call(s32[7]{0:T(128)S(1)} %stack.31.scal.refs_0_, f32[8,512]{1,0:T(8,128)S(1)} %get-tuple-element.26.samp_ref, f32[8,512]{1,0:T(8,128)S(1)} %collective-permute-done.8.other_ref, ...), custom_call_target="tpu_custom_call" | custom-call | tf_op jit(solution)/shard_map/loads/pallas_call | solution.py:496
  52.1 2.7 %collective-permute-start.10 = (f32[448,128]{1,0:T(8,128)S(1)}, f32[448,128]{1,0:T(8,128)S(1)}, u32[]{:S(2)}, u32[]{:S(2)}) collective-permute-start(f32[448,128]{1,0:T(8,128)S(1)} %get-tuple-element.36), channel_id=1, source_target_pairs={{0,3},{1,2},{2,1},{3,0},{4,7},{5,6},{6,5},{7,4},{8,11},{9,10},{10,... | collective-permute-start | bytes 688136 | tf_op jit(solution)/shard_map/ppermute | solution.py:504
  54.8 0.8 collective-permute-start.13
  55.6 4.5 %collective-permute-done.9.rec_c.refs_9_ = f32[448,128]{1,0:T(8,128)S(1)} collective-permute-done((f32[448,128]{1,0:T(8,128)S(1)}, f32[448,128]{1,0:T(8,128)S(1)}, u32[]{:S(2)}, u32[]{:S(2)}) %collective-permute-start.9) | collective-permute-done | bytes 229408 | tf_op jit(solution)/shard_map/ppermute | solution.py:502
  60.1 6.0 %collective-permute-done.10.rec_d.refs_10_ = f32[448,128]{1,0:T(8,128)S(1)} collective-permute-done((f32[448,128]{1,0:T(8,128)S(1)}, f32[448,128]{1,0:T(8,128)S(1)}, u32[]{:S(2)}, u32[]{:S(2)}) %collective-permute-start.10) | collective-permute-done | bytes 229408 | tf_op jit(solution)/shard_map/ppermute | solution.py:504
  66.1 0.6 xpack.1
  66.8 0.7 collective-permute-start.12
  67.5 4.4 %collective-permute-start.16 = (f32[64,128]{1,0:T(8,128)S(1)}, f32[64,128]{1,0:T(8,128)S(1)}, u32[]{:S(2)}, u32[]{:S(2)}) collective-permute-start(f32[64,128]{1,0:T(8,128)S(1)} %pad_maximum_fusion.refs_11_), channel_id=1, source_target_pairs={{0,24},{4,28},{8,16},{12,20},{16,8},{20,12},{24,0},{28,4},{1,25},{... | collective-permute-start | bytes 98312 | tf_op jit(solution)/shard_map/ppermute | solution.py:515
  72.4 0.9 %collective-permute-start.14 = (f32[64,128]{1,0:T(8,128)S(1)}, f32[64,128]{1,0:T(8,128)S(1)}, u32[]{:S(2)}, u32[]{:S(2)}) collective-permute-start(f32[64,128]{1,0:T(8,128)S(1)} %pad_maximum_fusion.refs_11_), channel_id=1, source_target_pairs={{0,8},{4,12},{8,0},{12,4},{16,24},{20,28},{24,16},{28,20},{1,9},{5... | collective-permute-start | bytes 98312 | tf_op jit(solution)/shard_map/ppermute | solution.py:515
  73.3 5.6 %spread.1.refs_1_ = f32[3,64,32,128]{3,2,1,0:T(8,128)S(1)} custom-call(f32[512,384]{1,0:T(8,128)S(1)} %get-tuple-element.32.lines_ref, f32[72,512]{1,0:T(8,128)S(1)} %get-tuple-element.29.gx_ref, f32[40,512]{1,0:T(8,128)S(1)} %get-tuple-element.30.gy_ref, f32[3,64,32,128]{3,2,1,0:T(8,128)} %copy-done.1), custom_call_target="tpu_custom_call" | custom-call | tf_op jit(solution)/shard_map/spread/pallas_call | solution.py:341
  78.9 5.2 %final.1 = (f32[3,64,32,128]{3,2,1,0:T(8,128)}, f32[3,256]{1,0:T(4,128)}) custom-call(s32[7]{0:T(128)S(1)} %stack.31.scal.refs_0_, f32[3,64,32,128]{3,2,1,0:T(8,128)S(1)} %spread.1.refs_1_, f32[3,64,32,128]{3,2,1,0:T(8,128)} %refs_2_.3, f32[112,128]{1,0:T(8,128)S(1)} %collective-permute-done.refs_3_.refs_4_, ...), custom_call_target="tpu_custom_call" | custom-call | tf_op jit(solution)/shard_map/final/pallas_call | solution.py:517
  (31 shorter events, 1.2 us)
Async XLA Ops:
  0.6 41.7 %copy-start = (f32[3,64,32,128]{3,2,1,0:T(8,128)S(1)}, f32[3,64,32,128]{3,2,1,0:T(8,128)}, u32[]{:S(2)}) copy-start(f32[3,64,32,128]{3,2,1,0:T(8,128)} %refs_2_.3) | copy-start | bytes 9437188
  0.6 41.7 %copy-start.3 = (f32[3,512]{1,0:T(4,128)S(1)}, f32[3,512]{1,0:T(4,128)}, u32[]{:S(2)}) copy-start(f32[3,512]{1,0:T(4,128)} %refs_3_.1) | copy-start | bytes 18436
  0.7 41.7 %copy-start.2 = (s32[3,512]{1,0:T(4,128)S(1)}, s32[3,512]{1,0:T(4,128)}, u32[]{:S(2)}) copy-start(s32[3,512]{1,0:T(4,128)} %refs_2_.2) | copy-start | bytes 18436
  5.3 1.4 %collective-permute-start = (f32[112,128]{1,0:T(8,128)S(1)}, f32[112,128]{1,0:T(8,128)S(1)}, u32[]{:S(2)}, u32[]{:S(2)}) collective-permute-start(f32[112,128]{1,0:T(8,128)S(1)} %concatenate.14), channel_id=1, source_target_pairs={{0,4},{4,0},{8,12},{12,8},{16,20},{20,16},{24,28},{28,24},{1,5},{5... | collective-permute-start | bytes 172040 | tf_op jit(solution)/shard_map/ppermute | solution.py:469
  5.8 20.9 %collective-permute-start.1 = (f32[96,128]{1,0:T(8,128)S(1)}, f32[96,128]{1,0:T(8,128)S(1)}, u32[]{:S(2)}, u32[]{:S(2)}) collective-permute-start(f32[96,128]{1,0:T(8,128)S(1)} %bitcast.25), channel_id=1, source_target_pairs={{4,8},{12,16},{20,24},{8,4},{16,12},{24,20},{5,9},{13,17},{21,25},... | collective-permute-start | bytes 147464 | tf_op jit(solution)/shard_map/ppermute | solution.py:470
  7.5 19.3 %collective-permute-start.4 = (f32[32,128]{1,0:T(8,128)S(1)}, f32[32,128]{1,0:T(8,128)S(1)}, u32[]{:S(2)}, u32[]{:S(2)}) collective-permute-start(f32[32,128]{1,0:T(8,128)S(1)} %concatenate.16), channel_id=1, source_target_pairs={{0,24},{4,28},{8,16},{12,20},{16,8},{20,12},{24,0},{28,4},{1,25},{... | collective-permute-start | bytes 49160 | tf_op jit(solution)/shard_map/ppermute | solution.py:473
  12.6 14.1 %collective-permute-start.3 = (f32[32,128]{1,0:T(8,128)S(1)}, f32[32,128]{1,0:T(8,128)S(1)}, u32[]{:S(2)}, u32[]{:S(2)}) collective-permute-start(f32[32,128]{1,0:T(8,128)S(1)} %concatenate.16), channel_id=1, source_target_pairs={{0,16},{4,20},{8,24},{12,28},{16,0},{20,4},{24,8},{28,12},{1,17},{... | collective-permute-start | bytes 49160 | tf_op jit(solution)/shard_map/ppermute | solution.py:473
  12.7 14.1 %collective-permute-start.2 = (f32[32,128]{1,0:T(8,128)S(1)}, f32[32,128]{1,0:T(8,128)S(1)}, u32[]{:S(2)}, u32[]{:S(2)}) collective-permute-start(f32[32,128]{1,0:T(8,128)S(1)} %concatenate.16), channel_id=1, source_target_pairs={{0,8},{4,12},{8,0},{12,4},{16,24},{20,28},{24,16},{28,20},{1,9},{5... | collective-permute-start | bytes 49160 | tf_op jit(solution)/shard_map/ppermute | solution.py:473
  25.1 1.7 %copy-start.1 = (f32[3,64,32,128]{3,2,1,0:T(8,128)}, f32[3,64,32,128]{3,2,1,0:T(8,128)S(1)}, u32[]{:S(2)}) copy-start(f32[3,64,32,128]{3,2,1,0:T(8,128)S(1)} %get-tuple-element.33.base_ref) | copy-start | bytes 9437188
  27.4 14.9 %collective-permute-start.5 = (f32[344,128]{1,0:T(8,128)S(1)}, f32[344,128]{1,0:T(8,128)S(1)}, u32[]{:S(2)}, u32[]{:S(2)}) collective-permute-start(f32[344,128]{1,0:T(8,128)S(1)} %get-tuple-element.23), channel_id=1, source_target_pairs={{0,1},{1,0},{2,3},{3,2},{4,5},{5,4},{6,7},{7,6},{8,9},{9,8},{10,11... | collective-permute-start | bytes 528392 | tf_op jit(solution)/shard_map/ppermute | solution.py:481
  29.0 13.3 %collective-permute-start.6 = (f32[344,128]{1,0:T(8,128)S(1)}, f32[344,128]{1,0:T(8,128)S(1)}, u32[]{:S(2)}, u32[]{:S(2)}) collective-permute-start(f32[344,128]{1,0:T(8,128)S(1)} %get-tuple-element.24), channel_id=1, source_target_pairs={{0,3},{1,2},{2,1},{3,0},{4,7},{5,6},{6,5},{7,4},{8,11},{9,10},{10,... | collective-permute-start | bytes 528392 | tf_op jit(solution)/shard_map/ppermute | solution.py:483
  31.5 10.8 %collective-permute-start.7 = (f32[128,128]{1,0:T(8,128)S(1)}, f32[128,128]{1,0:T(8,128)S(1)}, u32[]{:S(2)}, u32[]{:S(2)}) collective-permute-start(f32[128,128]{1,0:T(8,128)S(1)} %get-tuple-element.25.refs_8_), channel_id=1, source_target_pairs={{0,2},{1,3},{2,0},{3,1},{4,6},{5,7},{6,4},{7,5},{8,10},{9,11},{10,... | collective-permute-start | bytes 196616 | tf_op jit(solution)/shard_map/ppermute | solution.py:487
  48.4 1.3 %collective-permute-start.8 = (f32[8,512]{1,0:T(8,128)S(1)}, f32[8,512]{1,0:T(8,128)S(1)}, u32[]{:S(2)}, u32[]{:S(2)}) collective-permute-start(f32[8,512]{1,0:T(8,128)S(1)} %get-tuple-element.26.samp_ref), channel_id=1, source_target_pairs={{0,4},{4,0},{8,12},{12,8},{16,20},{20,16},{24,28},{28,24},{1,5},{5... | collective-permute-start | bytes 49160 | tf_op jit(solution)/shard_map/ppermute | solution.py:494
  52.0 8.1 %collective-permute-start.9 = (f32[448,128]{1,0:T(8,128)S(1)}, f32[448,128]{1,0:T(8,128)S(1)}, u32[]{:S(2)}, u32[]{:S(2)}) collective-permute-start(f32[448,128]{1,0:T(8,128)S(1)} %get-tuple-element.35), channel_id=1, source_target_pairs={{0,1},{1,0},{2,3},{3,2},{4,5},{5,4},{6,7},{7,6},{8,9},{9,8},{10,11... | collective-permute-start | bytes 688136 | tf_op jit(solution)/shard_map/ppermute | solution.py:502
  52.1 14.0 %collective-permute-start.10 = (f32[448,128]{1,0:T(8,128)S(1)}, f32[448,128]{1,0:T(8,128)S(1)}, u32[]{:S(2)}, u32[]{:S(2)}) collective-permute-start(f32[448,128]{1,0:T(8,128)S(1)} %get-tuple-element.36), channel_id=1, source_target_pairs={{0,3},{1,2},{2,1},{3,0},{4,7},{5,6},{6,5},{7,4},{8,11},{9,10},{10,... | collective-permute-start | bytes 688136 | tf_op jit(solution)/shard_map/ppermute | solution.py:504
  54.8 12.7 %collective-permute-start.13 = (f32[16,128]{1,0:T(8,128)S(1)}, f32[16,128]{1,0:T(8,128)S(1)}, u32[]{:S(2)}, u32[]{:S(2)}) collective-permute-start(f32[16,128]{1,0:T(8,128)S(1)} %get-tuple-element.39), channel_id=1, source_target_pairs={{0,2},{1,3},{2,0},{3,1},{4,6},{5,7},{6,4},{7,5},{8,10},{9,11},{10,... | collective-permute-start | bytes 24584 | tf_op jit(solution)/shard_map/ppermute | solution.py:509
  66.7 12.2 %collective-permute-start.11 = (f32[192,128]{1,0:T(8,128)S(1)}, f32[192,128]{1,0:T(8,128)S(1)}, u32[]{:S(2)}, u32[]{:S(2)}) collective-permute-start(f32[192,128]{1,0:T(8,128)S(1)} %get-tuple-element.37), channel_id=1, source_target_pairs={{0,4},{4,0},{8,12},{12,8},{16,20},{20,16},{24,28},{28,24},{1,5},{5... | collective-permute-start | bytes 294920 | tf_op jit(solution)/shard_map/ppermute | solution.py:513
  66.8 12.2 %collective-permute-start.12 = (f32[192,128]{1,0:T(8,128)S(1)}, f32[192,128]{1,0:T(8,128)S(1)}, u32[]{:S(2)}, u32[]{:S(2)}) collective-permute-start(f32[192,128]{1,0:T(8,128)S(1)} %get-tuple-element.38), channel_id=1, source_target_pairs={{4,8},{12,16},{20,24},{8,4},{16,12},{24,20},{5,9},{13,17},{21,25},... | collective-permute-start | bytes 294920 | tf_op jit(solution)/shard_map/ppermute | solution.py:514
  67.5 11.4 %collective-permute-start.16 = (f32[64,128]{1,0:T(8,128)S(1)}, f32[64,128]{1,0:T(8,128)S(1)}, u32[]{:S(2)}, u32[]{:S(2)}) collective-permute-start(f32[64,128]{1,0:T(8,128)S(1)} %pad_maximum_fusion.refs_11_), channel_id=1, source_target_pairs={{0,24},{4,28},{8,16},{12,20},{16,8},{20,12},{24,0},{28,4},{1,25},{... | collective-permute-start | bytes 98312 | tf_op jit(solution)/shard_map/ppermute | solution.py:515
  71.9 7.0 %collective-permute-start.15 = (f32[64,128]{1,0:T(8,128)S(1)}, f32[64,128]{1,0:T(8,128)S(1)}, u32[]{:S(2)}, u32[]{:S(2)}) collective-permute-start(f32[64,128]{1,0:T(8,128)S(1)} %pad_maximum_fusion.refs_11_), channel_id=1, source_target_pairs={{0,16},{4,20},{8,24},{12,28},{16,0},{20,4},{24,8},{28,12},{1,17},{... | collective-permute-start | bytes 98312 | tf_op jit(solution)/shard_map/ppermute | solution.py:515
  72.4 6.5 %collective-permute-start.14 = (f32[64,128]{1,0:T(8,128)S(1)}, f32[64,128]{1,0:T(8,128)S(1)}, u32[]{:S(2)}, u32[]{:S(2)}) collective-permute-start(f32[64,128]{1,0:T(8,128)S(1)} %pad_maximum_fusion.refs_11_), channel_id=1, source_target_pairs={{0,8},{4,12},{8,0},{12,4},{16,24},{20,28},{24,16},{28,20},{1,9},{5... | collective-permute-start | bytes 98312 | tf_op jit(solution)/shard_map/ppermute | solution.py:515

commit v2 on v1

v2 whole, which is shorter than its diff:
```python
import math

import jax
import jax.numpy as jnp
from jax import lax
from jax.experimental import pallas as pl
from jax.experimental.pallas import tpu as pltpu
from jax.sharding import PartitionSpec as P

CX = 64
CY = 32
CZ = 128
P_SIZE = 256
HOST = 512
PTS = 2 * P_SIZE

DT_STEP = 0.2
NU_VISC = 0.5
EPS_SQ = 1.44
CORE_SQ = 0.01

ROWS = 16
BACK = 8
YROWS = 72
XROWS = 40
FACE_Y = 3 * CX
FACE_X = 3 * XROWS
RIM_Y = 2 * 3 * YROWS
RIM_X = 2 * 3 * CY
CHUNK = 8
N_CHUNK = CX // CHUNK

F32 = jnp.float32
BF16 = jnp.bfloat16
VM = pl.BlockSpec(memory_space=pltpu.MemorySpace.VMEM)
SM = pl.BlockSpec(memory_space=pltpu.MemorySpace.SMEM)
HB = pl.BlockSpec(memory_space=pltpu.MemorySpace.HBM)
PARAMS = pltpu.CompilerParams(vmem_limit_bytes=48 * 1024 * 1024)


def call(body, outs, n_in, name, scratch=(), first=VM, second=VM, out_specs=None, aliases=None):
    return pl.pallas_call(
        body,
        out_shape=[jax.ShapeDtypeStruct(s, F32) for s in outs],
        in_specs=([first, second] + [VM] * n_in)[:n_in],
        out_specs=out_specs or [VM] * len(outs),
        scratch_shapes=list(scratch),
        input_output_aliases=aliases or {},
        compiler_params=PARAMS,
        name=name,
    )


def place():
    ny = lax.axis_size("gy")
    ix, iy = lax.axis_index("gx"), lax.axis_index("gy")
    px, py = lax.rem(ix, 2), lax.rem(iy, 2)
    return px == 0, py == 0, ix * ny + iy, (ix - px) * ny + iy, ny


def split(value):
    high = value.astype(BF16)
    low = (value - high.astype(F32)).astype(BF16)
    return high, low


def dot3(a_high, a_low, b_high, b_low):
    def one(a, b):
        return jnp.dot(a, b, preferred_element_type=F32)

    return one(a_high, b_high) + (one(a_high, b_low) + one(a_low, b_high))


def reduce_list(items, op):
    result = items[0]
    for item in items[1:]:
        result = op(result, item)
    return result


def pack_body(v_ref, spin_ref, radius, chord, twist, angle, source, pay_c, pay_d, blk_ref, low, high, sems):
    _, even_y, _, _, _ = place()
    copies = [
        pltpu.make_async_copy(v_ref.at[:, :, pl.ds(0, 8)], low, sems.at[0]),
        pltpu.make_async_copy(v_ref.at[:, :, pl.ds(CY - 8, 8)], high, sems.at[1]),
    ]
    for copy in copies:
        copy.start()
    parts = [
        radius[...],
        chord[...],
        radius[...] * spin_ref[0],
        jnp.cos(twist[...]),
        jnp.sin(twist[...]),
        jnp.cos(angle[...]),
        jnp.sin(angle[...]),
        source[...].astype(F32),
    ]
    block = jnp.concatenate(parts, axis=0)
    blk_ref[...] = block
    pay_c[FACE_Y:] = block
    for copy in copies:
        copy.wait()
    for c in range(3):
        y_low = low[c, :, 0, :]
        y_high = high[c, :, 7, :]
        pay_c[c * CX : (c + 1) * CX] = jnp.where(even_y, y_high, y_low)
        pay_d[c * CX : (c + 1) * CX] = jnp.where(even_y, y_low, y_high)


def stencil_body(v_ref, out_ref, y_ref, x_ref, buf, sems):
    row = lax.broadcasted_iota(jnp.int32, (CY, CZ), 0)
    lane = lax.broadcasted_iota(jnp.int32, (CY, CZ), 1)
    copies = []
    for k in range(N_CHUNK):
        part = pl.ds(k * CHUNK, CHUNK)
        copies.append(pltpu.make_async_copy(v_ref.at[:, part], buf.at[:, part], sems.at[k]))
        copies[-1].start()
    half = 0.5 * DT_STEP
    visc = DT_STEP * NU_VISC
    not_last_y, not_first_y = row < CY - 1, row > 0
    not_last_z, not_first_z = lane < CZ - 1, lane > 0

    def step(x, carry):
        up = jnp.minimum(x + 1, CX - 1)
        down = jnp.maximum(x - 1, 0)
        v0, v1, v2 = v_ref_of(buf, x)
        a_x = jnp.where(x < CX - 1, visc - half * v0, 0.0)
        b_x = jnp.where(x > 0, visc + half * v0, 0.0)
        a_y = jnp.where(not_last_y, visc - half * v1, 0.0)
        b_y = jnp.where(not_first_y, visc + half * v1, 0.0)
        a_z = jnp.where(not_last_z, visc - half * v2, 0.0)
        b_z = jnp.where(not_first_z, visc + half * v2, 0.0)
        for c in range(3):
            mid = (v0, v1, v2)[c]
            along_x = a_x * buf[c, up] + b_x * buf[c, down]
            along_y = a_y * pltpu.roll(mid, CY - 1, 0) + b_y * pltpu.roll(mid, 1, 0)
            along_z = a_z * pltpu.roll(mid, CZ - 1, 1) + b_z * pltpu.roll(mid, 1, 1)
            out_ref[c, x] = (1.0 - 6.0 * visc) * mid + along_x + (along_y + along_z)
            y_ref[c, pl.ds(x, 1)] = mid[0:1]
            y_ref[c + 3, pl.ds(x, 1)] = mid[CY - 1 : CY]
        return carry

    copies[0].wait()
    for k in range(N_CHUNK):
        if k + 1 < N_CHUNK:
            copies[k + 1].wait()
        lax.fori_loop(k * CHUNK, (k + 1) * CHUNK, step, 0, unroll=2)
    for c in range(3):
        x_ref[c] = buf[c, 0]
        x_ref[c + 3] = buf[c, CX - 1]


def v_ref_of(buf, x):
    return buf[0, x], buf[1, x], buf[2, x]


def weight(coord, base, frac):
    return jnp.where(coord == base, 1.0 - frac, jnp.where(coord == base + 1, frac, 0.0))


def sample_body(v_ref, cell_ref, frac_ref, tab_ref):
    rows = jnp.concatenate([cell_ref[...].astype(F32), frac_ref[...], jnp.zeros((CZ - 6, HOST), F32)], axis=0)
    turned = rows.T
    x_col, y_col, z_col = [turned[:, k : k + 1].astype(jnp.int32) for k in range(3)]
    fx, fy, fz = [turned[:, k : k + 1] for k in range(3, 6)]
    lane = lax.broadcasted_iota(jnp.int32, (HOST, CZ), 1)
    wy = weight(lane % CY, y_col, fy)
    x_lane = lane // CY - x_col
    acc = None
    per = 4
    nx = CZ * per // CY
    for j in range(CX // nx):
        parts = []
        for i in range(per):
            shift = (CZ // CY) * (j * per + i)
            wx = jnp.where(x_lane == -shift, 1.0 - fx, jnp.where(x_lane == 1 - shift, fx, 0.0))
            parts.append(wx * wy)
        w_high, w_low = split(jnp.concatenate(parts, axis=1))
        field = [v_ref[c, j * nx : (j + 1) * nx].reshape(nx * CY, CZ) for c in range(3)]
        f_high, f_low = split(jnp.concatenate(field, axis=1))
        part = dot3(w_high, w_low, f_high, f_low)
        acc = part if acc is None else acc + part
    wz = weight(lane, z_col, fz)
    out = turned
    for c in range(3):
        value = jnp.sum(acc[:, c * CZ : (c + 1) * CZ] * wz, axis=1, keepdims=True)
        out = jnp.where(lane == 6 + c, value, out)
    tab_ref[...] = out


def xpack_body(n_z, x_ref, own_ref, rec_c, rec_d, *rest):
    others, (pay_a, pay_b, blk_ref) = rest[:n_z], rest[n_z:]
    even_x, even_y, _, _, _ = place()
    for c in range(3):
        at = c * CX
        y_high = jnp.where(even_y, rec_c[at : at + 1], rec_d[at : at + 1])
        tail = jnp.concatenate([y_high, jnp.zeros((XROWS - CY - 1, CZ), F32)], axis=0)
        low, high = x_ref[c], x_ref[c + 3]
        at = c * XROWS
        pay_a[at : at + CY] = jnp.where(even_x, high, low)
        pay_b[at : at + CY] = jnp.where(even_x, low, high)
        pay_a[at + CY : at + XROWS] = tail
        pay_b[at + CY : at + XROWS] = tail
    blocks = jnp.concatenate([own_ref[...], rec_c[FACE_Y:]] + [o[...] for o in others], axis=0)
    blk_ref[...] = blocks
    pay_a[FACE_X:] = blocks


def select_body(n_blk, tab_ref, face_a, face_b, rec_c, rec_d, blk_ref, *rest):
    others, (samp_ref, sel_ref, pts_ref) = rest[:n_blk], rest[n_blk:]
    even_x, even_y, brick, b0, ny = place()
    b1 = b0 + ny
    keys, members, values = [], [], []
    for ref, first in [(blk_ref, 0), (face_a, FACE_X)] + [(o, 0) for o in others]:
        for k in range((ref.shape[0] - first) // ROWS):
            value = ref[first + k * ROWS : first + (k + 1) * ROWS]
            key = value[14:15, 0:1]
            home = key.astype(jnp.int32) // HOST
            keys.append(key)
            members.append((home == b0) | (home == b1))
            values.append(value)
    low_key = reduce_list([jnp.where(m, k, 1e9) for k, m in zip(keys, members)], jnp.minimum)
    high_key = reduce_list([jnp.where(m, k, -1.0) for k, m in zip(keys, members)], jnp.maximum)
    turbine_a = jnp.zeros((ROWS, CZ), F32)
    turbine_b = jnp.zeros((ROWS, CZ), F32)
    for key, value in zip(keys, values):
        turbine_a = jnp.where(key == low_key, value, turbine_a)
        turbine_b = jnp.where(key == high_key, value, turbine_b)
    sel = jnp.concatenate([turbine_a, turbine_b], axis=0)
    sel_ref[...] = sel
    turned = jnp.concatenate([sel, jnp.zeros((CZ - 2 * ROWS, CZ), F32)], axis=0).T

    def column(k):
        picks = (2 * k, 2 * k + 1, ROWS + 2 * k, ROWS + 2 * k + 1)
        return jnp.concatenate([turned[:, j : j + 1] for j in picks], axis=0)

    table = tab_ref[...]
    lane = lax.broadcasted_iota(jnp.int32, (PTS, CZ), 1)
    x_col, y_col, z_col = [table[:, k : k + 1].astype(jnp.int32) for k in range(3)]
    fx, fy, fz = [table[:, k : k + 1] for k in range(3, 6)]
    on_line = lane >= CX
    edge_x = jnp.where(on_line, lane - CX, CX)
    edge_y = jnp.where(on_line, CY, lane)
    edge_w = jnp.where(on_line | (lane <= CY), weight(edge_x, x_col, fx) * weight(edge_y, y_col, fy), 0.0)
    field = []
    for c in range(3):
        at = c * XROWS
        plane = jnp.where(even_x, face_a[at : at + XROWS], face_b[at : at + XROWS])
        at = c * CX
        line = jnp.where(even_y, rec_c[at : at + CX], rec_d[at : at + CX])
        field.append(jnp.concatenate([plane, jnp.zeros((CX - XROWS, CZ), F32), line], axis=0))
    w_high, w_low = split(edge_w)
    f_high, f_low = split(jnp.concatenate(field, axis=1))
    acc = dot3(w_high, w_low, f_high, f_low)
    wz = weight(lane, z_col, fz)
    for c in range(3):
        value = jnp.sum(acc[:, c * CZ : (c + 1) * CZ] * wz, axis=1, keepdims=True)
        table = table + jnp.where(lane == 6 + c, value, 0.0)
    by_slot = table.T[0:16]
    slot = column(7).astype(jnp.int32)
    mine = (slot // HOST) == brick
    local = jnp.where(mine, slot % HOST, -1)
    hit = lax.broadcasted_iota(jnp.int32, (PTS, HOST), 1) == local
    code = (by_slot[0:1] * CY + by_slot[1:2]) * CZ + by_slot[2:3]

    def pull(row):
        return jnp.sum(jnp.where(hit, row, 0.0), axis=1, keepdims=True)

    code_col = pull(code).astype(jnp.int32)
    pulled = [pull(by_slot[k : k + 1]) for k in range(3, 9)]
    columns = [
        jnp.where(mine, code_col // (CY * CZ), -100).astype(F32),
        ((code_col // CZ) % CY).astype(F32),
        (code_col % CZ).astype(F32),
        *pulled[0:3],
        column(0),
        *pulled[3:6],
    ]
    points = jnp.zeros((PTS, CZ), F32)
    for k, col in enumerate(columns):
        points = jnp.where(lane == k, col, points)
    pts_ref[...] = points
    samp_ref[...] = points.T[7:15]


def weights_body(pts_ref, gx_ref, gy_ref, pz_ref):
    table = pts_ref[...].T

    def offsets(frac):
        raw = [jnp.exp(-((o - frac) ** 2) / EPS_SQ) for o in (-1.0, 0.0, 1.0, 2.0)]
        total = (raw[0] + raw[1]) + (raw[2] + raw[3])
        return [value / total for value in raw]

    def profile(rows, inner, base, frac):
        index = lax.broadcasted_iota(jnp.int32, (rows, PTS), 0)
        late = index - inner
        index = jnp.where(index < inner, index, jnp.where(late < 2, late - 2, late - 2 + inner))
        rel = index - base.astype(jnp.int32)
        result = jnp.zeros((rows, PTS), F32)
        for k, w in enumerate(offsets(frac)):
            result = jnp.where(rel == k - 1, w, result)
        return result

    gx_ref[...] = profile(YROWS, CX, table[0:1], table[3:4])
    gy_ref[...] = profile(CY + 8, CY, table[1:2], table[4:5])
    wz = offsets(table[5:6])
    stack = jnp.concatenate(wz + [jnp.zeros((CZ - 4, PTS), F32)], axis=0).T
    z_rel = lax.broadcasted_iota(jnp.int32, (PTS, CZ), 1) - pts_ref[:, 2:3].astype(jnp.int32)
    pz = jnp.zeros((PTS, CZ), F32)
    for k in range(4):
        pz = jnp.where(z_rel == k - 1, stack[:, k : k + 1], pz)
    pz_ref[...] = pz


def attack(axial_flow, tangent, cos_twist, sin_twist):
    rel_speed = jnp.sqrt(axial_flow * axial_flow + tangent * tangent + 1.0)
    cos_phi = tangent / rel_speed
    sin_phi = axial_flow / rel_speed
    sin_alpha = sin_phi * cos_twist - cos_phi * sin_twist
    cos_alpha = cos_phi * cos_twist + sin_phi * sin_twist
    lift_coef = 2.0 * jnp.pi * sin_alpha * cos_alpha / (1.0 + 4.0 * sin_alpha * sin_alpha)
    drag_coef = 0.02 + 0.8 * sin_alpha * sin_alpha
    return rel_speed, cos_phi, sin_phi, lift_coef, drag_coef


def loads_body(samp_ref, other_ref, sel_ref, pts_ref, gx_ref, gy_ref, pz_ref, lh_ref, pay_c, pay_d, ret_ref, xrim_ref):
    even_x, even_y, _, _, _ = place()

    def row(k):
        picks = (2 * k, 2 * k + 1, ROWS + 2 * k, ROWS + 2 * k + 1)
        return jnp.concatenate([sel_ref[j : j + 1] for j in picks], axis=1)

    radius, chord, spin, cos_t, sin_t, cos_a, sin_a = [row(k) for k in range(7)]
    flow = samp_ref[...] + other_ref[...]
    axial = flow[0:1]
    tangent = spin - (cos_a * flow[2:3] - sin_a * flow[1:2])
    rel_speed, cos_phi, sin_phi, lift_coef, drag_coef = attack(axial, tangent, cos_t, sin_t)
    circ = 0.5 * chord * rel_speed * lift_coef
    parts = []
    for t in range(2):
        seg = slice(t * P_SIZE, (t + 1) * P_SIZE)
        spacing = radius[:, seg] - pts_ref[seg, 6:7]
        kernel = spacing / (spacing * spacing + CORE_SQ)
        lhs = jnp.concatenate([cos_a[:, seg] * circ[:, seg], sin_a[:, seg] * circ[:, seg], jnp.zeros((6, P_SIZE), F32)], axis=0)
        both = jnp.dot(lhs, kernel, preferred_element_type=F32, precision=lax.Precision.HIGHEST)
        parts.append((cos_a[:, seg] * both[0:1] + sin_a[:, seg] * both[1:2]) / (4.0 * math.pi))
    induced = jnp.concatenate(parts, axis=1)
    rel_speed, cos_phi, sin_phi, lift_coef, drag_coef = attack(axial + induced, tangent, cos_t, sin_t)
    dynamic = 0.5 * chord * rel_speed * rel_speed
    lift = dynamic * lift_coef
    drag = dynamic * drag_coef
    thrust = lift * cos_phi + drag * sin_phi
    torque = lift * sin_phi - drag * cos_phi
    force = [-thrust, torque * sin_a, -torque * cos_a]
    pieces = []
    for c in range(3):
        chosen = jnp.where(even_x, force[c][:, 0:P_SIZE], force[c][:, P_SIZE:])
        pieces += [chosen[:, 0:CZ], chosen[:, CZ:]]
    key = jnp.where(even_x, sel_ref[14:15, 0:1], sel_ref[ROWS + 14 : ROWS + 15, 0:1])
    pieces.append(jnp.broadcast_to(key, (2, CZ)))
    blocks = jnp.concatenate(pieces, axis=0)
    ret_ref[...] = blocks
    pay_c[RIM_Y:] = blocks
    cols = jnp.concatenate(force + [jnp.zeros((CZ - 3, PTS), F32)], axis=0).T
    pz = pz_ref[...] * DT_STEP
    lines = jnp.concatenate([cols[:, c : c + 1] * pz for c in range(3)], axis=1)
    l_high, l_low = split(lines)
    lh_ref[...] = lines
    gx = gx_ref[...]
    gy = gy_ref[...]
    planes = [gx * gy[CY + k : CY + k + 1] for k in range(4)]
    planes += [gx[CX + k : CX + k + 1] * gy[0:CY] for k in range(4)]
    w_high, w_low = split(jnp.concatenate(planes, axis=0))
    rim = dot3(w_high, w_low, l_high, l_low)
    for k in range(2):
        for c in range(3):
            low = rim[k * YROWS : (k + 1) * YROWS, c * CZ : (c + 1) * CZ]
            high = rim[(k + 2) * YROWS : (k + 3) * YROWS, c * CZ : (c + 1) * CZ]
            at = (k * 3 + c) * YROWS
            pay_c[at : at + YROWS] = jnp.where(even_y, high, low)
            pay_d[at : at + YROWS] = jnp.where(even_y, low, high)
    first = 4 * YROWS
    for k in range(4):
        for c in range(3):
            at = (k * 3 + c) * CY
            xrim_ref[at : at + CY] = rim[first + k * CY : first + (k + 1) * CY, c * CZ : (c + 1) * CZ]


SPREAD_X = 8


def spread_body(lines_ref, gx_ref, gy_ref, base_ref, out_ref):
    l_high, l_low = split(lines_ref[...])
    gy = gy_ref[0:CY]
    for k in range(CX // SPREAD_X):
        first = k * SPREAD_X
        planes = jnp.concatenate([gx_ref[first + i : first + i + 1] * gy for i in range(SPREAD_X)], axis=0)
        w_high, w_low = split(planes)
        value = dot3(w_high, w_low, l_high, l_low)
        for c in range(3):
            part = value[:, c * CZ : (c + 1) * CZ].reshape(SPREAD_X, CY, CZ)
            out_ref[c, first : first + SPREAD_X] = base_ref[c, first : first + SPREAD_X] + part


def rimpack_body(n_z, xrim_ref, ret_ref, rec_c, rec_d, *rest):
    others, (pay_a, pay_b, back_ref) = rest[:n_z], rest[n_z:]
    even_x, even_y, _, _, _ = place()
    zero = jnp.zeros((CY - 4, CZ), F32)
    for k in range(2):
        for c in range(3):
            sides = []
            for s in range(2):
                near, far = [], []
                for y in range(2):
                    at = (y * 3 + c) * YROWS + CX + 2 * s + k
                    from_c, from_d = rec_c[at : at + 1], rec_d[at : at + 1]
                    near.append(jnp.where(even_y, from_d, from_c))
                    far.append(jnp.where(even_y, from_c, from_d))
                at = ((2 * s + k) * 3 + c) * CY
                sides.append(xrim_ref[at : at + CY] + jnp.concatenate(near + [zero] + far, axis=0))
            at = (k * 3 + c) * CY
            pay_a[at : at + CY] = jnp.where(even_x, sides[1], sides[0])
            pay_b[at : at + CY] = jnp.where(even_x, sides[0], sides[1])
    back = jnp.concatenate([ret_ref[...], rec_c[RIM_Y:]] + [o[...] for o in others], axis=0)
    back_ref[...] = back
    pay_a[RIM_X:] = back


def final_body(n_ret, main_ref, x_ref, y_ref, own_ref, face_a, face_b, yc_ref, yd_ref, rim_a, rim_b, rim_c, rim_d, back_ref, *rest):
    rets, (out_ref, pf_ref, buf, sems) = rest[:n_ret], rest[n_ret:]
    even_x, even_y, _, _, _ = place()
    half = 0.5 * DT_STEP
    visc = DT_STEP * NU_VISC
    copies = []
    for k in range(N_CHUNK):
        first = k * CHUNK
        part = slice(first, first + CHUNK)
        for c in range(3):
            buf[c, part] = main_ref[c, part]
            if k in (0, N_CHUNK - 1):
                a, b = face_a[c * XROWS : c * XROWS + CY], face_b[c * XROWS : c * XROWS + CY]
                if k == 0:
                    buf[c, 0] += jnp.where(even_x, b, a) * (visc + half * x_ref[0])
                else:
                    buf[c, CX - 1] += jnp.where(even_x, a, b) * (visc - half * x_ref[3])
                for i in range(2):
                    rows = slice((i * 3 + c) * CY, (i * 3 + c + 1) * CY)
                    a, b = rim_a[rows], rim_b[rows]
                    if k == 0:
                        buf[c, i] += jnp.where(even_x, b, a)
                    else:
                        buf[c, CX - 2 + i] += jnp.where(even_x, a, b)
            rows = slice(c * CX + first, c * CX + first + CHUNK)
            a, b = yc_ref[rows], yd_ref[rows]
            low = [jnp.where(even_y, b, a) * (visc + half * y_ref[1, part]), 0.0]
            high = [0.0, jnp.where(even_y, a, b) * (visc - half * y_ref[4, part])]
            for i in range(2):
                at = (i * 3 + c) * YROWS + first
                a, b = rim_c[at : at + CHUNK], rim_d[at : at + CHUNK]
                buf[c, part, i, :] += jnp.where(even_y, b, a) + low[i]
                buf[c, part, CY - 2 + i, :] += jnp.where(even_y, a, b) + high[i]
        copies.append(pltpu.make_async_copy(buf.at[:, pl.ds(first, CHUNK)], out_ref.at[:, pl.ds(first, CHUNK)], sems.at[k]))
        copies[-1].start()
    mine = own_ref[14:15, 0:1]
    found = jnp.zeros((BACK, CZ), F32)
    for ref, first in [(back_ref, 0), (rim_a, RIM_X)] + [(r, 0) for r in rets]:
        for k in range((ref.shape[0] - first) // BACK):
            value = ref[first + BACK * k : first + BACK * k + BACK]
            found = jnp.where(value[6:7, 0:1] == mine, value, found)
    for c in range(3):
        pf_ref[c : c + 1] = jnp.concatenate([found[2 * c : 2 * c + 1], found[2 * c + 1 : 2 * c + 2]], axis=1)
    for copy in copies:
        copy.wait()


def per_device(
    velocity,
    host_cell,
    host_frac,
    host_dst,
    owner_src,
    rotor_speed,
    blade_radius,
    blade_chord,
    blade_twist,
    blade_angle,
):
    nx, ny = lax.axis_size("gx"), lax.axis_size("gy")

    def flip(n, bits):
        return [(i, i ^ bits) for i in range(n)]

    def odd_pairs(n):
        up = [(i, i + 1) for i in range(1, n - 1, 2)]
        return up + [(t, s) for s, t in up]

    def gather_y(block):
        return [lax.ppermute(block, "gy", flip(ny, o)) for o in range(2, ny)]

    def gather_x(block):
        return [lax.ppermute(block, "gx", flip(nx, 2 * o)) for o in range(1, nx // 2)]

    def swap(blocks):
        return [lax.ppermute(block, "gx", flip(nx, 1)) for block in blocks]

    dma = pltpu.SemaphoreType.DMA
    tiles = pltpu.VMEM((3, CX, 8, CZ), F32)
    pay_c, pay_d, block = call(
        pack_body,
        [(FACE_Y + ROWS, CZ), (FACE_Y, CZ), (ROWS, CZ)],
        7,
        "pack",
        scratch=[tiles, tiles, dma((2,))],
        first=HB,
        second=SM,
    )(velocity, rotor_speed, *[a.reshape(2, CZ) for a in (blade_radius, blade_chord, blade_twist, blade_angle, owner_src)])
    rec_c = lax.ppermute(pay_c, "gy", flip(ny, 1))
    rec_d = lax.ppermute(pay_d, "gy", odd_pairs(ny))
    from_y = gather_y(block)
    base, y_faces, x_faces = call(
        stencil_body,
        [velocity.shape, (6, CX, CZ), (6, CY, CZ)],
        1,
        "stencil",
        scratch=[pltpu.VMEM(velocity.shape, F32), dma((N_CHUNK,))],
        first=HB,
    )(velocity)
    n_rows = ny * ROWS
    pay_a, pay_b, blocks = call(
        lambda *refs: xpack_body(len(from_y), *refs),
        [(FACE_X + n_rows, CZ), (FACE_X, CZ), (n_rows, CZ)],
        4 + len(from_y),
        "xpack",
    )(x_faces, block, rec_c, rec_d, *from_y)
    face_a = lax.ppermute(pay_a, "gx", flip(nx, 1))
    face_b = lax.ppermute(pay_b, "gx", odd_pairs(nx))
    from_x = gather_x(blocks)
    table = call(sample_body, [(HOST, CZ)], 3, "sample")(velocity, host_cell, host_frac)[0]
    from_x += swap(from_x)
    samp, sel, pts = call(
        lambda *refs: select_body(len(from_x), *refs),
        [(8, PTS), (2 * ROWS, CZ), (PTS, CZ)],
        6 + len(from_x),
        "select",
    )(table, face_a, face_b, rec_c, rec_d, blocks, *from_x)
    other = swap([samp])[0]
    gx, gy, pz = call(weights_body, [(YROWS, PTS), (CY + 8, PTS), (PTS, CZ)], 1, "weights")(pts)
    lines, pay_c, pay_d, ret, xrim = call(
        loads_body,
        [(PTS, 3 * CZ), (RIM_Y + BACK, CZ), (RIM_Y, CZ), (BACK, CZ), (2 * RIM_X, CZ)],
        7,
        "loads",
    )(samp, other, sel, pts, gx, gy, pz)
    rim_c = lax.ppermute(pay_c, "gy", flip(ny, 1))
    rim_d = lax.ppermute(pay_d, "gy", odd_pairs(ny))
    ret_y = gather_y(ret)
    main = call(spread_body, [velocity.shape], 4, "spread")(lines, gx, gy, base)[0]
    pay_a, pay_b, back = call(
        lambda *refs: rimpack_body(len(ret_y), *refs),
        [(RIM_X + ny * BACK, CZ), (RIM_X, CZ), (ny * BACK, CZ)],
        4 + len(ret_y),
        "rimpack",
    )(xrim, ret, rim_c, rim_d, *ret_y)
    rim_a = lax.ppermute(pay_a, "gx", flip(nx, 1))
    rim_b = lax.ppermute(pay_b, "gx", odd_pairs(nx))
    rets = gather_x(back)
    rets += swap(rets)
    return tuple(
        call(
            lambda *refs: final_body(len(rets), *refs),
            [velocity.shape, (3, P_SIZE)],
            13 + len(rets),
            "final",
            scratch=[pltpu.VMEM(velocity.shape, F32), dma((N_CHUNK,))],
            out_specs=[HB, VM],
        )(main, x_faces, y_faces, block, face_a, face_b, rec_c, rec_d, rim_a, rim_b, rim_c, rim_d, back, *rets)
    )


def solution(mesh):
    return jax.shard_map(
        per_device,
        mesh=mesh,
        in_specs=(
            P(None, "gx", "gy", None),
            P(None, ("gx", "gy")),
            P(None, ("gx", "gy")),
            P(("gx", "gy")),
            P(("gx", "gy")),
            P(("gx", "gy")),
            P(("gx", "gy")),
            P(("gx", "gy")),
            P(("gx", "gy")),
            P(("gx", "gy")),
        ),
        out_specs=(P(None, "gx", "gy", None), P(None, ("gx", "gy"))),
        check_vma=False,
    )
```

time: 84.6 us -> 70.9 us (0.84)
  waiting for transfers between devices: 21.5 us -> 9.33 us
  starting transfers between devices: 22.2 us -> 29.2 us
  Pallas kernels: 30 us -> 23.3 us
  other arithmetic: 1.51 us -> 0 us
    ppermute x13 -> x21, waiting for transfers between devices: 16.9 us -> 9.32 us  [the longest x4 5.38 us: gather_y(): return [lax.ppermute(block, 'gy', flip(ny, o)) for o in range(2, ny)]]
    ppermute x13 -> x21, starting transfers between devices: 19.7 us -> 25.1 us  [the longest x4 10.8 us: gather_y(): return [lax.ppermute(block, 'gy', flip(ny, o)) for o in range(2, ny)]]
    unnamed x8 -> x20, local copies, waits for them, and re-layouts: 1.67 us -> 6.95 us
    ppermute x1, waiting for transfers between devices: 4.52 us -> 0.01 us  [per_device(): rim_c = lax.ppermute(pay_c, 'gy', flip(ny, 1))]
    pallas_call x7 -> x9, Pallas kernels: 24.8 us -> 20.9 us  [the longest x1 5.34 us: per_device(): call(spread_body, [velocity.shape], 4, 'spread')(lines, gx, gy, base)[0]]
    pallas_call x1, Pallas kernels: 5.22 us -> 2.46 us  [per_device(): call(lambda *refs: final_body(len(rets), *refs), [velocity.shape, (3, P_S...]
    concatenate x3 -> x0, local copies, waits for them, and re-layouts: 2.2 us -> none  [the longest x1 0.74 us: per_device(): jnp.concatenate([edge_a, block], axis=0)]
    reshape x2 -> x0, other arithmetic: 1.51 us -> none  [per_device(): value.reshape(2, CZ)]
  transfers between devices with their start and end apart: 17 -> 25, of which waited for: 4 -> 7; matrix products, arithmetic and copies ran while one was open for 4% -> 0% of each run, Pallas kernels for 19% -> 22%
where the time goes in v2:
time: 70.9 us; the launch traced here: 70.5 us
  starting transfers between devices  29.2 us (41%)
  Pallas kernels  23.3 us (33%)
  waiting for transfers between devices  9.33 us (13%)
  local copies, waits for them, and re-layouts  6.95 us (10%)
  between operations  1.68 us (2%)
    ppermute x4, starting transfers between devices, gather_y(): return [lax.ppermute(block, 'gy', flip(ny, o)) for o in range(2, ny)]  10.8 us
    ppermute x6, starting transfers between devices, gather_x(): lax.ppermute(block, 'gx', flip(nx, 2 * o))  9.37 us
    unnamed x20, local copies, waits for them, and re-layouts  6.95 us
    ppermute x4, waiting for transfers between devices, gather_y(): return [lax.ppermute(block, 'gy', flip(ny, o)) for o in range(2, ny)]  5.38 us
    pallas_call x1, Pallas kernels, per_device(): call(spread_body, [velocity.shape], 4, 'spread')(lines, gx, gy, base)[0]  5.34 us
    pallas_call x1, Pallas kernels, per_device(): call(stencil_body, [velocity.shape, (6, CX, CZ), (6, CY, CZ)], 1, 'stenci...  5.07 us
    pallas_call x1, Pallas kernels, per_device(): call(sample_body, [(HOST, CZ)], 3, 'sample')(velocity, host_cell, host_frac)  4.38 us
    ppermute x6, waiting for transfers between devices, gather_x(): lax.ppermute(block, 'gx', flip(nx, 2 * o))  3.47 us
  transfers between devices with their start and end apart: 25, of which 7 were waited for; matrix products, arithmetic and copies ran while one was open for 0% of the time, Pallas kernels for 22%

profile of v2, /device:TPU:0, one launch (start us, length us, event | category | flops | bytes accessed | tf_op | source)
XLA Modules:
  0.0 70.5 jit_solution(10767075729314541196)
XLA Ops:
  1.3 1.9 %copy-done = f32[3,64,32,128]{3,2,1,0:T(8,128)S(1)} copy-done((f32[3,64,32,128]{3,2,1,0:T(8,128)S(1)}, f32[3,64,32,128]{3,2,1,0:T(8,128)}, u32[]{:S(2)}) %copy-start) | copy-done | bytes 3145752
  3.2 0.7 copy-done.5
  3.9 0.7 copy-done.6
  4.5 0.7 copy-done.7
  5.2 0.7 copy-done.8
  5.9 0.7 copy-done.9
  7.0 3.1 %collective-permute-start = (f32[208,128]{1,0:T(8,128)S(1)}, f32[208,128]{1,0:T(8,128)S(1)}, u32[]{:S(2)}, u32[]{:S(2)}) collective-permute-start(f32[208,128]{1,0:T(8,128)S(1)} %get-tuple-element.27), channel_id=1, source_target_pairs={{0,1},{1,0},{2,3},{3,2},{4,5},{5,4},{6,7},{7,6},{8,9},{9,8},{10,11... | collective-permute-start | bytes 319496 | tf_op jit(solution)/shard_map/ppermute | solution.py:518
  10.1 0.7 collective-permute-start.1
  10.8 2.5 %collective-permute-start.3 = (f32[16,128]{1,0:T(8,128)S(1)}, f32[16,128]{1,0:T(8,128)S(1)}, u32[]{:S(2)}, u32[]{:S(2)}) collective-permute-start(f32[16,128]{1,0:T(8,128)S(1)} %get-tuple-element.26.refs_1_.refs_3_), channel_id=1, source_target_pairs={{0,3},{1,2},{2,1},{3,0},{4,7},{5,6},{6,5},{7,4},{8,11},{9,10},{10,... | collective-permute-start | bytes 24584 | tf_op jit(solution)/shard_map/ppermute | solution.py:499
  13.3 3.4 %collective-permute-start.2 = (f32[16,128]{1,0:T(8,128)S(1)}, f32[16,128]{1,0:T(8,128)S(1)}, u32[]{:S(2)}, u32[]{:S(2)}) collective-permute-start(f32[16,128]{1,0:T(8,128)S(1)} %get-tuple-element.26.refs_1_.refs_3_), channel_id=1, source_target_pairs={{0,2},{1,3},{2,0},{3,1},{4,6},{5,7},{6,4},{7,5},{8,10},{9,11},{10,... | collective-permute-start | bytes 24584 | tf_op jit(solution)/shard_map/ppermute | solution.py:499
  16.7 5.1 %stencil.1 = (f32[3,64,32,128]{3,2,1,0:T(8,128)S(1)}, f32[6,64,128]{2,1,0:T(8,128)S(1)}, f32[6,32,128]{2,1,0:T(8,128)S(1)}) custom-call(f32[3,64,32,128]{3,2,1,0:T(8,128)} %v_ref.5), custom_call_target="tpu_custom_call" | custom-call | tf_op jit(solution)/shard_map/stencil/pallas_call | solution.py:521
  21.8 1.7 %copy-done.2 = f32[3,64,32,128]{3,2,1,0:T(8,128)} copy-done((f32[3,64,32,128]{3,2,1,0:T(8,128)}, f32[3,64,32,128]{3,2,1,0:T(8,128)S(1)}, u32[]{:S(2)}) %copy-start.2) | copy-done | bytes 3145752
  23.6 2.5 %collective-permute-start.8 = (f32[64,128]{1,0:T(8,128)S(1)}, f32[64,128]{1,0:T(8,128)S(1)}, u32[]{:S(2)}, u32[]{:S(2)}) collective-permute-start(f32[64,128]{1,0:T(8,128)S(1)} %get-tuple-element.31.refs_5_), channel_id=1, source_target_pairs={{0,24},{4,28},{8,16},{12,20},{16,8},{20,12},{24,0},{28,4},{1,25},{... | collective-permute-start | bytes 98312 | tf_op jit(solution)/shard_map/ppermute | solution.py:502
  27.1 0.7 collective-permute-start.5
  27.8 0.7 collective-permute-done.8.refs_8_
  28.5 2.3 %collective-permute-start.11 = (f32[64,128]{1,0:T(8,128)S(1)}, f32[64,128]{1,0:T(8,128)S(1)}, u32[]{:S(2)}, u32[]{:S(2)}) collective-permute-start(f32[64,128]{1,0:T(8,128)S(1)} %collective-permute-done.8.refs_8_), channel_id=1, source_target_pairs={{0,4},{4,0},{8,12},{12,8},{16,20},{20,16},{24,28},{28,24},{1,5},{5... | collective-permute-start | bytes 98312 | tf_op jit(solution)/shard_map/ppermute | solution.py:505
  31.3 4.4 %sample.1.refs_0_ = f32[512,128]{1,0:T(8,128)S(1)} custom-call(f32[3,64,32,128]{3,2,1,0:T(8,128)S(1)} %copy-done.1, s32[3,512]{1,0:T(4,128)S(1)} %copy-done.3, f32[3,512]{1,0:T(4,128)S(1)} %copy-done.4), custom_call_target="tpu_custom_call" | custom-call | tf_op jit(solution)/shard_map/sample/pallas_call | solution.py:539
  35.7 3.1 %select.1 = (f32[8,512]{1,0:T(8,128)S(1)}, f32[32,128]{1,0:T(8,128)S(1)}, f32[512,128]{1,0:T(8,128)S(1)}) custom-call(f32[512,128]{1,0:T(8,128)S(1)} %sample.1.refs_0_, f32[184,128]{1,0:T(8,128)S(1)} %collective-permute-done.4.refs_1_.refs_4_, f32[120,128]{1,0:T(8,128)S(1)} %collective-permute-done.5.refs_2_.refs_5_, ...), custom_call_target="tpu_custom_call" | custom-call | tf_op jit(solution)/shard_map/select/pallas_call | solution.py:541
  38.9 0.7 weights.1
  40.0 1.8 %loads.1 = (f32[512,384]{1,0:T(8,128)S(1)}, f32[440,128]{1,0:T(8,128)S(1)}, f32[432,128]{1,0:T(8,128)S(1)}, f32[8,128]{1,0:T(8,128)S(1)}, f32[384,128]{1,0:T(8,128)S(1)}) custom-call(f32[8,512]{1,0:T(8,128)S(1)} %get-tuple-element.32.samp_ref, f32[8,512]{1,0:T(8,128)S(1)} %collective-permute-done.12.other_ref, f32[32,128]{1,0:T(8,128)S(1)} %get-tuple-element.33.sel_ref, ...), custom_call_target="tpu_custom_call" | custom-call | tf_op jit(solution)/shard_map/loads/pallas_call | solution.py:549
  41.9 0.7 collective-permute-start.14
  42.6 1.5 %collective-permute-start.16 = (f32[8,128]{1,0:T(8,128)S(1)}, f32[8,128]{1,0:T(8,128)S(1)}, u32[]{:S(2)}, u32[]{:S(2)}) collective-permute-start(f32[8,128]{1,0:T(8,128)S(1)} %get-tuple-element.42.refs_1_), channel_id=1, source_target_pairs={{0,3},{1,2},{2,1},{3,0},{4,7},{5,6},{6,5},{7,4},{8,11},{9,10},{10,... | collective-permute-start | bytes 12296 | tf_op jit(solution)/shard_map/ppermute | solution.py:499
  44.1 3.3 %collective-permute-start.15 = (f32[8,128]{1,0:T(8,128)S(1)}, f32[8,128]{1,0:T(8,128)S(1)}, u32[]{:S(2)}, u32[]{:S(2)}) collective-permute-start(f32[8,128]{1,0:T(8,128)S(1)} %get-tuple-element.42.refs_1_), channel_id=1, source_target_pairs={{0,2},{1,3},{2,0},{3,1},{4,6},{5,7},{6,4},{7,5},{8,10},{9,11},{10,... | collective-permute-start | bytes 12296 | tf_op jit(solution)/shard_map/ppermute | solution.py:499
  47.4 1.7 %collective-permute-done.16.refs_5_ = f32[8,128]{1,0:T(8,128)S(1)} collective-permute-done((f32[8,128]{1,0:T(8,128)S(1)}, f32[8,128]{1,0:T(8,128)S(1)}, u32[]{:S(2)}, u32[]{:S(2)}) %collective-permute-start.16) | collective-permute-done | bytes 4128 | tf_op jit(solution)/shard_map/ppermute | solution.py:499
  49.1 3.7 %collective-permute-done.15.refs_4_ = f32[8,128]{1,0:T(8,128)S(1)} collective-permute-done((f32[8,128]{1,0:T(8,128)S(1)}, f32[8,128]{1,0:T(8,128)S(1)}, u32[]{:S(2)}, u32[]{:S(2)}) %collective-permute-start.15) | collective-permute-done | bytes 4128 | tf_op jit(solution)/shard_map/ppermute | solution.py:499
  53.0 0.8 %collective-permute-start.18 = (f32[192,128]{1,0:T(8,128)S(1)}, f32[192,128]{1,0:T(8,128)S(1)}, u32[]{:S(2)}, u32[]{:S(2)}) collective-permute-start(f32[192,128]{1,0:T(8,128)S(1)} %get-tuple-element.46), channel_id=1, source_target_pairs={{4,8},{12,16},{20,24},{8,4},{16,12},{24,20},{5,9},{13,17},{21,25},... | collective-permute-start | bytes 294920 | tf_op jit(solution)/shard_map/ppermute | solution.py:566
  53.8 4.4 %collective-permute-start.21 = (f32[32,128]{1,0:T(8,128)S(1)}, f32[32,128]{1,0:T(8,128)S(1)}, u32[]{:S(2)}, u32[]{:S(2)}) collective-permute-start(f32[32,128]{1,0:T(8,128)S(1)} %get-tuple-element.47.refs_12_), channel_id=1, source_target_pairs={{0,24},{4,28},{8,16},{12,20},{16,8},{20,12},{24,0},{28,4},{1,25},{... | collective-permute-start | bytes 49160 | tf_op jit(solution)/shard_map/ppermute | solution.py:502
  58.7 0.9 %collective-permute-start.19 = (f32[32,128]{1,0:T(8,128)S(1)}, f32[32,128]{1,0:T(8,128)S(1)}, u32[]{:S(2)}, u32[]{:S(2)}) collective-permute-start(f32[32,128]{1,0:T(8,128)S(1)} %get-tuple-element.47.refs_12_), channel_id=1, source_target_pairs={{0,8},{4,12},{8,0},{12,4},{16,24},{20,28},{24,16},{28,20},{1,9},{5... | collective-permute-start | bytes 49160 | tf_op jit(solution)/shard_map/ppermute | solution.py:502
  59.6 1.2 %collective-permute-done.21.refs_15_ = f32[32,128]{1,0:T(8,128)S(1)} collective-permute-done((f32[32,128]{1,0:T(8,128)S(1)}, f32[32,128]{1,0:T(8,128)S(1)}, u32[]{:S(2)}, u32[]{:S(2)}) %collective-permute-start.21) | collective-permute-done | bytes 16416 | tf_op jit(solution)/shard_map/ppermute | solution.py:502
  60.9 1.1 %collective-permute-done.20.refs_14_ = f32[32,128]{1,0:T(8,128)S(1)} collective-permute-done((f32[32,128]{1,0:T(8,128)S(1)}, f32[32,128]{1,0:T(8,128)S(1)}, u32[]{:S(2)}, u32[]{:S(2)}) %collective-permute-start.20) | collective-permute-done | bytes 16416 | tf_op jit(solution)/shard_map/ppermute | solution.py:502
  62.4 5.3 %spread.1.refs_0_ = f32[3,64,32,128]{3,2,1,0:T(8,128)S(1)} custom-call(f32[512,384]{1,0:T(8,128)S(1)} %get-tuple-element.38.lines_ref, f32[72,512]{1,0:T(8,128)S(1)} %get-tuple-element.35.gx_ref, f32[40,512]{1,0:T(8,128)S(1)} %get-tuple-element.36.gy_ref, f32[3,64,32,128]{3,2,1,0:T(8,128)} %copy-done.2), custom_call_target="tpu_custom_call" | custom-call | tf_op jit(solution)/shard_map/spread/pallas_call | solution.py:558
  67.8 2.5 %final.1 = (f32[3,64,32,128]{3,2,1,0:T(8,128)}, f32[3,256]{1,0:T(4,128)}) custom-call(f32[3,64,32,128]{3,2,1,0:T(8,128)S(1)} %spread.1.refs_0_, f32[6,32,128]{2,1,0:T(8,128)S(1)} %get-tuple-element.25.refs_0_.refs_1_, f32[6,64,128]{2,1,0:T(8,128)S(1)} %get-tuple-element.40.refs_2_, f32[16,128]{1,0:T(8,128)S(1)} %get-tuple-element.26.refs_1_.refs_3_, ...), custom_call_target="tpu_custom_call" | custom-call | tf_op jit(solution)/shard_map/final/pallas_call | solution.py:570
  (48 shorter events, 3.9 us)
Async XLA Ops:
  1.3 1.9 %copy-start = (f32[3,64,32,128]{3,2,1,0:T(8,128)S(1)}, f32[3,64,32,128]{3,2,1,0:T(8,128)}, u32[]{:S(2)}) copy-start(f32[3,64,32,128]{3,2,1,0:T(8,128)} %v_ref.5) | copy-start | bytes 9437188
  3.2 0.7 copy-start.5
  5.2 0.7 copy-start.8
  6.6 24.7 %copy-start.1 = (f32[3,64,32,128]{3,2,1,0:T(8,128)S(1)}, f32[3,64,32,128]{3,2,1,0:T(8,128)}, u32[]{:S(2)}) copy-start(f32[3,64,32,128]{3,2,1,0:T(8,128)} %v_ref.5) | copy-start | bytes 9437188
  6.6 24.7 %copy-start.3 = (s32[3,512]{1,0:T(4,128)S(1)}, s32[3,512]{1,0:T(4,128)}, u32[]{:S(2)}) copy-start(s32[3,512]{1,0:T(4,128)} %cell_ref.1) | copy-start | bytes 18436
  6.6 24.7 %copy-start.4 = (f32[3,512]{1,0:T(4,128)S(1)}, f32[3,512]{1,0:T(4,128)}, u32[]{:S(2)}) copy-start(f32[3,512]{1,0:T(4,128)} %frac_ref.1) | copy-start | bytes 18436
  7.0 16.4 %collective-permute-start = (f32[208,128]{1,0:T(8,128)S(1)}, f32[208,128]{1,0:T(8,128)S(1)}, u32[]{:S(2)}, u32[]{:S(2)}) collective-permute-start(f32[208,128]{1,0:T(8,128)S(1)} %get-tuple-element.27), channel_id=1, source_target_pairs={{0,1},{1,0},{2,3},{3,2},{4,5},{5,4},{6,7},{7,6},{8,9},{9,8},{10,11... | collective-permute-start | bytes 319496 | tf_op jit(solution)/shard_map/ppermute | solution.py:518
  10.1 13.3 %collective-permute-start.1 = (f32[192,128]{1,0:T(8,128)S(1)}, f32[192,128]{1,0:T(8,128)S(1)}, u32[]{:S(2)}, u32[]{:S(2)}) collective-permute-start(f32[192,128]{1,0:T(8,128)S(1)} %get-tuple-element.28), channel_id=1, source_target_pairs={{1,2},{2,1},{5,6},{6,5},{9,10},{10,9},{13,14},{14,13},{17,18},{18,... | collective-permute-start | bytes 294920 | tf_op jit(solution)/shard_map/ppermute | solution.py:519
  10.8 12.7 %collective-permute-start.3 = (f32[16,128]{1,0:T(8,128)S(1)}, f32[16,128]{1,0:T(8,128)S(1)}, u32[]{:S(2)}, u32[]{:S(2)}) collective-permute-start(f32[16,128]{1,0:T(8,128)S(1)} %get-tuple-element.26.refs_1_.refs_3_), channel_id=1, source_target_pairs={{0,3},{1,2},{2,1},{3,0},{4,7},{5,6},{6,5},{7,4},{8,11},{9,10},{10,... | collective-permute-start | bytes 24584 | tf_op jit(solution)/shard_map/ppermute | solution.py:499
  13.3 10.1 %collective-permute-start.2 = (f32[16,128]{1,0:T(8,128)S(1)}, f32[16,128]{1,0:T(8,128)S(1)}, u32[]{:S(2)}, u32[]{:S(2)}) collective-permute-start(f32[16,128]{1,0:T(8,128)S(1)} %get-tuple-element.26.refs_1_.refs_3_), channel_id=1, source_target_pairs={{0,2},{1,3},{2,0},{3,1},{4,6},{5,7},{6,4},{7,5},{8,10},{9,11},{10,... | collective-permute-start | bytes 24584 | tf_op jit(solution)/shard_map/ppermute | solution.py:499
  21.8 1.7 %copy-start.2 = (f32[3,64,32,128]{3,2,1,0:T(8,128)}, f32[3,64,32,128]{3,2,1,0:T(8,128)S(1)}, u32[]{:S(2)}) copy-start(f32[3,64,32,128]{3,2,1,0:T(8,128)S(1)} %get-tuple-element.39.base_ref) | copy-start | bytes 9437188
  23.5 12.2 %collective-permute-start.4 = (f32[184,128]{1,0:T(8,128)S(1)}, f32[184,128]{1,0:T(8,128)S(1)}, u32[]{:S(2)}, u32[]{:S(2)}) collective-permute-start(f32[184,128]{1,0:T(8,128)S(1)} %get-tuple-element.29), channel_id=1, source_target_pairs={{0,4},{4,0},{8,12},{12,8},{16,20},{20,16},{24,28},{28,24},{1,5},{5... | collective-permute-start | bytes 282632 | tf_op jit(solution)/shard_map/ppermute | solution.py:536
  23.6 4.9 %collective-permute-start.8 = (f32[64,128]{1,0:T(8,128)S(1)}, f32[64,128]{1,0:T(8,128)S(1)}, u32[]{:S(2)}, u32[]{:S(2)}) collective-permute-start(f32[64,128]{1,0:T(8,128)S(1)} %get-tuple-element.31.refs_5_), channel_id=1, source_target_pairs={{0,24},{4,28},{8,16},{12,20},{16,8},{20,12},{24,0},{28,4},{1,25},{... | collective-permute-start | bytes 98312 | tf_op jit(solution)/shard_map/ppermute | solution.py:502
  26.1 4.6 %collective-permute-start.7 = (f32[64,128]{1,0:T(8,128)S(1)}, f32[64,128]{1,0:T(8,128)S(1)}, u32[]{:S(2)}, u32[]{:S(2)}) collective-permute-start(f32[64,128]{1,0:T(8,128)S(1)} %get-tuple-element.31.refs_5_), channel_id=1, source_target_pairs={{0,16},{4,20},{8,24},{12,28},{16,0},{20,4},{24,8},{28,12},{1,17},{... | collective-permute-start | bytes 98312 | tf_op jit(solution)/shard_map/ppermute | solution.py:502
  26.6 4.2 %collective-permute-start.6 = (f32[64,128]{1,0:T(8,128)S(1)}, f32[64,128]{1,0:T(8,128)S(1)}, u32[]{:S(2)}, u32[]{:S(2)}) collective-permute-start(f32[64,128]{1,0:T(8,128)S(1)} %get-tuple-element.31.refs_5_), channel_id=1, source_target_pairs={{0,8},{4,12},{8,0},{12,4},{16,24},{20,28},{24,16},{28,20},{1,9},{5... | collective-permute-start | bytes 98312 | tf_op jit(solution)/shard_map/ppermute | solution.py:502
  27.1 8.5 %collective-permute-start.5 = (f32[120,128]{1,0:T(8,128)S(1)}, f32[120,128]{1,0:T(8,128)S(1)}, u32[]{:S(2)}, u32[]{:S(2)}) collective-permute-start(f32[120,128]{1,0:T(8,128)S(1)} %get-tuple-element.30), channel_id=1, source_target_pairs={{4,8},{12,16},{20,24},{8,4},{16,12},{24,20},{5,9},{13,17},{21,25},... | collective-permute-start | bytes 184328 | tf_op jit(solution)/shard_map/ppermute | solution.py:537
  28.5 7.2 %collective-permute-start.11 = (f32[64,128]{1,0:T(8,128)S(1)}, f32[64,128]{1,0:T(8,128)S(1)}, u32[]{:S(2)}, u32[]{:S(2)}) collective-permute-start(f32[64,128]{1,0:T(8,128)S(1)} %collective-permute-done.8.refs_8_), channel_id=1, source_target_pairs={{0,4},{4,0},{8,12},{12,8},{16,20},{20,16},{24,28},{28,24},{1,5},{5... | collective-permute-start | bytes 98312 | tf_op jit(solution)/shard_map/ppermute | solution.py:505
  30.7 4.9 %collective-permute-start.10 = (f32[64,128]{1,0:T(8,128)S(1)}, f32[64,128]{1,0:T(8,128)S(1)}, u32[]{:S(2)}, u32[]{:S(2)}) collective-permute-start(f32[64,128]{1,0:T(8,128)S(1)} %collective-permute-done.7.refs_7_), channel_id=1, source_target_pairs={{0,4},{4,0},{8,12},{12,8},{16,20},{20,16},{24,28},{28,24},{1,5},{5... | collective-permute-start | bytes 98312 | tf_op jit(solution)/shard_map/ppermute | solution.py:505
  30.8 4.8 %collective-permute-start.9 = (f32[64,128]{1,0:T(8,128)S(1)}, f32[64,128]{1,0:T(8,128)S(1)}, u32[]{:S(2)}, u32[]{:S(2)}) collective-permute-start(f32[64,128]{1,0:T(8,128)S(1)} %collective-permute-done.6.refs_6_), channel_id=1, source_target_pairs={{0,4},{4,0},{8,12},{12,8},{16,20},{20,16},{24,28},{28,24},{1,5},{5... | collective-permute-start | bytes 98312 | tf_op jit(solution)/shard_map/ppermute | solution.py:505
  38.8 1.2 %collective-permute-start.12 = (f32[8,512]{1,0:T(8,128)S(1)}, f32[8,512]{1,0:T(8,128)S(1)}, u32[]{:S(2)}, u32[]{:S(2)}) collective-permute-start(f32[8,512]{1,0:T(8,128)S(1)} %get-tuple-element.32.samp_ref), channel_id=1, source_target_pairs={{0,4},{4,0},{8,12},{12,8},{16,20},{20,16},{24,28},{28,24},{1,5},{5... | collective-permute-start | bytes 49160 | tf_op jit(solution)/shard_map/ppermute | solution.py:505
  41.8 11.0 %collective-permute-start.13 = (f32[440,128]{1,0:T(8,128)S(1)}, f32[440,128]{1,0:T(8,128)S(1)}, u32[]{:S(2)}, u32[]{:S(2)}) collective-permute-start(f32[440,128]{1,0:T(8,128)S(1)} %get-tuple-element.43), channel_id=1, source_target_pairs={{0,1},{1,0},{2,3},{3,2},{4,5},{5,4},{6,7},{7,6},{8,9},{9,8},{10,11... | collective-permute-start | bytes 675848 | tf_op jit(solution)/shard_map/ppermute | solution.py:555
  41.9 10.9 %collective-permute-start.14 = (f32[432,128]{1,0:T(8,128)S(1)}, f32[432,128]{1,0:T(8,128)S(1)}, u32[]{:S(2)}, u32[]{:S(2)}) collective-permute-start(f32[432,128]{1,0:T(8,128)S(1)} %get-tuple-element.44), channel_id=1, source_target_pairs={{1,2},{2,1},{5,6},{6,5},{9,10},{10,9},{13,14},{14,13},{17,18},{18,... | collective-permute-start | bytes 663560 | tf_op jit(solution)/shard_map/ppermute | solution.py:556
  42.6 6.5 %collective-permute-start.16 = (f32[8,128]{1,0:T(8,128)S(1)}, f32[8,128]{1,0:T(8,128)S(1)}, u32[]{:S(2)}, u32[]{:S(2)}) collective-permute-start(f32[8,128]{1,0:T(8,128)S(1)} %get-tuple-element.42.refs_1_), channel_id=1, source_target_pairs={{0,3},{1,2},{2,1},{3,0},{4,7},{5,6},{6,5},{7,4},{8,11},{9,10},{10,... | collective-permute-start | bytes 12296 | tf_op jit(solution)/shard_map/ppermute | solution.py:499
  44.1 8.7 %collective-permute-start.15 = (f32[8,128]{1,0:T(8,128)S(1)}, f32[8,128]{1,0:T(8,128)S(1)}, u32[]{:S(2)}, u32[]{:S(2)}) collective-permute-start(f32[8,128]{1,0:T(8,128)S(1)} %get-tuple-element.42.refs_1_), channel_id=1, source_target_pairs={{0,2},{1,3},{2,0},{3,1},{4,6},{5,7},{6,4},{7,5},{8,10},{9,11},{10,... | collective-permute-start | bytes 12296 | tf_op jit(solution)/shard_map/ppermute | solution.py:499
  52.9 15.0 %collective-permute-start.17 = (f32[224,128]{1,0:T(8,128)S(1)}, f32[224,128]{1,0:T(8,128)S(1)}, u32[]{:S(2)}, u32[]{:S(2)}) collective-permute-start(f32[224,128]{1,0:T(8,128)S(1)} %get-tuple-element.45), channel_id=1, source_target_pairs={{0,4},{4,0},{8,12},{12,8},{16,20},{20,16},{24,28},{28,24},{1,5},{5... | collective-permute-start | bytes 344072 | tf_op jit(solution)/shard_map/ppermute | solution.py:565
  53.0 14.9 %collective-permute-start.18 = (f32[192,128]{1,0:T(8,128)S(1)}, f32[192,128]{1,0:T(8,128)S(1)}, u32[]{:S(2)}, u32[]{:S(2)}) collective-permute-start(f32[192,128]{1,0:T(8,128)S(1)} %get-tuple-element.46), channel_id=1, source_target_pairs={{4,8},{12,16},{20,24},{8,4},{16,12},{24,20},{5,9},{13,17},{21,25},... | collective-permute-start | bytes 294920 | tf_op jit(solution)/shard_map/ppermute | solution.py:566
  53.8 7.0 %collective-permute-start.21 = (f32[32,128]{1,0:T(8,128)S(1)}, f32[32,128]{1,0:T(8,128)S(1)}, u32[]{:S(2)}, u32[]{:S(2)}) collective-permute-start(f32[32,128]{1,0:T(8,128)S(1)} %get-tuple-element.47.refs_12_), channel_id=1, source_target_pairs={{0,24},{4,28},{8,16},{12,20},{16,8},{20,12},{24,0},{28,4},{1,25},{... | collective-permute-start | bytes 49160 | tf_op jit(solution)/shard_map/ppermute | solution.py:502
  58.2 3.7 %collective-permute-start.20 = (f32[32,128]{1,0:T(8,128)S(1)}, f32[32,128]{1,0:T(8,128)S(1)}, u32[]{:S(2)}, u32[]{:S(2)}) collective-permute-start(f32[32,128]{1,0:T(8,128)S(1)} %get-tuple-element.47.refs_12_), channel_id=1, source_target_pairs={{0,16},{4,20},{8,24},{12,28},{16,0},{20,4},{24,8},{28,12},{1,17},{... | collective-permute-start | bytes 49160 | tf_op jit(solution)/shard_map/ppermute | solution.py:502
  58.7 3.7 %collective-permute-start.19 = (f32[32,128]{1,0:T(8,128)S(1)}, f32[32,128]{1,0:T(8,128)S(1)}, u32[]{:S(2)}, u32[]{:S(2)}) collective-permute-start(f32[32,128]{1,0:T(8,128)S(1)} %get-tuple-element.47.refs_12_), channel_id=1, source_target_pairs={{0,8},{4,12},{8,0},{12,4},{16,24},{20,28},{24,16},{28,20},{1,9},{5... | collective-permute-start | bytes 49160 | tf_op jit(solution)/shard_map/ppermute | solution.py:502
  60.9 6.9 %collective-permute-start.24 = (f32[32,128]{1,0:T(8,128)S(1)}, f32[32,128]{1,0:T(8,128)S(1)}, u32[]{:S(2)}, u32[]{:S(2)}) collective-permute-start(f32[32,128]{1,0:T(8,128)S(1)} %collective-permute-done.21.refs_15_), channel_id=1, source_target_pairs={{0,4},{4,0},{8,12},{12,8},{16,20},{20,16},{24,28},{28,24},{1,5},{5... | collective-permute-start | bytes 49160 | tf_op jit(solution)/shard_map/ppermute | solution.py:505
  61.9 5.9 %collective-permute-start.23 = (f32[32,128]{1,0:T(8,128)S(1)}, f32[32,128]{1,0:T(8,128)S(1)}, u32[]{:S(2)}, u32[]{:S(2)}) collective-permute-start(f32[32,128]{1,0:T(8,128)S(1)} %collective-permute-done.20.refs_14_), channel_id=1, source_target_pairs={{0,4},{4,0},{8,12},{12,8},{16,20},{20,16},{24,28},{28,24},{1,5},{5... | collective-permute-start | bytes 49160 | tf_op jit(solution)/shard_map/ppermute | solution.py:505
  62.4 5.4 %collective-permute-start.22 = (f32[32,128]{1,0:T(8,128)S(1)}, f32[32,128]{1,0:T(8,128)S(1)}, u32[]{:S(2)}, u32[]{:S(2)}) collective-permute-start(f32[32,128]{1,0:T(8,128)S(1)} %collective-permute-done.19.refs_13_), channel_id=1, source_target_pairs={{0,4},{4,0},{8,12},{12,8},{16,20},{20,16},{24,28},{28,24},{1,5},{5... | collective-permute-start | bytes 49160 | tf_op jit(solution)/shard_map/ppermute | solution.py:505
  (3 other events, 2.0 us)

commit v3 on v2

--- a/solution.py
+++ b/solution.py
@@ -35,27 +35,27 @@
 VM = pl.BlockSpec(memory_space=pltpu.MemorySpace.VMEM)
 SM = pl.BlockSpec(memory_space=pltpu.MemorySpace.SMEM)
 HB = pl.BlockSpec(memory_space=pltpu.MemorySpace.HBM)
-PARAMS = pltpu.CompilerParams(vmem_limit_bytes=48 * 1024 * 1024)
-
-
-def call(body, outs, n_in, name, scratch=(), first=VM, second=VM, out_specs=None, aliases=None):
+MIB = 1024 * 1024
+
+
+def call(body, outs, n_in, name, scratch=(), first=VM, second=VM, out_specs=None, in_specs=None, vmem=12):
     return pl.pallas_call(
         body,
         out_shape=[jax.ShapeDtypeStruct(s, F32) for s in outs],
-        in_specs=([first, second] + [VM] * n_in)[:n_in],
+        in_specs=in_specs or ([first, second] + [VM] * n_in)[:n_in],
         out_specs=out_specs or [VM] * len(outs),
         scratch_shapes=list(scratch),
-        input_output_aliases=aliases or {},
-        compiler_params=PARAMS,
+        compiler_params=pltpu.CompilerParams(vmem_limit_bytes=vmem * MIB),
         name=name,
     )
 
 
 def place():
-    ny = lax.axis_size("gy")
+    nx, ny = lax.axis_size("gx"), lax.axis_size("gy")
     ix, iy = lax.axis_index("gx"), lax.axis_index("gy")
     px, py = lax.rem(ix, 2), lax.rem(iy, 2)
-    return px == 0, py == 0, ix * ny + iy, (ix - px) * ny + iy, ny
+    inner = (ix + px > 0) & (ix + px < nx)
+    return px == 0, py == 0, inner, ix * ny + iy, (ix - px) * ny + iy, ny
 
 
 def split(value):
@@ -78,23 +78,30 @@
     return result
 
 
-def pack_body(v_ref, spin_ref, radius, chord, twist, angle, source, pay_c, pay_d, blk_ref, low, high, sems):
-    _, even_y, _, _, _ = place()
+def pack_body(v_ref, spin_hbm, *rest):
+    params, (pay_c, pay_d, blk_ref, low, high, held, held_int, spin_ref, sems) = rest[:5], rest[5:]
+    _, even_y, _, _, _, _ = place()
+    small = [pltpu.make_async_copy(spin_hbm, spin_ref, sems.at[2])]
+    small += [pltpu.make_async_copy(p, held.at[k], sems.at[3 + k]) for k, p in enumerate(params[:4])]
+    small.append(pltpu.make_async_copy(params[4], held_int, sems.at[7]))
     copies = [
         pltpu.make_async_copy(v_ref.at[:, :, pl.ds(0, 8)], low, sems.at[0]),
         pltpu.make_async_copy(v_ref.at[:, :, pl.ds(CY - 8, 8)], high, sems.at[1]),
     ]
-    for copy in copies:
+    for copy in small + copies:
         copy.start()
+    for copy in small:
+        copy.wait()
+    radius, chord, twist, angle = [held[k] for k in range(4)]
     parts = [
-        radius[...],
-        chord[...],
-        radius[...] * spin_ref[0],
-        jnp.cos(twist[...]),
-        jnp.sin(twist[...]),
-        jnp.cos(angle[...]),
-        jnp.sin(angle[...]),
-        source[...].astype(F32),
+        radius,
+        chord,
+        radius * spin_ref[0],
+        jnp.cos(twist),
+        jnp.sin(twist),
+        jnp.cos(angle),
+        jnp.sin(angle),
+        held_int[...].astype(F32),
     ]
     block = jnp.concatenate(parts, axis=0)
     blk_ref[...] = block
@@ -189,9 +196,9 @@
     tab_ref[...] = out
 
 
-def xpack_body(n_z, x_ref, own_ref, rec_c, rec_d, *rest):
-    others, (pay_a, pay_b, blk_ref) = rest[:n_z], rest[n_z:]
-    even_x, even_y, _, _, _ = place()
+def xpack_body(n_blk, x_ref, rec_c, rec_d, *rest):
+    pieces, (pay_a, pay_b, blk_ref) = rest[:n_blk], rest[n_blk:]
+    even_x, even_y, inner, _, _, _ = place()
     for c in range(3):
         at = c * CX
         y_high = jnp.where(even_y, rec_c[at : at + 1], rec_d[at : at + 1])
@@ -202,17 +209,18 @@
         pay_b[at : at + CY] = jnp.where(even_x, low, high)
         pay_a[at + CY : at + XROWS] = tail
         pay_b[at + CY : at + XROWS] = tail
-    blocks = jnp.concatenate([own_ref[...], rec_c[FACE_Y:]] + [o[...] for o in others], axis=0)
+    blocks = jnp.concatenate([p[...] for p in pieces], axis=0)
     blk_ref[...] = blocks
-    pay_a[FACE_X:] = blocks
+    if pay_b.shape[0] > FACE_X:
+        pay_b[FACE_X:] = blocks
 
 
 def select_body(n_blk, tab_ref, face_a, face_b, rec_c, rec_d, blk_ref, *rest):
     others, (samp_ref, sel_ref, pts_ref) = rest[:n_blk], rest[n_blk:]
-    even_x, even_y, brick, b0, ny = place()
+    even_x, even_y, inner, brick, b0, ny = place()
     b1 = b0 + ny
     keys, members, values = [], [], []
-    for ref, first in [(blk_ref, 0), (face_a, FACE_X)] + [(o, 0) for o in others]:
+    for ref, first in [(blk_ref, 0), (face_b, FACE_X)] + [(o, 0) for o in others]:
         for k in range((ref.shape[0] - first) // ROWS):
             value = ref[first + k * ROWS : first + (k + 1) * ROWS]
             key = value[14:15, 0:1]
@@ -246,7 +254,8 @@
     field = []
     for c in range(3):
         at = c * XROWS
-        plane = jnp.where(even_x, face_a[at : at + XROWS], face_b[at : at + XROWS])
+        past = jnp.where(inner, face_b[at : at + XROWS], 0.0)
+        plane = jnp.where(even_x, face_a[at : at + XROWS], past)
         at = c * CX
         line = jnp.where(even_y, rec_c[at : at + CX], rec_d[at : at + CX])
         field.append(jnp.concatenate([plane, jnp.zeros((CX - XROWS, CZ), F32), line], axis=0))
@@ -257,31 +266,17 @@
     for c in range(3):
         value = jnp.sum(acc[:, c * CZ : (c + 1) * CZ] * wz, axis=1, keepdims=True)
         table = table + jnp.where(lane == 6 + c, value, 0.0)
-    by_slot = table.T[0:16]
     slot = column(7).astype(jnp.int32)
     mine = (slot // HOST) == brick
     local = jnp.where(mine, slot % HOST, -1)
-    hit = lax.broadcasted_iota(jnp.int32, (PTS, HOST), 1) == local
-    code = (by_slot[0:1] * CY + by_slot[1:2]) * CZ + by_slot[2:3]
-
-    def pull(row):
-        return jnp.sum(jnp.where(hit, row, 0.0), axis=1, keepdims=True)
-
-    code_col = pull(code).astype(jnp.int32)
-    pulled = [pull(by_slot[k : k + 1]) for k in range(3, 9)]
-    columns = [
-        jnp.where(mine, code_col // (CY * CZ), -100).astype(F32),
-        ((code_col // CZ) % CY).astype(F32),
-        (code_col % CZ).astype(F32),
-        *pulled[0:3],
-        column(0),
-        *pulled[3:6],
-    ]
-    points = jnp.zeros((PTS, CZ), F32)
-    for k, col in enumerate(columns):
-        points = jnp.where(lane == k, col, points)
-    pts_ref[...] = points
-    samp_ref[...] = points.T[7:15]
+    hit = (lax.broadcasted_iota(jnp.int32, (PTS, HOST), 1) == local).astype(F32).astype(BF16)
+    first, second = split(table)
+    third = (table - first.astype(F32) - second.astype(F32)).astype(BF16)
+    pulled = [jnp.dot(hit, part, preferred_element_type=F32) for part in (first, second, third)]
+    points = pulled[0] + pulled[1] + pulled[2]
+    points = jnp.where(lane == 9, column(0), points)
+    pts_ref[...] = jnp.where((lane == 0) & jnp.logical_not(mine), -100.0, points)
+    samp_ref[...] = points.T[6:14]
 
 
 def weights_body(pts_ref, gx_ref, gy_ref, pz_ref):
@@ -325,7 +320,7 @@
 
 
 def loads_body(samp_ref, other_ref, sel_ref, pts_ref, gx_ref, gy_ref, pz_ref, lh_ref, pay_c, pay_d, ret_ref, xrim_ref):
-    even_x, even_y, _, _, _ = place()
+    even_x, even_y, inner, _, _, _ = place()
 
     def row(k):
         picks = (2 * k, 2 * k + 1, ROWS + 2 * k, ROWS + 2 * k + 1)
@@ -340,7 +335,7 @@
     parts = []
     for t in range(2):
         seg = slice(t * P_SIZE, (t + 1) * P_SIZE)
-        spacing = radius[:, seg] - pts_ref[seg, 6:7]
+        spacing = radius[:, seg] - pts_ref[seg, 9:10]
         kernel = spacing / (spacing * spacing + CORE_SQ)
         lhs = jnp.concatenate([cos_a[:, seg] * circ[:, seg], sin_a[:, seg] * circ[:, seg], jnp.zeros((6, P_SIZE), F32)], axis=0)
         both = jnp.dot(lhs, kernel, preferred_element_type=F32, precision=lax.Precision.HIGHEST)
@@ -354,11 +349,13 @@
     torque = lift * sin_phi - drag * cos_phi
     force = [-thrust, torque * sin_a, -torque * cos_a]
     pieces = []
-    for c in range(3):
-        chosen = jnp.where(even_x, force[c][:, 0:P_SIZE], force[c][:, P_SIZE:])
-        pieces += [chosen[:, 0:CZ], chosen[:, CZ:]]
-    key = jnp.where(even_x, sel_ref[14:15, 0:1], sel_ref[ROWS + 14 : ROWS + 15, 0:1])
-    pieces.append(jnp.broadcast_to(key, (2, CZ)))
+    for t in range(2):
+        for c in range(3):
+            for h in range(2):
+                at = t * P_SIZE + h * CZ
+                pieces.append(force[c][:, at : at + CZ])
+        key = sel_ref[t * ROWS + 14 : t * ROWS + 15, 0:1]
+        pieces.append(jnp.broadcast_to(key, (2, CZ)))
     blocks = jnp.concatenate(pieces, axis=0)
     ret_ref[...] = blocks
     pay_c[RIM_Y:] = blocks
@@ -390,22 +387,23 @@
 SPREAD_X = 8
 
 
-def spread_body(lines_ref, gx_ref, gy_ref, base_ref, out_ref):
+def spread_body(start, lines_ref, gx_ref, gy_ref, base_ref, out_ref):
     l_high, l_low = split(lines_ref[...])
     gy = gy_ref[0:CY]
-    for k in range(CX // SPREAD_X):
-        first = k * SPREAD_X
+    for k in range(out_ref.shape[1] // SPREAD_X):
+        at = k * SPREAD_X
+        first = start + at
         planes = jnp.concatenate([gx_ref[first + i : first + i + 1] * gy for i in range(SPREAD_X)], axis=0)
         w_high, w_low = split(planes)
         value = dot3(w_high, w_low, l_high, l_low)
         for c in range(3):
             part = value[:, c * CZ : (c + 1) * CZ].reshape(SPREAD_X, CY, CZ)
-            out_ref[c, first : first + SPREAD_X] = base_ref[c, first : first + SPREAD_X] + part
-
-
-def rimpack_body(n_z, xrim_ref, ret_ref, rec_c, rec_d, *rest):
-    others, (pay_a, pay_b, back_ref) = rest[:n_z], rest[n_z:]
-    even_x, even_y, _, _, _ = place()
+            out_ref[c, at : at + SPREAD_X] = base_ref[c, first : first + SPREAD_X] + part
+
+
+def rimpack_body(n_blk, xrim_ref, rec_c, rec_d, *rest):
+    pieces, (pay_a, pay_b, back_ref) = rest[:n_blk], rest[n_blk:]
+    even_x, even_y, inner, _, _, _ = place()
     zero = jnp.zeros((CY - 4, CZ), F32)
     for k in range(2):
         for c in range(3):
@@ -422,14 +420,15 @@
             at = (k * 3 + c) * CY
             pay_a[at : at + CY] = jnp.where(even_x, sides[1], sides[0])
             pay_b[at : at + CY] = jnp.where(even_x, sides[0], sides[1])
-    back = jnp.concatenate([ret_ref[...], rec_c[RIM_Y:]] + [o[...] for o in others], axis=0)
+    back = jnp.concatenate([p[...] for p in pieces], axis=0)
     back_ref[...] = back
-    pay_a[RIM_X:] = back
-
-
-def final_body(n_ret, main_ref, x_ref, y_ref, own_ref, face_a, face_b, yc_ref, yd_ref, rim_a, rim_b, rim_c, rim_d, back_ref, *rest):
+    if pay_b.shape[0] > RIM_X:
+        pay_b[RIM_X:] = back
+
+
+def final_body(n_ret, main_low, main_high, x_ref, y_ref, own_ref, face_a, face_b, yc_ref, yd_ref, rim_a, rim_b, rim_c, rim_d, back_ref, *rest):
     rets, (out_ref, pf_ref, buf, sems) = rest[:n_ret], rest[n_ret:]
-    even_x, even_y, _, _, _ = place()
+    even_x, even_y, inner, _, _, _ = place()
     half = 0.5 * DT_STEP
     visc = DT_STEP * NU_VISC
     copies = []
@@ -437,16 +436,19 @@
         first = k * CHUNK
         part = slice(first, first + CHUNK)
         for c in range(3):
-            buf[c, part] = main_ref[c, part]
+            half_of = main_low if k < N_CHUNK // 2 else main_high
+            at = first % (CX // 2)
+            buf[c, part] = half_of[c, at : at + CHUNK]
             if k in (0, N_CHUNK - 1):
-                a, b = face_a[c * XROWS : c * XROWS + CY], face_b[c * XROWS : c * XROWS + CY]
+                a = face_a[c * XROWS : c * XROWS + CY]
+                b = jnp.where(inner, face_b[c * XROWS : c * XROWS + CY], 0.0)
                 if k == 0:
                     buf[c, 0] += jnp.where(even_x, b, a) * (visc + half * x_ref[0])
                 else:
                     buf[c, CX - 1] += jnp.where(even_x, a, b) * (visc - half * x_ref[3])
                 for i in range(2):
                     rows = slice((i * 3 + c) * CY, (i * 3 + c + 1) * CY)
-                    a, b = rim_a[rows], rim_b[rows]
+                    a, b = rim_a[rows], jnp.where(inner, rim_b[rows], 0.0)
                     if k == 0:
                         buf[c, i] += jnp.where(even_x, b, a)
                     else:
@@ -464,7 +466,7 @@
         copies[-1].start()
     mine = own_ref[14:15, 0:1]
     found = jnp.zeros((BACK, CZ), F32)
-    for ref, first in [(back_ref, 0), (rim_a, RIM_X)] + [(r, 0) for r in rets]:
+    for ref, first in [(back_ref, 0), (rim_b, RIM_X)] + [(r, 0) for r in rets]:
         for k in range((ref.shape[0] - first) // BACK):
             value = ref[first + BACK * k : first + BACK * k + BACK]
             found = jnp.where(value[6:7, 0:1] == mine, value, found)
@@ -487,22 +489,40 @@
     blade_angle,
 ):
     nx, ny = lax.axis_size("gx"), lax.axis_size("gy")
+    ring = nx == 8
 
     def flip(n, bits):
         return [(i, i ^ bits) for i in range(n)]
 
-    def odd_pairs(n):
-        up = [(i, i + 1) for i in range(1, n - 1, 2)]
+    def odd_pairs(n, closed=False):
+        up = [(i, (i + 1) % n) for i in range(1, n if closed else n - 1, 2)]
         return up + [(t, s) for s, t in up]
 
-    def gather_y(block):
-        return [lax.ppermute(block, "gy", flip(ny, o)) for o in range(2, ny)]
-
-    def gather_x(block):
-        return [lax.ppermute(block, "gx", flip(nx, 2 * o)) for o in range(1, nx // 2)]
-
-    def swap(blocks):
-        return [lax.ppermute(block, "gx", flip(nx, 1)) for block in blocks]
+    def swap(block):
+        return lax.ppermute(block, "gx", flip(nx, 1))
+
+    def join(pieces):
+        return pieces[0] if len(pieces) == 1 else jnp.concatenate(pieces, axis=0)
+
+    def after(values, other):
+        return lax.optimization_barrier((values, other))
+
+    def gather_y(first, filler):
+        pieces = [first]
+        for bit in [b for b in (2, 4, 8) if b < ny]:
+            got = lax.ppermute(join(pieces), "gy", flip(ny, bit))
+            if filler is not None:
+                got, filler = after(got, filler())
+                yield filler
+                filler = None
+            pieces.append(got)
+        yield pieces
+
+    def gather_x(blocks):
+        pieces = []
+        for bit in [4] if ring else [b for b in (2, 4, 8, 16) if b < nx]:
+            pieces.append(lax.ppermute(join([blocks] + pieces) if not ring else blocks, "gx", flip(nx, bit)))
+        return pieces
 
     dma = pltpu.SemaphoreType.DMA
     tiles = pltpu.VMEM((3, CX, 8, CZ), F32)
@@ -511,70 +531,80 @@
         [(FACE_Y + ROWS, CZ), (FACE_Y, CZ), (ROWS, CZ)],
         7,
         "pack",
-        scratch=[tiles, tiles, dma((2,))],
-        first=HB,
-        second=SM,
+        scratch=[tiles, tiles, pltpu.VMEM((4, 2, CZ), F32), pltpu.VMEM((2, CZ), jnp.int32), pltpu.SMEM((1,), F32), dma((8,))],
+        in_specs=[HB] * 7,
     )(velocity, rotor_speed, *[a.reshape(2, CZ) for a in (blade_radius, blade_chord, blade_twist, blade_angle, owner_src)])
     rec_c = lax.ppermute(pay_c, "gy", flip(ny, 1))
     rec_d = lax.ppermute(pay_d, "gy", odd_pairs(ny))
-    from_y = gather_y(block)
     base, y_faces, x_faces = call(
         stencil_body,
         [velocity.shape, (6, CX, CZ), (6, CY, CZ)],
         1,
         "stencil",
         scratch=[pltpu.VMEM(velocity.shape, F32), dma((N_CHUNK,))],
-        first=HB,
+        in_specs=[HB],
     )(velocity)
-    n_rows = ny * ROWS
+    rec_c, base = after(rec_c, base)
+    sampled = lambda: call(sample_body, [(HOST, CZ)], 3, "sample", vmem=24)(velocity, host_cell, host_frac)[0]
+    table, pieces = list(gather_y(join([block, rec_c[FACE_Y:]]), sampled))
+    pieces = pieces + [swap(p) for p in pieces]
+    n_rows = 2 * ny * ROWS
     pay_a, pay_b, blocks = call(
-        lambda *refs: xpack_body(len(from_y), *refs),
-        [(FACE_X + n_rows, CZ), (FACE_X, CZ), (n_rows, CZ)],
-        4 + len(from_y),
+        lambda *refs: xpack_body(len(pieces), *refs),
+        [(FACE_X, CZ), (FACE_X + (n_rows if ring else 0), CZ), (n_rows, CZ)],
+        3 + len(pieces),
         "xpack",
-    )(x_faces, block, rec_c, rec_d, *from_y)
-    face_a = lax.ppermute(pay_a, "gx", flip(nx, 1))
-    face_b = lax.ppermute(pay_b, "gx", odd_pairs(nx))
+    )(x_faces, rec_c, rec_d, *pieces)
+    face_b = lax.ppermute(pay_b, "gx", odd_pairs(nx, ring))
     from_x = gather_x(blocks)
-    table = call(sample_body, [(HOST, CZ)], 3, "sample")(velocity, host_cell, host_frac)[0]
-    from_x += swap(from_x)
+    face_a = swap(pay_a)
+    if ring:
+        from_x.append(swap(face_b[FACE_X:]))
     samp, sel, pts = call(
         lambda *refs: select_body(len(from_x), *refs),
         [(8, PTS), (2 * ROWS, CZ), (PTS, CZ)],
         6 + len(from_x),
         "select",
     )(table, face_a, face_b, rec_c, rec_d, blocks, *from_x)
-    other = swap([samp])[0]
+    other = swap(samp)
     gx, gy, pz = call(weights_body, [(YROWS, PTS), (CY + 8, PTS), (PTS, CZ)], 1, "weights")(pts)
     lines, pay_c, pay_d, ret, xrim = call(
         loads_body,
-        [(PTS, 3 * CZ), (RIM_Y + BACK, CZ), (RIM_Y, CZ), (BACK, CZ), (2 * RIM_X, CZ)],
+        [(PTS, 3 * CZ), (RIM_Y + 2 * BACK, CZ), (RIM_Y, CZ), (2 * BACK, CZ), (2 * RIM_X, CZ)],
         7,
         "loads",
     )(samp, other, sel, pts, gx, gy, pz)
     rim_c = lax.ppermute(pay_c, "gy", flip(ny, 1))
     rim_d = lax.ppermute(pay_d, "gy", odd_pairs(ny))
-    ret_y = gather_y(ret)
-    main = call(spread_body, [velocity.shape], 4, "spread")(lines, gx, gy, base)[0]
+
+    def spread(start):
+        return call(
+            lambda *refs: spread_body(start, *refs), [(3, CX // 2, CY, CZ)], 4, "spread"
+        )(lines, gx, gy, base)[0]
+
+    rim_c, main_low = after(rim_c, spread(0))
+    main_high, pieces = list(gather_y(join([ret, rim_c[RIM_Y:]]), lambda: spread(CX // 2)))
+    n_rows = 2 * ny * BACK
     pay_a, pay_b, back = call(
-        lambda *refs: rimpack_body(len(ret_y), *refs),
-        [(RIM_X + ny * BACK, CZ), (RIM_X, CZ), (ny * BACK, CZ)],
-        4 + len(ret_y),
+        lambda *refs: rimpack_body(len(pieces), *refs),
+        [(RIM_X, CZ), (RIM_X + (n_rows if ring else 0), CZ), (n_rows, CZ)],
+        3 + len(pieces),
         "rimpack",
-    )(xrim, ret, rim_c, rim_d, *ret_y)
-    rim_a = lax.ppermute(pay_a, "gx", flip(nx, 1))
-    rim_b = lax.ppermute(pay_b, "gx", odd_pairs(nx))
+    )(xrim, rim_c, rim_d, *pieces)
+    rim_b = lax.ppermute(pay_b, "gx", odd_pairs(nx, ring))
     rets = gather_x(back)
-    rets += swap(rets)
+    rim_a = swap(pay_a)
+    if ring:
+        rets.append(swap(rim_b[RIM_X:]))
     return tuple(
         call(
             lambda *refs: final_body(len(rets), *refs),
             [velocity.shape, (3, P_SIZE)],
-            13 + len(rets),
+            14 + len(rets),
             "final",
             scratch=[pltpu.VMEM(velocity.shape, F32), dma((N_CHUNK,))],
             out_specs=[HB, VM],
-        )(main, x_faces, y_faces, block, face_a, face_b, rec_c, rec_d, rim_a, rim_b, rim_c, rim_d, back, *rets)
+        )(main_low, main_high, x_faces, y_faces, block, face_a, face_b, rec_c, rec_d, rim_a, rim_b, rim_c, rim_d, back, *rets)
     )
 
 

time: 70.9 us -> 61.6 us (0.87)
  starting transfers between devices: 29.2 us -> 17.8 us
  waiting for transfers between devices: 9.33 us -> 16 us
  Pallas kernels: 23.3 us -> 20.7 us
  local copies, waits for them, and re-layouts: 6.95 us -> 5.3 us
    ppermute x21 -> x13, starting transfers between devices: 24.7 us -> 12.5 us  [the longest x2 5.66 us: gather_y(): got = lax.ppermute(join(pieces), 'gy', flip(ny, bit))]
    ppermute x1, waiting for transfers between devices: 0.01 us -> 4.61 us  [per_device(): rim_c = lax.ppermute(pay_c, 'gy', flip(ny, 1))]
    ppermute x21 -> x13, waiting for transfers between devices: 9.32 us -> 11.3 us  [the longest x1 3.78 us: per_device(): rim_b = lax.ppermute(pay_b, 'gx', odd_pairs(nx, ring))]
    pallas_call x5 -> x6, Pallas kernels: 11.6 us -> 9.88 us  [the longest x1 4.37 us: per_device(): call(sample_body, [(HOST, CZ)], 3, 'sample', vmem=24)]
    unnamed x20 -> x18, local copies, waits for them, and re-layouts: 6.95 us -> 5.29 us
  transfers between devices with their start and end apart: 25 -> 17, of which waited for: 7 -> 10; matrix products, arithmetic and copies ran while one was open for 0% -> 0% of each run, Pallas kernels for 22% -> 21%
where the time goes in v3:
time: 61.6 us; the launch traced here: 61.4 us
  Pallas kernels  20.7 us (34%)
  starting transfers between devices  17.8 us (29%)
  waiting for transfers between devices  16 us (26%)
  local copies, waits for them, and re-layouts  5.3 us (9%)
  between operations  1.6 us (3%)
    ppermute x2, starting transfers between devices, gather_y(): got = lax.ppermute(join(pieces), 'gy', flip(ny, bit))  5.66 us
    unnamed x18, local copies, waits for them, and re-layouts  5.29 us
    ppermute x1, waiting for transfers between devices, per_device(): rim_c = lax.ppermute(pay_c, 'gy', flip(ny, 1))  4.61 us
    pallas_call x1, Pallas kernels, per_device(): call(stencil_body, [velocity.shape, (6, CX, CZ), (6, CY, CZ)], 1, 'stenci...  4.46 us
    pallas_call x1, Pallas kernels, per_device(): call(sample_body, [(HOST, CZ)], 3, 'sample', vmem=24)  4.37 us
    ppermute x1, waiting for transfers between devices, per_device(): rim_b = lax.ppermute(pay_b, 'gx', odd_pairs(nx, ring))  3.78 us
    pallas_call x2, Pallas kernels, spread(): call(lambda *refs: spread_body(start, *refs), [(3, CX // 2, CY, CZ)], 4,...  3.6 us
    ppermute x1, waiting for transfers between devices, per_device(): face_b = lax.ppermute(pay_b, 'gx', odd_pairs(nx, ring))  3.18 us
  transfers between devices with their start and end apart: 17, of which 10 were waited for; matrix products, arithmetic and copies ran while one was open for 0% of the time, Pallas kernels for 21%

profile of v3, /device:TPU:0, one launch (start us, length us, event | category | flops | bytes accessed | tf_op | source)
XLA Modules:
  0.0 61.4 jit_solution(16667992612655034402)
XLA Ops:
  1.3 1.9 %copy-done = f32[3,64,32,128]{3,2,1,0:T(8,128)S(1)} copy-done((f32[3,64,32,128]{3,2,1,0:T(8,128)S(1)}, f32[3,64,32,128]{3,2,1,0:T(8,128)}, u32[]{:S(2)}) %copy-start) | copy-done | bytes 3145752
  3.2 0.7 %copy-done.4 = f32[256]{0:T(256)S(1)} copy-done((f32[256]{0:T(256)S(1)}, f32[256]{0:T(256)}, u32[]{:S(2)}) %copy-start.4) | copy-done | bytes 1048
  3.9 0.7 %copy-done.5 = f32[256]{0:T(256)S(1)} copy-done((f32[256]{0:T(256)S(1)}, f32[256]{0:T(256)}, u32[]{:S(2)}) %copy-start.5) | copy-done | bytes 1048
  4.5 0.7 %copy-done.6 = f32[256]{0:T(256)S(1)} copy-done((f32[256]{0:T(256)S(1)}, f32[256]{0:T(256)}, u32[]{:S(2)}) %copy-start.6) | copy-done | bytes 1048
  5.2 0.7 %copy-done.7 = f32[256]{0:T(256)S(1)} copy-done((f32[256]{0:T(256)S(1)}, f32[256]{0:T(256)}, u32[]{:S(2)}) %copy-start.7) | copy-done | bytes 1048
  5.9 0.7 %copy-done.8 = s32[256]{0:T(256)S(1)} copy-done((s32[256]{0:T(256)S(1)}, s32[256]{0:T(256)}, u32[]{:S(2)}) %copy-start.8) | copy-done | bytes 1048
  6.6 0.8 %pack.1 = (f32[208,128]{1,0:T(8,128)S(1)}, f32[192,128]{1,0:T(8,128)S(1)}, f32[16,128]{1,0:T(8,128)S(1)}) custom-call(f32[3,64,32,128]{3,2,1,0:T(8,128)S(1)} %copy-done, f32[1]{0:T(128)S(6)} %copy.11.spin_hbm, f32[2,128]{1,0:T(2,128)S(1)} %bitcast.5, f32[2,128]{1,0:T(2,128)S(1)} %bitcast.6, f32[2,128]{1,0:T(2,128)S(1)} %bitcast.7, f32[2,128]{1,0:T(2,128)S(1)} %bitcast.8, ...), custom_call_target="tpu_custom_call" | custom-call | tf_op jit(solution)/shard_map/pack/pallas_call | solution.py:529
  7.4 3.1 %collective-permute-start = (f32[208,128]{1,0:T(8,128)S(1)}, f32[208,128]{1,0:T(8,128)S(1)}, u32[]{:S(2)}, u32[]{:S(2)}) collective-permute-start(f32[208,128]{1,0:T(8,128)S(1)} %get-tuple-element.34), channel_id=1, source_target_pairs={{0,1},{1,0},{2,3},{3,2},{4,5},{5,4},{6,7},{7,6},{8,9},{9,8},{10,11... | collective-permute-start | bytes 319496 | tf_op jit(solution)/shard_map/ppermute | solution.py:537
  10.5 0.7 %collective-permute-start.2 = (f32[192,128]{1,0:T(8,128)S(1)}, f32[192,128]{1,0:T(8,128)S(1)}, u32[]{:S(2)}, u32[]{:S(2)}) collective-permute-start(f32[192,128]{1,0:T(8,128)S(1)} %get-tuple-element.39), channel_id=1, source_target_pairs={{1,2},{2,1},{5,6},{6,5},{9,10},{10,9},{13,14},{14,13},{17,18},{18,... | collective-permute-start | bytes 294920 | tf_op jit(solution)/shard_map/ppermute | solution.py:538
  11.2 4.5 %stencil.1 = (f32[3,64,32,128]{3,2,1,0:T(8,128)S(1)}, f32[6,64,128]{2,1,0:T(8,128)S(1)}, f32[6,32,128]{2,1,0:T(8,128)S(1)}) custom-call(f32[3,64,32,128]{3,2,1,0:T(8,128)S(1)} %copy-done), custom_call_target="tpu_custom_call" | custom-call | tf_op jit(solution)/shard_map/stencil/pallas_call | solution.py:539
  15.7 3.9 %collective-permute-start.1 = (f32[32,128]{1,0:T(8,128)S(1)}, f32[32,128]{1,0:T(8,128)S(1)}, u32[]{:S(2)}, u32[]{:S(2)}) collective-permute-start(f32[32,128]{1,0:T(8,128)S(1)} %pad_maximum_fusion.refs_3_), channel_id=1, source_target_pairs={{0,2},{1,3},{2,0},{3,1},{4,6},{5,7},{6,4},{7,5},{8,10},{9,11},{10,... | collective-permute-start | bytes 49160 | tf_op jit(solution)/shard_map/ppermute | solution.py:513
  19.6 4.4 %sample.1.refs_0_ = f32[512,128]{1,0:T(8,128)S(1)} custom-call(f32[3,64,32,128]{3,2,1,0:T(8,128)S(1)} %copy-done.1, s32[3,512]{1,0:T(4,128)S(1)} %copy-done.2, f32[3,512]{1,0:T(4,128)S(1)} %copy-done.3), custom_call_target="tpu_custom_call" | custom-call | tf_op jit(solution)/shard_map/sample/pallas_call | solution.py:548
  24.6 0.7 %collective-permute-done.3.refs_5_ = f32[32,128]{1,0:T(8,128)S(1)} collective-permute-done((f32[32,128]{1,0:T(8,128)S(1)}, f32[32,128]{1,0:T(8,128)S(1)}, u32[]{:S(2)}, u32[]{:S(2)}) %collective-permute-start.3) | collective-permute-done | bytes 16416 | tf_op jit(solution)/shard_map/ppermute | solution.py:502
  25.4 2.5 %collective-permute-start.6 = (f32[248,128]{1,0:T(8,128)S(1)}, f32[248,128]{1,0:T(8,128)S(1)}, u32[]{:S(2)}, u32[]{:S(2)}) collective-permute-start(f32[248,128]{1,0:T(8,128)S(1)} %get-tuple-element.42), channel_id=1, source_target_pairs={{4,8},{12,16},{20,24},{28,0},{8,4},{16,12},{24,20},{0,28},{5,9},{1... | collective-permute-start | bytes 380936 | tf_op jit(solution)/shard_map/ppermute | solution.py:558
  27.9 0.5 collective-permute-start.7
  28.4 3.2 %collective-permute-done.6.refs_2_.refs_6_ = f32[248,128]{1,0:T(8,128)S(1)} collective-permute-done((f32[248,128]{1,0:T(8,128)S(1)}, f32[248,128]{1,0:T(8,128)S(1)}, u32[]{:S(2)}, u32[]{:S(2)}) %collective-permute-start.6) | collective-permute-done | bytes 127008 | tf_op jit(solution)/shard_map/ppermute | solution.py:558
  32.1 0.9 %collective-permute-done.5.refs_1_.refs_5_ = f32[120,128]{1,0:T(8,128)S(1)} collective-permute-done((f32[120,128]{1,0:T(8,128)S(1)}, f32[120,128]{1,0:T(8,128)S(1)}, u32[]{:S(2)}, u32[]{:S(2)}) %collective-permute-start.5) | collective-permute-done | bytes 61472 | tf_op jit(solution)/shard_map/ppermute | solution.py:502
  33.0 2.4 %select.1 = (f32[8,512]{1,0:T(8,128)S(1)}, f32[32,128]{1,0:T(8,128)S(1)}, f32[512,128]{1,0:T(8,128)S(1)}) custom-call(f32[512,128]{1,0:T(8,128)S(1)} %sample.1.refs_0_, f32[120,128]{1,0:T(8,128)S(1)} %collective-permute-done.5.refs_1_.refs_5_, f32[248,128]{1,0:T(8,128)S(1)} %collective-permute-done.6.refs_2_.refs_6_, ...), custom_call_target="tpu_custom_call" | custom-call | tf_op jit(solution)/shard_map/select/pallas_call | solution.py:563
  35.8 0.7 %weights.1 = (f32[72,512]{1,0:T(8,128)S(1)}, f32[40,512]{1,0:T(8,128)S(1)}, f32[512,128]{1,0:T(8,128)S(1)}) custom-call(f32[512,128]{1,0:T(8,128)S(1)} %get-tuple-element.46.pts_ref), custom_call_target="tpu_custom_call" | custom-call | tf_op jit(solution)/shard_map/weights/pallas_call | solution.py:570
  36.7 1.8 %loads.1 = (f32[512,384]{1,0:T(8,128)S(1)}, f32[448,128]{1,0:T(8,128)S(1)}, f32[432,128]{1,0:T(8,128)S(1)}, f32[16,128]{1,0:T(8,128)S(1)}, f32[384,128]{1,0:T(8,128)S(1)}) custom-call(f32[8,512]{1,0:T(8,128)S(1)} %get-tuple-element.44.samp_ref, f32[8,512]{1,0:T(8,128)S(1)} %collective-permute-done.9.other_ref, f32[32,128]{1,0:T(8,128)S(1)} %get-tuple-element.45.sel_ref, ...), custom_call_target="tpu_custom_call" | custom-call | tf_op jit(solution)/shard_map/loads/pallas_call | solution.py:571
  38.5 0.7 %collective-permute-start.10 = (f32[448,128]{1,0:T(8,128)S(1)}, f32[448,128]{1,0:T(8,128)S(1)}, u32[]{:S(2)}, u32[]{:S(2)}) collective-permute-start(f32[448,128]{1,0:T(8,128)S(1)} %get-tuple-element.50), channel_id=1, source_target_pairs={{0,1},{1,0},{2,3},{3,2},{4,5},{5,4},{6,7},{7,6},{8,9},{9,8},{10,11... | collective-permute-start | bytes 688136 | tf_op jit(solution)/shard_map/ppermute | solution.py:577
  39.2 0.8 %collective-permute-start.12 = (f32[432,128]{1,0:T(8,128)S(1)}, f32[432,128]{1,0:T(8,128)S(1)}, u32[]{:S(2)}, u32[]{:S(2)}) collective-permute-start(f32[432,128]{1,0:T(8,128)S(1)} %get-tuple-element.59), channel_id=1, source_target_pairs={{1,2},{2,1},{5,6},{6,5},{9,10},{10,9},{13,14},{14,13},{17,18},{18,... | collective-permute-start | bytes 663560 | tf_op jit(solution)/shard_map/ppermute | solution.py:578
  40.0 1.8 %spread.2.refs_0_ = f32[3,32,32,128]{3,2,1,0:T(8,128)S(1)} custom-call(f32[512,384]{1,0:T(8,128)S(1)} %get-tuple-element.51.refs_0_, f32[72,512]{1,0:T(8,128)S(1)} %get-tuple-element.47.gx_ref.refs_1_, f32[40,512]{1,0:T(8,128)S(1)} %get-tuple-element.48.gy_ref.refs_2_, f32[3,64,32,128]{3,2,1,0:T(8,128)S(1)} %get-tuple-element.52.refs_3_), custom_call_target="tpu_custom_call" | custom-call | tf_op jit(solution)/shard_map/spread/pallas_call | solution.py:581
  41.8 4.6 %collective-permute-done.10.refs_1_.refs_11_ = f32[448,128]{1,0:T(8,128)S(1)} collective-permute-done((f32[448,128]{1,0:T(8,128)S(1)}, f32[448,128]{1,0:T(8,128)S(1)}, u32[]{:S(2)}, u32[]{:S(2)}) %collective-permute-start.10) | collective-permute-done | bytes 229408 | tf_op jit(solution)/shard_map/ppermute | solution.py:577
  46.4 1.8 %collective-permute-start.11 = (f32[32,128]{1,0:T(8,128)S(1)}, f32[32,128]{1,0:T(8,128)S(1)}, u32[]{:S(2)}, u32[]{:S(2)}) collective-permute-start(f32[32,128]{1,0:T(8,128)S(1)} %pad_maximum_fusion.1.refs_3_), channel_id=1, source_target_pairs={{0,2},{1,3},{2,0},{3,1},{4,6},{5,7},{6,4},{7,5},{8,10},{9,11},{10,... | collective-permute-start | bytes 49160 | tf_op jit(solution)/shard_map/ppermute | solution.py:513
  48.2 1.8 %spread.3.refs_1_ = f32[3,32,32,128]{3,2,1,0:T(8,128)S(1)} custom-call(f32[512,384]{1,0:T(8,128)S(1)} %get-tuple-element.51.refs_0_, f32[72,512]{1,0:T(8,128)S(1)} %get-tuple-element.47.gx_ref.refs_1_, f32[40,512]{1,0:T(8,128)S(1)} %get-tuple-element.48.gy_ref.refs_2_, f32[3,64,32,128]{3,2,1,0:T(8,128)S(1)} %get-tuple-element.52.refs_3_), custom_call_target="tpu_custom_call" | custom-call | tf_op jit(solution)/shard_map/spread/pallas_call | solution.py:581
  50.0 1.3 %collective-permute-done.11.refs_4_ = f32[32,128]{1,0:T(8,128)S(1)} collective-permute-done((f32[32,128]{1,0:T(8,128)S(1)}, f32[32,128]{1,0:T(8,128)S(1)}, u32[]{:S(2)}, u32[]{:S(2)}) %collective-permute-start.11) | collective-permute-done | bytes 16416 | tf_op jit(solution)/shard_map/ppermute | solution.py:513
  51.4 1.7 %collective-permute-start.13 = (f32[192,128]{1,0:T(8,128)S(1)}, f32[192,128]{1,0:T(8,128)S(1)}, u32[]{:S(2)}, u32[]{:S(2)}) collective-permute-start(f32[192,128]{1,0:T(8,128)S(1)} %get-tuple-element.61), channel_id=1, source_target_pairs={{0,4},{4,0},{8,12},{12,8},{16,20},{20,16},{24,28},{28,24},{1,5},{5... | collective-permute-start | bytes 294920 | tf_op jit(solution)/shard_map/ppermute | solution.py:502
  53.1 0.7 %collective-permute-start.15 = (f32[64,128]{1,0:T(8,128)S(1)}, f32[64,128]{1,0:T(8,128)S(1)}, u32[]{:S(2)}, u32[]{:S(2)}) collective-permute-start(f32[64,128]{1,0:T(8,128)S(1)} %get-tuple-element.63.refs_13_), channel_id=1, source_target_pairs={{0,16},{4,20},{8,24},{12,28},{16,0},{20,4},{24,8},{28,12},{1,17},{... | collective-permute-start | bytes 98312 | tf_op jit(solution)/shard_map/ppermute | solution.py:524
  53.8 3.8 %collective-permute-done.14.refs_10_ = f32[256,128]{1,0:T(8,128)S(1)} collective-permute-done((f32[256,128]{1,0:T(8,128)S(1)}, f32[256,128]{1,0:T(8,128)S(1)}, u32[]{:S(2)}, u32[]{:S(2)}) %collective-permute-start.14) | collective-permute-done | bytes 131104 | tf_op jit(solution)/shard_map/ppermute | solution.py:594
  57.7 1.1 %collective-permute-done.16.refs_15_ = f32[64,128]{1,0:T(8,128)S(1)} collective-permute-done((f32[64,128]{1,0:T(8,128)S(1)}, f32[64,128]{1,0:T(8,128)S(1)}, u32[]{:S(2)}, u32[]{:S(2)}) %collective-permute-start.16) | collective-permute-done | bytes 32800 | tf_op jit(solution)/shard_map/ppermute | solution.py:502
  58.8 2.4 %final.1 = (f32[3,64,32,128]{3,2,1,0:T(8,128)}, f32[3,256]{1,0:T(4,128)}) custom-call(f32[3,32,32,128]{3,2,1,0:T(8,128)S(1)} %spread.2.refs_0_, f32[3,32,32,128]{3,2,1,0:T(8,128)S(1)} %spread.3.refs_1_, f32[6,32,128]{2,1,0:T(8,128)S(1)} %get-tuple-element.38.refs_0_.refs_2_, f32[6,64,128]{2,1,0:T(8,128)S(1)} %get-tuple-element.57.refs_3_, ...), custom_call_target="tpu_custom_call" | custom-call | tf_op jit(solution)/shard_map/final/pallas_call | solution.py:600
  (37 shorter events, 2.1 us)
Async XLA Ops:
  1.3 1.9 %copy-start = (f32[3,64,32,128]{3,2,1,0:T(8,128)S(1)}, f32[3,64,32,128]{3,2,1,0:T(8,128)}, u32[]{:S(2)}) copy-start(f32[3,64,32,128]{3,2,1,0:T(8,128)} %v_ref.5) | copy-start | bytes 9437188
  3.2 0.7 %copy-start.4 = (f32[256]{0:T(256)S(1)}, f32[256]{0:T(256)}, u32[]{:S(2)}) copy-start(f32[256]{0:T(256)} %param.15) | copy-start | bytes 3076
  3.8 0.7 %copy-start.5 = (f32[256]{0:T(256)S(1)}, f32[256]{0:T(256)}, u32[]{:S(2)}) copy-start(f32[256]{0:T(256)} %param.16) | copy-start | bytes 3076
  4.5 0.7 %copy-start.6 = (f32[256]{0:T(256)S(1)}, f32[256]{0:T(256)}, u32[]{:S(2)}) copy-start(f32[256]{0:T(256)} %param.17) | copy-start | bytes 3076
  5.2 0.7 %copy-start.7 = (f32[256]{0:T(256)S(1)}, f32[256]{0:T(256)}, u32[]{:S(2)}) copy-start(f32[256]{0:T(256)} %param.18) | copy-start | bytes 3076
  5.9 0.7 %copy-start.8 = (s32[256]{0:T(256)S(1)}, s32[256]{0:T(256)}, u32[]{:S(2)}) copy-start(s32[256]{0:T(256)} %param.13) | copy-start | bytes 3076
  6.6 13.0 %copy-start.1 = (f32[3,64,32,128]{3,2,1,0:T(8,128)S(1)}, f32[3,64,32,128]{3,2,1,0:T(8,128)}, u32[]{:S(2)}) copy-start(f32[3,64,32,128]{3,2,1,0:T(8,128)} %v_ref.5) | copy-start | bytes 9437188
  6.6 13.0 %copy-start.2 = (s32[3,512]{1,0:T(4,128)S(1)}, s32[3,512]{1,0:T(4,128)}, u32[]{:S(2)}) copy-start(s32[3,512]{1,0:T(4,128)} %cell_ref.1) | copy-start | bytes 18436
  6.6 13.0 %copy-start.3 = (f32[3,512]{1,0:T(4,128)S(1)}, f32[3,512]{1,0:T(4,128)}, u32[]{:S(2)}) copy-start(f32[3,512]{1,0:T(4,128)} %frac_ref.1) | copy-start | bytes 18436
  7.4 8.2 %collective-permute-start = (f32[208,128]{1,0:T(8,128)S(1)}, f32[208,128]{1,0:T(8,128)S(1)}, u32[]{:S(2)}, u32[]{:S(2)}) collective-permute-start(f32[208,128]{1,0:T(8,128)S(1)} %get-tuple-element.34), channel_id=1, source_target_pairs={{0,1},{1,0},{2,3},{3,2},{4,5},{5,4},{6,7},{7,6},{8,9},{9,8},{10,11... | collective-permute-start | bytes 319496 | tf_op jit(solution)/shard_map/ppermute | solution.py:537
  10.5 14.0 %collective-permute-start.2 = (f32[192,128]{1,0:T(8,128)S(1)}, f32[192,128]{1,0:T(8,128)S(1)}, u32[]{:S(2)}, u32[]{:S(2)}) collective-permute-start(f32[192,128]{1,0:T(8,128)S(1)} %get-tuple-element.39), channel_id=1, source_target_pairs={{1,2},{2,1},{5,6},{6,5},{9,10},{10,9},{13,14},{14,13},{17,18},{18,... | collective-permute-start | bytes 294920 | tf_op jit(solution)/shard_map/ppermute | solution.py:538
  15.7 8.4 %collective-permute-start.1 = (f32[32,128]{1,0:T(8,128)S(1)}, f32[32,128]{1,0:T(8,128)S(1)}, u32[]{:S(2)}, u32[]{:S(2)}) collective-permute-start(f32[32,128]{1,0:T(8,128)S(1)} %pad_maximum_fusion.refs_3_), channel_id=1, source_target_pairs={{0,2},{1,3},{2,0},{3,1},{4,6},{5,7},{6,4},{7,5},{8,10},{9,11},{10,... | collective-permute-start | bytes 49160 | tf_op jit(solution)/shard_map/ppermute | solution.py:513
  24.0 1.2 %collective-permute-start.3 = (f32[32,128]{1,0:T(8,128)S(1)}, f32[32,128]{1,0:T(8,128)S(1)}, u32[]{:S(2)}, u32[]{:S(2)}) collective-permute-start(f32[32,128]{1,0:T(8,128)S(1)} %pad_maximum_fusion.refs_3_), channel_id=1, source_target_pairs={{0,4},{4,0},{8,12},{12,8},{16,20},{20,16},{24,28},{28,24},{1,5},{5... | collective-permute-start | bytes 49160 | tf_op jit(solution)/shard_map/ppermute | solution.py:502
  24.1 1.3 %collective-permute-start.4 = (f32[32,128]{1,0:T(8,128)S(1)}, f32[32,128]{1,0:T(8,128)S(1)}, u32[]{:S(2)}, u32[]{:S(2)}) collective-permute-start(f32[32,128]{1,0:T(8,128)S(1)} %collective-permute-done.1.refs_4_), channel_id=1, source_target_pairs={{0,4},{4,0},{8,12},{12,8},{16,20},{20,16},{24,28},{28,24},{1,5},{5... | collective-permute-start | bytes 49160 | tf_op jit(solution)/shard_map/ppermute | solution.py:502
  25.4 6.1 %collective-permute-start.6 = (f32[248,128]{1,0:T(8,128)S(1)}, f32[248,128]{1,0:T(8,128)S(1)}, u32[]{:S(2)}, u32[]{:S(2)}) collective-permute-start(f32[248,128]{1,0:T(8,128)S(1)} %get-tuple-element.42), channel_id=1, source_target_pairs={{4,8},{12,16},{20,24},{28,0},{8,4},{16,12},{24,20},{0,28},{5,9},{1... | collective-permute-start | bytes 380936 | tf_op jit(solution)/shard_map/ppermute | solution.py:558
  27.9 5.1 %collective-permute-start.7 = (f32[128,128]{1,0:T(8,128)S(1)}, f32[128,128]{1,0:T(8,128)S(1)}, u32[]{:S(2)}, u32[]{:S(2)}) collective-permute-start(f32[128,128]{1,0:T(8,128)S(1)} %get-tuple-element.43.refs_5_), channel_id=1, source_target_pairs={{0,16},{4,20},{8,24},{12,28},{16,0},{20,4},{24,8},{28,12},{1,17},{... | collective-permute-start | bytes 196616 | tf_op jit(solution)/shard_map/ppermute | solution.py:524
  31.6 1.4 %collective-permute-start.8 = (f32[128,128]{1,0:T(8,128)S(1)}, f32[128,128]{1,0:T(8,128)S(1)}, u32[]{:S(2)}, u32[]{:S(2)}) collective-permute-start(f32[128,128]{1,0:T(8,128)S(1)} %slice.16), channel_id=1, source_target_pairs={{0,4},{4,0},{8,12},{12,8},{16,20},{20,16},{24,28},{28,24},{1,5},{5... | collective-permute-start | bytes 196616 | tf_op jit(solution)/shard_map/ppermute | solution.py:502
  31.6 1.4 %collective-permute-start.5 = (f32[120,128]{1,0:T(8,128)S(1)}, f32[120,128]{1,0:T(8,128)S(1)}, u32[]{:S(2)}, u32[]{:S(2)}) collective-permute-start(f32[120,128]{1,0:T(8,128)S(1)} %get-tuple-element.41), channel_id=1, source_target_pairs={{0,4},{4,0},{8,12},{12,8},{16,20},{20,16},{24,28},{28,24},{1,5},{5... | collective-permute-start | bytes 184328 | tf_op jit(solution)/shard_map/ppermute | solution.py:502
  35.4 1.2 %collective-permute-start.9 = (f32[8,512]{1,0:T(8,128)S(1)}, f32[8,512]{1,0:T(8,128)S(1)}, u32[]{:S(2)}, u32[]{:S(2)}) collective-permute-start(f32[8,512]{1,0:T(8,128)S(1)} %get-tuple-element.44.samp_ref), channel_id=1, source_target_pairs={{0,4},{4,0},{8,12},{12,8},{16,20},{20,16},{24,28},{28,24},{1,5},{5... | collective-permute-start | bytes 49160 | tf_op jit(solution)/shard_map/ppermute | solution.py:502
  38.5 7.9 %collective-permute-start.10 = (f32[448,128]{1,0:T(8,128)S(1)}, f32[448,128]{1,0:T(8,128)S(1)}, u32[]{:S(2)}, u32[]{:S(2)}) collective-permute-start(f32[448,128]{1,0:T(8,128)S(1)} %get-tuple-element.50), channel_id=1, source_target_pairs={{0,1},{1,0},{2,3},{3,2},{4,5},{5,4},{6,7},{7,6},{8,9},{9,8},{10,11... | collective-permute-start | bytes 688136 | tf_op jit(solution)/shard_map/ppermute | solution.py:577
  39.2 12.1 %collective-permute-start.12 = (f32[432,128]{1,0:T(8,128)S(1)}, f32[432,128]{1,0:T(8,128)S(1)}, u32[]{:S(2)}, u32[]{:S(2)}) collective-permute-start(f32[432,128]{1,0:T(8,128)S(1)} %get-tuple-element.59), channel_id=1, source_target_pairs={{1,2},{2,1},{5,6},{6,5},{9,10},{10,9},{13,14},{14,13},{17,18},{18,... | collective-permute-start | bytes 663560 | tf_op jit(solution)/shard_map/ppermute | solution.py:578
  46.4 4.8 %collective-permute-start.11 = (f32[32,128]{1,0:T(8,128)S(1)}, f32[32,128]{1,0:T(8,128)S(1)}, u32[]{:S(2)}, u32[]{:S(2)}) collective-permute-start(f32[32,128]{1,0:T(8,128)S(1)} %pad_maximum_fusion.1.refs_3_), channel_id=1, source_target_pairs={{0,2},{1,3},{2,0},{3,1},{4,6},{5,7},{6,4},{7,5},{8,10},{9,11},{10,... | collective-permute-start | bytes 49160 | tf_op jit(solution)/shard_map/ppermute | solution.py:513
  51.3 6.2 %collective-permute-start.14 = (f32[256,128]{1,0:T(8,128)S(1)}, f32[256,128]{1,0:T(8,128)S(1)}, u32[]{:S(2)}, u32[]{:S(2)}) collective-permute-start(f32[256,128]{1,0:T(8,128)S(1)} %get-tuple-element.62), channel_id=1, source_target_pairs={{4,8},{12,16},{20,24},{28,0},{8,4},{16,12},{24,20},{0,28},{5,9},{1... | collective-permute-start | bytes 393224 | tf_op jit(solution)/shard_map/ppermute | solution.py:594
  51.4 6.3 %collective-permute-start.13 = (f32[192,128]{1,0:T(8,128)S(1)}, f32[192,128]{1,0:T(8,128)S(1)}, u32[]{:S(2)}, u32[]{:S(2)}) collective-permute-start(f32[192,128]{1,0:T(8,128)S(1)} %get-tuple-element.61), channel_id=1, source_target_pairs={{0,4},{4,0},{8,12},{12,8},{16,20},{20,16},{24,28},{28,24},{1,5},{5... | collective-permute-start | bytes 294920 | tf_op jit(solution)/shard_map/ppermute | solution.py:502
  53.1 4.6 %collective-permute-start.15 = (f32[64,128]{1,0:T(8,128)S(1)}, f32[64,128]{1,0:T(8,128)S(1)}, u32[]{:S(2)}, u32[]{:S(2)}) collective-permute-start(f32[64,128]{1,0:T(8,128)S(1)} %get-tuple-element.63.refs_13_), channel_id=1, source_target_pairs={{0,16},{4,20},{8,24},{12,28},{16,0},{20,4},{24,8},{28,12},{1,17},{... | collective-permute-start | bytes 98312 | tf_op jit(solution)/shard_map/ppermute | solution.py:524
  57.6 1.2 %collective-permute-start.16 = (f32[64,128]{1,0:T(8,128)S(1)}, f32[64,128]{1,0:T(8,128)S(1)}, u32[]{:S(2)}, u32[]{:S(2)}) collective-permute-start(f32[64,128]{1,0:T(8,128)S(1)} %slice.17), channel_id=1, source_target_pairs={{0,4},{4,0},{8,12},{12,8},{16,20},{20,16},{24,28},{28,24},{1,5},{5... | collective-permute-start | bytes 98312 | tf_op jit(solution)/shard_map/ppermute | solution.py:502

commit v4 on v3

--- a/solution.py
+++ b/solution.py
@@ -79,14 +79,16 @@
 
 
 def pack_body(v_ref, spin_hbm, *rest):
-    params, (pay_c, pay_d, blk_ref, low, high, held, held_int, spin_ref, sems) = rest[:5], rest[5:]
-    _, even_y, _, _, _, _ = place()
+    params, (pay_c, pay_d, blk_ref, x_ref, y_ref, low, high, held, held_int, spin_ref, sems) = rest[:5], rest[5:]
+    _, even_y, _, brick, _, _ = place()
     small = [pltpu.make_async_copy(spin_hbm, spin_ref, sems.at[2])]
     small += [pltpu.make_async_copy(p, held.at[k], sems.at[3 + k]) for k, p in enumerate(params[:4])]
     small.append(pltpu.make_async_copy(params[4], held_int, sems.at[7]))
     copies = [
         pltpu.make_async_copy(v_ref.at[:, :, pl.ds(0, 8)], low, sems.at[0]),
         pltpu.make_async_copy(v_ref.at[:, :, pl.ds(CY - 8, 8)], high, sems.at[1]),
+        pltpu.make_async_copy(v_ref.at[:, 0], x_ref.at[pl.ds(0, 3)], sems.at[8]),
+        pltpu.make_async_copy(v_ref.at[:, CX - 1], x_ref.at[pl.ds(3, 3)], sems.at[9]),
     ]
     for copy in small + copies:
         copy.start()
@@ -96,12 +98,13 @@
     parts = [
         radius,
         chord,
-        radius * spin_ref[0],
         jnp.cos(twist),
         jnp.sin(twist),
         jnp.cos(angle),
         jnp.sin(angle),
         held_int[...].astype(F32),
+        jnp.full((1, CZ), spin_ref[0], F32),
+        jnp.full((1, CZ), brick.astype(F32), F32),
     ]
     block = jnp.concatenate(parts, axis=0)
     blk_ref[...] = block
@@ -111,27 +114,25 @@
     for c in range(3):
         y_low = low[c, :, 0, :]
         y_high = high[c, :, 7, :]
+        y_ref[c] = y_low
+        y_ref[c + 3] = y_high
         pay_c[c * CX : (c + 1) * CX] = jnp.where(even_y, y_high, y_low)
         pay_d[c * CX : (c + 1) * CX] = jnp.where(even_y, y_low, y_high)
 
 
-def stencil_body(v_ref, out_ref, y_ref, x_ref, buf, sems):
+def stencil_body(start, v_ref, out_ref):
     row = lax.broadcasted_iota(jnp.int32, (CY, CZ), 0)
     lane = lax.broadcasted_iota(jnp.int32, (CY, CZ), 1)
-    copies = []
-    for k in range(N_CHUNK):
-        part = pl.ds(k * CHUNK, CHUNK)
-        copies.append(pltpu.make_async_copy(v_ref.at[:, part], buf.at[:, part], sems.at[k]))
-        copies[-1].start()
     half = 0.5 * DT_STEP
     visc = DT_STEP * NU_VISC
     not_last_y, not_first_y = row < CY - 1, row > 0
     not_last_z, not_first_z = lane < CZ - 1, lane > 0
 
-    def step(x, carry):
+    def step(k, carry):
+        x = start + k
         up = jnp.minimum(x + 1, CX - 1)
         down = jnp.maximum(x - 1, 0)
-        v0, v1, v2 = v_ref_of(buf, x)
+        v0, v1, v2 = v_ref[0, x], v_ref[1, x], v_ref[2, x]
         a_x = jnp.where(x < CX - 1, visc - half * v0, 0.0)
         b_x = jnp.where(x > 0, visc + half * v0, 0.0)
         a_y = jnp.where(not_last_y, visc - half * v1, 0.0)
@@ -140,26 +141,13 @@
         b_z = jnp.where(not_first_z, visc + half * v2, 0.0)
         for c in range(3):
             mid = (v0, v1, v2)[c]
-            along_x = a_x * buf[c, up] + b_x * buf[c, down]
+            along_x = a_x * v_ref[c, up] + b_x * v_ref[c, down]
             along_y = a_y * pltpu.roll(mid, CY - 1, 0) + b_y * pltpu.roll(mid, 1, 0)
             along_z = a_z * pltpu.roll(mid, CZ - 1, 1) + b_z * pltpu.roll(mid, 1, 1)
-            out_ref[c, x] = (1.0 - 6.0 * visc) * mid + along_x + (along_y + along_z)
-            y_ref[c, pl.ds(x, 1)] = mid[0:1]
-            y_ref[c + 3, pl.ds(x, 1)] = mid[CY - 1 : CY]
+            out_ref[c, k] = (1.0 - 6.0 * visc) * mid + along_x + (along_y + along_z)
         return carry
 
-    copies[0].wait()
-    for k in range(N_CHUNK):
-        if k + 1 < N_CHUNK:
-            copies[k + 1].wait()
-        lax.fori_loop(k * CHUNK, (k + 1) * CHUNK, step, 0, unroll=2)
-    for c in range(3):
-        x_ref[c] = buf[c, 0]
-        x_ref[c + 3] = buf[c, CX - 1]
-
-
-def v_ref_of(buf, x):
-    return buf[0, x], buf[1, x], buf[2, x]
+    lax.fori_loop(0, CX // 2, step, 0, unroll=2)
 
 
 def weight(coord, base, frac):
@@ -196,9 +184,33 @@
     tab_ref[...] = out
 
 
+def split_blocks(sources):
+    return [
+        ref[first + k * ROWS : first + (k + 1) * ROWS]
+        for ref, first in sources
+        for k in range((ref.shape[0] - first) // ROWS)
+    ]
+
+
+def pick_pair(values, b0, ny):
+    keys = [value[12:13, 0:1] for value in values]
+    members = []
+    for key in keys:
+        home = jnp.floor(key * (1.0 / HOST)).astype(jnp.int32)
+        members.append((home == b0) | (home == b0 + ny))
+    low_key = reduce_list([jnp.where(m, k, 1e9) for k, m in zip(keys, members)], jnp.minimum)
+    high_key = reduce_list([jnp.where(m, k, -9.0) for k, m in zip(keys, members)], jnp.maximum)
+    low = jnp.full((ROWS, CZ), -1.0, F32)
+    high = low
+    for key, value in zip(keys, values):
+        low = jnp.where(key == low_key, value, low)
+        high = jnp.where(key == high_key, value, high)
+    return low, high
+
+
 def xpack_body(n_blk, x_ref, rec_c, rec_d, *rest):
-    pieces, (pay_a, pay_b, blk_ref) = rest[:n_blk], rest[n_blk:]
-    even_x, even_y, inner, _, _, _ = place()
+    pieces, (pay_a, pay_b, own_ref, *others) = rest[:n_blk], rest[n_blk:]
+    even_x, even_y, inner, _, b0, ny = place()
     for c in range(3):
         at = c * CX
         y_high = jnp.where(even_y, rec_c[at : at + 1], rec_d[at : at + 1])
@@ -209,32 +221,23 @@
         pay_b[at : at + CY] = jnp.where(even_x, low, high)
         pay_a[at + CY : at + XROWS] = tail
         pay_b[at + CY : at + XROWS] = tail
-    blocks = jnp.concatenate([p[...] for p in pieces], axis=0)
-    blk_ref[...] = blocks
-    if pay_b.shape[0] > FACE_X:
-        pay_b[FACE_X:] = blocks
+    if not others:
+        own_ref[...] = jnp.concatenate([p[...] for p in pieces], axis=0)
+        return
+    values = split_blocks([(p, 0) for p in pieces])
+    chips = ny * 2
+    side = jnp.where(even_x, -chips, chips)
+    total = lax.axis_size("gx") * ny
+    own_ref[...] = jnp.concatenate(pick_pair(values, b0, ny), axis=0)
+    pay_b[FACE_X:] = jnp.concatenate(pick_pair(values, lax.rem(b0 + side + total, total), ny), axis=0)
+    others[0][...] = jnp.concatenate(pick_pair(values, lax.rem(b0 + 2 * chips, total), ny), axis=0)
 
 
 def select_body(n_blk, tab_ref, face_a, face_b, rec_c, rec_d, blk_ref, *rest):
     others, (samp_ref, sel_ref, pts_ref) = rest[:n_blk], rest[n_blk:]
     even_x, even_y, inner, brick, b0, ny = place()
-    b1 = b0 + ny
-    keys, members, values = [], [], []
-    for ref, first in [(blk_ref, 0), (face_b, FACE_X)] + [(o, 0) for o in others]:
-        for k in range((ref.shape[0] - first) // ROWS):
-            value = ref[first + k * ROWS : first + (k + 1) * ROWS]
-            key = value[14:15, 0:1]
-            home = key.astype(jnp.int32) // HOST
-            keys.append(key)
-            members.append((home == b0) | (home == b1))
-            values.append(value)
-    low_key = reduce_list([jnp.where(m, k, 1e9) for k, m in zip(keys, members)], jnp.minimum)
-    high_key = reduce_list([jnp.where(m, k, -1.0) for k, m in zip(keys, members)], jnp.maximum)
-    turbine_a = jnp.zeros((ROWS, CZ), F32)
-    turbine_b = jnp.zeros((ROWS, CZ), F32)
-    for key, value in zip(keys, values):
-        turbine_a = jnp.where(key == low_key, value, turbine_a)
-        turbine_b = jnp.where(key == high_key, value, turbine_b)
+    sources = [(blk_ref, 0), (face_b, FACE_X)] + [(o, 0) for o in others]
+    turbine_a, turbine_b = pick_pair(split_blocks(sources), b0, ny)
     sel = jnp.concatenate([turbine_a, turbine_b], axis=0)
     sel_ref[...] = sel
     turned = jnp.concatenate([sel, jnp.zeros((CZ - 2 * ROWS, CZ), F32)], axis=0).T
@@ -266,7 +269,7 @@
     for c in range(3):
         value = jnp.sum(acc[:, c * CZ : (c + 1) * CZ] * wz, axis=1, keepdims=True)
         table = table + jnp.where(lane == 6 + c, value, 0.0)
-    slot = column(7).astype(jnp.int32)
+    slot = column(6).astype(jnp.int32)
     mine = (slot // HOST) == brick
     local = jnp.where(mine, slot % HOST, -1)
     hit = (lax.broadcasted_iota(jnp.int32, (PTS, HOST), 1) == local).astype(F32).astype(BF16)
@@ -326,7 +329,8 @@
         picks = (2 * k, 2 * k + 1, ROWS + 2 * k, ROWS + 2 * k + 1)
         return jnp.concatenate([sel_ref[j : j + 1] for j in picks], axis=1)
 
-    radius, chord, spin, cos_t, sin_t, cos_a, sin_a = [row(k) for k in range(7)]
+    radius, chord, cos_t, sin_t, cos_a, sin_a = [row(k) for k in range(6)]
+    spin = radius * jnp.concatenate([sel_ref[j : j + 1] for j in (14, 14, ROWS + 14, ROWS + 14)], axis=1)
     flow = samp_ref[...] + other_ref[...]
     axial = flow[0:1]
     tangent = spin - (cos_a * flow[2:3] - sin_a * flow[1:2])
@@ -354,11 +358,9 @@
             for h in range(2):
                 at = t * P_SIZE + h * CZ
                 pieces.append(force[c][:, at : at + CZ])
-        key = sel_ref[t * ROWS + 14 : t * ROWS + 15, 0:1]
-        pieces.append(jnp.broadcast_to(key, (2, CZ)))
+        pieces += [sel_ref[t * ROWS + 15 : t * ROWS + 16]] * 2
     blocks = jnp.concatenate(pieces, axis=0)
     ret_ref[...] = blocks
-    pay_c[RIM_Y:] = blocks
     cols = jnp.concatenate(force + [jnp.zeros((CZ - 3, PTS), F32)], axis=0).T
     pz = pz_ref[...] * DT_STEP
     lines = jnp.concatenate([cols[:, c : c + 1] * pz for c in range(3)], axis=1)
@@ -398,12 +400,12 @@
         value = dot3(w_high, w_low, l_high, l_low)
         for c in range(3):
             part = value[:, c * CZ : (c + 1) * CZ].reshape(SPREAD_X, CY, CZ)
-            out_ref[c, at : at + SPREAD_X] = base_ref[c, first : first + SPREAD_X] + part
+            out_ref[c, at : at + SPREAD_X] = base_ref[c, at : at + SPREAD_X] + part
 
 
 def rimpack_body(n_blk, xrim_ref, rec_c, rec_d, *rest):
-    pieces, (pay_a, pay_b, back_ref) = rest[:n_blk], rest[n_blk:]
-    even_x, even_y, inner, _, _, _ = place()
+    pieces, (pay_a, pay_b, back_ref, *others) = rest[:n_blk], rest[n_blk:]
+    even_x, even_y, inner, _, b0, ny = place()
     zero = jnp.zeros((CY - 4, CZ), F32)
     for k in range(2):
         for c in range(3):
@@ -422,13 +424,26 @@
             pay_b[at : at + CY] = jnp.where(even_x, sides[0], sides[1])
     back = jnp.concatenate([p[...] for p in pieces], axis=0)
     back_ref[...] = back
-    if pay_b.shape[0] > RIM_X:
-        pay_b[RIM_X:] = back
-
-
-def final_body(n_ret, main_low, main_high, x_ref, y_ref, own_ref, face_a, face_b, yc_ref, yd_ref, rim_a, rim_b, rim_c, rim_d, back_ref, *rest):
+    if others:
+        chips = ny * 2
+        side = jnp.where(even_x, -chips, chips)
+        total = lax.axis_size("gx") * ny
+        for ref, at, target in (
+            (pay_b, RIM_X, lax.rem(b0 + side + total, total)),
+            (others[0], 0, lax.rem(b0 + 2 * chips, total)),
+        ):
+            for core in range(2):
+                wanted = (target + core * ny).astype(F32)
+                found = jnp.full((BACK, CZ), -1.0, F32)
+                for k in range(back.shape[0] // BACK):
+                    value = back[k * BACK : (k + 1) * BACK]
+                    found = jnp.where(value[6:7, 0:1] == wanted, value, found)
+                ref[at + core * BACK : at + (core + 1) * BACK] = found
+
+
+def final_body(n_ret, main_low, main_high, x_ref, y_ref, face_a, face_b, yc_ref, yd_ref, rim_a, rim_b, rim_c, rim_d, back_ref, *rest):
     rets, (out_ref, pf_ref, buf, sems) = rest[:n_ret], rest[n_ret:]
-    even_x, even_y, inner, _, _, _ = place()
+    even_x, even_y, inner, brick, _, _ = place()
     half = 0.5 * DT_STEP
     visc = DT_STEP * NU_VISC
     copies = []
@@ -464,7 +479,7 @@
                 buf[c, part, CY - 2 + i, :] += jnp.where(even_y, a, b) + high[i]
         copies.append(pltpu.make_async_copy(buf.at[:, pl.ds(first, CHUNK)], out_ref.at[:, pl.ds(first, CHUNK)], sems.at[k]))
         copies[-1].start()
-    mine = own_ref[14:15, 0:1]
+    mine = brick.astype(F32)
     found = jnp.zeros((BACK, CZ), F32)
     for ref, first in [(back_ref, 0), (rim_b, RIM_X)] + [(r, 0) for r in rets]:
         for k in range((ref.shape[0] - first) // BACK):
@@ -520,44 +535,44 @@
 
     def gather_x(blocks):
         pieces = []
-        for bit in [4] if ring else [b for b in (2, 4, 8, 16) if b < nx]:
-            pieces.append(lax.ppermute(join([blocks] + pieces) if not ring else blocks, "gx", flip(nx, bit)))
+        for bit in [b for b in (2, 4, 8, 16) if b < nx]:
+            pieces.append(lax.ppermute(join([blocks] + pieces), "gx", flip(nx, bit)))
         return pieces
 
     dma = pltpu.SemaphoreType.DMA
     tiles = pltpu.VMEM((3, CX, 8, CZ), F32)
-    pay_c, pay_d, block = call(
+    pay_c, pay_d, block, x_faces, y_faces = call(
         pack_body,
-        [(FACE_Y + ROWS, CZ), (FACE_Y, CZ), (ROWS, CZ)],
+        [(FACE_Y + ROWS, CZ), (FACE_Y, CZ), (ROWS, CZ), (6, CY, CZ), (6, CX, CZ)],
         7,
         "pack",
-        scratch=[tiles, tiles, pltpu.VMEM((4, 2, CZ), F32), pltpu.VMEM((2, CZ), jnp.int32), pltpu.SMEM((1,), F32), dma((8,))],
+        scratch=[tiles, tiles, pltpu.VMEM((4, 2, CZ), F32), pltpu.VMEM((2, CZ), jnp.int32), pltpu.SMEM((1,), F32), dma((10,))],
         in_specs=[HB] * 7,
+        vmem=56,
     )(velocity, rotor_speed, *[a.reshape(2, CZ) for a in (blade_radius, blade_chord, blade_twist, blade_angle, owner_src)])
     rec_c = lax.ppermute(pay_c, "gy", flip(ny, 1))
     rec_d = lax.ppermute(pay_d, "gy", odd_pairs(ny))
-    base, y_faces, x_faces = call(
-        stencil_body,
-        [velocity.shape, (6, CX, CZ), (6, CY, CZ)],
-        1,
-        "stencil",
-        scratch=[pltpu.VMEM(velocity.shape, F32), dma((N_CHUNK,))],
-        in_specs=[HB],
-    )(velocity)
-    rec_c, base = after(rec_c, base)
+
+    def stencil(start):
+        return call(lambda *refs: stencil_body(start, *refs), [(3, CX // 2, CY, CZ)], 1, "stencil")(velocity)[0]
+
+    rec_c, base_low = after(rec_c, stencil(0))
     sampled = lambda: call(sample_body, [(HOST, CZ)], 3, "sample", vmem=24)(velocity, host_cell, host_frac)[0]
     table, pieces = list(gather_y(join([block, rec_c[FACE_Y:]]), sampled))
     pieces = pieces + [swap(p) for p in pieces]
     n_rows = 2 * ny * ROWS
-    pay_a, pay_b, blocks = call(
+    pair = (2 * ROWS, CZ)
+    pay_a, pay_b, blocks, *across = call(
         lambda *refs: xpack_body(len(pieces), *refs),
-        [(FACE_X, CZ), (FACE_X + (n_rows if ring else 0), CZ), (n_rows, CZ)],
+        [(FACE_X, CZ), (FACE_X + 2 * ROWS, CZ), pair, pair] if ring else [(FACE_X, CZ), (FACE_X, CZ), (n_rows, CZ)],
         3 + len(pieces),
         "xpack",
     )(x_faces, rec_c, rec_d, *pieces)
     face_b = lax.ppermute(pay_b, "gx", odd_pairs(nx, ring))
-    from_x = gather_x(blocks)
+    from_x = [lax.ppermute(across[0], "gx", flip(nx, 4))] if ring else gather_x(blocks)
     face_a = swap(pay_a)
+    base_high = stencil(CX // 2)
+    face_b, base_high = after(face_b, base_high)
     if ring:
         from_x.append(swap(face_b[FACE_X:]))
     samp, sel, pts = call(
@@ -570,29 +585,32 @@
     gx, gy, pz = call(weights_body, [(YROWS, PTS), (CY + 8, PTS), (PTS, CZ)], 1, "weights")(pts)
     lines, pay_c, pay_d, ret, xrim = call(
         loads_body,
-        [(PTS, 3 * CZ), (RIM_Y + 2 * BACK, CZ), (RIM_Y, CZ), (2 * BACK, CZ), (2 * RIM_X, CZ)],
+        [(PTS, 3 * CZ), (RIM_Y, CZ), (RIM_Y, CZ), (2 * BACK, CZ), (2 * RIM_X, CZ)],
         7,
         "loads",
     )(samp, other, sel, pts, gx, gy, pz)
+    ret_c = lax.ppermute(ret, "gy", flip(ny, 1))
     rim_c = lax.ppermute(pay_c, "gy", flip(ny, 1))
     rim_d = lax.ppermute(pay_d, "gy", odd_pairs(ny))
 
-    def spread(start):
+    def spread(start, base):
         return call(
             lambda *refs: spread_body(start, *refs), [(3, CX // 2, CY, CZ)], 4, "spread"
         )(lines, gx, gy, base)[0]
 
-    rim_c, main_low = after(rim_c, spread(0))
-    main_high, pieces = list(gather_y(join([ret, rim_c[RIM_Y:]]), lambda: spread(CX // 2)))
+    ret_c, main_low = after(ret_c, spread(0, base_low))
+    main_high, pieces = list(gather_y(join([ret, ret_c]), lambda: spread(CX // 2, base_high)))
+    rim_c, main_high = after(rim_c, main_high)
     n_rows = 2 * ny * BACK
-    pay_a, pay_b, back = call(
+    pair = (2 * BACK, CZ)
+    pay_a, pay_b, back, *across = call(
         lambda *refs: rimpack_body(len(pieces), *refs),
-        [(RIM_X, CZ), (RIM_X + (n_rows if ring else 0), CZ), (n_rows, CZ)],
+        [(RIM_X, CZ), (RIM_X + 2 * BACK, CZ), (n_rows, CZ), pair] if ring else [(RIM_X, CZ), (RIM_X, CZ), (n_rows, CZ)],
         3 + len(pieces),
         "rimpack",
     )(xrim, rim_c, rim_d, *pieces)
     rim_b = lax.ppermute(pay_b, "gx", odd_pairs(nx, ring))
-    rets = gather_x(back)
+    rets = [lax.ppermute(across[0], "gx", flip(nx, 4))] if ring else gather_x(back)
     rim_a = swap(pay_a)
     if ring:
         rets.append(swap(rim_b[RIM_X:]))
@@ -600,11 +618,11 @@
         call(
             lambda *refs: final_body(len(rets), *refs),
             [velocity.shape, (3, P_SIZE)],
-            14 + len(rets),
+            13 + len(rets),
             "final",
             scratch=[pltpu.VMEM(velocity.shape, F32), dma((N_CHUNK,))],
             out_specs=[HB, VM],
-        )(main_low, main_high, x_faces, y_faces, block, face_a, face_b, rec_c, rec_d, rim_a, rim_b, rim_c, rim_d, back, *rets)
+        )(main_low, main_high, x_faces, y_faces, face_a, face_b, rec_c, rec_d, rim_a, rim_b, rim_c, rim_d, back, *rets)
     )
 
 

time: 61.6 us -> 54.3 us (0.88)
  local copies, waits for them, and re-layouts: 5.3 us -> 0.04 us
  waiting for transfers between devices: 16 us -> 11.2 us
  starting transfers between devices: 17.8 us -> 19.2 us
  Pallas kernels: 20.7 us -> 22 us
    unnamed x18 -> x13, local copies, waits for them, and re-layouts: 5.29 us -> 0.03 us
    ppermute x1, waiting for transfers between devices: 4.61 us -> 0.01 us  [per_device(): rim_c = lax.ppermute(pay_c, 'gy', flip(ny, 1))]
    ppermute x1, waiting for transfers between devices: 3.18 us -> 0.01 us  [per_device(): face_b = lax.ppermute(pay_b, 'gx', odd_pairs(nx, ring))]
    ppermute x2 -> x3, waiting for transfers between devices: 0.13 us -> 3.01 us  [the longest x2 3.01 us: per_device(): lax.ppermute(across[0], 'gx', flip(nx, 4))]
    ppermute x7, starting transfers between devices: 3.15 us -> 1.41 us  [swap(): return lax.ppermute(block, 'gx', flip(nx, 1))]
    ppermute x2, starting transfers between devices: 5.66 us -> 7.15 us  [gather_y(): got = lax.ppermute(join(pieces), 'gy', flip(ny, bit))]
    pallas_call x3 -> x4, Pallas kernels: 7.15 us -> 8.43 us  [the longest x2 3.9 us: stencil(): call(lambda *refs: stencil_body(start, *refs), [(3, CX // 2, CY, CZ)], 1,...]
    ppermute x2 -> x3, starting transfers between devices: 1.2 us -> 2.23 us  [the longest x2 1.3 us: per_device(): lax.ppermute(across[0], 'gx', flip(nx, 4))]
  transfers between devices with their start and end apart: 17 -> 18, of which waited for: 10 -> 8; matrix products, arithmetic and copies ran while one was open for 0% -> 0% of each run, Pallas kernels for 21% -> 23%
where the time goes in v4:
time: 54.3 us; the launch traced here: 54.1 us
  Pallas kernels  22 us (41%)
  starting transfers between devices  19.2 us (35%)
  waiting for transfers between devices  11.2 us (21%)
  between operations  1.62 us (3%)
    ppermute x2, starting transfers between devices, gather_y(): got = lax.ppermute(join(pieces), 'gy', flip(ny, bit))  7.15 us
    pallas_call x1, Pallas kernels, per_device(): call(sample_body, [(HOST, CZ)], 3, 'sample', vmem=24)  4.37 us
    pallas_call x2, Pallas kernels, stencil(): call(lambda *refs: stencil_body(start, *refs), [(3, CX // 2, CY, CZ)], 1,...  3.9 us
    ppermute x1, waiting for transfers between devices, per_device(): rim_b = lax.ppermute(pay_b, 'gx', odd_pairs(nx, ring))  3.78 us
    pallas_call x2, Pallas kernels, spread(): call(lambda *refs: spread_body(start, *refs), [(3, CX // 2, CY, CZ)], 4,...  3.65 us
    ppermute x1, starting transfers between devices, per_device(): rec_c = lax.ppermute(pay_c, 'gy', flip(ny, 1))  3.09 us
    ppermute x2, waiting for transfers between devices, per_device(): lax.ppermute(across[0], 'gx', flip(nx, 4))  3.01 us
    pallas_call x1, Pallas kernels, per_device(): call(pack_body, [(FACE_Y + ROWS, CZ), (FACE_Y, CZ), (ROWS, CZ), (6, CY, C...  2.7 us
  transfers between devices with their start and end apart: 18, of which 8 were waited for; matrix products, arithmetic and copies ran while one was open for 0% of the time, Pallas kernels for 23%

profile of v4, /device:TPU:0, one launch (start us, length us, event | category | flops | bytes accessed | tf_op | source)
XLA Modules:
  0.0 54.1 jit_solution(3707303933161801198)
XLA Ops:
  1.3 2.7 %pack.1 = (f32[208,128]{1,0:T(8,128)}, f32[192,128]{1,0:T(8,128)}, f32[16,128]{1,0:T(8,128)}, f32[6,32,128]{2,1,0:T(8,128)}, f32[6,64,128]{2,1,0:T(8,128)}) custom-call(f32[3,64,32,128]{3,2,1,0:T(8,128)} %refs_0_.3, f32[1]{0:T(128)S(6)} %copy.12.spin_hbm, f32[2,128]{1,0:T(2,128)} %bitcast.5, f32[2,128]{1,0:T(2,128)} %bitcast.6, f32[2,128]{1,0:T(2,128)} %bitcast.7, ...), custom_call_target="tpu_custom_call" | custom-call | tf_op jit(solution)/shard_map/pack/pallas_call | solution.py:544
  4.0 3.1 %collective-permute-start = (f32[208,128]{1,0:T(8,128)}, f32[208,128]{1,0:T(8,128)S(1)}, u32[]{:S(2)}, u32[]{:S(2)}) collective-permute-start(f32[208,128]{1,0:T(8,128)} %get-tuple-element.39), channel_id=1, source_target_pairs={{0,1},{1,0},{2,3},{3,2},{4,5},{5,4},{6,7},{7,6},{8,9},{9,8},{10,11... | collective-permute-start | bytes 319496 | tf_op jit(solution)/shard_map/ppermute | solution.py:553
  7.1 0.8 %collective-permute-start.2 = (f32[192,128]{1,0:T(8,128)}, f32[192,128]{1,0:T(8,128)S(1)}, u32[]{:S(2)}, u32[]{:S(2)}) collective-permute-start(f32[192,128]{1,0:T(8,128)} %get-tuple-element.43), channel_id=1, source_target_pairs={{1,2},{2,1},{5,6},{6,5},{9,10},{10,9},{13,14},{14,13},{17,18},{18,... | collective-permute-start | bytes 294920 | tf_op jit(solution)/shard_map/ppermute | solution.py:554
  7.9 1.9 %stencil.2.refs_3_ = f32[3,32,32,128]{3,2,1,0:T(8,128)S(1)} custom-call(f32[3,64,32,128]{3,2,1,0:T(8,128)S(1)} %copy-done), custom_call_target="tpu_custom_call" | custom-call | tf_op jit(solution)/shard_map/stencil/pallas_call | solution.py:557
  9.8 0.4 collective-permute-done.refs_1_.refs_3_.refs_6_
  10.3 3.5 %collective-permute-start.1 = (f32[32,128]{1,0:T(8,128)S(1)}, f32[32,128]{1,0:T(8,128)S(1)}, u32[]{:S(2)}, u32[]{:S(2)}) collective-permute-start(f32[32,128]{1,0:T(8,128)S(1)} %pad_maximum_fusion.refs_3_), channel_id=1, source_target_pairs={{0,2},{1,3},{2,0},{3,1},{4,6},{5,7},{6,4},{7,5},{8,10},{9,11},{10,... | collective-permute-start | bytes 49160 | tf_op jit(solution)/shard_map/ppermute | solution.py:528
  13.8 4.4 %sample.1.refs_0_ = f32[512,128]{1,0:T(8,128)S(1)} custom-call(f32[3,64,32,128]{3,2,1,0:T(8,128)S(1)} %copy-done, s32[3,512]{1,0:T(4,128)S(1)} %copy-done.3, f32[3,512]{1,0:T(4,128)S(1)} %copy-done.4), custom_call_target="tpu_custom_call" | custom-call | tf_op jit(solution)/shard_map/sample/pallas_call | solution.py:560
  18.3 0.5 collective-permute-start.4
  18.8 0.7 %collective-permute-done.3.refs_5_ = f32[32,128]{1,0:T(8,128)S(1)} collective-permute-done((f32[32,128]{1,0:T(8,128)S(1)}, f32[32,128]{1,0:T(8,128)S(1)}, u32[]{:S(2)}, u32[]{:S(2)}) %collective-permute-start.3) | collective-permute-done | bytes 16416 | tf_op jit(solution)/shard_map/ppermute | solution.py:517
  19.4 0.2 collective-permute-done.4.refs_6_
  19.6 0.1 xpack.1
  19.7 2.5 %collective-permute-start.6 = (f32[152,128]{1,0:T(8,128)S(1)}, f32[152,128]{1,0:T(8,128)S(1)}, u32[]{:S(2)}, u32[]{:S(2)}) collective-permute-start(f32[152,128]{1,0:T(8,128)S(1)} %get-tuple-element.46), channel_id=1, source_target_pairs={{4,8},{12,16},{20,24},{28,0},{8,4},{16,12},{24,20},{0,28},{5,9},{1... | collective-permute-start | bytes 233480 | tf_op jit(solution)/shard_map/ppermute | solution.py:571
  22.2 1.9 %stencil.3.refs_3_ = f32[3,32,32,128]{3,2,1,0:T(8,128)S(1)} custom-call(f32[3,64,32,128]{3,2,1,0:T(8,128)S(1)} %copy-done), custom_call_target="tpu_custom_call" | custom-call | tf_op jit(solution)/shard_map/stencil/pallas_call | solution.py:557
  24.1 0.8 %collective-permute-start.7 = (f32[32,128]{1,0:T(8,128)S(1)}, f32[32,128]{1,0:T(8,128)S(1)}, u32[]{:S(2)}, u32[]{:S(2)}) collective-permute-start(f32[32,128]{1,0:T(8,128)S(1)} %get-tuple-element.49), channel_id=1, source_target_pairs={{0,16},{4,20},{8,24},{12,28},{16,0},{20,4},{24,8},{28,12},{1,17},{... | collective-permute-start | bytes 49160 | tf_op jit(solution)/shard_map/ppermute | solution.py:572
  24.9 3.0 %collective-permute-done.7.refs_6_ = f32[32,128]{1,0:T(8,128)S(1)} collective-permute-done((f32[32,128]{1,0:T(8,128)S(1)}, f32[32,128]{1,0:T(8,128)S(1)}, u32[]{:S(2)}, u32[]{:S(2)}) %collective-permute-start.7) | collective-permute-done | bytes 16416 | tf_op jit(solution)/shard_map/ppermute | solution.py:572
  28.0 2.3 %select.1 = (f32[8,512]{1,0:T(8,128)S(1)}, f32[32,128]{1,0:T(8,128)S(1)}, f32[512,128]{1,0:T(8,128)S(1)}) custom-call(f32[512,128]{1,0:T(8,128)S(1)} %sample.1.refs_0_, f32[120,128]{1,0:T(8,128)S(1)} %collective-permute-done.5.refs_1_.refs_4_, f32[152,128]{1,0:T(8,128)S(1)} %collective-permute-done.6.refs_2_.refs_5_, ...), custom_call_target="tpu_custom_call" | custom-call | tf_op jit(solution)/shard_map/select/pallas_call | solution.py:578
  30.3 0.7 %weights.1 = (f32[72,512]{1,0:T(8,128)S(1)}, f32[40,512]{1,0:T(8,128)S(1)}, f32[512,128]{1,0:T(8,128)S(1)}) custom-call(f32[512,128]{1,0:T(8,128)S(1)} %get-tuple-element.52.pts_ref), custom_call_target="tpu_custom_call" | custom-call | tf_op jit(solution)/shard_map/weights/pallas_call | solution.py:585
  31.0 0.5 collective-permute-done.9.other_ref
  31.5 1.8 %loads.1 = (f32[512,384]{1,0:T(8,128)S(1)}, f32[432,128]{1,0:T(8,128)S(1)}, f32[432,128]{1,0:T(8,128)S(1)}, f32[16,128]{1,0:T(8,128)S(1)}, f32[384,128]{1,0:T(8,128)S(1)}) custom-call(f32[8,512]{1,0:T(8,128)S(1)} %get-tuple-element.50.samp_ref, f32[8,512]{1,0:T(8,128)S(1)} %collective-permute-done.9.other_ref, f32[32,128]{1,0:T(8,128)S(1)} %get-tuple-element.51.sel_ref, ...), custom_call_target="tpu_custom_call" | custom-call | tf_op jit(solution)/shard_map/loads/pallas_call | solution.py:586
  33.3 0.9 %collective-permute-start.10 = (f32[16,128]{1,0:T(8,128)S(1)}, f32[16,128]{1,0:T(8,128)S(1)}, u32[]{:S(2)}, u32[]{:S(2)}) collective-permute-start(f32[16,128]{1,0:T(8,128)S(1)} %get-tuple-element.56), channel_id=1, source_target_pairs={{0,1},{1,0},{2,3},{3,2},{4,5},{5,4},{6,7},{7,6},{8,9},{9,8},{10,11... | collective-permute-start | bytes 24584 | tf_op jit(solution)/shard_map/ppermute | solution.py:592
  34.3 1.2 %collective-permute-start.11 = (f32[432,128]{1,0:T(8,128)S(1)}, f32[432,128]{1,0:T(8,128)S(1)}, u32[]{:S(2)}, u32[]{:S(2)}) collective-permute-start(f32[432,128]{1,0:T(8,128)S(1)} %get-tuple-element.60), channel_id=1, source_target_pairs={{0,1},{1,0},{2,3},{3,2},{4,5},{5,4},{6,7},{7,6},{8,9},{9,8},{10,11... | collective-permute-start | bytes 663560 | tf_op jit(solution)/shard_map/ppermute | solution.py:593
  35.4 0.8 %collective-permute-start.13 = (f32[432,128]{1,0:T(8,128)S(1)}, f32[432,128]{1,0:T(8,128)S(1)}, u32[]{:S(2)}, u32[]{:S(2)}) collective-permute-start(f32[432,128]{1,0:T(8,128)S(1)} %get-tuple-element.68), channel_id=1, source_target_pairs={{1,2},{2,1},{5,6},{6,5},{9,10},{10,9},{13,14},{14,13},{17,18},{18,... | collective-permute-start | bytes 663560 | tf_op jit(solution)/shard_map/ppermute | solution.py:594
  36.3 1.8 %spread.2.refs_0_ = f32[3,32,32,128]{3,2,1,0:T(8,128)S(1)} custom-call(f32[512,384]{1,0:T(8,128)S(1)} %get-tuple-element.57.refs_0_, f32[72,512]{1,0:T(8,128)S(1)} %get-tuple-element.53.gx_ref.refs_1_, f32[40,512]{1,0:T(8,128)S(1)} %get-tuple-element.54.gy_ref.refs_2_, f32[3,32,32,128]{3,2,1,0:T(8,128)S(1)} %stencil.2.refs_3_), custom_call_target="tpu_custom_call" | custom-call | tf_op jit(solution)/shard_map/spread/pallas_call | solution.py:597
  38.1 3.6 %collective-permute-start.12 = (f32[32,128]{1,0:T(8,128)S(1)}, f32[32,128]{1,0:T(8,128)S(1)}, u32[]{:S(2)}, u32[]{:S(2)}) collective-permute-start(f32[32,128]{1,0:T(8,128)S(1)} %constant_dynamic-update-slice_fusion.refs_3_), channel_id=1, source_target_pairs={{0,2},{1,3},{2,0},{3,1},{4,6},{5,7},{6,4},{7,5},{8,10},{9,11},{10,... | collective-permute-start | bytes 49160 | tf_op jit(solution)/shard_map/ppermute | solution.py:528
  41.8 1.8 %spread.3.refs_1_ = f32[3,32,32,128]{3,2,1,0:T(8,128)S(1)} custom-call(f32[512,384]{1,0:T(8,128)S(1)} %get-tuple-element.57.refs_0_, f32[72,512]{1,0:T(8,128)S(1)} %get-tuple-element.53.gx_ref.refs_1_, f32[40,512]{1,0:T(8,128)S(1)} %get-tuple-element.54.gy_ref.refs_2_, f32[3,32,32,128]{3,2,1,0:T(8,128)S(1)} %stencil.3.refs_3_), custom_call_target="tpu_custom_call" | custom-call | tf_op jit(solution)/shard_map/spread/pallas_call | solution.py:597
  43.6 1.5 %collective-permute-done.12.refs_4_ = f32[32,128]{1,0:T(8,128)S(1)} collective-permute-done((f32[32,128]{1,0:T(8,128)S(1)}, f32[32,128]{1,0:T(8,128)S(1)}, u32[]{:S(2)}, u32[]{:S(2)}) %collective-permute-start.12) | collective-permute-done | bytes 16416 | tf_op jit(solution)/shard_map/ppermute | solution.py:528
  45.1 0.1 rimpack.1
  45.2 0.8 %collective-permute-start.14 = (f32[192,128]{1,0:T(8,128)S(1)}, f32[192,128]{1,0:T(8,128)S(1)}, u32[]{:S(2)}, u32[]{:S(2)}) collective-permute-start(f32[192,128]{1,0:T(8,128)S(1)} %get-tuple-element.70), channel_id=1, source_target_pairs={{0,4},{4,0},{8,12},{12,8},{16,20},{20,16},{24,28},{28,24},{1,5},{5... | collective-permute-start | bytes 294920 | tf_op jit(solution)/shard_map/ppermute | solution.py:517
  46.0 0.5 collective-permute-start.16
  46.5 3.8 %collective-permute-done.15.refs_9_ = f32[208,128]{1,0:T(8,128)S(1)} collective-permute-done((f32[208,128]{1,0:T(8,128)S(1)}, f32[208,128]{1,0:T(8,128)S(1)}, u32[]{:S(2)}, u32[]{:S(2)}) %collective-permute-start.15) | collective-permute-done | bytes 106528 | tf_op jit(solution)/shard_map/ppermute | solution.py:612
  50.4 1.2 %collective-permute-done.17.refs_14_ = f32[16,128]{1,0:T(8,128)S(1)} collective-permute-done((f32[16,128]{1,0:T(8,128)S(1)}, f32[16,128]{1,0:T(8,128)S(1)}, u32[]{:S(2)}, u32[]{:S(2)}) %collective-permute-start.17) | collective-permute-done | bytes 8224 | tf_op jit(solution)/shard_map/ppermute | solution.py:517
  51.5 2.4 %final.1 = (f32[3,64,32,128]{3,2,1,0:T(8,128)}, f32[3,256]{1,0:T(4,128)}) custom-call(f32[3,32,32,128]{3,2,1,0:T(8,128)S(1)} %spread.2.refs_0_, f32[3,32,32,128]{3,2,1,0:T(8,128)S(1)} %spread.3.refs_1_, f32[6,32,128]{2,1,0:T(8,128)S(1)} %copy-done.1, f32[6,64,128]{2,1,0:T(8,128)S(1)} %copy-done.2, f32[120,128]{1,0:T(8,128)S(1)} %collective-permute-done.5.refs_1_.refs_4_, ...), custom_call_target="tpu_custom_call" | custom-call | tf_op jit(solution)/shard_map/final/pallas_call | solution.py:618
  (34 shorter events, 0.3 us)
Async XLA Ops:
  1.3 6.6 %copy-start = (f32[3,64,32,128]{3,2,1,0:T(8,128)S(1)}, f32[3,64,32,128]{3,2,1,0:T(8,128)}, u32[]{:S(2)}) copy-start(f32[3,64,32,128]{3,2,1,0:T(8,128)} %refs_0_.3) | copy-start | bytes 9437188
  4.0 6.3 %collective-permute-start = (f32[208,128]{1,0:T(8,128)}, f32[208,128]{1,0:T(8,128)S(1)}, u32[]{:S(2)}, u32[]{:S(2)}) collective-permute-start(f32[208,128]{1,0:T(8,128)} %get-tuple-element.39), channel_id=1, source_target_pairs={{0,1},{1,0},{2,3},{3,2},{4,5},{5,4},{6,7},{7,6},{8,9},{9,8},{10,11... | collective-permute-start | bytes 319496 | tf_op jit(solution)/shard_map/ppermute | solution.py:553
  7.1 3.2 %copy-start.5 = (f32[16,128]{1,0:T(8,128)S(1)}, f32[16,128]{1,0:T(8,128)}, u32[]{:S(2)}) copy-start(f32[16,128]{1,0:T(8,128)} %get-tuple-element.38) | copy-start | bytes 24580
  7.1 6.7 %copy-start.3 = (s32[3,512]{1,0:T(4,128)S(1)}, s32[3,512]{1,0:T(4,128)}, u32[]{:S(2)}) copy-start(s32[3,512]{1,0:T(4,128)} %cell_ref.1) | copy-start | bytes 18436
  7.1 6.7 %copy-start.4 = (f32[3,512]{1,0:T(4,128)S(1)}, f32[3,512]{1,0:T(4,128)}, u32[]{:S(2)}) copy-start(f32[3,512]{1,0:T(4,128)} %frac_ref.1) | copy-start | bytes 18436
  7.1 11.7 %collective-permute-start.2 = (f32[192,128]{1,0:T(8,128)}, f32[192,128]{1,0:T(8,128)S(1)}, u32[]{:S(2)}, u32[]{:S(2)}) collective-permute-start(f32[192,128]{1,0:T(8,128)} %get-tuple-element.43), channel_id=1, source_target_pairs={{1,2},{2,1},{5,6},{6,5},{9,10},{10,9},{13,14},{14,13},{17,18},{18,... | collective-permute-start | bytes 294920 | tf_op jit(solution)/shard_map/ppermute | solution.py:554
  10.3 9.3 %copy-start.1 = (f32[6,32,128]{2,1,0:T(8,128)S(1)}, f32[6,32,128]{2,1,0:T(8,128)}, u32[]{:S(2)}) copy-start(f32[6,32,128]{2,1,0:T(8,128)} %get-tuple-element.42.refs_0_.refs_2_) | copy-start | bytes 294916
  10.3 8.0 %collective-permute-start.1 = (f32[32,128]{1,0:T(8,128)S(1)}, f32[32,128]{1,0:T(8,128)S(1)}, u32[]{:S(2)}, u32[]{:S(2)}) collective-permute-start(f32[32,128]{1,0:T(8,128)S(1)} %pad_maximum_fusion.refs_3_), channel_id=1, source_target_pairs={{0,2},{1,3},{2,0},{3,1},{4,6},{5,7},{6,4},{7,5},{8,10},{9,11},{10,... | collective-permute-start | bytes 49160 | tf_op jit(solution)/shard_map/ppermute | solution.py:528
  18.2 1.2 %collective-permute-start.3 = (f32[32,128]{1,0:T(8,128)S(1)}, f32[32,128]{1,0:T(8,128)S(1)}, u32[]{:S(2)}, u32[]{:S(2)}) collective-permute-start(f32[32,128]{1,0:T(8,128)S(1)} %pad_maximum_fusion.refs_3_), channel_id=1, source_target_pairs={{0,4},{4,0},{8,12},{12,8},{16,20},{20,16},{24,28},{28,24},{1,5},{5... | collective-permute-start | bytes 49160 | tf_op jit(solution)/shard_map/ppermute | solution.py:517
  18.3 1.3 %collective-permute-start.4 = (f32[32,128]{1,0:T(8,128)S(1)}, f32[32,128]{1,0:T(8,128)S(1)}, u32[]{:S(2)}, u32[]{:S(2)}) collective-permute-start(f32[32,128]{1,0:T(8,128)S(1)} %collective-permute-done.1.refs_4_), channel_id=1, source_target_pairs={{0,4},{4,0},{8,12},{12,8},{16,20},{20,16},{24,28},{28,24},{1,5},{5... | collective-permute-start | bytes 49160 | tf_op jit(solution)/shard_map/ppermute | solution.py:517
  19.7 5.2 %collective-permute-start.6 = (f32[152,128]{1,0:T(8,128)S(1)}, f32[152,128]{1,0:T(8,128)S(1)}, u32[]{:S(2)}, u32[]{:S(2)}) collective-permute-start(f32[152,128]{1,0:T(8,128)S(1)} %get-tuple-element.46), channel_id=1, source_target_pairs={{4,8},{12,16},{20,24},{28,0},{8,4},{16,12},{24,20},{0,28},{5,9},{1... | collective-permute-start | bytes 233480 | tf_op jit(solution)/shard_map/ppermute | solution.py:571
  22.2 5.8 %collective-permute-start.5 = (f32[120,128]{1,0:T(8,128)S(1)}, f32[120,128]{1,0:T(8,128)S(1)}, u32[]{:S(2)}, u32[]{:S(2)}) collective-permute-start(f32[120,128]{1,0:T(8,128)S(1)} %get-tuple-element.45), channel_id=1, source_target_pairs={{0,4},{4,0},{8,12},{12,8},{16,20},{20,16},{24,28},{28,24},{1,5},{5... | collective-permute-start | bytes 184328 | tf_op jit(solution)/shard_map/ppermute | solution.py:517
  24.1 3.8 %collective-permute-start.7 = (f32[32,128]{1,0:T(8,128)S(1)}, f32[32,128]{1,0:T(8,128)S(1)}, u32[]{:S(2)}, u32[]{:S(2)}) collective-permute-start(f32[32,128]{1,0:T(8,128)S(1)} %get-tuple-element.49), channel_id=1, source_target_pairs={{0,16},{4,20},{8,24},{12,28},{16,0},{20,4},{24,8},{28,12},{1,17},{... | collective-permute-start | bytes 49160 | tf_op jit(solution)/shard_map/ppermute | solution.py:572
  24.9 3.0 %collective-permute-start.8 = (f32[32,128]{1,0:T(8,128)S(1)}, f32[32,128]{1,0:T(8,128)S(1)}, u32[]{:S(2)}, u32[]{:S(2)}) collective-permute-start(f32[32,128]{1,0:T(8,128)S(1)} %slice.10), channel_id=1, source_target_pairs={{0,4},{4,0},{8,12},{12,8},{16,20},{20,16},{24,28},{28,24},{1,5},{5... | collective-permute-start | bytes 49160 | tf_op jit(solution)/shard_map/ppermute | solution.py:517
  30.3 1.2 %collective-permute-start.9 = (f32[8,512]{1,0:T(8,128)S(1)}, f32[8,512]{1,0:T(8,128)S(1)}, u32[]{:S(2)}, u32[]{:S(2)}) collective-permute-start(f32[8,512]{1,0:T(8,128)S(1)} %get-tuple-element.50.samp_ref), channel_id=1, source_target_pairs={{0,4},{4,0},{8,12},{12,8},{16,20},{20,16},{24,28},{28,24},{1,5},{5... | collective-permute-start | bytes 49160 | tf_op jit(solution)/shard_map/ppermute | solution.py:517
  33.3 4.8 %collective-permute-start.10 = (f32[16,128]{1,0:T(8,128)S(1)}, f32[16,128]{1,0:T(8,128)S(1)}, u32[]{:S(2)}, u32[]{:S(2)}) collective-permute-start(f32[16,128]{1,0:T(8,128)S(1)} %get-tuple-element.56), channel_id=1, source_target_pairs={{0,1},{1,0},{2,3},{3,2},{4,5},{5,4},{6,7},{7,6},{8,9},{9,8},{10,11... | collective-permute-start | bytes 24584 | tf_op jit(solution)/shard_map/ppermute | solution.py:592
  34.3 10.8 %collective-permute-start.11 = (f32[432,128]{1,0:T(8,128)S(1)}, f32[432,128]{1,0:T(8,128)S(1)}, u32[]{:S(2)}, u32[]{:S(2)}) collective-permute-start(f32[432,128]{1,0:T(8,128)S(1)} %get-tuple-element.60), channel_id=1, source_target_pairs={{0,1},{1,0},{2,3},{3,2},{4,5},{5,4},{6,7},{7,6},{8,9},{9,8},{10,11... | collective-permute-start | bytes 663560 | tf_op jit(solution)/shard_map/ppermute | solution.py:593
  35.4 9.7 %collective-permute-start.13 = (f32[432,128]{1,0:T(8,128)S(1)}, f32[432,128]{1,0:T(8,128)S(1)}, u32[]{:S(2)}, u32[]{:S(2)}) collective-permute-start(f32[432,128]{1,0:T(8,128)S(1)} %get-tuple-element.68), channel_id=1, source_target_pairs={{1,2},{2,1},{5,6},{6,5},{9,10},{10,9},{13,14},{14,13},{17,18},{18,... | collective-permute-start | bytes 663560 | tf_op jit(solution)/shard_map/ppermute | solution.py:594
  38.1 13.4 %copy-start.2 = (f32[6,64,128]{2,1,0:T(8,128)S(1)}, f32[6,64,128]{2,1,0:T(8,128)}, u32[]{:S(2)}) copy-start(f32[6,64,128]{2,1,0:T(8,128)} %get-tuple-element.65.refs_3_) | copy-start | bytes 589828
  38.1 6.9 %collective-permute-start.12 = (f32[32,128]{1,0:T(8,128)S(1)}, f32[32,128]{1,0:T(8,128)S(1)}, u32[]{:S(2)}, u32[]{:S(2)}) collective-permute-start(f32[32,128]{1,0:T(8,128)S(1)} %constant_dynamic-update-slice_fusion.refs_3_), channel_id=1, source_target_pairs={{0,2},{1,3},{2,0},{3,1},{4,6},{5,7},{6,4},{7,5},{8,10},{9,11},{10,... | collective-permute-start | bytes 49160 | tf_op jit(solution)/shard_map/ppermute | solution.py:528
  45.2 5.2 %collective-permute-start.15 = (f32[208,128]{1,0:T(8,128)S(1)}, f32[208,128]{1,0:T(8,128)S(1)}, u32[]{:S(2)}, u32[]{:S(2)}) collective-permute-start(f32[208,128]{1,0:T(8,128)S(1)} %get-tuple-element.71), channel_id=1, source_target_pairs={{4,8},{12,16},{20,24},{28,0},{8,4},{16,12},{24,20},{0,28},{5,9},{1... | collective-permute-start | bytes 319496 | tf_op jit(solution)/shard_map/ppermute | solution.py:612
  45.2 5.1 %collective-permute-start.14 = (f32[192,128]{1,0:T(8,128)S(1)}, f32[192,128]{1,0:T(8,128)S(1)}, u32[]{:S(2)}, u32[]{:S(2)}) collective-permute-start(f32[192,128]{1,0:T(8,128)S(1)} %get-tuple-element.70), channel_id=1, source_target_pairs={{0,4},{4,0},{8,12},{12,8},{16,20},{20,16},{24,28},{28,24},{1,5},{5... | collective-permute-start | bytes 294920 | tf_op jit(solution)/shard_map/ppermute | solution.py:517
  46.0 4.3 %collective-permute-start.16 = (f32[16,128]{1,0:T(8,128)S(1)}, f32[16,128]{1,0:T(8,128)S(1)}, u32[]{:S(2)}, u32[]{:S(2)}) collective-permute-start(f32[16,128]{1,0:T(8,128)S(1)} %get-tuple-element.73), channel_id=1, source_target_pairs={{0,16},{4,20},{8,24},{12,28},{16,0},{20,4},{24,8},{28,12},{1,17},{... | collective-permute-start | bytes 24584 | tf_op jit(solution)/shard_map/ppermute | solution.py:613
  50.3 1.2 %collective-permute-start.17 = (f32[16,128]{1,0:T(8,128)S(1)}, f32[16,128]{1,0:T(8,128)S(1)}, u32[]{:S(2)}, u32[]{:S(2)}) collective-permute-start(f32[16,128]{1,0:T(8,128)S(1)} %slice.12), channel_id=1, source_target_pairs={{0,4},{4,0},{8,12},{12,8},{16,20},{20,16},{24,28},{28,24},{1,5},{5... | collective-permute-start | bytes 24584 | tf_op jit(solution)/shard_map/ppermute | solution.py:517

commit v5 on v4

--- a/solution.py
+++ b/solution.py
@@ -38,13 +38,14 @@
 MIB = 1024 * 1024
 
 
-def call(body, outs, n_in, name, scratch=(), first=VM, second=VM, out_specs=None, in_specs=None, vmem=12):
+def call(body, outs, n_in, name, scratch=(), first=VM, second=VM, out_specs=None, in_specs=None, vmem=12, aliases=None):
     return pl.pallas_call(
         body,
         out_shape=[jax.ShapeDtypeStruct(s, F32) for s in outs],
         in_specs=in_specs or ([first, second] + [VM] * n_in)[:n_in],
         out_specs=out_specs or [VM] * len(outs),
         scratch_shapes=list(scratch),
+        input_output_aliases=aliases or {},
         compiler_params=pltpu.CompilerParams(vmem_limit_bytes=vmem * MIB),
         name=name,
     )
@@ -229,7 +230,9 @@
     side = jnp.where(even_x, -chips, chips)
     total = lax.axis_size("gx") * ny
     own_ref[...] = jnp.concatenate(pick_pair(values, b0, ny), axis=0)
-    pay_b[FACE_X:] = jnp.concatenate(pick_pair(values, lax.rem(b0 + side + total, total), ny), axis=0)
+    beside = jnp.concatenate(pick_pair(values, lax.rem(b0 + side + total, total), ny), axis=0)
+    pay_b[FACE_X:] = beside
+    others[1][...] = beside
     others[0][...] = jnp.concatenate(pick_pair(values, lax.rem(b0 + 2 * chips, total), ny), axis=0)
 
 
@@ -439,45 +442,69 @@
                     value = back[k * BACK : (k + 1) * BACK]
                     found = jnp.where(value[6:7, 0:1] == wanted, value, found)
                 ref[at + core * BACK : at + (core + 1) * BACK] = found
-
-
-def final_body(n_ret, main_low, main_high, x_ref, y_ref, face_a, face_b, yc_ref, yd_ref, rim_a, rim_b, rim_c, rim_d, back_ref, *rest):
+        others[1][...] = pay_b[RIM_X:]
+
+
+def face_terms(buf, at, first, main_low, main_high, y_ref, rec_c, rec_d, rim_c, rim_d, even_y):
+    half = 0.5 * DT_STEP
+    visc = DT_STEP * NU_VISC
+    part = slice(first, first + CHUNK)
+    here = slice(at, at + CHUNK)
+    half_of = main_low if first < CX // 2 else main_high
+    inner = first % (CX // 2)
+    for c in range(3):
+        buf[c, here] = half_of[c, inner : inner + CHUNK]
+        rows = slice(c * CX + first, c * CX + first + CHUNK)
+        a, b = rec_c[rows], rec_d[rows]
+        low = [jnp.where(even_y, b, a) * (visc + half * y_ref[1, part]), 0.0]
+        high = [0.0, jnp.where(even_y, a, b) * (visc - half * y_ref[4, part])]
+        for i in range(2):
+            row = (i * 3 + c) * YROWS + first
+            a, b = rim_c[row : row + CHUNK], rim_d[row : row + CHUNK]
+            buf[c, here, i, :] += jnp.where(even_y, b, a) + low[i]
+            buf[c, here, CY - 2 + i, :] += jnp.where(even_y, a, b) + high[i]
+
+
+def chunk_copy(buf, at, out_ref, first, sem):
+    return pltpu.make_async_copy(buf.at[:, pl.ds(at, CHUNK)], out_ref.at[:, pl.ds(first, CHUNK)], sem)
+
+
+def inside_body(main_low, main_high, y_ref, rec_c, rec_d, rim_c, rim_d, out_ref, buf, sems):
+    _, even_y, _, _, _, _ = place()
+    copies = []
+    for k in range(N_CHUNK - 2):
+        first = (k + 1) * CHUNK
+        face_terms(buf, k * CHUNK, first, main_low, main_high, y_ref, rec_c, rec_d, rim_c, rim_d, even_y)
+        copies.append(chunk_copy(buf, k * CHUNK, out_ref, first, sems.at[k]))
+        copies[-1].start()
+    for copy in copies:
+        copy.wait()
+
+
+def final_body(n_ret, _, main_low, main_high, x_ref, y_ref, face_a, face_b, rec_c, rec_d, rim_a, rim_b, rim_c, rim_d, back_ref, *rest):
     rets, (out_ref, pf_ref, buf, sems) = rest[:n_ret], rest[n_ret:]
     even_x, even_y, inner, brick, _, _ = place()
     half = 0.5 * DT_STEP
     visc = DT_STEP * NU_VISC
     copies = []
-    for k in range(N_CHUNK):
-        first = k * CHUNK
-        part = slice(first, first + CHUNK)
+    for k in range(2):
+        first, at = k * (CX - CHUNK), k * CHUNK
+        face_terms(buf, at, first, main_low, main_high, y_ref, rec_c, rec_d, rim_c, rim_d, even_y)
         for c in range(3):
-            half_of = main_low if k < N_CHUNK // 2 else main_high
-            at = first % (CX // 2)
-            buf[c, part] = half_of[c, at : at + CHUNK]
-            if k in (0, N_CHUNK - 1):
-                a = face_a[c * XROWS : c * XROWS + CY]
-                b = jnp.where(inner, face_b[c * XROWS : c * XROWS + CY], 0.0)
+            a = face_a[c * XROWS : c * XROWS + CY]
+            b = jnp.where(inner, face_b[c * XROWS : c * XROWS + CY], 0.0)
+            if k == 0:
+                buf[c, 0] += jnp.where(even_x, b, a) * (visc + half * x_ref[0])
+            else:
+                buf[c, 2 * CHUNK - 1] += jnp.where(even_x, a, b) * (visc - half * x_ref[3])
+            for i in range(2):
+                rows = slice((i * 3 + c) * CY, (i * 3 + c + 1) * CY)
+                a, b = rim_a[rows], jnp.where(inner, rim_b[rows], 0.0)
                 if k == 0:
-                    buf[c, 0] += jnp.where(even_x, b, a) * (visc + half * x_ref[0])
+                    buf[c, i] += jnp.where(even_x, b, a)
                 else:
-                    buf[c, CX - 1] += jnp.where(even_x, a, b) * (visc - half * x_ref[3])
-                for i in range(2):
-                    rows = slice((i * 3 + c) * CY, (i * 3 + c + 1) * CY)
-                    a, b = rim_a[rows], jnp.where(inner, rim_b[rows], 0.0)
-                    if k == 0:
-                        buf[c, i] += jnp.where(even_x, b, a)
-                    else:
-                        buf[c, CX - 2 + i] += jnp.where(even_x, a, b)
-            rows = slice(c * CX + first, c * CX + first + CHUNK)
-            a, b = yc_ref[rows], yd_ref[rows]
-            low = [jnp.where(even_y, b, a) * (visc + half * y_ref[1, part]), 0.0]
-            high = [0.0, jnp.where(even_y, a, b) * (visc - half * y_ref[4, part])]
-            for i in range(2):
-                at = (i * 3 + c) * YROWS + first
-                a, b = rim_c[at : at + CHUNK], rim_d[at : at + CHUNK]
-                buf[c, part, i, :] += jnp.where(even_y, b, a) + low[i]
-                buf[c, part, CY - 2 + i, :] += jnp.where(even_y, a, b) + high[i]
-        copies.append(pltpu.make_async_copy(buf.at[:, pl.ds(first, CHUNK)], out_ref.at[:, pl.ds(first, CHUNK)], sems.at[k]))
+                    buf[c, 2 * CHUNK - 2 + i] += jnp.where(even_x, a, b)
+        copies.append(chunk_copy(buf, at, out_ref, first, sems.at[k]))
         copies[-1].start()
     mine = brick.astype(F32)
     found = jnp.zeros((BACK, CZ), F32)
@@ -513,6 +540,12 @@
         up = [(i, (i + 1) % n) for i in range(1, n if closed else n - 1, 2)]
         return up + [(t, s) for s, t in up]
 
+    def same_side(n):
+        return [(i, (i + (2 if i % 2 else n - 2)) % n) for i in range(n)]
+
+    def across_x(blocks):
+        return [lax.ppermute(b, "gx", p) for b, p in zip(blocks, (flip(nx, 4), same_side(nx)))]
+
     def swap(block):
         return lax.ppermute(block, "gx", flip(nx, 1))
 
@@ -557,24 +590,24 @@
         return call(lambda *refs: stencil_body(start, *refs), [(3, CX // 2, CY, CZ)], 1, "stencil")(velocity)[0]
 
     rec_c, base_low = after(rec_c, stencil(0))
-    sampled = lambda: call(sample_body, [(HOST, CZ)], 3, "sample", vmem=24)(velocity, host_cell, host_frac)[0]
-    table, pieces = list(gather_y(join([block, rec_c[FACE_Y:]]), sampled))
-    pieces = pieces + [swap(p) for p in pieces]
+    two = join([block, rec_c[FACE_Y:]])
+    beside = swap(two)
+    cells, beside = after(host_cell, beside)
+    sampled = lambda: call(sample_body, [(HOST, CZ)], 3, "sample", vmem=24)(velocity, cells, host_frac)[0]
+    table, pieces = list(gather_y(two, sampled))
+    pieces = pieces + [beside] + [swap(p) for p in pieces[1:]]
     n_rows = 2 * ny * ROWS
     pair = (2 * ROWS, CZ)
     pay_a, pay_b, blocks, *across = call(
         lambda *refs: xpack_body(len(pieces), *refs),
-        [(FACE_X, CZ), (FACE_X + 2 * ROWS, CZ), pair, pair] if ring else [(FACE_X, CZ), (FACE_X, CZ), (n_rows, CZ)],
+        [(FACE_X, CZ), (FACE_X + 2 * ROWS, CZ), pair, pair, pair] if ring else [(FACE_X, CZ), (FACE_X, CZ), (n_rows, CZ)],
         3 + len(pieces),
         "xpack",
     )(x_faces, rec_c, rec_d, *pieces)
     face_b = lax.ppermute(pay_b, "gx", odd_pairs(nx, ring))
-    from_x = [lax.ppermute(across[0], "gx", flip(nx, 4))] if ring else gather_x(blocks)
+    from_x = across_x(across) if ring else gather_x(blocks)
     face_a = swap(pay_a)
-    base_high = stencil(CX // 2)
-    face_b, base_high = after(face_b, base_high)
-    if ring:
-        from_x.append(swap(face_b[FACE_X:]))
+    (face_a, face_b), base_high = after((face_a, face_b), stencil(CX // 2))
     samp, sel, pts = call(
         lambda *refs: select_body(len(from_x), *refs),
         [(8, PTS), (2 * ROWS, CZ), (PTS, CZ)],
@@ -605,24 +638,34 @@
     pair = (2 * BACK, CZ)
     pay_a, pay_b, back, *across = call(
         lambda *refs: rimpack_body(len(pieces), *refs),
-        [(RIM_X, CZ), (RIM_X + 2 * BACK, CZ), (n_rows, CZ), pair] if ring else [(RIM_X, CZ), (RIM_X, CZ), (n_rows, CZ)],
+        [(RIM_X, CZ), (RIM_X + 2 * BACK, CZ), (n_rows, CZ), pair, pair] if ring else [(RIM_X, CZ), (RIM_X, CZ), (n_rows, CZ)],
         3 + len(pieces),
         "rimpack",
     )(xrim, rim_c, rim_d, *pieces)
     rim_b = lax.ppermute(pay_b, "gx", odd_pairs(nx, ring))
-    rets = [lax.ppermute(across[0], "gx", flip(nx, 4))] if ring else gather_x(back)
+    rets = across_x(across) if ring else gather_x(back)
     rim_a = swap(pay_a)
-    if ring:
-        rets.append(swap(rim_b[RIM_X:]))
+    inside = call(
+        inside_body,
+        [velocity.shape],
+        7,
+        "inside",
+        scratch=[pltpu.VMEM((3, CX - 2 * CHUNK, CY, CZ), F32), dma((N_CHUNK - 2,))],
+        out_specs=[HB],
+        vmem=16,
+    )(main_low, main_high, y_faces, rec_c, rec_d, rim_c, rim_d)[0]
+    (rim_a, rim_b), inside = after((rim_a, rim_b), inside)
     return tuple(
         call(
             lambda *refs: final_body(len(rets), *refs),
             [velocity.shape, (3, P_SIZE)],
-            13 + len(rets),
+            14 + len(rets),
             "final",
-            scratch=[pltpu.VMEM(velocity.shape, F32), dma((N_CHUNK,))],
+            scratch=[pltpu.VMEM((3, 2 * CHUNK, CY, CZ), F32), dma((2,))],
+            first=HB,
             out_specs=[HB, VM],
-        )(main_low, main_high, x_faces, y_faces, face_a, face_b, rec_c, rec_d, rim_a, rim_b, rim_c, rim_d, back, *rets)
+            aliases={0: 0},
+        )(inside, main_low, main_high, x_faces, y_faces, face_a, face_b, rec_c, rec_d, rim_a, rim_b, rim_c, rim_d, back, *rets)
     )
 
 

time: 54.3 us -> 53.4 us (0.983)
  waiting for transfers between devices: 11.2 us -> 4.89 us
  starting transfers between devices: 19.2 us -> 23.9 us
  Pallas kernels: 22 us -> 22.7 us
    ppermute x2 -> x4, starting transfers between devices: 1.3 us -> 5 us  [across_x(): lax.ppermute(b, 'gx', p)]
    ppermute x1, waiting for transfers between devices: 3.78 us -> 0.43 us  [per_device(): rim_b = lax.ppermute(pay_b, 'gx', odd_pairs(nx, ring))]
    ppermute x2 -> x4, waiting for transfers between devices: 3.01 us -> 0.83 us  [across_x(): lax.ppermute(b, 'gx', p)]
    pallas_call x0 -> x1, Pallas kernels: none -> 1.55 us  [per_device(): call(inside_body, [velocity.shape], 7, 'inside', scratch=[pltpu.VMEM((3,...]
    ppermute x7 -> x5, waiting for transfers between devices: 2.51 us -> 1.53 us  [swap(): return lax.ppermute(block, 'gx', flip(nx, 1))]
    pallas_call x1, Pallas kernels: 2.44 us -> 1.61 us  [per_device(): call(lambda *refs: final_body(len(rets), *refs), [velocity.shape, (3, P_S...]
    ppermute x1, starting transfers between devices: 0.93 us -> 1.71 us  [per_device(): ret_c = lax.ppermute(ret, 'gy', flip(ny, 1))]
    ppermute x1, starting transfers between devices: 1.16 us -> 0.38 us  [per_device(): rim_c = lax.ppermute(pay_c, 'gy', flip(ny, 1))]
  transfers between devices with their start and end apart: 18 -> 18, of which waited for: 8 -> 7; matrix products, arithmetic and copies ran while one was open for 0% -> 0% of each run, Pallas kernels for 23% -> 26%
where the time goes in v5:
time: 53.4 us; the launch traced here: 53.3 us
  starting transfers between devices  23.9 us (45%)
  Pallas kernels  22.7 us (43%)
  waiting for transfers between devices  4.89 us (9%)
  between operations  1.65 us (3%)
    ppermute x2, starting transfers between devices, gather_y(): got = lax.ppermute(join(pieces), 'gy', flip(ny, bit))  7.94 us
    ppermute x4, starting transfers between devices, across_x(): lax.ppermute(b, 'gx', p)  5 us
    pallas_call x1, Pallas kernels, per_device(): call(sample_body, [(HOST, CZ)], 3, 'sample', vmem=24)  4.37 us
    pallas_call x2, Pallas kernels, stencil(): call(lambda *refs: stencil_body(start, *refs), [(3, CX // 2, CY, CZ)], 1,...  3.9 us
    pallas_call x2, Pallas kernels, spread(): call(lambda *refs: spread_body(start, *refs), [(3, CX // 2, CY, CZ)], 4,...  3.63 us
    ppermute x1, starting transfers between devices, per_device(): rec_c = lax.ppermute(pay_c, 'gy', flip(ny, 1))  3.09 us
    pallas_call x1, Pallas kernels, per_device(): call(pack_body, [(FACE_Y + ROWS, CZ), (FACE_Y, CZ), (ROWS, CZ), (6, CY, C...  2.7 us
    pallas_call x1, Pallas kernels, per_device(): call(lambda *refs: select_body(len(from_x), *refs), [(8, PTS), (2 * ROWS,...  2.31 us
  transfers between devices with their start and end apart: 18, of which 7 were waited for; matrix products, arithmetic and copies ran while one was open for 0% of the time, Pallas kernels for 26%

profile of v5, /device:TPU:0, one launch (start us, length us, event | category | flops | bytes accessed | tf_op | source)
XLA Modules:
  0.0 53.3 jit_solution(10285249810091989581)
XLA Ops:
  1.3 2.7 %pack.1 = (f32[208,128]{1,0:T(8,128)}, f32[192,128]{1,0:T(8,128)}, f32[16,128]{1,0:T(8,128)}, f32[6,32,128]{2,1,0:T(8,128)}, f32[6,64,128]{2,1,0:T(8,128)}) custom-call(f32[3,64,32,128]{3,2,1,0:T(8,128)} %refs_0_.3, f32[1]{0:T(128)S(6)} %copy.14.spin_hbm, f32[2,128]{1,0:T(2,128)} %bitcast.5, f32[2,128]{1,0:T(2,128)} %bitcast.6, f32[2,128]{1,0:T(2,128)} %bitcast.7, ...), custom_call_target="tpu_custom_call" | custom-call | tf_op jit(solution)/shard_map/pack/pallas_call | solution.py:577
  4.0 3.1 %collective-permute-start = (f32[208,128]{1,0:T(8,128)}, f32[208,128]{1,0:T(8,128)S(1)}, u32[]{:S(2)}, u32[]{:S(2)}) collective-permute-start(f32[208,128]{1,0:T(8,128)} %get-tuple-element.47), channel_id=1, source_target_pairs={{0,1},{1,0},{2,3},{3,2},{4,5},{5,4},{6,7},{7,6},{8,9},{9,8},{10,11... | collective-permute-start | bytes 319496 | tf_op jit(solution)/shard_map/ppermute | solution.py:586
  7.1 0.8 %collective-permute-start.3 = (f32[192,128]{1,0:T(8,128)}, f32[192,128]{1,0:T(8,128)S(1)}, u32[]{:S(2)}, u32[]{:S(2)}) collective-permute-start(f32[192,128]{1,0:T(8,128)} %get-tuple-element.52), channel_id=1, source_target_pairs={{1,2},{2,1},{5,6},{6,5},{9,10},{10,9},{13,14},{14,13},{17,18},{18,... | collective-permute-start | bytes 294920 | tf_op jit(solution)/shard_map/ppermute | solution.py:587
  7.9 1.9 %stencil.2.refs_3_ = f32[3,32,32,128]{3,2,1,0:T(8,128)S(1)} custom-call(f32[3,64,32,128]{3,2,1,0:T(8,128)S(1)} %copy-done), custom_call_target="tpu_custom_call" | custom-call | tf_op jit(solution)/shard_map/stencil/pallas_call | solution.py:590
  9.8 0.4 collective-permute-done.refs_1_.refs_3_.rec_c.refs_7_
  10.4 3.5 %collective-permute-start.1 = (f32[32,128]{1,0:T(8,128)S(1)}, f32[32,128]{1,0:T(8,128)S(1)}, u32[]{:S(2)}, u32[]{:S(2)}) collective-permute-start(f32[32,128]{1,0:T(8,128)S(1)} %pad_maximum_fusion.refs_3_), channel_id=1, source_target_pairs={{0,2},{1,3},{2,0},{3,1},{4,6},{5,7},{6,4},{7,5},{8,10},{9,11},{10,... | collective-permute-start | bytes 49160 | tf_op jit(solution)/shard_map/ppermute | solution.py:561
  13.9 4.4 %sample.1.refs_0_ = f32[512,128]{1,0:T(8,128)S(1)} custom-call(f32[3,64,32,128]{3,2,1,0:T(8,128)S(1)} %copy-done, s32[3,512]{1,0:T(4,128)S(1)} %copy-done.3, f32[3,512]{1,0:T(4,128)S(1)} %copy-done.4), custom_call_target="tpu_custom_call" | custom-call | tf_op jit(solution)/shard_map/sample/pallas_call | solution.py:596
  18.5 1.0 %collective-permute-done.4.refs_6_ = f32[32,128]{1,0:T(8,128)S(1)} collective-permute-done((f32[32,128]{1,0:T(8,128)S(1)}, f32[32,128]{1,0:T(8,128)S(1)}, u32[]{:S(2)}, u32[]{:S(2)}) %collective-permute-start.4) | collective-permute-done | bytes 16416 | tf_op jit(solution)/shard_map/ppermute | solution.py:550
  19.6 2.3 %collective-permute-start.6 = (f32[152,128]{1,0:T(8,128)S(1)}, f32[152,128]{1,0:T(8,128)S(1)}, u32[]{:S(2)}, u32[]{:S(2)}) collective-permute-start(f32[152,128]{1,0:T(8,128)S(1)} %get-tuple-element.56), channel_id=1, source_target_pairs={{4,8},{12,16},{20,24},{28,0},{8,4},{16,12},{24,20},{0,28},{5,9},{1... | collective-permute-start | bytes 233480 | tf_op jit(solution)/shard_map/ppermute | solution.py:607
  21.9 0.9 %collective-permute-start.7 = (f32[32,128]{1,0:T(8,128)S(1)}, f32[32,128]{1,0:T(8,128)S(1)}, u32[]{:S(2)}, u32[]{:S(2)}) collective-permute-start(f32[32,128]{1,0:T(8,128)S(1)} %get-tuple-element.60), channel_id=1, source_target_pairs={{0,16},{4,20},{8,24},{12,28},{16,0},{20,4},{24,8},{28,12},{1,17},{... | collective-permute-start | bytes 49160 | tf_op jit(solution)/shard_map/ppermute | solution.py:547
  22.8 1.4 %collective-permute-start.8 = (f32[32,128]{1,0:T(8,128)S(1)}, f32[32,128]{1,0:T(8,128)S(1)}, u32[]{:S(2)}, u32[]{:S(2)}) collective-permute-start(f32[32,128]{1,0:T(8,128)S(1)} %get-tuple-element.61), channel_id=1, source_target_pairs={{0,24},{4,12},{8,0},{12,20},{16,8},{20,28},{24,16},{28,4},{1,25},{... | collective-permute-start | bytes 49160 | tf_op jit(solution)/shard_map/ppermute | solution.py:547
  24.3 1.9 %stencil.3.refs_3_ = f32[3,32,32,128]{3,2,1,0:T(8,128)S(1)} custom-call(f32[3,64,32,128]{3,2,1,0:T(8,128)S(1)} %copy-done), custom_call_target="tpu_custom_call" | custom-call | tf_op jit(solution)/shard_map/stencil/pallas_call | solution.py:590
  26.3 0.3 collective-permute-done.8.refs_7_
  26.6 2.3 %select.1 = (f32[8,512]{1,0:T(8,128)S(1)}, f32[32,128]{1,0:T(8,128)S(1)}, f32[512,128]{1,0:T(8,128)S(1)}) custom-call(f32[512,128]{1,0:T(8,128)S(1)} %sample.1.refs_0_, f32[120,128]{1,0:T(8,128)S(1)} %collective-permute-done.5.refs_1_.refs_5_, f32[152,128]{1,0:T(8,128)S(1)} %collective-permute-done.6.refs_2_.refs_6_, ...), custom_call_target="tpu_custom_call" | custom-call | tf_op jit(solution)/shard_map/select/pallas_call | solution.py:611
  28.9 0.7 %weights.1 = (f32[72,512]{1,0:T(8,128)S(1)}, f32[40,512]{1,0:T(8,128)S(1)}, f32[512,128]{1,0:T(8,128)S(1)}) custom-call(f32[512,128]{1,0:T(8,128)S(1)} %get-tuple-element.64.pts_ref), custom_call_target="tpu_custom_call" | custom-call | tf_op jit(solution)/shard_map/weights/pallas_call | solution.py:618
  29.6 0.5 collective-permute-done.9.other_ref
  30.1 1.8 %loads.1 = (f32[512,384]{1,0:T(8,128)S(1)}, f32[432,128]{1,0:T(8,128)S(1)}, f32[432,128]{1,0:T(8,128)S(1)}, f32[16,128]{1,0:T(8,128)S(1)}, f32[384,128]{1,0:T(8,128)S(1)}) custom-call(f32[8,512]{1,0:T(8,128)S(1)} %get-tuple-element.62.samp_ref, f32[8,512]{1,0:T(8,128)S(1)} %collective-permute-done.9.other_ref, f32[32,128]{1,0:T(8,128)S(1)} %get-tuple-element.63.sel_ref, ...), custom_call_target="tpu_custom_call" | custom-call | tf_op jit(solution)/shard_map/loads/pallas_call | solution.py:619
  32.0 1.7 %collective-permute-start.11 = (f32[16,128]{1,0:T(8,128)S(1)}, f32[16,128]{1,0:T(8,128)S(1)}, u32[]{:S(2)}, u32[]{:S(2)}) collective-permute-start(f32[16,128]{1,0:T(8,128)S(1)} %get-tuple-element.70), channel_id=1, source_target_pairs={{0,1},{1,0},{2,3},{3,2},{4,5},{5,4},{6,7},{7,6},{8,9},{9,8},{10,11... | collective-permute-start | bytes 24584 | tf_op jit(solution)/shard_map/ppermute | solution.py:625
  33.7 0.4 collective-permute-start.10
  34.1 0.8 %collective-permute-start.13 = (f32[432,128]{1,0:T(8,128)S(1)}, f32[432,128]{1,0:T(8,128)S(1)}, u32[]{:S(2)}, u32[]{:S(2)}) collective-permute-start(f32[432,128]{1,0:T(8,128)S(1)} %get-tuple-element.77), channel_id=1, source_target_pairs={{1,2},{2,1},{5,6},{6,5},{9,10},{10,9},{13,14},{14,13},{17,18},{18,... | collective-permute-start | bytes 663560 | tf_op jit(solution)/shard_map/ppermute | solution.py:627
  34.9 1.8 %spread.2.main_low.refs_1_ = f32[3,32,32,128]{3,2,1,0:T(8,128)S(1)} custom-call(f32[512,384]{1,0:T(8,128)S(1)} %get-tuple-element.71.refs_0_, f32[72,512]{1,0:T(8,128)S(1)} %get-tuple-element.65.gx_ref.refs_1_, f32[40,512]{1,0:T(8,128)S(1)} %get-tuple-element.66.gy_ref.refs_2_, f32[3,32,32,128]{3,2,1,0:T(8,128)S(1)} %stencil.2.refs_3_), custom_call_target="tpu_custom_call" | custom-call | tf_op jit(solution)/shard_map/spread/pallas_call | solution.py:630
  36.8 4.4 %collective-permute-start.12 = (f32[32,128]{1,0:T(8,128)S(1)}, f32[32,128]{1,0:T(8,128)S(1)}, u32[]{:S(2)}, u32[]{:S(2)}) collective-permute-start(f32[32,128]{1,0:T(8,128)S(1)} %constant_dynamic-update-slice_fusion.refs_3_), channel_id=1, source_target_pairs={{0,2},{1,3},{2,0},{3,1},{4,6},{5,7},{6,4},{7,5},{8,10},{9,11},{10,... | collective-permute-start | bytes 49160 | tf_op jit(solution)/shard_map/ppermute | solution.py:561
  41.2 1.8 %spread.3.main_high.refs_2_ = f32[3,32,32,128]{3,2,1,0:T(8,128)S(1)} custom-call(f32[512,384]{1,0:T(8,128)S(1)} %get-tuple-element.71.refs_0_, f32[72,512]{1,0:T(8,128)S(1)} %get-tuple-element.65.gx_ref.refs_1_, f32[40,512]{1,0:T(8,128)S(1)} %get-tuple-element.66.gy_ref.refs_2_, f32[3,32,32,128]{3,2,1,0:T(8,128)S(1)} %stencil.3.refs_3_), custom_call_target="tpu_custom_call" | custom-call | tf_op jit(solution)/shard_map/spread/pallas_call | solution.py:630
  43.0 1.7 %collective-permute-done.12.refs_4_ = f32[32,128]{1,0:T(8,128)S(1)} collective-permute-done((f32[32,128]{1,0:T(8,128)S(1)}, f32[32,128]{1,0:T(8,128)S(1)}, u32[]{:S(2)}, u32[]{:S(2)}) %collective-permute-start.12) | collective-permute-done | bytes 16416 | tf_op jit(solution)/shard_map/ppermute | solution.py:561
  44.8 0.2 collective-permute-start.15
  45.0 1.3 %collective-permute-start.14 = (f32[192,128]{1,0:T(8,128)S(1)}, f32[192,128]{1,0:T(8,128)S(1)}, u32[]{:S(2)}, u32[]{:S(2)}) collective-permute-start(f32[192,128]{1,0:T(8,128)S(1)} %get-tuple-element.79), channel_id=1, source_target_pairs={{0,4},{4,0},{8,12},{12,8},{16,20},{20,16},{24,28},{28,24},{1,5},{5... | collective-permute-start | bytes 294920 | tf_op jit(solution)/shard_map/ppermute | solution.py:550
  46.3 1.5 %collective-permute-start.16 = (f32[16,128]{1,0:T(8,128)S(1)}, f32[16,128]{1,0:T(8,128)S(1)}, u32[]{:S(2)}, u32[]{:S(2)}) collective-permute-start(f32[16,128]{1,0:T(8,128)S(1)} %get-tuple-element.88), channel_id=1, source_target_pairs={{0,16},{4,20},{8,24},{12,28},{16,0},{20,4},{24,8},{28,12},{1,17},{... | collective-permute-start | bytes 24584 | tf_op jit(solution)/shard_map/ppermute | solution.py:547
  47.8 1.1 %collective-permute-start.17 = (f32[16,128]{1,0:T(8,128)S(1)}, f32[16,128]{1,0:T(8,128)S(1)}, u32[]{:S(2)}, u32[]{:S(2)}) collective-permute-start(f32[16,128]{1,0:T(8,128)S(1)} %get-tuple-element.89), channel_id=1, source_target_pairs={{0,24},{4,12},{8,0},{12,20},{16,8},{20,28},{24,16},{28,4},{1,25},{... | collective-permute-start | bytes 24584 | tf_op jit(solution)/shard_map/ppermute | solution.py:547
  49.0 1.6 %inside.1.refs_0_ = f32[3,64,32,128]{3,2,1,0:T(8,128)} custom-call(f32[3,32,32,128]{3,2,1,0:T(8,128)S(1)} %spread.2.main_low.refs_1_, f32[3,32,32,128]{3,2,1,0:T(8,128)S(1)} %spread.3.main_high.refs_2_, f32[6,64,128]{2,1,0:T(8,128)S(1)} %copy-done.1, f32[208,128]{1,0:T(8,128)S(1)} %collective-permute-done.refs_1_.refs_3_.rec_c.refs_7_, ...), custom_call_target="tpu_custom_call" | custom-call | tf_op jit(solution)/shard_map/inside/pallas_call | solution.py:648
  50.5 0.4 collective-permute-done.15.refs_10_
  51.0 0.5 collective-permute-done.17.refs_15_
  51.5 1.6 %final.1 = (f32[3,64,32,128]{3,2,1,0:T(8,128)}, f32[3,256]{1,0:T(4,128)}) custom-call(f32[3,64,32,128]{3,2,1,0:T(8,128)} %inside.1.refs_0_, f32[3,32,32,128]{3,2,1,0:T(8,128)S(1)} %spread.2.main_low.refs_1_, f32[3,32,32,128]{3,2,1,0:T(8,128)S(1)} %spread.3.main_high.refs_2_, f32[6,32,128]{2,1,0:T(8,128)S(1)} %copy-done.2, ...), custom_call_target="tpu_custom_call", output_to_operand_aliasing={{0}: (0, {})} | custom-call | tf_op jit(solution)/shard_map/final/pallas_call | solution.py:659
  (33 shorter events, 0.6 us)
Async XLA Ops:
  1.3 6.6 %copy-start = (f32[3,64,32,128]{3,2,1,0:T(8,128)S(1)}, f32[3,64,32,128]{3,2,1,0:T(8,128)}, u32[]{:S(2)}) copy-start(f32[3,64,32,128]{3,2,1,0:T(8,128)} %refs_0_.3) | copy-start | bytes 9437188
  4.0 6.3 %collective-permute-start = (f32[208,128]{1,0:T(8,128)}, f32[208,128]{1,0:T(8,128)S(1)}, u32[]{:S(2)}, u32[]{:S(2)}) collective-permute-start(f32[208,128]{1,0:T(8,128)} %get-tuple-element.47), channel_id=1, source_target_pairs={{0,1},{1,0},{2,3},{3,2},{4,5},{5,4},{6,7},{7,6},{8,9},{9,8},{10,11... | collective-permute-start | bytes 319496 | tf_op jit(solution)/shard_map/ppermute | solution.py:586
  7.1 3.2 %copy-start.5 = (f32[16,128]{1,0:T(8,128)S(1)}, f32[16,128]{1,0:T(8,128)}, u32[]{:S(2)}) copy-start(f32[16,128]{1,0:T(8,128)} %get-tuple-element.46) | copy-start | bytes 24580
  7.1 6.8 %copy-start.3 = (s32[3,512]{1,0:T(4,128)S(1)}, s32[3,512]{1,0:T(4,128)}, u32[]{:S(2)}) copy-start(s32[3,512]{1,0:T(4,128)} %cell_ref) | copy-start | bytes 18436
  7.1 6.8 %copy-start.4 = (f32[3,512]{1,0:T(4,128)S(1)}, f32[3,512]{1,0:T(4,128)}, u32[]{:S(2)}) copy-start(f32[3,512]{1,0:T(4,128)} %frac_ref.1) | copy-start | bytes 18436
  7.1 11.4 %collective-permute-start.3 = (f32[192,128]{1,0:T(8,128)}, f32[192,128]{1,0:T(8,128)S(1)}, u32[]{:S(2)}, u32[]{:S(2)}) collective-permute-start(f32[192,128]{1,0:T(8,128)} %get-tuple-element.52), channel_id=1, source_target_pairs={{1,2},{2,1},{5,6},{6,5},{9,10},{10,9},{13,14},{14,13},{17,18},{18,... | collective-permute-start | bytes 294920 | tf_op jit(solution)/shard_map/ppermute | solution.py:587
  10.3 9.3 %copy-start.2 = (f32[6,32,128]{2,1,0:T(8,128)S(1)}, f32[6,32,128]{2,1,0:T(8,128)}, u32[]{:S(2)}) copy-start(f32[6,32,128]{2,1,0:T(8,128)} %get-tuple-element.51.refs_0_.refs_3_) | copy-start | bytes 294916
  10.3 3.6 %collective-permute-start.2 = (f32[32,128]{1,0:T(8,128)S(1)}, f32[32,128]{1,0:T(8,128)S(1)}, u32[]{:S(2)}, u32[]{:S(2)}) collective-permute-start(f32[32,128]{1,0:T(8,128)S(1)} %pad_maximum_fusion.refs_3_), channel_id=1, source_target_pairs={{0,4},{4,0},{8,12},{12,8},{16,20},{20,16},{24,28},{28,24},{1,5},{5... | collective-permute-start | bytes 49160 | tf_op jit(solution)/shard_map/ppermute | solution.py:550
  10.4 7.9 %collective-permute-start.1 = (f32[32,128]{1,0:T(8,128)S(1)}, f32[32,128]{1,0:T(8,128)S(1)}, u32[]{:S(2)}, u32[]{:S(2)}) collective-permute-start(f32[32,128]{1,0:T(8,128)S(1)} %pad_maximum_fusion.refs_3_), channel_id=1, source_target_pairs={{0,2},{1,3},{2,0},{3,1},{4,6},{5,7},{6,4},{7,5},{8,10},{9,11},{10,... | collective-permute-start | bytes 49160 | tf_op jit(solution)/shard_map/ppermute | solution.py:561
  18.3 1.2 %collective-permute-start.4 = (f32[32,128]{1,0:T(8,128)S(1)}, f32[32,128]{1,0:T(8,128)S(1)}, u32[]{:S(2)}, u32[]{:S(2)}) collective-permute-start(f32[32,128]{1,0:T(8,128)S(1)} %collective-permute-done.1.refs_4_), channel_id=1, source_target_pairs={{0,4},{4,0},{8,12},{12,8},{16,20},{20,16},{24,28},{28,24},{1,5},{5... | collective-permute-start | bytes 49160 | tf_op jit(solution)/shard_map/ppermute | solution.py:550
  19.6 6.6 %collective-permute-start.6 = (f32[152,128]{1,0:T(8,128)S(1)}, f32[152,128]{1,0:T(8,128)S(1)}, u32[]{:S(2)}, u32[]{:S(2)}) collective-permute-start(f32[152,128]{1,0:T(8,128)S(1)} %get-tuple-element.56), channel_id=1, source_target_pairs={{4,8},{12,16},{20,24},{28,0},{8,4},{16,12},{24,20},{0,28},{5,9},{1... | collective-permute-start | bytes 233480 | tf_op jit(solution)/shard_map/ppermute | solution.py:607
  21.9 4.3 %collective-permute-start.5 = (f32[120,128]{1,0:T(8,128)S(1)}, f32[120,128]{1,0:T(8,128)S(1)}, u32[]{:S(2)}, u32[]{:S(2)}) collective-permute-start(f32[120,128]{1,0:T(8,128)S(1)} %get-tuple-element.55), channel_id=1, source_target_pairs={{0,4},{4,0},{8,12},{12,8},{16,20},{20,16},{24,28},{28,24},{1,5},{5... | collective-permute-start | bytes 184328 | tf_op jit(solution)/shard_map/ppermute | solution.py:550
  21.9 4.3 %collective-permute-start.7 = (f32[32,128]{1,0:T(8,128)S(1)}, f32[32,128]{1,0:T(8,128)S(1)}, u32[]{:S(2)}, u32[]{:S(2)}) collective-permute-start(f32[32,128]{1,0:T(8,128)S(1)} %get-tuple-element.60), channel_id=1, source_target_pairs={{0,16},{4,20},{8,24},{12,28},{16,0},{20,4},{24,8},{28,12},{1,17},{... | collective-permute-start | bytes 49160 | tf_op jit(solution)/shard_map/ppermute | solution.py:547
  22.8 3.7 %collective-permute-start.8 = (f32[32,128]{1,0:T(8,128)S(1)}, f32[32,128]{1,0:T(8,128)S(1)}, u32[]{:S(2)}, u32[]{:S(2)}) collective-permute-start(f32[32,128]{1,0:T(8,128)S(1)} %get-tuple-element.61), channel_id=1, source_target_pairs={{0,24},{4,12},{8,0},{12,20},{16,8},{20,28},{24,16},{28,4},{1,25},{... | collective-permute-start | bytes 49160 | tf_op jit(solution)/shard_map/ppermute | solution.py:547
  28.9 1.2 %collective-permute-start.9 = (f32[8,512]{1,0:T(8,128)S(1)}, f32[8,512]{1,0:T(8,128)S(1)}, u32[]{:S(2)}, u32[]{:S(2)}) collective-permute-start(f32[8,512]{1,0:T(8,128)S(1)} %get-tuple-element.62.samp_ref), channel_id=1, source_target_pairs={{0,4},{4,0},{8,12},{12,8},{16,20},{20,16},{24,28},{28,24},{1,5},{5... | collective-permute-start | bytes 49160 | tf_op jit(solution)/shard_map/ppermute | solution.py:550
  32.0 4.8 %collective-permute-start.11 = (f32[16,128]{1,0:T(8,128)S(1)}, f32[16,128]{1,0:T(8,128)S(1)}, u32[]{:S(2)}, u32[]{:S(2)}) collective-permute-start(f32[16,128]{1,0:T(8,128)S(1)} %get-tuple-element.70), channel_id=1, source_target_pairs={{0,1},{1,0},{2,3},{3,2},{4,5},{5,4},{6,7},{7,6},{8,9},{9,8},{10,11... | collective-permute-start | bytes 24584 | tf_op jit(solution)/shard_map/ppermute | solution.py:625
  33.7 11.0 %collective-permute-start.10 = (f32[432,128]{1,0:T(8,128)S(1)}, f32[432,128]{1,0:T(8,128)S(1)}, u32[]{:S(2)}, u32[]{:S(2)}) collective-permute-start(f32[432,128]{1,0:T(8,128)S(1)} %get-tuple-element.69), channel_id=1, source_target_pairs={{0,1},{1,0},{2,3},{3,2},{4,5},{5,4},{6,7},{7,6},{8,9},{9,8},{10,11... | collective-permute-start | bytes 663560 | tf_op jit(solution)/shard_map/ppermute | solution.py:626
  34.1 10.6 %collective-permute-start.13 = (f32[432,128]{1,0:T(8,128)S(1)}, f32[432,128]{1,0:T(8,128)S(1)}, u32[]{:S(2)}, u32[]{:S(2)}) collective-permute-start(f32[432,128]{1,0:T(8,128)S(1)} %get-tuple-element.77), channel_id=1, source_target_pairs={{1,2},{2,1},{5,6},{6,5},{9,10},{10,9},{13,14},{14,13},{17,18},{18,... | collective-permute-start | bytes 663560 | tf_op jit(solution)/shard_map/ppermute | solution.py:627
  36.8 12.2 %copy-start.1 = (f32[6,64,128]{2,1,0:T(8,128)S(1)}, f32[6,64,128]{2,1,0:T(8,128)}, u32[]{:S(2)}) copy-start(f32[6,64,128]{2,1,0:T(8,128)} %get-tuple-element.83.y_ref.refs_4_) | copy-start | bytes 589828
  36.8 7.9 %collective-permute-start.12 = (f32[32,128]{1,0:T(8,128)S(1)}, f32[32,128]{1,0:T(8,128)S(1)}, u32[]{:S(2)}, u32[]{:S(2)}) collective-permute-start(f32[32,128]{1,0:T(8,128)S(1)} %constant_dynamic-update-slice_fusion.refs_3_), channel_id=1, source_target_pairs={{0,2},{1,3},{2,0},{3,1},{4,6},{5,7},{6,4},{7,5},{8,10},{9,11},{10,... | collective-permute-start | bytes 49160 | tf_op jit(solution)/shard_map/ppermute | solution.py:561
  44.8 6.2 %collective-permute-start.15 = (f32[208,128]{1,0:T(8,128)S(1)}, f32[208,128]{1,0:T(8,128)S(1)}, u32[]{:S(2)}, u32[]{:S(2)}) collective-permute-start(f32[208,128]{1,0:T(8,128)S(1)} %get-tuple-element.80), channel_id=1, source_target_pairs={{4,8},{12,16},{20,24},{28,0},{8,4},{16,12},{24,20},{0,28},{5,9},{1... | collective-permute-start | bytes 319496 | tf_op jit(solution)/shard_map/ppermute | solution.py:645
  45.0 5.6 %collective-permute-start.14 = (f32[192,128]{1,0:T(8,128)S(1)}, f32[192,128]{1,0:T(8,128)S(1)}, u32[]{:S(2)}, u32[]{:S(2)}) collective-permute-start(f32[192,128]{1,0:T(8,128)S(1)} %get-tuple-element.79), channel_id=1, source_target_pairs={{0,4},{4,0},{8,12},{12,8},{16,20},{20,16},{24,28},{28,24},{1,5},{5... | collective-permute-start | bytes 294920 | tf_op jit(solution)/shard_map/ppermute | solution.py:550
  46.3 4.7 %collective-permute-start.16 = (f32[16,128]{1,0:T(8,128)S(1)}, f32[16,128]{1,0:T(8,128)S(1)}, u32[]{:S(2)}, u32[]{:S(2)}) collective-permute-start(f32[16,128]{1,0:T(8,128)S(1)} %get-tuple-element.88), channel_id=1, source_target_pairs={{0,16},{4,20},{8,24},{12,28},{16,0},{20,4},{24,8},{28,12},{1,17},{... | collective-permute-start | bytes 24584 | tf_op jit(solution)/shard_map/ppermute | solution.py:547
  47.8 3.7 %collective-permute-start.17 = (f32[16,128]{1,0:T(8,128)S(1)}, f32[16,128]{1,0:T(8,128)S(1)}, u32[]{:S(2)}, u32[]{:S(2)}) collective-permute-start(f32[16,128]{1,0:T(8,128)S(1)} %get-tuple-element.89), channel_id=1, source_target_pairs={{0,24},{4,12},{8,0},{12,20},{16,8},{20,28},{24,16},{28,4},{1,25},{... | collective-permute-start | bytes 24584 | tf_op jit(solution)/shard_map/ppermute | solution.py:547

commit v6 on v5

--- a/solution.py
+++ b/solution.py
@@ -80,18 +80,30 @@
 
 
 def pack_body(v_ref, spin_hbm, *rest):
-    params, (pay_c, pay_d, blk_ref, x_ref, y_ref, low, high, held, held_int, spin_ref, sems) = rest[:5], rest[5:]
+    params, (pay_c, pay_d, blk_ref, held, held_int, spin_ref, sems) = rest[:5], rest[5:]
     _, even_y, _, brick, _, _ = place()
-    small = [pltpu.make_async_copy(spin_hbm, spin_ref, sems.at[2])]
-    small += [pltpu.make_async_copy(p, held.at[k], sems.at[3 + k]) for k, p in enumerate(params[:4])]
-    small.append(pltpu.make_async_copy(params[4], held_int, sems.at[7]))
-    copies = [
-        pltpu.make_async_copy(v_ref.at[:, :, pl.ds(0, 8)], low, sems.at[0]),
-        pltpu.make_async_copy(v_ref.at[:, :, pl.ds(CY - 8, 8)], high, sems.at[1]),
-        pltpu.make_async_copy(v_ref.at[:, 0], x_ref.at[pl.ds(0, 3)], sems.at[8]),
-        pltpu.make_async_copy(v_ref.at[:, CX - 1], x_ref.at[pl.ds(3, 3)], sems.at[9]),
-    ]
-    for copy in small + copies:
+
+    def faces(first, second):
+        made = []
+        for k, (ref, y) in enumerate(((pay_c, first), (pay_d, second))):
+            for c in range(3):
+                made.append(pltpu.make_async_copy(v_ref.at[c, :, y], ref.at[pl.ds(c * CX, CX)], sems.at[3 * k + c]))
+        return made
+
+    @pl.when(even_y)
+    def _():
+        for copy in faces(CY - 1, 0):
+            copy.start()
+
+    @pl.when(jnp.logical_not(even_y))
+    def _():
+        for copy in faces(0, CY - 1):
+            copy.start()
+
+    small = [pltpu.make_async_copy(spin_hbm, spin_ref, sems.at[6])]
+    small += [pltpu.make_async_copy(p, held.at[k], sems.at[7 + k]) for k, p in enumerate(params[:4])]
+    small.append(pltpu.make_async_copy(params[4], held_int, sems.at[11]))
+    for copy in small:
         copy.start()
     for copy in small:
         copy.wait()
@@ -110,15 +122,8 @@
     block = jnp.concatenate(parts, axis=0)
     blk_ref[...] = block
     pay_c[FACE_Y:] = block
-    for copy in copies:
+    for copy in faces(0, 0):
         copy.wait()
-    for c in range(3):
-        y_low = low[c, :, 0, :]
-        y_high = high[c, :, 7, :]
-        y_ref[c] = y_low
-        y_ref[c + 3] = y_high
-        pay_c[c * CX : (c + 1) * CX] = jnp.where(even_y, y_high, y_low)
-        pay_d[c * CX : (c + 1) * CX] = jnp.where(even_y, y_low, y_high)
 
 
 def stencil_body(start, v_ref, out_ref):
@@ -155,7 +160,12 @@
     return jnp.where(coord == base, 1.0 - frac, jnp.where(coord == base + 1, frac, 0.0))
 
 
-def sample_body(v_ref, cell_ref, frac_ref, tab_ref):
+def sample_body(v_ref, cell_ref, frac_ref, tab_ref, x_ref, y_ref):
+    for c in range(3):
+        x_ref[c] = v_ref[c, 0]
+        x_ref[c + 3] = v_ref[c, CX - 1]
+    y_ref[0] = v_ref[1, :, 0, :]
+    y_ref[1] = v_ref[1, :, CY - 1, :]
     rows = jnp.concatenate([cell_ref[...].astype(F32), frac_ref[...], jnp.zeros((CZ - 6, HOST), F32)], axis=0)
     turned = rows.T
     x_col, y_col, z_col = [turned[:, k : k + 1].astype(jnp.int32) for k in range(3)]
@@ -285,33 +295,38 @@
     samp_ref[...] = points.T[6:14]
 
 
-def weights_body(pts_ref, gx_ref, gy_ref, pz_ref):
+def offsets(frac):
+    raw = [jnp.exp(-((o - frac) ** 2) / EPS_SQ) for o in (-1.0, 0.0, 1.0, 2.0)]
+    total = (raw[0] + raw[1]) + (raw[2] + raw[3])
+    return [value / total for value in raw]
+
+
+def profile(rows, inner, base, frac):
+    index = lax.broadcasted_iota(jnp.int32, (rows, PTS), 0)
+    late = index - inner
+    index = jnp.where(index < inner, index, jnp.where(late < 2, late - 2, late - 2 + inner))
+    rel = index - base.astype(jnp.int32)
+    result = jnp.zeros((rows, PTS), F32)
+    for k, w in enumerate(offsets(frac)):
+        result = jnp.where(rel == k - 1, w, result)
+    return result
+
+
+def line_profile(base, frac, extra):
+    stack = jnp.concatenate(offsets(frac) + [base] + extra + [jnp.zeros((CZ - 5 - len(extra), PTS), F32)], axis=0).T
+    rel = lax.broadcasted_iota(jnp.int32, (PTS, CZ), 1) - stack[:, 4:5].astype(jnp.int32)
+    result = jnp.zeros((PTS, CZ), F32)
+    for k in range(4):
+        result = jnp.where(rel == k - 1, stack[:, k : k + 1], result)
+    return result, [stack[:, 5 + k : 6 + k] for k in range(len(extra))]
+
+
+def weights_body(pts_ref, gx_ref, gy_ref, pz_ref, pos_ref):
     table = pts_ref[...].T
-
-    def offsets(frac):
-        raw = [jnp.exp(-((o - frac) ** 2) / EPS_SQ) for o in (-1.0, 0.0, 1.0, 2.0)]
-        total = (raw[0] + raw[1]) + (raw[2] + raw[3])
-        return [value / total for value in raw]
-
-    def profile(rows, inner, base, frac):
-        index = lax.broadcasted_iota(jnp.int32, (rows, PTS), 0)
-        late = index - inner
-        index = jnp.where(index < inner, index, jnp.where(late < 2, late - 2, late - 2 + inner))
-        rel = index - base.astype(jnp.int32)
-        result = jnp.zeros((rows, PTS), F32)
-        for k, w in enumerate(offsets(frac)):
-            result = jnp.where(rel == k - 1, w, result)
-        return result
-
     gx_ref[...] = profile(YROWS, CX, table[0:1], table[3:4])
-    gy_ref[...] = profile(CY + 8, CY, table[1:2], table[4:5])
-    wz = offsets(table[5:6])
-    stack = jnp.concatenate(wz + [jnp.zeros((CZ - 4, PTS), F32)], axis=0).T
-    z_rel = lax.broadcasted_iota(jnp.int32, (PTS, CZ), 1) - pts_ref[:, 2:3].astype(jnp.int32)
-    pz = jnp.zeros((PTS, CZ), F32)
-    for k in range(4):
-        pz = jnp.where(z_rel == k - 1, stack[:, k : k + 1], pz)
-    pz_ref[...] = pz
+    gy_ref[...] = profile(CY, CY, table[1:2], table[4:5])
+    pz_ref[...] = line_profile(table[2:3], table[5:6], [])[0]
+    pos_ref[...] = jnp.concatenate([table[q : q + 1, k * CZ : (k + 1) * CZ] for q in range(6) for k in range(4)], axis=0)
 
 
 def attack(axial_flow, tangent, cos_twist, sin_twist):
@@ -325,9 +340,7 @@
     return rel_speed, cos_phi, sin_phi, lift_coef, drag_coef
 
 
-def loads_body(samp_ref, other_ref, sel_ref, pts_ref, gx_ref, gy_ref, pz_ref, lh_ref, pay_c, pay_d, ret_ref, xrim_ref):
-    even_x, even_y, inner, _, _, _ = place()
-
+def loads_body(samp_ref, other_ref, sel_ref, pts_ref, gx_ref, gy_ref, pz_ref, pos_ref, lh_ref, pay_ref, xrim_ref):
     def row(k):
         picks = (2 * k, 2 * k + 1, ROWS + 2 * k, ROWS + 2 * k + 1)
         return jnp.concatenate([sel_ref[j : j + 1] for j in picks], axis=1)
@@ -363,7 +376,8 @@
                 pieces.append(force[c][:, at : at + CZ])
         pieces += [sel_ref[t * ROWS + 15 : t * ROWS + 16]] * 2
     blocks = jnp.concatenate(pieces, axis=0)
-    ret_ref[...] = blocks
+    pay_ref[0 : 2 * BACK] = blocks
+    pay_ref[2 * BACK :] = pos_ref[...]
     cols = jnp.concatenate(force + [jnp.zeros((CZ - 3, PTS), F32)], axis=0).T
     pz = pz_ref[...] * DT_STEP
     lines = jnp.concatenate([cols[:, c : c + 1] * pz for c in range(3)], axis=1)
@@ -371,22 +385,43 @@
     lh_ref[...] = lines
     gx = gx_ref[...]
     gy = gy_ref[...]
-    planes = [gx * gy[CY + k : CY + k + 1] for k in range(4)]
-    planes += [gx[CX + k : CX + k + 1] * gy[0:CY] for k in range(4)]
+    planes = [gx[CX + k : CX + k + 1] * gy for k in range(4)]
     w_high, w_low = split(jnp.concatenate(planes, axis=0))
     rim = dot3(w_high, w_low, l_high, l_low)
-    for k in range(2):
-        for c in range(3):
-            low = rim[k * YROWS : (k + 1) * YROWS, c * CZ : (c + 1) * CZ]
-            high = rim[(k + 2) * YROWS : (k + 3) * YROWS, c * CZ : (c + 1) * CZ]
-            at = (k * 3 + c) * YROWS
-            pay_c[at : at + YROWS] = jnp.where(even_y, high, low)
-            pay_d[at : at + YROWS] = jnp.where(even_y, low, high)
-    first = 4 * YROWS
     for k in range(4):
         for c in range(3):
             at = (k * 3 + c) * CY
-            xrim_ref[at : at + CY] = rim[first + k * CY : first + (k + 1) * CY, c * CZ : (c + 1) * CZ]
+            xrim_ref[at : at + CY] = rim[k * CY : (k + 1) * CY, c * CZ : (c + 1) * CZ]
+
+
+def near_body(rec_c, rec_d, low_ref, high_ref):
+    _, even_y, _, _, _, _ = place()
+    c_all, d_all = rec_c[...], rec_d[...]
+    for side, out_ref in ((0, low_ref), (1, high_ref)):
+        got = jnp.where(even_y, d_all, c_all) if side == 0 else jnp.where(even_y, c_all, d_all)
+
+        def wide(first, picks):
+            return jnp.concatenate([got[first + j : first + j + 1] for j in picks], axis=1)
+
+        x, y, z, fx, fy, fz = [wide(2 * BACK + 4 * q, range(4)) for q in range(6)]
+        force = [wide(2 * c, (0, 1, BACK, BACK + 1)) * DT_STEP for c in range(3)]
+        pz, columns = line_profile(z, fz, force)
+        l_high, l_low = split(jnp.concatenate([col * pz for col in columns], axis=1))
+        gx = profile(YROWS, CX, x, fx)
+        wy = offsets(fy)
+        planes = []
+        for i in range(2):
+            rel = (CY + i if side == 0 else i - 2) - y.astype(jnp.int32)
+            gy = jnp.zeros((1, PTS), F32)
+            for k in range(4):
+                gy = jnp.where(rel == k - 1, wy[k], gy)
+            planes.append(gx * gy)
+        w_high, w_low = split(jnp.concatenate(planes, axis=0))
+        rim = dot3(w_high, w_low, l_high, l_low)
+        for i in range(2):
+            for c in range(3):
+                at = (i * 3 + c) * YROWS
+                out_ref[at : at + YROWS] = rim[i * YROWS : (i + 1) * YROWS, c * CZ : (c + 1) * CZ]
 
 
 SPREAD_X = 8
@@ -406,7 +441,7 @@
             out_ref[c, at : at + SPREAD_X] = base_ref[c, at : at + SPREAD_X] + part
 
 
-def rimpack_body(n_blk, xrim_ref, rec_c, rec_d, *rest):
+def rimpack_body(n_blk, xrim_ref, low_ref, high_ref, *rest):
     pieces, (pay_a, pay_b, back_ref, *others) = rest[:n_blk], rest[n_blk:]
     even_x, even_y, inner, _, b0, ny = place()
     zero = jnp.zeros((CY - 4, CZ), F32)
@@ -417,9 +452,8 @@
                 near, far = [], []
                 for y in range(2):
                     at = (y * 3 + c) * YROWS + CX + 2 * s + k
-                    from_c, from_d = rec_c[at : at + 1], rec_d[at : at + 1]
-                    near.append(jnp.where(even_y, from_d, from_c))
-                    far.append(jnp.where(even_y, from_c, from_d))
+                    near.append(low_ref[at : at + 1])
+                    far.append(high_ref[at : at + 1])
                 at = ((2 * s + k) * 3 + c) * CY
                 sides.append(xrim_ref[at : at + CY] + jnp.concatenate(near + [zero] + far, axis=0))
             at = (k * 3 + c) * CY
@@ -445,7 +479,7 @@
         others[1][...] = pay_b[RIM_X:]
 
 
-def face_terms(buf, at, first, main_low, main_high, y_ref, rec_c, rec_d, rim_c, rim_d, even_y):
+def face_terms(buf, at, first, main_low, main_high, y_ref, rec_c, rec_d, rim_low, rim_high, even_y):
     half = 0.5 * DT_STEP
     visc = DT_STEP * NU_VISC
     part = slice(first, first + CHUNK)
@@ -456,32 +490,31 @@
         buf[c, here] = half_of[c, inner : inner + CHUNK]
         rows = slice(c * CX + first, c * CX + first + CHUNK)
         a, b = rec_c[rows], rec_d[rows]
-        low = [jnp.where(even_y, b, a) * (visc + half * y_ref[1, part]), 0.0]
-        high = [0.0, jnp.where(even_y, a, b) * (visc - half * y_ref[4, part])]
+        low = [jnp.where(even_y, b, a) * (visc + half * y_ref[0, part]), 0.0]
+        high = [0.0, jnp.where(even_y, a, b) * (visc - half * y_ref[1, part])]
         for i in range(2):
             row = (i * 3 + c) * YROWS + first
-            a, b = rim_c[row : row + CHUNK], rim_d[row : row + CHUNK]
-            buf[c, here, i, :] += jnp.where(even_y, b, a) + low[i]
-            buf[c, here, CY - 2 + i, :] += jnp.where(even_y, a, b) + high[i]
+            buf[c, here, i, :] += rim_low[row : row + CHUNK] + low[i]
+            buf[c, here, CY - 2 + i, :] += rim_high[row : row + CHUNK] + high[i]
 
 
 def chunk_copy(buf, at, out_ref, first, sem):
     return pltpu.make_async_copy(buf.at[:, pl.ds(at, CHUNK)], out_ref.at[:, pl.ds(first, CHUNK)], sem)
 
 
-def inside_body(main_low, main_high, y_ref, rec_c, rec_d, rim_c, rim_d, out_ref, buf, sems):
+def inside_body(main_low, main_high, y_ref, rec_c, rec_d, rim_low, rim_high, out_ref, buf, sems):
     _, even_y, _, _, _, _ = place()
     copies = []
     for k in range(N_CHUNK - 2):
         first = (k + 1) * CHUNK
-        face_terms(buf, k * CHUNK, first, main_low, main_high, y_ref, rec_c, rec_d, rim_c, rim_d, even_y)
+        face_terms(buf, k * CHUNK, first, main_low, main_high, y_ref, rec_c, rec_d, rim_low, rim_high, even_y)
         copies.append(chunk_copy(buf, k * CHUNK, out_ref, first, sems.at[k]))
         copies[-1].start()
     for copy in copies:
         copy.wait()
 
 
-def final_body(n_ret, _, main_low, main_high, x_ref, y_ref, face_a, face_b, rec_c, rec_d, rim_a, rim_b, rim_c, rim_d, back_ref, *rest):
+def final_body(n_ret, _, main_low, main_high, x_ref, y_ref, face_a, face_b, rec_c, rec_d, rim_a, rim_b, rim_low, rim_high, back_ref, *rest):
     rets, (out_ref, pf_ref, buf, sems) = rest[:n_ret], rest[n_ret:]
     even_x, even_y, inner, brick, _, _ = place()
     half = 0.5 * DT_STEP
@@ -489,7 +522,7 @@
     copies = []
     for k in range(2):
         first, at = k * (CX - CHUNK), k * CHUNK
-        face_terms(buf, at, first, main_low, main_high, y_ref, rec_c, rec_d, rim_c, rim_d, even_y)
+        face_terms(buf, at, first, main_low, main_high, y_ref, rec_c, rec_d, rim_low, rim_high, even_y)
         for c in range(3):
             a = face_a[c * XROWS : c * XROWS + CY]
             b = jnp.where(inner, face_b[c * XROWS : c * XROWS + CY], 0.0)
@@ -573,13 +606,12 @@
         return pieces
 
     dma = pltpu.SemaphoreType.DMA
-    tiles = pltpu.VMEM((3, CX, 8, CZ), F32)
-    pay_c, pay_d, block, x_faces, y_faces = call(
+    pay_c, pay_d, block = call(
         pack_body,
-        [(FACE_Y + ROWS, CZ), (FACE_Y, CZ), (ROWS, CZ), (6, CY, CZ), (6, CX, CZ)],
+        [(FACE_Y + ROWS, CZ), (FACE_Y, CZ), (ROWS, CZ)],
         7,
         "pack",
-        scratch=[tiles, tiles, pltpu.VMEM((4, 2, CZ), F32), pltpu.VMEM((2, CZ), jnp.int32), pltpu.SMEM((1,), F32), dma((10,))],
+        scratch=[pltpu.VMEM((4, 2, CZ), F32), pltpu.VMEM((2, CZ), jnp.int32), pltpu.SMEM((1,), F32), dma((12,))],
         in_specs=[HB] * 7,
         vmem=56,
     )(velocity, rotor_speed, *[a.reshape(2, CZ) for a in (blade_radius, blade_chord, blade_twist, blade_angle, owner_src)])
@@ -593,8 +625,8 @@
     two = join([block, rec_c[FACE_Y:]])
     beside = swap(two)
     cells, beside = after(host_cell, beside)
-    sampled = lambda: call(sample_body, [(HOST, CZ)], 3, "sample", vmem=24)(velocity, cells, host_frac)[0]
-    table, pieces = list(gather_y(two, sampled))
+    sampled = lambda: call(sample_body, [(HOST, CZ), (6, CY, CZ), (2, CX, CZ)], 3, "sample", vmem=24)(velocity, cells, host_frac)
+    (table, x_faces, y_faces), pieces = list(gather_y(two, sampled))
     pieces = pieces + [beside] + [swap(p) for p in pieces[1:]]
     n_rows = 2 * ny * ROWS
     pair = (2 * ROWS, CZ)
@@ -615,25 +647,24 @@
         "select",
     )(table, face_a, face_b, rec_c, rec_d, blocks, *from_x)
     other = swap(samp)
-    gx, gy, pz = call(weights_body, [(YROWS, PTS), (CY + 8, PTS), (PTS, CZ)], 1, "weights")(pts)
-    lines, pay_c, pay_d, ret, xrim = call(
+    gx, gy, pz, pos = call(weights_body, [(YROWS, PTS), (CY, PTS), (PTS, CZ), (24, CZ)], 1, "weights")(pts)
+    lines, points, xrim = call(
         loads_body,
-        [(PTS, 3 * CZ), (RIM_Y, CZ), (RIM_Y, CZ), (2 * BACK, CZ), (2 * RIM_X, CZ)],
-        7,
+        [(PTS, 3 * CZ), (2 * BACK + 24, CZ), (2 * RIM_X, CZ)],
+        8,
         "loads",
-    )(samp, other, sel, pts, gx, gy, pz)
-    ret_c = lax.ppermute(ret, "gy", flip(ny, 1))
-    rim_c = lax.ppermute(pay_c, "gy", flip(ny, 1))
-    rim_d = lax.ppermute(pay_d, "gy", odd_pairs(ny))
+    )(samp, other, sel, pts, gx, gy, pz, pos)
+    near_d = lax.ppermute(points, "gy", odd_pairs(ny))
+    near_c = lax.ppermute(points, "gy", flip(ny, 1))
 
     def spread(start, base):
         return call(
             lambda *refs: spread_body(start, *refs), [(3, CX // 2, CY, CZ)], 4, "spread"
         )(lines, gx, gy, base)[0]
 
-    ret_c, main_low = after(ret_c, spread(0, base_low))
-    main_high, pieces = list(gather_y(join([ret, ret_c]), lambda: spread(CX // 2, base_high)))
-    rim_c, main_high = after(rim_c, main_high)
+    (near_c, near_d), main_low = after((near_c, near_d), spread(0, base_low))
+    nearby = lambda: call(near_body, [(RIM_Y, CZ)] * 2, 2, "near")(near_c, near_d)
+    (rim_low, rim_high), pieces = list(gather_y(join([points[: 2 * BACK], near_c[: 2 * BACK]]), nearby))
     n_rows = 2 * ny * BACK
     pair = (2 * BACK, CZ)
     pay_a, pay_b, back, *across = call(
@@ -641,10 +672,12 @@
         [(RIM_X, CZ), (RIM_X + 2 * BACK, CZ), (n_rows, CZ), pair, pair] if ring else [(RIM_X, CZ), (RIM_X, CZ), (n_rows, CZ)],
         3 + len(pieces),
         "rimpack",
-    )(xrim, rim_c, rim_d, *pieces)
+    )(xrim, rim_low, rim_high, *pieces)
     rim_b = lax.ppermute(pay_b, "gx", odd_pairs(nx, ring))
     rets = across_x(across) if ring else gather_x(back)
     rim_a = swap(pay_a)
+    main_high = spread(CX // 2, base_high)
+    (main_low, main_high) = lax.optimization_barrier((main_low, main_high))
     inside = call(
         inside_body,
         [velocity.shape],
@@ -653,7 +686,7 @@
         scratch=[pltpu.VMEM((3, CX - 2 * CHUNK, CY, CZ), F32), dma((N_CHUNK - 2,))],
         out_specs=[HB],
         vmem=16,
-    )(main_low, main_high, y_faces, rec_c, rec_d, rim_c, rim_d)[0]
+    )(main_low, main_high, y_faces, rec_c, rec_d, rim_low, rim_high)[0]
     (rim_a, rim_b), inside = after((rim_a, rim_b), inside)
     return tuple(
         call(
@@ -665,7 +698,7 @@
             first=HB,
             out_specs=[HB, VM],
             aliases={0: 0},
-        )(inside, main_low, main_high, x_faces, y_faces, face_a, face_b, rec_c, rec_d, rim_a, rim_b, rim_c, rim_d, back, *rets)
+        )(inside, main_low, main_high, x_faces, y_faces, face_a, face_b, rec_c, rec_d, rim_a, rim_b, rim_low, rim_high, back, *rets)
     )
 
 

time: 53.4 us -> 51.3 us (0.961)
  waiting for transfers between devices: 4.89 us -> 2.23 us
  Pallas kernels: 22.7 us -> 23.3 us
    ppermute x2, waiting for transfers between devices: 1.66 us -> 0.01 us  [gather_y(): got = lax.ppermute(join(pieces), 'gy', flip(ny, bit))]
    ppermute x2, starting transfers between devices: 7.94 us -> 6.92 us  [gather_y(): got = lax.ppermute(join(pieces), 'gy', flip(ny, bit))]
    ppermute x3 -> x2, starting transfers between devices: 2.93 us -> 3.82 us  [the longest x1 2.98 us: per_device(): near_c = lax.ppermute(points, 'gy', flip(ny, 1))]
    pallas_call x4 -> x5, Pallas kernels: 9.55 us -> 10.2 us  [the longest x1 4.38 us: per_device(): call(sample_body, [(HOST, CZ), (6, CY, CZ), (2, CX, CZ)], 3, 'sample', vm...]
  transfers between devices with their start and end apart: 18 -> 17, of which waited for: 7 -> 4; matrix products, arithmetic and copies ran while one was open for 0% -> 0% of each run, Pallas kernels for 26% -> 31%
where the time goes in v6:
time: 51.3 us; the launch traced here: 51.1 us
  starting transfers between devices  23.8 us (46%)
  Pallas kernels  23.3 us (45%)
  waiting for transfers between devices  2.23 us (4%)
  between operations  1.67 us (3%)
    ppermute x2, starting transfers between devices, gather_y(): got = lax.ppermute(join(pieces), 'gy', flip(ny, bit))  6.92 us
    ppermute x4, starting transfers between devices, across_x(): lax.ppermute(b, 'gx', p)  5.01 us
    pallas_call x1, Pallas kernels, per_device(): call(sample_body, [(HOST, CZ), (6, CY, CZ), (2, CX, CZ)], 3, 'sample', vm...  4.38 us
    pallas_call x2, Pallas kernels, stencil(): call(lambda *refs: stencil_body(start, *refs), [(3, CX // 2, CY, CZ)], 1,...  3.9 us
    pallas_call x2, Pallas kernels, spread(): call(lambda *refs: spread_body(start, *refs), [(3, CX // 2, CY, CZ)], 4,...  3.59 us
    ppermute x1, starting transfers between devices, per_device(): rec_c = lax.ppermute(pay_c, 'gy', flip(ny, 1))  3.09 us
    ppermute x1, starting transfers between devices, per_device(): near_c = lax.ppermute(points, 'gy', flip(ny, 1))  2.98 us
    pallas_call x1, Pallas kernels, per_device(): call(lambda *refs: select_body(len(from_x), *refs), [(8, PTS), (2 * ROWS,...  2.31 us
  transfers between devices with their start and end apart: 17, of which 4 were waited for; matrix products, arithmetic and copies ran while one was open for 0% of the time, Pallas kernels for 31%

profile of v6, /device:TPU:0, one launch (start us, length us, event | category | flops | bytes accessed | tf_op | source)
XLA Modules:
  0.0 51.1 jit_solution(2212165245008918129)
XLA Ops:
  1.3 1.8 %pack.1 = (f32[208,128]{1,0:T(8,128)}, f32[192,128]{1,0:T(8,128)}, f32[16,128]{1,0:T(8,128)}) custom-call(f32[3,64,32,128]{3,2,1,0:T(8,128)} %refs_0_.3, f32[1]{0:T(128)S(6)} %copy.13.spin_hbm, f32[2,128]{1,0:T(2,128)} %bitcast.5, f32[2,128]{1,0:T(2,128)} %bitcast.6, f32[2,128]{1,0:T(2,128)} %bitcast.7, f32[2,128]{1,0:T(2,128)} %bitcast.8, s32[2,128]{1,0:T(2,128)} %bitcast.9), custom_call_target="tpu_custom_call" | custom-call | tf_op jit(solution)/shard_map/pack/pallas_call | solution.py:609
  3.1 3.1 %collective-permute-start = (f32[208,128]{1,0:T(8,128)}, f32[208,128]{1,0:T(8,128)S(1)}, u32[]{:S(2)}, u32[]{:S(2)}) collective-permute-start(f32[208,128]{1,0:T(8,128)} %get-tuple-element.53), channel_id=1, source_target_pairs={{0,1},{1,0},{2,3},{3,2},{4,5},{5,4},{6,7},{7,6},{8,9},{9,8},{10,11... | collective-permute-start | bytes 319496 | tf_op jit(solution)/shard_map/ppermute | solution.py:618
  6.2 0.8 %collective-permute-start.3 = (f32[192,128]{1,0:T(8,128)}, f32[192,128]{1,0:T(8,128)S(1)}, u32[]{:S(2)}, u32[]{:S(2)}) collective-permute-start(f32[192,128]{1,0:T(8,128)} %get-tuple-element.61), channel_id=1, source_target_pairs={{1,2},{2,1},{5,6},{6,5},{9,10},{10,9},{13,14},{14,13},{17,18},{18,... | collective-permute-start | bytes 294920 | tf_op jit(solution)/shard_map/ppermute | solution.py:619
  7.0 1.9 %stencil.2.refs_3_ = f32[3,32,32,128]{3,2,1,0:T(8,128)S(1)} custom-call(f32[3,64,32,128]{3,2,1,0:T(8,128)S(1)} %copy-done), custom_call_target="tpu_custom_call" | custom-call | tf_op jit(solution)/shard_map/stencil/pallas_call | solution.py:622
  9.0 0.4 collective-permute-done.refs_1_.refs_3_.rec_c.refs_7_
  9.5 3.5 %collective-permute-start.1 = (f32[32,128]{1,0:T(8,128)S(1)}, f32[32,128]{1,0:T(8,128)S(1)}, u32[]{:S(2)}, u32[]{:S(2)}) collective-permute-start(f32[32,128]{1,0:T(8,128)S(1)} %pad_maximum_fusion.refs_3_), channel_id=1, source_target_pairs={{0,2},{1,3},{2,0},{3,1},{4,6},{5,7},{6,4},{7,5},{8,10},{9,11},{10,... | collective-permute-start | bytes 49160 | tf_op jit(solution)/shard_map/ppermute | solution.py:594
  13.0 4.4 %sample.1 = (f32[512,128]{1,0:T(8,128)S(1)}, f32[6,32,128]{2,1,0:T(8,128)S(1)}, f32[2,64,128]{2,1,0:T(8,128)S(1)}) custom-call(f32[3,64,32,128]{3,2,1,0:T(8,128)S(1)} %copy-done, s32[3,512]{1,0:T(4,128)S(1)} %copy-done.1, f32[3,512]{1,0:T(4,128)S(1)} %copy-done.2), custom_call_target="tpu_custom_call" | custom-call | tf_op jit(solution)/shard_map/sample/pallas_call | solution.py:628
  17.4 0.2 collective-permute-start.4
  17.7 1.0 %collective-permute-done.4.refs_6_ = f32[32,128]{1,0:T(8,128)S(1)} collective-permute-done((f32[32,128]{1,0:T(8,128)S(1)}, f32[32,128]{1,0:T(8,128)S(1)}, u32[]{:S(2)}, u32[]{:S(2)}) %collective-permute-start.4) | collective-permute-done | bytes 16416 | tf_op jit(solution)/shard_map/ppermute | solution.py:583
  18.7 0.1 xpack.1
  18.8 2.3 %collective-permute-start.6 = (f32[152,128]{1,0:T(8,128)S(1)}, f32[152,128]{1,0:T(8,128)S(1)}, u32[]{:S(2)}, u32[]{:S(2)}) collective-permute-start(f32[152,128]{1,0:T(8,128)S(1)} %get-tuple-element.65), channel_id=1, source_target_pairs={{4,8},{12,16},{20,24},{28,0},{8,4},{16,12},{24,20},{0,28},{5,9},{1... | collective-permute-start | bytes 233480 | tf_op jit(solution)/shard_map/ppermute | solution.py:639
  21.1 0.9 %collective-permute-start.7 = (f32[32,128]{1,0:T(8,128)S(1)}, f32[32,128]{1,0:T(8,128)S(1)}, u32[]{:S(2)}, u32[]{:S(2)}) collective-permute-start(f32[32,128]{1,0:T(8,128)S(1)} %get-tuple-element.69), channel_id=1, source_target_pairs={{0,16},{4,20},{8,24},{12,28},{16,0},{20,4},{24,8},{28,12},{1,17},{... | collective-permute-start | bytes 49160 | tf_op jit(solution)/shard_map/ppermute | solution.py:580
  22.0 1.4 %collective-permute-start.8 = (f32[32,128]{1,0:T(8,128)S(1)}, f32[32,128]{1,0:T(8,128)S(1)}, u32[]{:S(2)}, u32[]{:S(2)}) collective-permute-start(f32[32,128]{1,0:T(8,128)S(1)} %get-tuple-element.70), channel_id=1, source_target_pairs={{0,24},{4,12},{8,0},{12,20},{16,8},{20,28},{24,16},{28,4},{1,25},{... | collective-permute-start | bytes 49160 | tf_op jit(solution)/shard_map/ppermute | solution.py:580
  23.4 1.9 %stencil.3.refs_3_ = f32[3,32,32,128]{3,2,1,0:T(8,128)S(1)} custom-call(f32[3,64,32,128]{3,2,1,0:T(8,128)S(1)} %copy-done), custom_call_target="tpu_custom_call" | custom-call | tf_op jit(solution)/shard_map/stencil/pallas_call | solution.py:622
  25.4 0.3 collective-permute-done.8.refs_7_
  25.7 2.3 %select.1 = (f32[8,512]{1,0:T(8,128)S(1)}, f32[32,128]{1,0:T(8,128)S(1)}, f32[512,128]{1,0:T(8,128)S(1)}) custom-call(f32[512,128]{1,0:T(8,128)S(1)} %get-tuple-element.59.refs_0_, f32[120,128]{1,0:T(8,128)S(1)} %collective-permute-done.5.refs_1_.refs_5_, f32[152,128]{1,0:T(8,128)S(1)} %collective-permute-done.6.refs_2_.refs_6_, ...), custom_call_target="tpu_custom_call" | custom-call | tf_op jit(solution)/shard_map/select/pallas_call | solution.py:643
  28.1 0.7 %weights.1 = (f32[72,512]{1,0:T(8,128)S(1)}, f32[32,512]{1,0:T(8,128)S(1)}, f32[512,128]{1,0:T(8,128)S(1)}, f32[24,128]{1,0:T(8,128)S(1)}) custom-call(f32[512,128]{1,0:T(8,128)S(1)} %get-tuple-element.73.pts_ref), custom_call_target="tpu_custom_call" | custom-call | tf_op jit(solution)/shard_map/weights/pallas_call | solution.py:650
  28.8 0.5 collective-permute-done.9.other_ref
  29.2 1.4 %loads.1 = (f32[512,384]{1,0:T(8,128)S(1)}, f32[40,128]{1,0:T(8,128)S(1)}, f32[384,128]{1,0:T(8,128)S(1)}) custom-call(f32[8,512]{1,0:T(8,128)S(1)} %get-tuple-element.71.samp_ref, f32[8,512]{1,0:T(8,128)S(1)} %collective-permute-done.9.other_ref, f32[32,128]{1,0:T(8,128)S(1)} %get-tuple-element.72.sel_ref, f32[512,128]{1,0:T(8,128)S(1)} %get-tuple-element.73.pts_ref, ...), custom_call_target="tpu_custom_call" | custom-call | tf_op jit(solution)/shard_map/loads/pallas_call | solution.py:651
  30.6 0.8 %collective-permute-start.11 = (f32[40,128]{1,0:T(8,128)S(1)}, f32[40,128]{1,0:T(8,128)S(1)}, u32[]{:S(2)}, u32[]{:S(2)}) collective-permute-start(f32[40,128]{1,0:T(8,128)S(1)} %get-tuple-element.79), channel_id=1, source_target_pairs={{1,2},{2,1},{5,6},{6,5},{9,10},{10,9},{13,14},{14,13},{17,18},{18,... | collective-permute-start | bytes 61448 | tf_op jit(solution)/shard_map/ppermute | solution.py:657
  31.5 3.0 %collective-permute-start.10 = (f32[40,128]{1,0:T(8,128)S(1)}, f32[40,128]{1,0:T(8,128)S(1)}, u32[]{:S(2)}, u32[]{:S(2)}) collective-permute-start(f32[40,128]{1,0:T(8,128)S(1)} %get-tuple-element.79), channel_id=1, source_target_pairs={{0,1},{1,0},{2,3},{3,2},{4,5},{5,4},{6,7},{7,6},{8,9},{9,8},{10,11... | collective-permute-start | bytes 61448 | tf_op jit(solution)/shard_map/ppermute | solution.py:658
  34.5 1.8 %spread.2.main_low.refs_1_ = f32[3,32,32,128]{3,2,1,0:T(8,128)S(1)} custom-call(f32[512,384]{1,0:T(8,128)S(1)} %get-tuple-element.80.refs_0_, f32[72,512]{1,0:T(8,128)S(1)} %get-tuple-element.74.gx_ref.refs_1_, f32[32,512]{1,0:T(8,128)S(1)} %get-tuple-element.75.gy_ref.refs_2_, f32[3,32,32,128]{3,2,1,0:T(8,128)S(1)} %stencil.2.refs_3_), custom_call_target="tpu_custom_call" | custom-call | tf_op jit(solution)/shard_map/spread/pallas_call | solution.py:661
  36.3 3.4 %collective-permute-start.12 = (f32[32,128]{1,0:T(8,128)S(1)}, f32[32,128]{1,0:T(8,128)S(1)}, u32[]{:S(2)}, u32[]{:S(2)}) collective-permute-start(f32[32,128]{1,0:T(8,128)S(1)} %pad_maximum_fusion.1.refs_3_), channel_id=1, source_target_pairs={{0,2},{1,3},{2,0},{3,1},{4,6},{5,7},{6,4},{7,5},{8,10},{9,11},{10,... | collective-permute-start | bytes 49160 | tf_op jit(solution)/shard_map/ppermute | solution.py:594
  39.7 1.9 %near.1 = (f32[432,128]{1,0:T(8,128)S(1)}, f32[432,128]{1,0:T(8,128)S(1)}) custom-call(f32[40,128]{1,0:T(8,128)S(1)} %collective-permute-done.10.rec_c, f32[40,128]{1,0:T(8,128)S(1)} %collective-permute-done.11.rec_d), custom_call_target="tpu_custom_call" | custom-call | tf_op jit(solution)/shard_map/near/pallas_call | solution.py:666
  41.6 0.1 rimpack.1
  41.7 0.5 collective-permute-start.14
  42.2 1.1 %collective-permute-start.13 = (f32[192,128]{1,0:T(8,128)S(1)}, f32[192,128]{1,0:T(8,128)S(1)}, u32[]{:S(2)}, u32[]{:S(2)}) collective-permute-start(f32[192,128]{1,0:T(8,128)S(1)} %get-tuple-element.89), channel_id=1, source_target_pairs={{0,4},{4,0},{8,12},{12,8},{16,20},{20,16},{24,28},{28,24},{1,5},{5... | collective-permute-start | bytes 294920 | tf_op jit(solution)/shard_map/ppermute | solution.py:583
  43.3 1.5 %collective-permute-start.15 = (f32[16,128]{1,0:T(8,128)S(1)}, f32[16,128]{1,0:T(8,128)S(1)}, u32[]{:S(2)}, u32[]{:S(2)}) collective-permute-start(f32[16,128]{1,0:T(8,128)S(1)} %get-tuple-element.100), channel_id=1, source_target_pairs={{0,16},{4,20},{8,24},{12,28},{16,0},{20,4},{24,8},{28,12},{1,17},{... | collective-permute-start | bytes 24584 | tf_op jit(solution)/shard_map/ppermute | solution.py:580
  44.8 1.1 %collective-permute-start.16 = (f32[16,128]{1,0:T(8,128)S(1)}, f32[16,128]{1,0:T(8,128)S(1)}, u32[]{:S(2)}, u32[]{:S(2)}) collective-permute-start(f32[16,128]{1,0:T(8,128)S(1)} %get-tuple-element.101), channel_id=1, source_target_pairs={{0,24},{4,12},{8,0},{12,20},{16,8},{20,28},{24,16},{28,4},{1,25},{... | collective-permute-start | bytes 24584 | tf_op jit(solution)/shard_map/ppermute | solution.py:580
  45.9 1.8 %spread.3.main_high.refs_2_ = f32[3,32,32,128]{3,2,1,0:T(8,128)S(1)} custom-call(f32[512,384]{1,0:T(8,128)S(1)} %get-tuple-element.80.refs_0_, f32[72,512]{1,0:T(8,128)S(1)} %get-tuple-element.74.gx_ref.refs_1_, f32[32,512]{1,0:T(8,128)S(1)} %get-tuple-element.75.gy_ref.refs_2_, f32[3,32,32,128]{3,2,1,0:T(8,128)S(1)} %stencil.3.refs_3_), custom_call_target="tpu_custom_call" | custom-call | tf_op jit(solution)/shard_map/spread/pallas_call | solution.py:661
  47.7 1.5 %inside.1.refs_0_ = f32[3,64,32,128]{3,2,1,0:T(8,128)} custom-call(f32[3,32,32,128]{3,2,1,0:T(8,128)S(1)} %spread.2.main_low.refs_1_, f32[3,32,32,128]{3,2,1,0:T(8,128)S(1)} %spread.3.main_high.refs_2_, f32[2,64,128]{2,1,0:T(8,128)S(1)} %get-tuple-element.95.y_ref.refs_4_, f32[208,128]{1,0:T(8,128)S(1)} %collective-permute-done.refs_1_.refs_3_.rec_c.refs_7_, ...), custom_call_target="tpu_custom_call" | custom-call | tf_op jit(solution)/shard_map/inside/pallas_call | solution.py:681
  49.3 1.6 %final.1 = (f32[3,64,32,128]{3,2,1,0:T(8,128)}, f32[3,256]{1,0:T(4,128)}) custom-call(f32[3,64,32,128]{3,2,1,0:T(8,128)} %inside.1.refs_0_, f32[3,32,32,128]{3,2,1,0:T(8,128)S(1)} %spread.2.main_low.refs_1_, f32[3,32,32,128]{3,2,1,0:T(8,128)S(1)} %spread.3.main_high.refs_2_, ...), custom_call_target="tpu_custom_call", output_to_operand_aliasing={{0}: (0, {})} | custom-call | tf_op jit(solution)/shard_map/final/pallas_call | solution.py:692
  (29 shorter events, 0.2 us)
Async XLA Ops:
  1.3 5.7 %copy-start = (f32[3,64,32,128]{3,2,1,0:T(8,128)S(1)}, f32[3,64,32,128]{3,2,1,0:T(8,128)}, u32[]{:S(2)}) copy-start(f32[3,64,32,128]{3,2,1,0:T(8,128)} %refs_0_.3) | copy-start | bytes 9437188
  3.1 6.3 %collective-permute-start = (f32[208,128]{1,0:T(8,128)}, f32[208,128]{1,0:T(8,128)S(1)}, u32[]{:S(2)}, u32[]{:S(2)}) collective-permute-start(f32[208,128]{1,0:T(8,128)} %get-tuple-element.53), channel_id=1, source_target_pairs={{0,1},{1,0},{2,3},{3,2},{4,5},{5,4},{6,7},{7,6},{8,9},{9,8},{10,11... | collective-permute-start | bytes 319496 | tf_op jit(solution)/shard_map/ppermute | solution.py:618
  6.2 3.2 %copy-start.3 = (f32[16,128]{1,0:T(8,128)S(1)}, f32[16,128]{1,0:T(8,128)}, u32[]{:S(2)}) copy-start(f32[16,128]{1,0:T(8,128)} %get-tuple-element.52) | copy-start | bytes 24580
  6.2 6.8 %copy-start.1 = (s32[3,512]{1,0:T(4,128)S(1)}, s32[3,512]{1,0:T(4,128)}, u32[]{:S(2)}) copy-start(s32[3,512]{1,0:T(4,128)} %cell_ref) | copy-start | bytes 18436
  6.2 6.8 %copy-start.2 = (f32[3,512]{1,0:T(4,128)S(1)}, f32[3,512]{1,0:T(4,128)}, u32[]{:S(2)}) copy-start(f32[3,512]{1,0:T(4,128)} %frac_ref.1) | copy-start | bytes 18436
  6.2 11.4 %collective-permute-start.3 = (f32[192,128]{1,0:T(8,128)}, f32[192,128]{1,0:T(8,128)S(1)}, u32[]{:S(2)}, u32[]{:S(2)}) collective-permute-start(f32[192,128]{1,0:T(8,128)} %get-tuple-element.61), channel_id=1, source_target_pairs={{1,2},{2,1},{5,6},{6,5},{9,10},{10,9},{13,14},{14,13},{17,18},{18,... | collective-permute-start | bytes 294920 | tf_op jit(solution)/shard_map/ppermute | solution.py:619
  9.4 3.6 %collective-permute-start.2 = (f32[32,128]{1,0:T(8,128)S(1)}, f32[32,128]{1,0:T(8,128)S(1)}, u32[]{:S(2)}, u32[]{:S(2)}) collective-permute-start(f32[32,128]{1,0:T(8,128)S(1)} %pad_maximum_fusion.refs_3_), channel_id=1, source_target_pairs={{0,4},{4,0},{8,12},{12,8},{16,20},{20,16},{24,28},{28,24},{1,5},{5... | collective-permute-start | bytes 49160 | tf_op jit(solution)/shard_map/ppermute | solution.py:583
  9.5 7.9 %collective-permute-start.1 = (f32[32,128]{1,0:T(8,128)S(1)}, f32[32,128]{1,0:T(8,128)S(1)}, u32[]{:S(2)}, u32[]{:S(2)}) collective-permute-start(f32[32,128]{1,0:T(8,128)S(1)} %pad_maximum_fusion.refs_3_), channel_id=1, source_target_pairs={{0,2},{1,3},{2,0},{3,1},{4,6},{5,7},{6,4},{7,5},{8,10},{9,11},{10,... | collective-permute-start | bytes 49160 | tf_op jit(solution)/shard_map/ppermute | solution.py:594
  17.4 1.2 %collective-permute-start.4 = (f32[32,128]{1,0:T(8,128)S(1)}, f32[32,128]{1,0:T(8,128)S(1)}, u32[]{:S(2)}, u32[]{:S(2)}) collective-permute-start(f32[32,128]{1,0:T(8,128)S(1)} %collective-permute-done.1.refs_4_), channel_id=1, source_target_pairs={{0,4},{4,0},{8,12},{12,8},{16,20},{20,16},{24,28},{28,24},{1,5},{5... | collective-permute-start | bytes 49160 | tf_op jit(solution)/shard_map/ppermute | solution.py:583
  18.8 6.6 %collective-permute-start.6 = (f32[152,128]{1,0:T(8,128)S(1)}, f32[152,128]{1,0:T(8,128)S(1)}, u32[]{:S(2)}, u32[]{:S(2)}) collective-permute-start(f32[152,128]{1,0:T(8,128)S(1)} %get-tuple-element.65), channel_id=1, source_target_pairs={{4,8},{12,16},{20,24},{28,0},{8,4},{16,12},{24,20},{0,28},{5,9},{1... | collective-permute-start | bytes 233480 | tf_op jit(solution)/shard_map/ppermute | solution.py:639
  21.1 4.3 %collective-permute-start.5 = (f32[120,128]{1,0:T(8,128)S(1)}, f32[120,128]{1,0:T(8,128)S(1)}, u32[]{:S(2)}, u32[]{:S(2)}) collective-permute-start(f32[120,128]{1,0:T(8,128)S(1)} %get-tuple-element.64), channel_id=1, source_target_pairs={{0,4},{4,0},{8,12},{12,8},{16,20},{20,16},{24,28},{28,24},{1,5},{5... | collective-permute-start | bytes 184328 | tf_op jit(solution)/shard_map/ppermute | solution.py:583
  21.1 4.3 %collective-permute-start.7 = (f32[32,128]{1,0:T(8,128)S(1)}, f32[32,128]{1,0:T(8,128)S(1)}, u32[]{:S(2)}, u32[]{:S(2)}) collective-permute-start(f32[32,128]{1,0:T(8,128)S(1)} %get-tuple-element.69), channel_id=1, source_target_pairs={{0,16},{4,20},{8,24},{12,28},{16,0},{20,4},{24,8},{28,12},{1,17},{... | collective-permute-start | bytes 49160 | tf_op jit(solution)/shard_map/ppermute | solution.py:580
  22.0 3.7 %collective-permute-start.8 = (f32[32,128]{1,0:T(8,128)S(1)}, f32[32,128]{1,0:T(8,128)S(1)}, u32[]{:S(2)}, u32[]{:S(2)}) collective-permute-start(f32[32,128]{1,0:T(8,128)S(1)} %get-tuple-element.70), channel_id=1, source_target_pairs={{0,24},{4,12},{8,0},{12,20},{16,8},{20,28},{24,16},{28,4},{1,25},{... | collective-permute-start | bytes 49160 | tf_op jit(solution)/shard_map/ppermute | solution.py:580
  28.0 1.2 %collective-permute-start.9 = (f32[8,512]{1,0:T(8,128)S(1)}, f32[8,512]{1,0:T(8,128)S(1)}, u32[]{:S(2)}, u32[]{:S(2)}) collective-permute-start(f32[8,512]{1,0:T(8,128)S(1)} %get-tuple-element.71.samp_ref), channel_id=1, source_target_pairs={{0,4},{4,0},{8,12},{12,8},{16,20},{20,16},{24,28},{28,24},{1,5},{5... | collective-permute-start | bytes 49160 | tf_op jit(solution)/shard_map/ppermute | solution.py:583
  30.6 5.6 %collective-permute-start.11 = (f32[40,128]{1,0:T(8,128)S(1)}, f32[40,128]{1,0:T(8,128)S(1)}, u32[]{:S(2)}, u32[]{:S(2)}) collective-permute-start(f32[40,128]{1,0:T(8,128)S(1)} %get-tuple-element.79), channel_id=1, source_target_pairs={{1,2},{2,1},{5,6},{6,5},{9,10},{10,9},{13,14},{14,13},{17,18},{18,... | collective-permute-start | bytes 61448 | tf_op jit(solution)/shard_map/ppermute | solution.py:657
  31.5 4.8 %collective-permute-start.10 = (f32[40,128]{1,0:T(8,128)S(1)}, f32[40,128]{1,0:T(8,128)S(1)}, u32[]{:S(2)}, u32[]{:S(2)}) collective-permute-start(f32[40,128]{1,0:T(8,128)S(1)} %get-tuple-element.79), channel_id=1, source_target_pairs={{0,1},{1,0},{2,3},{3,2},{4,5},{5,4},{6,7},{7,6},{8,9},{9,8},{10,11... | collective-permute-start | bytes 61448 | tf_op jit(solution)/shard_map/ppermute | solution.py:658
  36.3 5.3 %collective-permute-start.12 = (f32[32,128]{1,0:T(8,128)S(1)}, f32[32,128]{1,0:T(8,128)S(1)}, u32[]{:S(2)}, u32[]{:S(2)}) collective-permute-start(f32[32,128]{1,0:T(8,128)S(1)} %pad_maximum_fusion.1.refs_3_), channel_id=1, source_target_pairs={{0,2},{1,3},{2,0},{3,1},{4,6},{5,7},{6,4},{7,5},{8,10},{9,11},{10,... | collective-permute-start | bytes 49160 | tf_op jit(solution)/shard_map/ppermute | solution.py:594
  41.7 7.6 %collective-permute-start.14 = (f32[208,128]{1,0:T(8,128)S(1)}, f32[208,128]{1,0:T(8,128)S(1)}, u32[]{:S(2)}, u32[]{:S(2)}) collective-permute-start(f32[208,128]{1,0:T(8,128)S(1)} %get-tuple-element.90), channel_id=1, source_target_pairs={{4,8},{12,16},{20,24},{28,0},{8,4},{16,12},{24,20},{0,28},{5,9},{1... | collective-permute-start | bytes 319496 | tf_op jit(solution)/shard_map/ppermute | solution.py:676
  42.2 7.1 %collective-permute-start.13 = (f32[192,128]{1,0:T(8,128)S(1)}, f32[192,128]{1,0:T(8,128)S(1)}, u32[]{:S(2)}, u32[]{:S(2)}) collective-permute-start(f32[192,128]{1,0:T(8,128)S(1)} %get-tuple-element.89), channel_id=1, source_target_pairs={{0,4},{4,0},{8,12},{12,8},{16,20},{20,16},{24,28},{28,24},{1,5},{5... | collective-permute-start | bytes 294920 | tf_op jit(solution)/shard_map/ppermute | solution.py:583
  43.3 6.1 %collective-permute-start.15 = (f32[16,128]{1,0:T(8,128)S(1)}, f32[16,128]{1,0:T(8,128)S(1)}, u32[]{:S(2)}, u32[]{:S(2)}) collective-permute-start(f32[16,128]{1,0:T(8,128)S(1)} %get-tuple-element.100), channel_id=1, source_target_pairs={{0,16},{4,20},{8,24},{12,28},{16,0},{20,4},{24,8},{28,12},{1,17},{... | collective-permute-start | bytes 24584 | tf_op jit(solution)/shard_map/ppermute | solution.py:580
  44.8 4.5 %collective-permute-start.16 = (f32[16,128]{1,0:T(8,128)S(1)}, f32[16,128]{1,0:T(8,128)S(1)}, u32[]{:S(2)}, u32[]{:S(2)}) collective-permute-start(f32[16,128]{1,0:T(8,128)S(1)} %get-tuple-element.101), channel_id=1, source_target_pairs={{0,24},{4,12},{8,0},{12,20},{16,8},{20,28},{24,16},{28,4},{1,25},{... | collective-permute-start | bytes 24584 | tf_op jit(solution)/shard_map/ppermute | solution.py:580

commit v7 on v6

--- a/solution.py
+++ b/solution.py
@@ -57,6 +57,12 @@
     px, py = lax.rem(ix, 2), lax.rem(iy, 2)
     inner = (ix + px > 0) & (ix + px < nx)
     return px == 0, py == 0, inner, ix * ny + iy, (ix - px) * ny + iy, ny
+
+
+def odd_side():
+    ny, iy = lax.axis_size("gy"), lax.axis_index("gy")
+    py = lax.rem(iy, 2)
+    return (iy + py > 0) & (iy + py < ny)
 
 
 def split(value):
@@ -122,6 +128,7 @@
     block = jnp.concatenate(parts, axis=0)
     blk_ref[...] = block
     pay_c[FACE_Y:] = block
+    pay_d[FACE_Y:] = block
     for copy in faces(0, 0):
         copy.wait()
 
@@ -160,39 +167,47 @@
     return jnp.where(coord == base, 1.0 - frac, jnp.where(coord == base + 1, frac, 0.0))
 
 
-def sample_body(v_ref, cell_ref, frac_ref, tab_ref, x_ref, y_ref):
+def sample_part(start, v_ref, table, out_ref):
+    x_col, y_col, z_col = [table[:, k : k + 1].astype(jnp.int32) for k in range(3)]
+    fx, fy, fz = [table[:, k : k + 1] for k in range(3, 6)]
+    lane = lax.broadcasted_iota(jnp.int32, (HOST, CZ), 1)
+    wy = weight(lane % CY, y_col, fy)
+    x_lane = lane // CY + start - x_col
+    acc = None
+    per = 4
+    nx = CZ * per // CY
+    for j in range(CX // 2 // nx):
+        parts = []
+        for i in range(per):
+            shift = (CZ // CY) * (j * per + i)
+            wx = jnp.where(x_lane == -shift, 1.0 - fx, jnp.where(x_lane == 1 - shift, fx, 0.0))
+            parts.append(wx * wy)
+        w_high, w_low = split(jnp.concatenate(parts, axis=1))
+        first = start + j * nx
+        field = [v_ref[c, first : first + nx].reshape(nx * CY, CZ) for c in range(3)]
+        f_high, f_low = split(jnp.concatenate(field, axis=1))
+        part = dot3(w_high, w_low, f_high, f_low)
+        acc = part if acc is None else acc + part
+    wz = weight(lane, z_col, fz)
+    out = table
+    for c in range(3):
+        value = jnp.sum(acc[:, c * CZ : (c + 1) * CZ] * wz, axis=1, keepdims=True)
+        out = out + jnp.where(lane == 6 + c, value, 0.0)
+    out_ref[...] = out
+
+
+def sample_low_body(v_ref, cell_ref, frac_ref, tab_ref, x_ref, y_ref):
     for c in range(3):
         x_ref[c] = v_ref[c, 0]
         x_ref[c + 3] = v_ref[c, CX - 1]
     y_ref[0] = v_ref[1, :, 0, :]
     y_ref[1] = v_ref[1, :, CY - 1, :]
     rows = jnp.concatenate([cell_ref[...].astype(F32), frac_ref[...], jnp.zeros((CZ - 6, HOST), F32)], axis=0)
-    turned = rows.T
-    x_col, y_col, z_col = [turned[:, k : k + 1].astype(jnp.int32) for k in range(3)]
-    fx, fy, fz = [turned[:, k : k + 1] for k in range(3, 6)]
-    lane = lax.broadcasted_iota(jnp.int32, (HOST, CZ), 1)
-    wy = weight(lane % CY, y_col, fy)
-    x_lane = lane // CY - x_col
-    acc = None
-    per = 4
-    nx = CZ * per // CY
-    for j in range(CX // nx):
-        parts = []
-        for i in range(per):
-            shift = (CZ // CY) * (j * per + i)
-            wx = jnp.where(x_lane == -shift, 1.0 - fx, jnp.where(x_lane == 1 - shift, fx, 0.0))
-            parts.append(wx * wy)
-        w_high, w_low = split(jnp.concatenate(parts, axis=1))
-        field = [v_ref[c, j * nx : (j + 1) * nx].reshape(nx * CY, CZ) for c in range(3)]
-        f_high, f_low = split(jnp.concatenate(field, axis=1))
-        part = dot3(w_high, w_low, f_high, f_low)
-        acc = part if acc is None else acc + part
-    wz = weight(lane, z_col, fz)
-    out = turned
-    for c in range(3):
-        value = jnp.sum(acc[:, c * CZ : (c + 1) * CZ] * wz, axis=1, keepdims=True)
-        out = jnp.where(lane == 6 + c, value, out)
-    tab_ref[...] = out
+    sample_part(0, v_ref, rows.T, tab_ref)
+
+
+def sample_high_body(v_ref, low_ref, tab_ref):
+    sample_part(CX // 2, v_ref, low_ref[...], tab_ref)
 
 
 def split_blocks(sources):
@@ -224,7 +239,7 @@
     even_x, even_y, inner, _, b0, ny = place()
     for c in range(3):
         at = c * CX
-        y_high = jnp.where(even_y, rec_c[at : at + 1], rec_d[at : at + 1])
+        y_high = jnp.where(even_y, rec_c[at : at + 1], jnp.where(odd_side(), rec_d[at : at + 1], 0.0))
         tail = jnp.concatenate([y_high, jnp.zeros((XROWS - CY - 1, CZ), F32)], axis=0)
         low, high = x_ref[c], x_ref[c + 3]
         at = c * XROWS
@@ -273,7 +288,7 @@
         past = jnp.where(inner, face_b[at : at + XROWS], 0.0)
         plane = jnp.where(even_x, face_a[at : at + XROWS], past)
         at = c * CX
-        line = jnp.where(even_y, rec_c[at : at + CX], rec_d[at : at + CX])
+        line = jnp.where(even_y, rec_c[at : at + CX], jnp.where(odd_side(), rec_d[at : at + CX], 0.0))
         field.append(jnp.concatenate([plane, jnp.zeros((CX - XROWS, CZ), F32), line], axis=0))
     w_high, w_low = split(edge_w)
     f_high, f_low = split(jnp.concatenate(field, axis=1))
@@ -396,7 +411,7 @@
 
 def near_body(rec_c, rec_d, low_ref, high_ref):
     _, even_y, _, _, _, _ = place()
-    c_all, d_all = rec_c[...], rec_d[...]
+    c_all, d_all = rec_c[...], jnp.where(odd_side(), rec_d[...], 0.0)
     for side, out_ref in ((0, low_ref), (1, high_ref)):
         got = jnp.where(even_y, d_all, c_all) if side == 0 else jnp.where(even_y, c_all, d_all)
 
@@ -476,7 +491,6 @@
                     value = back[k * BACK : (k + 1) * BACK]
                     found = jnp.where(value[6:7, 0:1] == wanted, value, found)
                 ref[at + core * BACK : at + (core + 1) * BACK] = found
-        others[1][...] = pay_b[RIM_X:]
 
 
 def face_terms(buf, at, first, main_low, main_high, y_ref, rec_c, rec_d, rim_low, rim_high, even_y):
@@ -489,7 +503,7 @@
     for c in range(3):
         buf[c, here] = half_of[c, inner : inner + CHUNK]
         rows = slice(c * CX + first, c * CX + first + CHUNK)
-        a, b = rec_c[rows], rec_d[rows]
+        a, b = rec_c[rows], jnp.where(odd_side(), rec_d[rows], 0.0)
         low = [jnp.where(even_y, b, a) * (visc + half * y_ref[0, part]), 0.0]
         high = [0.0, jnp.where(even_y, a, b) * (visc - half * y_ref[1, part])]
         for i in range(2):
@@ -564,7 +578,7 @@
     blade_angle,
 ):
     nx, ny = lax.axis_size("gx"), lax.axis_size("gy")
-    ring = nx == 8
+    ring, short = nx == 8, ny == 4
 
     def flip(n, bits):
         return [(i, i ^ bits) for i in range(n)]
@@ -588,16 +602,22 @@
     def after(values, other):
         return lax.optimization_barrier((values, other))
 
-    def gather_y(first, filler):
+    def gather_y(first):
         pieces = [first]
         for bit in [b for b in (2, 4, 8) if b < ny]:
-            got = lax.ppermute(join(pieces), "gy", flip(ny, bit))
-            if filler is not None:
-                got, filler = after(got, filler())
-                yield filler
-                filler = None
-            pieces.append(got)
-        yield pieces
+            pieces.append(lax.ppermute(join(pieces), "gy", flip(ny, bit)))
+        return pieces
+
+    def exchange_y(to_c, to_d, block):
+        from_c = lax.ppermute(to_c, "gy", flip(ny, 1))
+        from_d = lax.ppermute(to_d, "gy", flip(ny, 3) if short else odd_pairs(ny))
+        return from_c, from_d, [lax.ppermute(block, "gy", flip(ny, 2))] if short else []
+
+    def blocks_y(block, from_c, from_d, far, size, at):
+        got = join([block, from_c[at : at + size]])
+        if short:
+            return [join([got, from_d[at : at + size]] + far)]
+        return gather_y(got)
 
     def gather_x(blocks):
         pieces = []
@@ -608,26 +628,27 @@
     dma = pltpu.SemaphoreType.DMA
     pay_c, pay_d, block = call(
         pack_body,
-        [(FACE_Y + ROWS, CZ), (FACE_Y, CZ), (ROWS, CZ)],
+        [(FACE_Y + ROWS, CZ)] * 2 + [(ROWS, CZ)],
         7,
         "pack",
         scratch=[pltpu.VMEM((4, 2, CZ), F32), pltpu.VMEM((2, CZ), jnp.int32), pltpu.SMEM((1,), F32), dma((12,))],
         in_specs=[HB] * 7,
         vmem=56,
     )(velocity, rotor_speed, *[a.reshape(2, CZ) for a in (blade_radius, blade_chord, blade_twist, blade_angle, owner_src)])
-    rec_c = lax.ppermute(pay_c, "gy", flip(ny, 1))
-    rec_d = lax.ppermute(pay_d, "gy", odd_pairs(ny))
+    rec_c, rec_d, far = exchange_y(pay_c, pay_d, block)
 
     def stencil(start):
         return call(lambda *refs: stencil_body(start, *refs), [(3, CX // 2, CY, CZ)], 1, "stencil")(velocity)[0]
 
-    rec_c, base_low = after(rec_c, stencil(0))
-    two = join([block, rec_c[FACE_Y:]])
-    beside = swap(two)
-    cells, beside = after(host_cell, beside)
-    sampled = lambda: call(sample_body, [(HOST, CZ), (6, CY, CZ), (2, CX, CZ)], 3, "sample", vmem=24)(velocity, cells, host_frac)
-    (table, x_faces, y_faces), pieces = list(gather_y(two, sampled))
-    pieces = pieces + [beside] + [swap(p) for p in pieces[1:]]
+    base_low = stencil(0)
+    table, x_faces, y_faces = call(
+        sample_low_body, [(HOST, CZ), (6, CY, CZ), (2, CX, CZ)], 3, "sample_low", vmem=24
+    )(velocity, host_cell, host_frac)
+    (rec_c, rec_d, far), (base_low, table) = after((rec_c, rec_d, far), (base_low, table))
+    pieces = blocks_y(block, rec_c, rec_d, far, ROWS, FACE_Y)
+    beside = [swap(p) for p in pieces]
+    beside, base_high = after(beside, stencil(CX // 2))
+    pieces = pieces + beside
     n_rows = 2 * ny * ROWS
     pair = (2 * ROWS, CZ)
     pay_a, pay_b, blocks, *across = call(
@@ -639,7 +660,8 @@
     face_b = lax.ppermute(pay_b, "gx", odd_pairs(nx, ring))
     from_x = across_x(across) if ring else gather_x(blocks)
     face_a = swap(pay_a)
-    (face_a, face_b), base_high = after((face_a, face_b), stencil(CX // 2))
+    table = call(sample_high_body, [(HOST, CZ)], 2, "sample_high", vmem=24)(velocity, table)[0]
+    (face_a, face_b, from_x), table = after((face_a, face_b, from_x), table)
     samp, sel, pts = call(
         lambda *refs: select_body(len(from_x), *refs),
         [(8, PTS), (2 * ROWS, CZ), (PTS, CZ)],
@@ -654,30 +676,32 @@
         8,
         "loads",
     )(samp, other, sel, pts, gx, gy, pz, pos)
-    near_d = lax.ppermute(points, "gy", odd_pairs(ny))
-    near_c = lax.ppermute(points, "gy", flip(ny, 1))
+    ret = points[: 2 * BACK]
+    near_c, near_d, far = exchange_y(points, points, ret)
 
     def spread(start, base):
         return call(
             lambda *refs: spread_body(start, *refs), [(3, CX // 2, CY, CZ)], 4, "spread"
         )(lines, gx, gy, base)[0]
 
-    (near_c, near_d), main_low = after((near_c, near_d), spread(0, base_low))
-    nearby = lambda: call(near_body, [(RIM_Y, CZ)] * 2, 2, "near")(near_c, near_d)
-    (rim_low, rim_high), pieces = list(gather_y(join([points[: 2 * BACK], near_c[: 2 * BACK]]), nearby))
+    (near_c, near_d, far), main_low = after((near_c, near_d, far), spread(0, base_low))
+    rim_low, rim_high = call(near_body, [(RIM_Y, CZ)] * 2, 2, "near")(near_c, near_d)
+    pieces = blocks_y(ret, near_c, near_d, far, 2 * BACK, 0)
     n_rows = 2 * ny * BACK
     pair = (2 * BACK, CZ)
     pay_a, pay_b, back, *across = call(
         lambda *refs: rimpack_body(len(pieces), *refs),
-        [(RIM_X, CZ), (RIM_X + 2 * BACK, CZ), (n_rows, CZ), pair, pair] if ring else [(RIM_X, CZ), (RIM_X, CZ), (n_rows, CZ)],
+        [(RIM_X, CZ), (RIM_X + 2 * BACK, CZ), (n_rows, CZ), pair] if ring else [(RIM_X, CZ), (RIM_X, CZ), (n_rows, CZ)],
         3 + len(pieces),
         "rimpack",
     )(xrim, rim_low, rim_high, *pieces)
     rim_b = lax.ppermute(pay_b, "gx", odd_pairs(nx, ring))
-    rets = across_x(across) if ring else gather_x(back)
+    rets = [lax.ppermute(across[0], "gx", flip(nx, 4))] if ring else gather_x(back)
     rim_a = swap(pay_a)
     main_high = spread(CX // 2, base_high)
-    (main_low, main_high) = lax.optimization_barrier((main_low, main_high))
+    (rim_a, rim_b), (main_low, main_high) = after((rim_a, rim_b), (main_low, main_high))
+    if ring:
+        rets.append(swap(rim_b[RIM_X:]))
     inside = call(
         inside_body,
         [velocity.shape],
@@ -687,7 +711,7 @@
         out_specs=[HB],
         vmem=16,
     )(main_low, main_high, y_faces, rec_c, rec_d, rim_low, rim_high)[0]
-    (rim_a, rim_b), inside = after((rim_a, rim_b), inside)
+    rets, inside = after(rets, inside)
     return tuple(
         call(
             lambda *refs: final_body(len(rets), *refs),

time: 51.3 us -> 47.5 us (0.926)
  starting transfers between devices: 23.8 us -> 17.7 us
  waiting for transfers between devices: 2.23 us -> 3.53 us
  Pallas kernels: 23.3 us -> 24.4 us
    ppermute x4 -> x2, starting transfers between devices: 5.01 us -> 2.01 us  [across_x(): lax.ppermute(b, 'gx', p)]
    ppermute x6 -> x7, starting transfers between devices: 14.6 us -> 11.7 us  [the longest x2 5.18 us: exchange_y(): from_d = lax.ppermute(to_d, 'gy', flip(ny, 3) if short else odd_pairs(ny))]
    ppermute x6 -> x7, waiting for transfers between devices: 0.43 us -> 1.78 us  [the longest x2 1.77 us: exchange_y(): lax.ppermute(block, 'gy', flip(ny, 2))]
    ppermute x1, waiting for transfers between devices: 0.01 us -> 1.28 us  [per_device(): rim_b = lax.ppermute(pay_b, 'gx', odd_pairs(nx, ring))]
    ppermute x5, waiting for transfers between devices: 1.47 us -> 0.47 us  [swap(): return lax.ppermute(block, 'gx', flip(nx, 1))]
    pallas_call x2 -> x3, Pallas kernels: 6.21 us -> 7.18 us  [the longest x1 2.76 us: per_device(): call(sample_low_body, [(HOST, CZ), (6, CY, CZ), (2, CX, CZ)], 3, 'sample_...]
  transfers between devices with their start and end apart: 17 -> 16, of which waited for: 4 -> 4; matrix products, arithmetic and copies ran while one was open for 0% -> 0% of each run, Pallas kernels for 31% -> 32%
where the time goes in v7:
time: 47.5 us; the launch traced here: 47.3 us
  Pallas kernels  24.4 us (51%)
  starting transfers between devices  17.7 us (37%)
  waiting for transfers between devices  3.53 us (7%)
  between operations  1.68 us (4%)
    ppermute x2, starting transfers between devices, exchange_y(): from_d = lax.ppermute(to_d, 'gy', flip(ny, 3) if short else odd_pairs(ny))  5.18 us
    pallas_call x2, Pallas kernels, stencil(): call(lambda *refs: stencil_body(start, *refs), [(3, CX // 2, CY, CZ)], 1,...  3.9 us
    pallas_call x2, Pallas kernels, spread(): call(lambda *refs: spread_body(start, *refs), [(3, CX // 2, CY, CZ)], 4,...  3.62 us
    ppermute x2, starting transfers between devices, exchange_y(): from_c = lax.ppermute(to_c, 'gy', flip(ny, 1))  3.1 us
    pallas_call x1, Pallas kernels, per_device(): call(sample_low_body, [(HOST, CZ), (6, CY, CZ), (2, CX, CZ)], 3, 'sample_...  2.76 us
    ppermute x1, starting transfers between devices, per_device(): face_b = lax.ppermute(pay_b, 'gx', odd_pairs(nx, ring))  2.61 us
    pallas_call x1, Pallas kernels, per_device(): call(sample_high_body, [(HOST, CZ)], 2, 'sample_high', vmem=24)  2.59 us
    pallas_call x1, Pallas kernels, per_device(): call(lambda *refs: select_body(len(from_x), *refs), [(8, PTS), (2 * ROWS,...  2.31 us
  transfers between devices with their start and end apart: 16, of which 4 were waited for; matrix products, arithmetic and copies ran while one was open for 0% of the time, Pallas kernels for 32%

profile of v7, /device:TPU:0, one launch (start us, length us, event | category | flops | bytes accessed | tf_op | source)
XLA Modules:
  0.0 47.3 jit_solution(7596643810795508082)
XLA Ops:
  1.3 1.8 %pack.1 = (f32[208,128]{1,0:T(8,128)}, f32[208,128]{1,0:T(8,128)}, f32[16,128]{1,0:T(8,128)}) custom-call(f32[3,64,32,128]{3,2,1,0:T(8,128)} %v_ref.5, f32[1]{0:T(128)S(6)} %copy.13.spin_hbm, f32[2,128]{1,0:T(2,128)} %bitcast.5, f32[2,128]{1,0:T(2,128)} %bitcast.6, f32[2,128]{1,0:T(2,128)} %bitcast.7, f32[2,128]{1,0:T(2,128)} %bitcast.8, s32[2,128]{1,0:T(2,128)} %bitcast.9), custom_call_target="tpu_custom_call" | custom-call | tf_op jit(solution)/shard_map/pack/pallas_call | solution.py:629
  3.1 3.1 %collective-permute-start = (f32[208,128]{1,0:T(8,128)}, f32[208,128]{1,0:T(8,128)S(1)}, u32[]{:S(2)}, u32[]{:S(2)}) collective-permute-start(f32[208,128]{1,0:T(8,128)} %get-tuple-element.53), channel_id=1, source_target_pairs={{0,1},{1,0},{2,3},{3,2},{4,5},{5,4},{6,7},{7,6},{8,9},{9,8},{10,11... | collective-permute-start | bytes 319496 | tf_op jit(solution)/shard_map/ppermute | solution.py:612
  6.2 2.5 %collective-permute-start.1 = (f32[208,128]{1,0:T(8,128)}, f32[208,128]{1,0:T(8,128)S(1)}, u32[]{:S(2)}, u32[]{:S(2)}) collective-permute-start(f32[208,128]{1,0:T(8,128)} %get-tuple-element.54), channel_id=1, source_target_pairs={{0,3},{1,2},{2,1},{3,0},{4,7},{5,6},{6,5},{7,4},{8,11},{9,10},{10,... | collective-permute-start | bytes 319496 | tf_op jit(solution)/shard_map/ppermute | solution.py:613
  8.7 0.1 collective-permute-start.2
  8.8 1.9 %stencil.2.refs_3_ = f32[3,32,32,128]{3,2,1,0:T(8,128)S(1)} custom-call(f32[3,64,32,128]{3,2,1,0:T(8,128)S(1)} %copy-done), custom_call_target="tpu_custom_call" | custom-call | tf_op jit(solution)/shard_map/stencil/pallas_call | solution.py:641
  10.8 2.8 %sample_low.1 = (f32[512,128]{1,0:T(8,128)S(1)}, f32[6,32,128]{2,1,0:T(8,128)S(1)}, f32[2,64,128]{2,1,0:T(8,128)S(1)}) custom-call(f32[3,64,32,128]{3,2,1,0:T(8,128)S(1)} %copy-done, s32[3,512]{1,0:T(4,128)S(1)} %copy-done.1, f32[3,512]{1,0:T(4,128)S(1)} %copy-done.2), custom_call_target="tpu_custom_call" | custom-call | tf_op jit(solution)/shard_map/sample_low/pallas_call | solution.py:644
  13.6 0.8 %collective-permute-done.2 = f32[16,128]{1,0:T(8,128)S(1)} collective-permute-done((f32[16,128]{1,0:T(8,128)}, f32[16,128]{1,0:T(8,128)S(1)}, u32[]{:S(2)}, u32[]{:S(2)}) %collective-permute-start.2) | collective-permute-done | bytes 8224 | tf_op jit(solution)/shard_map/ppermute | solution.py:614
  14.4 0.1 collective-permute-start.3
  14.5 1.9 %stencil.3.refs_3_ = f32[3,32,32,128]{3,2,1,0:T(8,128)S(1)} custom-call(f32[3,64,32,128]{3,2,1,0:T(8,128)S(1)} %copy-done), custom_call_target="tpu_custom_call" | custom-call | tf_op jit(solution)/shard_map/stencil/pallas_call | solution.py:641
  16.4 0.1 xpack.1
  16.5 2.6 %collective-permute-start.5 = (f32[152,128]{1,0:T(8,128)S(1)}, f32[152,128]{1,0:T(8,128)S(1)}, u32[]{:S(2)}, u32[]{:S(2)}) collective-permute-start(f32[152,128]{1,0:T(8,128)S(1)} %get-tuple-element.62), channel_id=1, source_target_pairs={{4,8},{12,16},{20,24},{28,0},{8,4},{16,12},{24,20},{0,28},{5,9},{1... | collective-permute-start | bytes 233480 | tf_op jit(solution)/shard_map/ppermute | solution.py:660
  19.2 0.6 %collective-permute-start.6 = (f32[32,128]{1,0:T(8,128)S(1)}, f32[32,128]{1,0:T(8,128)S(1)}, u32[]{:S(2)}, u32[]{:S(2)}) collective-permute-start(f32[32,128]{1,0:T(8,128)S(1)} %get-tuple-element.63), channel_id=1, source_target_pairs={{0,16},{4,20},{8,24},{12,28},{16,0},{20,4},{24,8},{28,12},{1,17},{... | collective-permute-start | bytes 49160 | tf_op jit(solution)/shard_map/ppermute | solution.py:594
  19.7 1.4 %collective-permute-start.7 = (f32[32,128]{1,0:T(8,128)S(1)}, f32[32,128]{1,0:T(8,128)S(1)}, u32[]{:S(2)}, u32[]{:S(2)}) collective-permute-start(f32[32,128]{1,0:T(8,128)S(1)} %get-tuple-element.64), channel_id=1, source_target_pairs={{0,24},{4,12},{8,0},{12,20},{16,8},{20,28},{24,16},{28,4},{1,25},{... | collective-permute-start | bytes 49160 | tf_op jit(solution)/shard_map/ppermute | solution.py:594
  21.2 2.6 %sample_high.1.refs_0_ = f32[512,128]{1,0:T(8,128)S(1)} custom-call(f32[3,64,32,128]{3,2,1,0:T(8,128)S(1)} %copy-done, f32[512,128]{1,0:T(8,128)S(1)} %get-tuple-element.65.low_ref), custom_call_target="tpu_custom_call" | custom-call | tf_op jit(solution)/shard_map/sample_high/pallas_call | solution.py:663
  23.8 2.3 %select.1 = (f32[8,512]{1,0:T(8,128)S(1)}, f32[32,128]{1,0:T(8,128)S(1)}, f32[512,128]{1,0:T(8,128)S(1)}) custom-call(f32[512,128]{1,0:T(8,128)S(1)} %sample_high.1.refs_0_, f32[120,128]{1,0:T(8,128)S(1)} %collective-permute-done.4.refs_1_.refs_5_, f32[152,128]{1,0:T(8,128)S(1)} %collective-permute-done.5.refs_2_.refs_6_, ...), custom_call_target="tpu_custom_call" | custom-call | tf_op jit(solution)/shard_map/select/pallas_call | solution.py:665
  26.1 0.0 collective-permute-start.8
  26.2 0.7 %weights.1 = (f32[72,512]{1,0:T(8,128)S(1)}, f32[32,512]{1,0:T(8,128)S(1)}, f32[512,128]{1,0:T(8,128)S(1)}, f32[24,128]{1,0:T(8,128)S(1)}) custom-call(f32[512,128]{1,0:T(8,128)S(1)} %get-tuple-element.74.pts_ref), custom_call_target="tpu_custom_call" | custom-call | tf_op jit(solution)/shard_map/weights/pallas_call | solution.py:672
  26.9 0.5 collective-permute-done.8.other_ref
  27.4 1.4 %loads.1 = (f32[512,384]{1,0:T(8,128)S(1)}, f32[40,128]{1,0:T(8,128)S(1)}, f32[384,128]{1,0:T(8,128)S(1)}) custom-call(f32[8,512]{1,0:T(8,128)S(1)} %get-tuple-element.72.samp_ref, f32[8,512]{1,0:T(8,128)S(1)} %collective-permute-done.8.other_ref, f32[32,128]{1,0:T(8,128)S(1)} %get-tuple-element.73.sel_ref, f32[512,128]{1,0:T(8,128)S(1)} %get-tuple-element.74.pts_ref, ...), custom_call_target="tpu_custom_call" | custom-call | tf_op jit(solution)/shard_map/loads/pallas_call | solution.py:673
  28.7 2.7 %collective-permute-start.10 = (f32[40,128]{1,0:T(8,128)S(1)}, f32[40,128]{1,0:T(8,128)S(1)}, u32[]{:S(2)}, u32[]{:S(2)}) collective-permute-start(f32[40,128]{1,0:T(8,128)S(1)} %get-tuple-element.80), channel_id=1, source_target_pairs={{0,3},{1,2},{2,1},{3,0},{4,7},{5,6},{6,5},{7,4},{8,11},{9,10},{10,... | collective-permute-start | bytes 61448 | tf_op jit(solution)/shard_map/ppermute | solution.py:613
  31.5 1.7 %collective-permute-start.11 = (f32[16,128]{1,0:T(8,128)S(1)}, f32[16,128]{1,0:T(8,128)S(1)}, u32[]{:S(2)}, u32[]{:S(2)}) collective-permute-start(f32[16,128]{1,0:T(8,128)S(1)} %slice.20), channel_id=1, source_target_pairs={{0,2},{1,3},{2,0},{3,1},{4,6},{5,7},{6,4},{7,5},{8,10},{9,11},{10,... | collective-permute-start | bytes 24584 | tf_op jit(solution)/shard_map/ppermute | solution.py:614
  33.2 1.8 %spread.2.main_low.refs_1_ = f32[3,32,32,128]{3,2,1,0:T(8,128)S(1)} custom-call(f32[512,384]{1,0:T(8,128)S(1)} %get-tuple-element.81.refs_0_, f32[72,512]{1,0:T(8,128)S(1)} %get-tuple-element.75.gx_ref.refs_1_, f32[32,512]{1,0:T(8,128)S(1)} %get-tuple-element.76.gy_ref.refs_2_, f32[3,32,32,128]{3,2,1,0:T(8,128)S(1)} %stencil.2.refs_3_), custom_call_target="tpu_custom_call" | custom-call | tf_op jit(solution)/shard_map/spread/pallas_call | solution.py:683
  35.0 1.0 %collective-permute-done.11 = f32[16,128]{1,0:T(8,128)S(1)} collective-permute-done((f32[16,128]{1,0:T(8,128)S(1)}, f32[16,128]{1,0:T(8,128)S(1)}, u32[]{:S(2)}, u32[]{:S(2)}) %collective-permute-start.11) | collective-permute-done | bytes 8224 | tf_op jit(solution)/shard_map/ppermute | solution.py:614
  36.0 1.9 %near.1 = (f32[432,128]{1,0:T(8,128)S(1)}, f32[432,128]{1,0:T(8,128)S(1)}) custom-call(f32[40,128]{1,0:T(8,128)S(1)} %collective-permute-done.9.rec_c, f32[40,128]{1,0:T(8,128)S(1)} %collective-permute-done.10.rec_d), custom_call_target="tpu_custom_call" | custom-call | tf_op jit(solution)/shard_map/near/pallas_call | solution.py:688
  37.9 0.1 rimpack.1
  38.0 0.4 collective-permute-start.14
  38.4 0.9 %collective-permute-start.13 = (f32[192,128]{1,0:T(8,128)S(1)}, f32[192,128]{1,0:T(8,128)S(1)}, u32[]{:S(2)}, u32[]{:S(2)}) collective-permute-start(f32[192,128]{1,0:T(8,128)S(1)} %get-tuple-element.89), channel_id=1, source_target_pairs={{0,4},{4,0},{8,12},{12,8},{16,20},{20,16},{24,28},{28,24},{1,5},{5... | collective-permute-start | bytes 294920 | tf_op jit(solution)/shard_map/ppermute | solution.py:597
  39.3 1.8 %spread.3.main_high.refs_2_ = f32[3,32,32,128]{3,2,1,0:T(8,128)S(1)} custom-call(f32[512,384]{1,0:T(8,128)S(1)} %get-tuple-element.81.refs_0_, f32[72,512]{1,0:T(8,128)S(1)} %get-tuple-element.75.gx_ref.refs_1_, f32[32,512]{1,0:T(8,128)S(1)} %get-tuple-element.76.gy_ref.refs_2_, f32[3,32,32,128]{3,2,1,0:T(8,128)S(1)} %stencil.3.refs_3_), custom_call_target="tpu_custom_call" | custom-call | tf_op jit(solution)/shard_map/spread/pallas_call | solution.py:683
  41.1 1.5 %collective-permute-start.12 = (f32[16,128]{1,0:T(8,128)S(1)}, f32[16,128]{1,0:T(8,128)S(1)}, u32[]{:S(2)}, u32[]{:S(2)}) collective-permute-start(f32[16,128]{1,0:T(8,128)S(1)} %get-tuple-element.88), channel_id=1, source_target_pairs={{0,16},{4,20},{8,24},{12,28},{16,0},{20,4},{24,8},{28,12},{1,17},{... | collective-permute-start | bytes 24584 | tf_op jit(solution)/shard_map/ppermute | solution.py:699
  42.7 1.3 %collective-permute-done.14.refs_10_ = f32[208,128]{1,0:T(8,128)S(1)} collective-permute-done((f32[208,128]{1,0:T(8,128)S(1)}, f32[208,128]{1,0:T(8,128)S(1)}, u32[]{:S(2)}, u32[]{:S(2)}) %collective-permute-start.14) | collective-permute-done | bytes 106528 | tf_op jit(solution)/shard_map/ppermute | solution.py:698
  43.9 1.5 %inside.1.refs_0_ = f32[3,64,32,128]{3,2,1,0:T(8,128)} custom-call(f32[3,32,32,128]{3,2,1,0:T(8,128)S(1)} %spread.2.main_low.refs_1_, f32[3,32,32,128]{3,2,1,0:T(8,128)S(1)} %spread.3.main_high.refs_2_, f32[2,64,128]{2,1,0:T(8,128)S(1)} %get-tuple-element.96.y_ref.refs_4_, f32[208,128]{1,0:T(8,128)S(1)} %collective-permute-done.refs_1_.refs_3_.rec_c.refs_7_, ...), custom_call_target="tpu_custom_call" | custom-call | tf_op jit(solution)/shard_map/inside/pallas_call | solution.py:705
  45.5 1.6 %final.1 = (f32[3,64,32,128]{3,2,1,0:T(8,128)}, f32[3,256]{1,0:T(4,128)}) custom-call(f32[3,64,32,128]{3,2,1,0:T(8,128)} %inside.1.refs_0_, f32[3,32,32,128]{3,2,1,0:T(8,128)S(1)} %spread.2.main_low.refs_1_, f32[3,32,32,128]{3,2,1,0:T(8,128)S(1)} %spread.3.main_high.refs_2_, ...), custom_call_target="tpu_custom_call", output_to_operand_aliasing={{0}: (0, {})} | custom-call | tf_op jit(solution)/shard_map/final/pallas_call | solution.py:716
  (31 shorter events, 0.1 us)
Async XLA Ops:
  1.3 7.5 %copy-start = (f32[3,64,32,128]{3,2,1,0:T(8,128)S(1)}, f32[3,64,32,128]{3,2,1,0:T(8,128)}, u32[]{:S(2)}) copy-start(f32[3,64,32,128]{3,2,1,0:T(8,128)} %v_ref.5) | copy-start | bytes 9437188
  3.1 11.2 %collective-permute-start = (f32[208,128]{1,0:T(8,128)}, f32[208,128]{1,0:T(8,128)S(1)}, u32[]{:S(2)}, u32[]{:S(2)}) collective-permute-start(f32[208,128]{1,0:T(8,128)} %get-tuple-element.53), channel_id=1, source_target_pairs={{0,1},{1,0},{2,3},{3,2},{4,5},{5,4},{6,7},{7,6},{8,9},{9,8},{10,11... | collective-permute-start | bytes 319496 | tf_op jit(solution)/shard_map/ppermute | solution.py:612
  6.2 8.1 %collective-permute-start.1 = (f32[208,128]{1,0:T(8,128)}, f32[208,128]{1,0:T(8,128)S(1)}, u32[]{:S(2)}, u32[]{:S(2)}) collective-permute-start(f32[208,128]{1,0:T(8,128)} %get-tuple-element.54), channel_id=1, source_target_pairs={{0,3},{1,2},{2,1},{3,0},{4,7},{5,6},{6,5},{7,4},{8,11},{9,10},{10,... | collective-permute-start | bytes 319496 | tf_op jit(solution)/shard_map/ppermute | solution.py:613
  8.7 2.1 %copy-start.1 = (s32[3,512]{1,0:T(4,128)S(1)}, s32[3,512]{1,0:T(4,128)}, u32[]{:S(2)}) copy-start(s32[3,512]{1,0:T(4,128)} %cell_ref.1) | copy-start | bytes 18436
  8.7 2.1 %copy-start.2 = (f32[3,512]{1,0:T(4,128)S(1)}, f32[3,512]{1,0:T(4,128)}, u32[]{:S(2)}) copy-start(f32[3,512]{1,0:T(4,128)} %frac_ref.1) | copy-start | bytes 18436
  8.7 5.6 %collective-permute-start.2 = (f32[16,128]{1,0:T(8,128)}, f32[16,128]{1,0:T(8,128)S(1)}, u32[]{:S(2)}, u32[]{:S(2)}) collective-permute-start(f32[16,128]{1,0:T(8,128)} %get-tuple-element.55), channel_id=1, source_target_pairs={{0,2},{1,3},{2,0},{3,1},{4,6},{5,7},{6,4},{7,5},{8,10},{9,11},{10,... | collective-permute-start | bytes 24584 | tf_op jit(solution)/shard_map/ppermute | solution.py:614
  10.8 3.6 %copy-start.3 = (f32[16,128]{1,0:T(8,128)S(1)}, f32[16,128]{1,0:T(8,128)}, u32[]{:S(2)}) copy-start(f32[16,128]{1,0:T(8,128)} %get-tuple-element.55) | copy-start | bytes 24580
  14.4 2.0 %collective-permute-start.3 = (f32[64,128]{1,0:T(8,128)S(1)}, f32[64,128]{1,0:T(8,128)S(1)}, u32[]{:S(2)}, u32[]{:S(2)}) collective-permute-start(f32[64,128]{1,0:T(8,128)S(1)} %pad_maximum_fusion.refs_3_), channel_id=1, source_target_pairs={{0,4},{4,0},{8,12},{12,8},{16,20},{20,16},{24,28},{28,24},{1,5},{5... | collective-permute-start | bytes 98312 | tf_op jit(solution)/shard_map/ppermute | solution.py:597
  16.5 7.3 %collective-permute-start.5 = (f32[152,128]{1,0:T(8,128)S(1)}, f32[152,128]{1,0:T(8,128)S(1)}, u32[]{:S(2)}, u32[]{:S(2)}) collective-permute-start(f32[152,128]{1,0:T(8,128)S(1)} %get-tuple-element.62), channel_id=1, source_target_pairs={{4,8},{12,16},{20,24},{28,0},{8,4},{16,12},{24,20},{0,28},{5,9},{1... | collective-permute-start | bytes 233480 | tf_op jit(solution)/shard_map/ppermute | solution.py:660
  19.2 4.6 %collective-permute-start.4 = (f32[120,128]{1,0:T(8,128)S(1)}, f32[120,128]{1,0:T(8,128)S(1)}, u32[]{:S(2)}, u32[]{:S(2)}) collective-permute-start(f32[120,128]{1,0:T(8,128)S(1)} %get-tuple-element.61), channel_id=1, source_target_pairs={{0,4},{4,0},{8,12},{12,8},{16,20},{20,16},{24,28},{28,24},{1,5},{5... | collective-permute-start | bytes 184328 | tf_op jit(solution)/shard_map/ppermute | solution.py:597
  19.2 4.6 %collective-permute-start.6 = (f32[32,128]{1,0:T(8,128)S(1)}, f32[32,128]{1,0:T(8,128)S(1)}, u32[]{:S(2)}, u32[]{:S(2)}) collective-permute-start(f32[32,128]{1,0:T(8,128)S(1)} %get-tuple-element.63), channel_id=1, source_target_pairs={{0,16},{4,20},{8,24},{12,28},{16,0},{20,4},{24,8},{28,12},{1,17},{... | collective-permute-start | bytes 49160 | tf_op jit(solution)/shard_map/ppermute | solution.py:594
  19.7 4.0 %collective-permute-start.7 = (f32[32,128]{1,0:T(8,128)S(1)}, f32[32,128]{1,0:T(8,128)S(1)}, u32[]{:S(2)}, u32[]{:S(2)}) collective-permute-start(f32[32,128]{1,0:T(8,128)S(1)} %get-tuple-element.64), channel_id=1, source_target_pairs={{0,24},{4,12},{8,0},{12,20},{16,8},{20,28},{24,16},{28,4},{1,25},{... | collective-permute-start | bytes 49160 | tf_op jit(solution)/shard_map/ppermute | solution.py:594
  26.1 1.2 %collective-permute-start.8 = (f32[8,512]{1,0:T(8,128)S(1)}, f32[8,512]{1,0:T(8,128)S(1)}, u32[]{:S(2)}, u32[]{:S(2)}) collective-permute-start(f32[8,512]{1,0:T(8,128)S(1)} %get-tuple-element.72.samp_ref), channel_id=1, source_target_pairs={{0,4},{4,0},{8,12},{12,8},{16,20},{20,16},{24,28},{28,24},{1,5},{5... | collective-permute-start | bytes 49160 | tf_op jit(solution)/shard_map/ppermute | solution.py:597
  28.7 7.3 %collective-permute-start.10 = (f32[40,128]{1,0:T(8,128)S(1)}, f32[40,128]{1,0:T(8,128)S(1)}, u32[]{:S(2)}, u32[]{:S(2)}) collective-permute-start(f32[40,128]{1,0:T(8,128)S(1)} %get-tuple-element.80), channel_id=1, source_target_pairs={{0,3},{1,2},{2,1},{3,0},{4,7},{5,6},{6,5},{7,4},{8,11},{9,10},{10,... | collective-permute-start | bytes 61448 | tf_op jit(solution)/shard_map/ppermute | solution.py:613
  31.5 4.6 %collective-permute-start.9 = (f32[40,128]{1,0:T(8,128)S(1)}, f32[40,128]{1,0:T(8,128)S(1)}, u32[]{:S(2)}, u32[]{:S(2)}) collective-permute-start(f32[40,128]{1,0:T(8,128)S(1)} %get-tuple-element.80), channel_id=1, source_target_pairs={{0,1},{1,0},{2,3},{3,2},{4,5},{5,4},{6,7},{7,6},{8,9},{9,8},{10,11... | collective-permute-start | bytes 61448 | tf_op jit(solution)/shard_map/ppermute | solution.py:612
  31.5 4.5 %collective-permute-start.11 = (f32[16,128]{1,0:T(8,128)S(1)}, f32[16,128]{1,0:T(8,128)S(1)}, u32[]{:S(2)}, u32[]{:S(2)}) collective-permute-start(f32[16,128]{1,0:T(8,128)S(1)} %slice.20), channel_id=1, source_target_pairs={{0,2},{1,3},{2,0},{3,1},{4,6},{5,7},{6,4},{7,5},{8,10},{9,11},{10,... | collective-permute-start | bytes 24584 | tf_op jit(solution)/shard_map/ppermute | solution.py:614
  38.0 5.9 %collective-permute-start.14 = (f32[208,128]{1,0:T(8,128)S(1)}, f32[208,128]{1,0:T(8,128)S(1)}, u32[]{:S(2)}, u32[]{:S(2)}) collective-permute-start(f32[208,128]{1,0:T(8,128)S(1)} %get-tuple-element.90), channel_id=1, source_target_pairs={{4,8},{12,16},{20,24},{28,0},{8,4},{16,12},{24,20},{0,28},{5,9},{1... | collective-permute-start | bytes 319496 | tf_op jit(solution)/shard_map/ppermute | solution.py:698
  38.4 4.2 %collective-permute-start.13 = (f32[192,128]{1,0:T(8,128)S(1)}, f32[192,128]{1,0:T(8,128)S(1)}, u32[]{:S(2)}, u32[]{:S(2)}) collective-permute-start(f32[192,128]{1,0:T(8,128)S(1)} %get-tuple-element.89), channel_id=1, source_target_pairs={{0,4},{4,0},{8,12},{12,8},{16,20},{20,16},{24,28},{28,24},{1,5},{5... | collective-permute-start | bytes 294920 | tf_op jit(solution)/shard_map/ppermute | solution.py:597
  41.1 4.4 %collective-permute-start.12 = (f32[16,128]{1,0:T(8,128)S(1)}, f32[16,128]{1,0:T(8,128)S(1)}, u32[]{:S(2)}, u32[]{:S(2)}) collective-permute-start(f32[16,128]{1,0:T(8,128)S(1)} %get-tuple-element.88), channel_id=1, source_target_pairs={{0,16},{4,20},{8,24},{12,28},{16,0},{20,4},{24,8},{28,12},{1,17},{... | collective-permute-start | bytes 24584 | tf_op jit(solution)/shard_map/ppermute | solution.py:699
  43.9 1.6 %collective-permute-start.15 = (f32[16,128]{1,0:T(8,128)S(1)}, f32[16,128]{1,0:T(8,128)S(1)}, u32[]{:S(2)}, u32[]{:S(2)}) collective-permute-start(f32[16,128]{1,0:T(8,128)S(1)} %slice.23), channel_id=1, source_target_pairs={{0,4},{4,0},{8,12},{12,8},{16,20},{20,16},{24,28},{28,24},{1,5},{5... | collective-permute-start | bytes 24584 | tf_op jit(solution)/shard_map/ppermute | solution.py:597

commit v8 on v7

--- a/solution.py
+++ b/solution.py
@@ -86,15 +86,15 @@
 
 
 def pack_body(v_ref, spin_hbm, *rest):
-    params, (pay_c, pay_d, blk_ref, held, held_int, spin_ref, sems) = rest[:5], rest[5:]
+    params, (pay_c, pay_d, blk_ref, held, held_int, made, spin_ref, sems) = rest[:5], rest[5:]
     _, even_y, _, brick, _, _ = place()
 
     def faces(first, second):
-        made = []
+        copies = []
         for k, (ref, y) in enumerate(((pay_c, first), (pay_d, second))):
             for c in range(3):
-                made.append(pltpu.make_async_copy(v_ref.at[c, :, y], ref.at[pl.ds(c * CX, CX)], sems.at[3 * k + c]))
-        return made
+                copies.append(pltpu.make_async_copy(v_ref.at[c, :, y], ref.at[pl.ds(c * CX, CX)], sems.at[3 * k + c]))
+        return copies
 
     @pl.when(even_y)
     def _():
@@ -125,11 +125,12 @@
         jnp.full((1, CZ), spin_ref[0], F32),
         jnp.full((1, CZ), brick.astype(F32), F32),
     ]
-    block = jnp.concatenate(parts, axis=0)
-    blk_ref[...] = block
-    pay_c[FACE_Y:] = block
-    pay_d[FACE_Y:] = block
-    for copy in faces(0, 0):
+    made[...] = jnp.concatenate(parts, axis=0)
+    targets = (pay_c.at[pl.ds(FACE_Y, ROWS)], pay_d.at[pl.ds(FACE_Y, ROWS)], blk_ref)
+    outward = [pltpu.make_async_copy(made, ref, sems.at[12 + k]) for k, ref in enumerate(targets)]
+    for copy in outward:
+        copy.start()
+    for copy in faces(0, 0) + outward:
         copy.wait()
 
 
@@ -141,39 +142,55 @@
     not_last_y, not_first_y = row < CY - 1, row > 0
     not_last_z, not_first_z = lane < CZ - 1, lane > 0
 
-    def step(k, carry):
-        x = start + k
-        up = jnp.minimum(x + 1, CX - 1)
-        down = jnp.maximum(x - 1, 0)
-        v0, v1, v2 = v_ref[0, x], v_ref[1, x], v_ref[2, x]
-        a_x = jnp.where(x < CX - 1, visc - half * v0, 0.0)
-        b_x = jnp.where(x > 0, visc + half * v0, 0.0)
+    def plane(x, down, up):
+        at = x * CY if isinstance(x, int) else pl.multiple_of(x * CY, CY)
+        v0, v1, v2 = [v_ref[c, pl.ds(at, CY)] for c in range(3)]
+        a_x, b_x = visc - half * v0, visc + half * v0
         a_y = jnp.where(not_last_y, visc - half * v1, 0.0)
         b_y = jnp.where(not_first_y, visc + half * v1, 0.0)
         a_z = jnp.where(not_last_z, visc - half * v2, 0.0)
         b_z = jnp.where(not_first_z, visc + half * v2, 0.0)
         for c in range(3):
             mid = (v0, v1, v2)[c]
-            along_x = a_x * v_ref[c, up] + b_x * v_ref[c, down]
-            along_y = a_y * pltpu.roll(mid, CY - 1, 0) + b_y * pltpu.roll(mid, 1, 0)
-            along_z = a_z * pltpu.roll(mid, CZ - 1, 1) + b_z * pltpu.roll(mid, 1, 1)
-            out_ref[c, k] = (1.0 - 6.0 * visc) * mid + along_x + (along_y + along_z)
+            total = (1.0 - 6.0 * visc) * mid
+            total += a_z * pltpu.roll(mid, CZ - 1, 1) + b_z * pltpu.roll(mid, 1, 1)
+            if up is None:
+                y_up = pltpu.roll(mid, CY - 1, 0)
+            else:
+                y_up = v_ref[c, pl.ds(at + 1, CY)]
+                total += a_x * v_ref[c, pl.ds(at + CY, CY)]
+            if down is None:
+                y_down = pltpu.roll(mid, 1, 0)
+            else:
+                y_down = v_ref[c, pl.ds(at - 1, CY)]
+                total += b_x * v_ref[c, pl.ds(at - CY, CY)]
+            out_ref[c, x - start] = total + (a_y * y_up + b_y * y_down)
+
+    first, last = start, start + CX // 2
+    if start == 0:
+        plane(0, None, True)
+        first = 1
+    if last == CX:
+        last = CX - 1
+        plane(last, True, None)
+
+    def step(x, carry):
+        plane(x, True, True)
         return carry
 
-    lax.fori_loop(0, CX // 2, step, 0, unroll=2)
+    lax.fori_loop(first, last, step, 0, unroll=2)
 
 
 def weight(coord, base, frac):
     return jnp.where(coord == base, 1.0 - frac, jnp.where(coord == base + 1, frac, 0.0))
 
 
-def sample_part(start, v_ref, table, out_ref):
-    x_col, y_col, z_col = [table[:, k : k + 1].astype(jnp.int32) for k in range(3)]
-    fx, fy, fz = [table[:, k : k + 1] for k in range(3, 6)]
+def sample_part(start, v_ref, table, acc):
+    x_col, y_col = [table[:, k : k + 1].astype(jnp.int32) for k in range(2)]
+    fx, fy = [table[:, k : k + 1] for k in range(3, 5)]
     lane = lax.broadcasted_iota(jnp.int32, (HOST, CZ), 1)
     wy = weight(lane % CY, y_col, fy)
     x_lane = lane // CY + start - x_col
-    acc = None
     per = 4
     nx = CZ * per // CY
     for j in range(CX // 2 // nx):
@@ -188,26 +205,23 @@
         f_high, f_low = split(jnp.concatenate(field, axis=1))
         part = dot3(w_high, w_low, f_high, f_low)
         acc = part if acc is None else acc + part
-    wz = weight(lane, z_col, fz)
-    out = table
-    for c in range(3):
-        value = jnp.sum(acc[:, c * CZ : (c + 1) * CZ] * wz, axis=1, keepdims=True)
-        out = out + jnp.where(lane == 6 + c, value, 0.0)
-    out_ref[...] = out
-
-
-def sample_low_body(v_ref, cell_ref, frac_ref, tab_ref, x_ref, y_ref):
+    return acc
+
+
+def sample_low_body(v_ref, cell_ref, frac_ref, tab_ref, acc_ref, x_ref, y_ref):
     for c in range(3):
         x_ref[c] = v_ref[c, 0]
         x_ref[c + 3] = v_ref[c, CX - 1]
     y_ref[0] = v_ref[1, :, 0, :]
     y_ref[1] = v_ref[1, :, CY - 1, :]
     rows = jnp.concatenate([cell_ref[...].astype(F32), frac_ref[...], jnp.zeros((CZ - 6, HOST), F32)], axis=0)
-    sample_part(0, v_ref, rows.T, tab_ref)
-
-
-def sample_high_body(v_ref, low_ref, tab_ref):
-    sample_part(CX // 2, v_ref, low_ref[...], tab_ref)
+    table = rows.T
+    tab_ref[...] = table
+    acc_ref[...] = sample_part(0, v_ref, table, None)
+
+
+def sample_high_body(v_ref, tab_ref, low_ref, acc_ref):
+    acc_ref[...] = sample_part(CX // 2, v_ref, tab_ref[...], low_ref[...])
 
 
 def split_blocks(sources):
@@ -261,7 +275,7 @@
     others[0][...] = jnp.concatenate(pick_pair(values, lax.rem(b0 + 2 * chips, total), ny), axis=0)
 
 
-def select_body(n_blk, tab_ref, face_a, face_b, rec_c, rec_d, blk_ref, *rest):
+def select_body(n_blk, tab_ref, acc_ref, face_a, face_b, rec_c, rec_d, blk_ref, *rest):
     others, (samp_ref, sel_ref, pts_ref) = rest[:n_blk], rest[n_blk:]
     even_x, even_y, inner, brick, b0, ny = place()
     sources = [(blk_ref, 0), (face_b, FACE_X)] + [(o, 0) for o in others]
@@ -292,7 +306,7 @@
         field.append(jnp.concatenate([plane, jnp.zeros((CX - XROWS, CZ), F32), line], axis=0))
     w_high, w_low = split(edge_w)
     f_high, f_low = split(jnp.concatenate(field, axis=1))
-    acc = dot3(w_high, w_low, f_high, f_low)
+    acc = acc_ref[...] + dot3(w_high, w_low, f_high, f_low)
     wz = weight(lane, z_col, fz)
     for c in range(3):
         value = jnp.sum(acc[:, c * CZ : (c + 1) * CZ] * wz, axis=1, keepdims=True)
@@ -336,12 +350,21 @@
     return result, [stack[:, 5 + k : 6 + k] for k in range(len(extra))]
 
 
-def weights_body(pts_ref, gx_ref, gy_ref, pz_ref, pos_ref):
+def weights_body(pts_ref, sel_ref, gx_ref, gy_ref, pz_ref, pos_ref, pair_ref, edge_ref):
     table = pts_ref[...].T
-    gx_ref[...] = profile(YROWS, CX, table[0:1], table[3:4])
-    gy_ref[...] = profile(CY, CY, table[1:2], table[4:5])
-    pz_ref[...] = line_profile(table[2:3], table[5:6], [])[0]
+    gx = profile(YROWS, CX, table[0:1], table[3:4])
+    gy = profile(CY, CY, table[1:2], table[4:5])
+    gx_ref[...] = gx
+    gy_ref[...] = gy
+    pz_ref[...] = line_profile(table[2:3], table[5:6], [])[0] * DT_STEP
     pos_ref[...] = jnp.concatenate([table[q : q + 1, k * CZ : (k + 1) * CZ] for q in range(6) for k in range(4)], axis=0)
+    for t in range(2):
+        at = t * ROWS
+        radius = jnp.concatenate([sel_ref[at : at + 1], sel_ref[at + 1 : at + 2]], axis=1)
+        spacing = radius - pts_ref[t * P_SIZE : (t + 1) * P_SIZE, 9:10]
+        pair_ref[t] = spacing / (spacing * spacing + CORE_SQ)
+    for k in range(4):
+        edge_ref[k * CY : (k + 1) * CY] = gx[CX + k : CX + k + 1] * gy
 
 
 def attack(axial_flow, tangent, cos_twist, sin_twist):
@@ -355,7 +378,7 @@
     return rel_speed, cos_phi, sin_phi, lift_coef, drag_coef
 
 
-def loads_body(samp_ref, other_ref, sel_ref, pts_ref, gx_ref, gy_ref, pz_ref, pos_ref, lh_ref, pay_ref, xrim_ref):
+def loads_body(samp_ref, other_ref, sel_ref, pz_ref, pos_ref, pair_ref, edge_ref, lh_ref, pay_ref, xrim_ref):
     def row(k):
         picks = (2 * k, 2 * k + 1, ROWS + 2 * k, ROWS + 2 * k + 1)
         return jnp.concatenate([sel_ref[j : j + 1] for j in picks], axis=1)
@@ -370,10 +393,8 @@
     parts = []
     for t in range(2):
         seg = slice(t * P_SIZE, (t + 1) * P_SIZE)
-        spacing = radius[:, seg] - pts_ref[seg, 9:10]
-        kernel = spacing / (spacing * spacing + CORE_SQ)
         lhs = jnp.concatenate([cos_a[:, seg] * circ[:, seg], sin_a[:, seg] * circ[:, seg], jnp.zeros((6, P_SIZE), F32)], axis=0)
-        both = jnp.dot(lhs, kernel, preferred_element_type=F32, precision=lax.Precision.HIGHEST)
+        both = jnp.dot(lhs, pair_ref[t], preferred_element_type=F32, precision=lax.Precision.HIGHEST)
         parts.append((cos_a[:, seg] * both[0:1] + sin_a[:, seg] * both[1:2]) / (4.0 * math.pi))
     induced = jnp.concatenate(parts, axis=1)
     rel_speed, cos_phi, sin_phi, lift_coef, drag_coef = attack(axial + induced, tangent, cos_t, sin_t)
@@ -394,14 +415,11 @@
     pay_ref[0 : 2 * BACK] = blocks
     pay_ref[2 * BACK :] = pos_ref[...]
     cols = jnp.concatenate(force + [jnp.zeros((CZ - 3, PTS), F32)], axis=0).T
-    pz = pz_ref[...] * DT_STEP
+    pz = pz_ref[...]
     lines = jnp.concatenate([cols[:, c : c + 1] * pz for c in range(3)], axis=1)
     l_high, l_low = split(lines)
     lh_ref[...] = lines
-    gx = gx_ref[...]
-    gy = gy_ref[...]
-    planes = [gx[CX + k : CX + k + 1] * gy for k in range(4)]
-    w_high, w_low = split(jnp.concatenate(planes, axis=0))
+    w_high, w_low = split(edge_ref[...])
     rim = dot3(w_high, w_low, l_high, l_low)
     for k in range(4):
         for c in range(3):
@@ -493,36 +511,38 @@
                 ref[at + core * BACK : at + (core + 1) * BACK] = found
 
 
-def face_terms(buf, at, first, main_low, main_high, y_ref, rec_c, rec_d, rim_low, rim_high, even_y):
+def face_terms(buf, at, first, size, main_low, main_high, y_ref, rec_c, rec_d, rim_low, rim_high, even_y):
     half = 0.5 * DT_STEP
     visc = DT_STEP * NU_VISC
-    part = slice(first, first + CHUNK)
-    here = slice(at, at + CHUNK)
+    part = slice(first, first + size)
+    here = slice(at, at + size)
     half_of = main_low if first < CX // 2 else main_high
     inner = first % (CX // 2)
     for c in range(3):
-        buf[c, here] = half_of[c, inner : inner + CHUNK]
-        rows = slice(c * CX + first, c * CX + first + CHUNK)
+        buf[c, here] = half_of[c, inner : inner + size]
+        rows = slice(c * CX + first, c * CX + first + size)
         a, b = rec_c[rows], jnp.where(odd_side(), rec_d[rows], 0.0)
         low = [jnp.where(even_y, b, a) * (visc + half * y_ref[0, part]), 0.0]
         high = [0.0, jnp.where(even_y, a, b) * (visc - half * y_ref[1, part])]
         for i in range(2):
             row = (i * 3 + c) * YROWS + first
-            buf[c, here, i, :] += rim_low[row : row + CHUNK] + low[i]
-            buf[c, here, CY - 2 + i, :] += rim_high[row : row + CHUNK] + high[i]
-
-
-def chunk_copy(buf, at, out_ref, first, sem):
-    return pltpu.make_async_copy(buf.at[:, pl.ds(at, CHUNK)], out_ref.at[:, pl.ds(first, CHUNK)], sem)
+            buf[c, here, i, :] += rim_low[row : row + size] + low[i]
+            buf[c, here, CY - 2 + i, :] += rim_high[row : row + size] + high[i]
+
+
+INNER = [(2, CHUNK - 2)] + [(k * CHUNK, CHUNK) for k in range(1, N_CHUNK - 1)] + [(CX - CHUNK, CHUNK - 2)]
+
+
+def chunk_copy(buf, at, out_ref, first, size, sem):
+    return pltpu.make_async_copy(buf.at[:, pl.ds(at, size)], out_ref.at[:, pl.ds(first, size)], sem)
 
 
 def inside_body(main_low, main_high, y_ref, rec_c, rec_d, rim_low, rim_high, out_ref, buf, sems):
     _, even_y, _, _, _, _ = place()
     copies = []
-    for k in range(N_CHUNK - 2):
-        first = (k + 1) * CHUNK
-        face_terms(buf, k * CHUNK, first, main_low, main_high, y_ref, rec_c, rec_d, rim_low, rim_high, even_y)
-        copies.append(chunk_copy(buf, k * CHUNK, out_ref, first, sems.at[k]))
+    for k, (first, size) in enumerate(INNER):
+        face_terms(buf, first - 2, first, size, main_low, main_high, y_ref, rec_c, rec_d, rim_low, rim_high, even_y)
+        copies.append(chunk_copy(buf, first - 2, out_ref, first, size, sems.at[k]))
         copies[-1].start()
     for copy in copies:
         copy.wait()
@@ -535,23 +555,23 @@
     visc = DT_STEP * NU_VISC
     copies = []
     for k in range(2):
-        first, at = k * (CX - CHUNK), k * CHUNK
-        face_terms(buf, at, first, main_low, main_high, y_ref, rec_c, rec_d, rim_low, rim_high, even_y)
+        first, at = k * (CX - 2), k * 2
+        face_terms(buf, at, first, 2, main_low, main_high, y_ref, rec_c, rec_d, rim_low, rim_high, even_y)
         for c in range(3):
             a = face_a[c * XROWS : c * XROWS + CY]
             b = jnp.where(inner, face_b[c * XROWS : c * XROWS + CY], 0.0)
             if k == 0:
                 buf[c, 0] += jnp.where(even_x, b, a) * (visc + half * x_ref[0])
             else:
-                buf[c, 2 * CHUNK - 1] += jnp.where(even_x, a, b) * (visc - half * x_ref[3])
+                buf[c, 3] += jnp.where(even_x, a, b) * (visc - half * x_ref[3])
             for i in range(2):
                 rows = slice((i * 3 + c) * CY, (i * 3 + c + 1) * CY)
                 a, b = rim_a[rows], jnp.where(inner, rim_b[rows], 0.0)
                 if k == 0:
                     buf[c, i] += jnp.where(even_x, b, a)
                 else:
-                    buf[c, 2 * CHUNK - 2 + i] += jnp.where(even_x, a, b)
-        copies.append(chunk_copy(buf, at, out_ref, first, sems.at[k]))
+                    buf[c, 2 + i] += jnp.where(even_x, a, b)
+        copies.append(chunk_copy(buf, at, out_ref, first, 2, sems.at[k]))
         copies[-1].start()
     mine = brick.astype(F32)
     found = jnp.zeros((BACK, CZ), F32)
@@ -631,20 +651,23 @@
         [(FACE_Y + ROWS, CZ)] * 2 + [(ROWS, CZ)],
         7,
         "pack",
-        scratch=[pltpu.VMEM((4, 2, CZ), F32), pltpu.VMEM((2, CZ), jnp.int32), pltpu.SMEM((1,), F32), dma((12,))],
+        scratch=[pltpu.VMEM((4, 2, CZ), F32), pltpu.VMEM((2, CZ), jnp.int32), pltpu.VMEM((ROWS, CZ), F32), pltpu.SMEM((1,), F32), dma((15,))],
         in_specs=[HB] * 7,
+        out_specs=[HB] * 3,
         vmem=56,
     )(velocity, rotor_speed, *[a.reshape(2, CZ) for a in (blade_radius, blade_chord, blade_twist, blade_angle, owner_src)])
     rec_c, rec_d, far = exchange_y(pay_c, pay_d, block)
 
     def stencil(start):
-        return call(lambda *refs: stencil_body(start, *refs), [(3, CX // 2, CY, CZ)], 1, "stencil")(velocity)[0]
+        return call(lambda *refs: stencil_body(start, *refs), [(3, CX // 2, CY, CZ)], 1, "stencil")(
+            velocity.reshape(3, CX * CY, CZ)
+        )[0]
 
     base_low = stencil(0)
-    table, x_faces, y_faces = call(
-        sample_low_body, [(HOST, CZ), (6, CY, CZ), (2, CX, CZ)], 3, "sample_low", vmem=24
+    table, sums, x_faces, y_faces = call(
+        sample_low_body, [(HOST, CZ), (HOST, 3 * CZ), (6, CY, CZ), (2, CX, CZ)], 3, "sample_low", vmem=24
     )(velocity, host_cell, host_frac)
-    (rec_c, rec_d, far), (base_low, table) = after((rec_c, rec_d, far), (base_low, table))
+    (rec_c, rec_d, far), (base_low, sums) = after((rec_c, rec_d, far), (base_low, sums))
     pieces = blocks_y(block, rec_c, rec_d, far, ROWS, FACE_Y)
     beside = [swap(p) for p in pieces]
     beside, base_high = after(beside, stencil(CX // 2))
@@ -660,22 +683,27 @@
     face_b = lax.ppermute(pay_b, "gx", odd_pairs(nx, ring))
     from_x = across_x(across) if ring else gather_x(blocks)
     face_a = swap(pay_a)
-    table = call(sample_high_body, [(HOST, CZ)], 2, "sample_high", vmem=24)(velocity, table)[0]
-    (face_a, face_b, from_x), table = after((face_a, face_b, from_x), table)
+    sums = call(sample_high_body, [(HOST, 3 * CZ)], 3, "sample_high", vmem=24)(velocity, table, sums)[0]
+    (face_a, face_b, from_x), sums = after((face_a, face_b, from_x), sums)
     samp, sel, pts = call(
         lambda *refs: select_body(len(from_x), *refs),
         [(8, PTS), (2 * ROWS, CZ), (PTS, CZ)],
-        6 + len(from_x),
+        7 + len(from_x),
         "select",
-    )(table, face_a, face_b, rec_c, rec_d, blocks, *from_x)
+    )(table, sums, face_a, face_b, rec_c, rec_d, blocks, *from_x)
     other = swap(samp)
-    gx, gy, pz, pos = call(weights_body, [(YROWS, PTS), (CY, PTS), (PTS, CZ), (24, CZ)], 1, "weights")(pts)
+    gx, gy, pz, pos, pair_kernel, edge = call(
+        weights_body,
+        [(YROWS, PTS), (CY, PTS), (PTS, CZ), (24, CZ), (2, P_SIZE, P_SIZE), (4 * CY, PTS)],
+        2,
+        "weights",
+    )(pts, sel)
     lines, points, xrim = call(
         loads_body,
         [(PTS, 3 * CZ), (2 * BACK + 24, CZ), (2 * RIM_X, CZ)],
-        8,
+        7,
         "loads",
-    )(samp, other, sel, pts, gx, gy, pz, pos)
+    )(samp, other, sel, pz, pos, pair_kernel, edge)
     ret = points[: 2 * BACK]
     near_c, near_d, far = exchange_y(points, points, ret)
 
@@ -684,8 +712,9 @@
             lambda *refs: spread_body(start, *refs), [(3, CX // 2, CY, CZ)], 4, "spread"
         )(lines, gx, gy, base)[0]
 
-    (near_c, near_d, far), main_low = after((near_c, near_d, far), spread(0, base_low))
+    (near_c, near_d), main_low = after((near_c, near_d), spread(0, base_low))
     rim_low, rim_high = call(near_body, [(RIM_Y, CZ)] * 2, 2, "near")(near_c, near_d)
+    far, rim_low = after(far, rim_low)
     pieces = blocks_y(ret, near_c, near_d, far, 2 * BACK, 0)
     n_rows = 2 * ny * BACK
     pair = (2 * BACK, CZ)
@@ -707,7 +736,7 @@
         [velocity.shape],
         7,
         "inside",
-        scratch=[pltpu.VMEM((3, CX - 2 * CHUNK, CY, CZ), F32), dma((N_CHUNK - 2,))],
+        scratch=[pltpu.VMEM((3, CX - 4, CY, CZ), F32), dma((N_CHUNK,))],
         out_specs=[HB],
         vmem=16,
     )(main_low, main_high, y_faces, rec_c, rec_d, rim_low, rim_high)[0]
@@ -718,7 +747,7 @@
             [velocity.shape, (3, P_SIZE)],
             14 + len(rets),
             "final",
-            scratch=[pltpu.VMEM((3, 2 * CHUNK, CY, CZ), F32), dma((2,))],
+            scratch=[pltpu.VMEM((3, 4, CY, CZ), F32), dma((2,))],
             first=HB,
             out_specs=[HB, VM],
             aliases={0: 0},

time: 47.5 us -> 52 us (1.095)
  Pallas kernels: 24.4 us -> 29.6 us
  waiting for transfers between devices: 3.53 us -> 2.64 us
    pallas_call x1, Pallas kernels: 1.83 us -> 7.21 us  [per_device(): call(pack_body, [(FACE_Y + ROWS, CZ)] * 2 + [(ROWS, CZ)], 7, 'pack', scra...]
    ppermute x2, waiting for transfers between devices: 1.77 us -> 0.79 us  [exchange_y(): lax.ppermute(block, 'gy', flip(ny, 2))]
    ppermute x1, starting transfers between devices: 0.41 us -> 0.98 us  [per_device(): rim_b = lax.ppermute(pay_b, 'gx', odd_pairs(nx, ring))]
  transfers between devices with their start and end apart: 16 -> 16, of which waited for: 4 -> 4; matrix products, arithmetic and copies ran while one was open for 0% -> 0% of each run, Pallas kernels for 32% -> 33%
where the time goes in v8:
time: 52 us; the launch traced here: 51.8 us
  Pallas kernels  29.6 us (57%)
  starting transfers between devices  17.8 us (34%)
  waiting for transfers between devices  2.64 us (5%)
  between operations  1.69 us (3%)
    pallas_call x1, Pallas kernels, per_device(): call(pack_body, [(FACE_Y + ROWS, CZ)] * 2 + [(ROWS, CZ)], 7, 'pack', scra...  7.21 us
    ppermute x2, starting transfers between devices, exchange_y(): from_d = lax.ppermute(to_d, 'gy', flip(ny, 3) if short else odd_pairs(ny))  5.18 us
    pallas_call x2, Pallas kernels, stencil(): call(lambda *refs: stencil_body(start, *refs), [(3, CX // 2, CY, CZ)], 1,...  4.15 us
    pallas_call x2, Pallas kernels, spread(): call(lambda *refs: spread_body(start, *refs), [(3, CX // 2, CY, CZ)], 4,...  3.63 us
    ppermute x2, starting transfers between devices, exchange_y(): from_c = lax.ppermute(to_c, 'gy', flip(ny, 1))  3.11 us
    pallas_call x1, Pallas kernels, per_device(): call(sample_low_body, [(HOST, CZ), (HOST, 3 * CZ), (6, CY, CZ), (2, CX, C...  2.62 us
    ppermute x1, starting transfers between devices, per_device(): face_b = lax.ppermute(pay_b, 'gx', odd_pairs(nx, ring))  2.61 us
    pallas_call x1, Pallas kernels, per_device(): call(sample_high_body, [(HOST, 3 * CZ)], 3, 'sample_high', vmem=24)  2.44 us
  transfers between devices with their start and end apart: 16, of which 4 were waited for; matrix products, arithmetic and copies ran while one was open for 0% of the time, Pallas kernels for 33%

profile of v8, /device:TPU:0, one launch (start us, length us, event | category | flops | bytes accessed | tf_op | source)
XLA Modules:
  0.0 51.8 jit_solution(5540774221157642791)
XLA Ops:
  1.3 7.2 %pack.1 = (f32[208,128]{1,0:T(8,128)}, f32[208,128]{1,0:T(8,128)}, f32[16,128]{1,0:T(8,128)}) custom-call(f32[3,64,32,128]{3,2,1,0:T(8,128)} %v_ref.5, f32[1]{0:T(128)S(6)} %copy.13.spin_hbm, f32[2,128]{1,0:T(2,128)} %bitcast.8, f32[2,128]{1,0:T(2,128)} %bitcast.9, f32[2,128]{1,0:T(2,128)} %bitcast.10, f32[2,128]{1,0:T(2,128)} %bitcast.11, s32[2,128]{1,0:T(2,128)} %bitcast.12), custom_call_target="tpu_custom_call" | custom-call | tf_op jit(solution)/shard_map/pack/pallas_call | solution.py:649
  8.5 3.1 %collective-permute-start = (f32[208,128]{1,0:T(8,128)}, f32[208,128]{1,0:T(8,128)S(1)}, u32[]{:S(2)}, u32[]{:S(2)}) collective-permute-start(f32[208,128]{1,0:T(8,128)} %get-tuple-element.58), channel_id=1, source_target_pairs={{0,1},{1,0},{2,3},{3,2},{4,5},{5,4},{6,7},{7,6},{8,9},{9,8},{10,11... | collective-permute-start | bytes 319496 | tf_op jit(solution)/shard_map/ppermute | solution.py:632
  11.6 2.5 %collective-permute-start.1 = (f32[208,128]{1,0:T(8,128)}, f32[208,128]{1,0:T(8,128)S(1)}, u32[]{:S(2)}, u32[]{:S(2)}) collective-permute-start(f32[208,128]{1,0:T(8,128)} %get-tuple-element.59), channel_id=1, source_target_pairs={{0,3},{1,2},{2,1},{3,0},{4,7},{5,6},{6,5},{7,4},{8,11},{9,10},{10,... | collective-permute-start | bytes 319496 | tf_op jit(solution)/shard_map/ppermute | solution.py:633
  14.1 0.1 collective-permute-start.2
  14.2 2.1 %stencil.2.refs_3_ = f32[3,32,32,128]{3,2,1,0:T(8,128)S(1)} custom-call(f32[3,2048,128]{2,1,0:T(8,128)S(1)} %bitcast.6), custom_call_target="tpu_custom_call" | custom-call | tf_op jit(solution)/shard_map/stencil/pallas_call | solution.py:662
  16.3 2.6 %sample_low.1 = (f32[512,128]{1,0:T(8,128)S(1)}, f32[512,384]{1,0:T(8,128)S(1)}, f32[6,32,128]{2,1,0:T(8,128)S(1)}, f32[2,64,128]{2,1,0:T(8,128)S(1)}) custom-call(f32[3,64,32,128]{3,2,1,0:T(8,128)S(1)} %copy-done, s32[3,512]{1,0:T(4,128)S(1)} %copy-done.1, f32[3,512]{1,0:T(4,128)S(1)} %copy-done.2), custom_call_target="tpu_custom_call" | custom-call | tf_op jit(solution)/shard_map/sample_low/pallas_call | solution.py:667
  18.9 0.8 %collective-permute-done.2 = f32[16,128]{1,0:T(8,128)S(1)} collective-permute-done((f32[16,128]{1,0:T(8,128)}, f32[16,128]{1,0:T(8,128)S(1)}, u32[]{:S(2)}, u32[]{:S(2)}) %collective-permute-start.2) | collective-permute-done | bytes 8224 | tf_op jit(solution)/shard_map/ppermute | solution.py:634
  19.8 0.1 collective-permute-start.3
  19.9 2.1 %stencil.3.refs_3_ = f32[3,32,32,128]{3,2,1,0:T(8,128)S(1)} custom-call(f32[3,2048,128]{2,1,0:T(8,128)S(1)} %bitcast.7), custom_call_target="tpu_custom_call" | custom-call | tf_op jit(solution)/shard_map/stencil/pallas_call | solution.py:662
  21.9 0.1 xpack.1
  22.1 2.6 %collective-permute-start.5 = (f32[152,128]{1,0:T(8,128)S(1)}, f32[152,128]{1,0:T(8,128)S(1)}, u32[]{:S(2)}, u32[]{:S(2)}) collective-permute-start(f32[152,128]{1,0:T(8,128)S(1)} %get-tuple-element.67), channel_id=1, source_target_pairs={{4,8},{12,16},{20,24},{28,0},{8,4},{16,12},{24,20},{0,28},{5,9},{1... | collective-permute-start | bytes 233480 | tf_op jit(solution)/shard_map/ppermute | solution.py:683
  24.7 0.6 %collective-permute-start.6 = (f32[32,128]{1,0:T(8,128)S(1)}, f32[32,128]{1,0:T(8,128)S(1)}, u32[]{:S(2)}, u32[]{:S(2)}) collective-permute-start(f32[32,128]{1,0:T(8,128)S(1)} %get-tuple-element.68), channel_id=1, source_target_pairs={{0,16},{4,20},{8,24},{12,28},{16,0},{20,4},{24,8},{28,12},{1,17},{... | collective-permute-start | bytes 49160 | tf_op jit(solution)/shard_map/ppermute | solution.py:614
  25.3 1.4 %collective-permute-start.7 = (f32[32,128]{1,0:T(8,128)S(1)}, f32[32,128]{1,0:T(8,128)S(1)}, u32[]{:S(2)}, u32[]{:S(2)}) collective-permute-start(f32[32,128]{1,0:T(8,128)S(1)} %get-tuple-element.69), channel_id=1, source_target_pairs={{0,24},{4,12},{8,0},{12,20},{16,8},{20,28},{24,16},{28,4},{1,25},{... | collective-permute-start | bytes 49160 | tf_op jit(solution)/shard_map/ppermute | solution.py:614
  26.7 2.4 %sample_high.1.refs_1_ = f32[512,384]{1,0:T(8,128)S(1)} custom-call(f32[3,64,32,128]{3,2,1,0:T(8,128)S(1)} %copy-done, f32[512,128]{1,0:T(8,128)S(1)} %get-tuple-element.56.tab_ref.refs_0_, f32[512,384]{1,0:T(8,128)S(1)} %get-tuple-element.70.low_ref), custom_call_target="tpu_custom_call" | custom-call | tf_op jit(solution)/shard_map/sample_high/pallas_call | solution.py:686
  29.2 2.3 %select.1 = (f32[8,512]{1,0:T(8,128)S(1)}, f32[32,128]{1,0:T(8,128)S(1)}, f32[512,128]{1,0:T(8,128)S(1)}) custom-call(f32[512,128]{1,0:T(8,128)S(1)} %get-tuple-element.56.tab_ref.refs_0_, f32[512,384]{1,0:T(8,128)S(1)} %sample_high.1.refs_1_, f32[120,128]{1,0:T(8,128)S(1)} %collective-permute-done.4.refs_2_.refs_5_, ...), custom_call_target="tpu_custom_call" | custom-call | tf_op jit(solution)/shard_map/select/pallas_call | solution.py:688
  31.5 0.0 collective-permute-start.8
  31.6 0.8 %weights.1 = (f32[72,512]{1,0:T(8,128)S(1)}, f32[32,512]{1,0:T(8,128)S(1)}, f32[512,128]{1,0:T(8,128)S(1)}, f32[24,128]{1,0:T(8,128)S(1)}, f32[2,256,256]{2,1,0:T(8,128)S(1)}, /*index=5*/f32[128,512]{1,0:T(8,128)S(1)}) custom-call(f32[512,128]{1,0:T(8,128)S(1)} %get-tuple-element.79.pts_ref, f32[32,128]{1,0:T(8,128)S(1)} %get-tuple-element.78.sel_ref), custom_call_target="tpu_custom_call" | custom-call | tf_op jit(solution)/shard_map/weights/pallas_call | solution.py:695
  32.4 0.3 collective-permute-done.8.other_ref
  32.7 1.2 %loads.1 = (f32[512,384]{1,0:T(8,128)S(1)}, f32[40,128]{1,0:T(8,128)S(1)}, f32[384,128]{1,0:T(8,128)S(1)}) custom-call(f32[8,512]{1,0:T(8,128)S(1)} %get-tuple-element.77.samp_ref, f32[8,512]{1,0:T(8,128)S(1)} %collective-permute-done.8.other_ref, f32[32,128]{1,0:T(8,128)S(1)} %get-tuple-element.78.sel_ref, f32[512,128]{1,0:T(8,128)S(1)} %get-tuple-element.80.pz_ref, ...), custom_call_target="tpu_custom_call" | custom-call | tf_op jit(solution)/shard_map/loads/pallas_call | solution.py:701
  34.0 2.7 %collective-permute-start.11 = (f32[40,128]{1,0:T(8,128)S(1)}, f32[40,128]{1,0:T(8,128)S(1)}, u32[]{:S(2)}, u32[]{:S(2)}) collective-permute-start(f32[40,128]{1,0:T(8,128)S(1)} %get-tuple-element.85), channel_id=1, source_target_pairs={{0,3},{1,2},{2,1},{3,0},{4,7},{5,6},{6,5},{7,4},{8,11},{9,10},{10,... | collective-permute-start | bytes 61448 | tf_op jit(solution)/shard_map/ppermute | solution.py:633
  36.7 1.7 %collective-permute-start.9 = (f32[16,128]{1,0:T(8,128)S(1)}, f32[16,128]{1,0:T(8,128)S(1)}, u32[]{:S(2)}, u32[]{:S(2)}) collective-permute-start(f32[16,128]{1,0:T(8,128)S(1)} %slice.20), channel_id=1, source_target_pairs={{0,2},{1,3},{2,0},{3,1},{4,6},{5,7},{6,4},{7,5},{8,10},{9,11},{10,... | collective-permute-start | bytes 24584 | tf_op jit(solution)/shard_map/ppermute | solution.py:634
  38.4 1.8 %spread.2.main_low.refs_1_ = f32[3,32,32,128]{3,2,1,0:T(8,128)S(1)} custom-call(f32[512,384]{1,0:T(8,128)S(1)} %get-tuple-element.86.refs_0_, f32[72,512]{1,0:T(8,128)S(1)} %get-tuple-element.87.refs_1_, f32[32,512]{1,0:T(8,128)S(1)} %get-tuple-element.88.refs_2_, f32[3,32,32,128]{3,2,1,0:T(8,128)S(1)} %stencil.2.refs_3_), custom_call_target="tpu_custom_call" | custom-call | tf_op jit(solution)/shard_map/spread/pallas_call | solution.py:711
  40.3 0.2 collective-permute-done.10.rec_c
  40.5 1.9 %near.1 = (f32[432,128]{1,0:T(8,128)S(1)}, f32[432,128]{1,0:T(8,128)S(1)}) custom-call(f32[40,128]{1,0:T(8,128)S(1)} %collective-permute-done.10.rec_c, f32[40,128]{1,0:T(8,128)S(1)} %collective-permute-done.11.rec_d), custom_call_target="tpu_custom_call" | custom-call | tf_op jit(solution)/shard_map/near/pallas_call | solution.py:716
  42.4 0.1 rimpack.1
  42.5 1.0 %collective-permute-start.14 = (f32[208,128]{1,0:T(8,128)S(1)}, f32[208,128]{1,0:T(8,128)S(1)}, u32[]{:S(2)}, u32[]{:S(2)}) collective-permute-start(f32[208,128]{1,0:T(8,128)S(1)} %get-tuple-element.98), channel_id=1, source_target_pairs={{4,8},{12,16},{20,24},{28,0},{8,4},{16,12},{24,20},{0,28},{5,9},{1... | collective-permute-start | bytes 319496 | tf_op jit(solution)/shard_map/ppermute | solution.py:727
  43.5 0.4 collective-permute-start.13
  43.9 1.8 %spread.3.main_high.refs_2_ = f32[3,32,32,128]{3,2,1,0:T(8,128)S(1)} custom-call(f32[512,384]{1,0:T(8,128)S(1)} %get-tuple-element.86.refs_0_, f32[72,512]{1,0:T(8,128)S(1)} %get-tuple-element.87.refs_1_, f32[32,512]{1,0:T(8,128)S(1)} %get-tuple-element.88.refs_2_, f32[3,32,32,128]{3,2,1,0:T(8,128)S(1)} %stencil.3.refs_3_), custom_call_target="tpu_custom_call" | custom-call | tf_op jit(solution)/shard_map/spread/pallas_call | solution.py:711
  45.7 1.5 %collective-permute-start.12 = (f32[16,128]{1,0:T(8,128)S(1)}, f32[16,128]{1,0:T(8,128)S(1)}, u32[]{:S(2)}, u32[]{:S(2)}) collective-permute-start(f32[16,128]{1,0:T(8,128)S(1)} %get-tuple-element.96), channel_id=1, source_target_pairs={{0,16},{4,20},{8,24},{12,28},{16,0},{20,4},{24,8},{28,12},{1,17},{... | collective-permute-start | bytes 24584 | tf_op jit(solution)/shard_map/ppermute | solution.py:728
  47.3 1.3 %collective-permute-done.14.refs_10_ = f32[208,128]{1,0:T(8,128)S(1)} collective-permute-done((f32[208,128]{1,0:T(8,128)S(1)}, f32[208,128]{1,0:T(8,128)S(1)}, u32[]{:S(2)}, u32[]{:S(2)}) %collective-permute-start.14) | collective-permute-done | bytes 106528 | tf_op jit(solution)/shard_map/ppermute | solution.py:727
  48.5 1.7 %inside.1.refs_0_ = f32[3,64,32,128]{3,2,1,0:T(8,128)} custom-call(f32[3,32,32,128]{3,2,1,0:T(8,128)S(1)} %spread.2.main_low.refs_1_, f32[3,32,32,128]{3,2,1,0:T(8,128)S(1)} %spread.3.main_high.refs_2_, f32[2,64,128]{2,1,0:T(8,128)S(1)} %get-tuple-element.104.y_ref.refs_4_, f32[208,128]{1,0:T(8,128)S(1)} %collective-permute-done.refs_1_.refs_4_.rec_c.refs_7_, ...), custom_call_target="tpu_custom_call" | custom-call | tf_op jit(solution)/shard_map/inside/pallas_call | solution.py:734
  50.3 1.4 %final.1 = (f32[3,64,32,128]{3,2,1,0:T(8,128)}, f32[3,256]{1,0:T(4,128)}) custom-call(f32[3,64,32,128]{3,2,1,0:T(8,128)} %inside.1.refs_0_, f32[3,32,32,128]{3,2,1,0:T(8,128)S(1)} %spread.2.main_low.refs_1_, f32[3,32,32,128]{3,2,1,0:T(8,128)S(1)} %spread.3.main_high.refs_2_, ...), custom_call_target="tpu_custom_call", output_to_operand_aliasing={{0}: (0, {})} | custom-call | tf_op jit(solution)/shard_map/final/pallas_call | solution.py:745
  (31 shorter events, 0.1 us)
Async XLA Ops:
  1.3 12.9 %copy-start = (f32[3,64,32,128]{3,2,1,0:T(8,128)S(1)}, f32[3,64,32,128]{3,2,1,0:T(8,128)}, u32[]{:S(2)}) copy-start(f32[3,64,32,128]{3,2,1,0:T(8,128)} %v_ref.5) | copy-start | bytes 9437188
  8.5 11.2 %collective-permute-start = (f32[208,128]{1,0:T(8,128)}, f32[208,128]{1,0:T(8,128)S(1)}, u32[]{:S(2)}, u32[]{:S(2)}) collective-permute-start(f32[208,128]{1,0:T(8,128)} %get-tuple-element.58), channel_id=1, source_target_pairs={{0,1},{1,0},{2,3},{3,2},{4,5},{5,4},{6,7},{7,6},{8,9},{9,8},{10,11... | collective-permute-start | bytes 319496 | tf_op jit(solution)/shard_map/ppermute | solution.py:632
  11.6 8.1 %collective-permute-start.1 = (f32[208,128]{1,0:T(8,128)}, f32[208,128]{1,0:T(8,128)S(1)}, u32[]{:S(2)}, u32[]{:S(2)}) collective-permute-start(f32[208,128]{1,0:T(8,128)} %get-tuple-element.59), channel_id=1, source_target_pairs={{0,3},{1,2},{2,1},{3,0},{4,7},{5,6},{6,5},{7,4},{8,11},{9,10},{10,... | collective-permute-start | bytes 319496 | tf_op jit(solution)/shard_map/ppermute | solution.py:633
  14.1 5.7 %collective-permute-start.2 = (f32[16,128]{1,0:T(8,128)}, f32[16,128]{1,0:T(8,128)S(1)}, u32[]{:S(2)}, u32[]{:S(2)}) collective-permute-start(f32[16,128]{1,0:T(8,128)} %get-tuple-element.60), channel_id=1, source_target_pairs={{0,2},{1,3},{2,0},{3,1},{4,6},{5,7},{6,4},{7,5},{8,10},{9,11},{10,... | collective-permute-start | bytes 24584 | tf_op jit(solution)/shard_map/ppermute | solution.py:634
  14.2 2.1 %copy-start.1 = (s32[3,512]{1,0:T(4,128)S(1)}, s32[3,512]{1,0:T(4,128)}, u32[]{:S(2)}) copy-start(s32[3,512]{1,0:T(4,128)} %cell_ref.1) | copy-start | bytes 18436
  14.2 2.1 %copy-start.2 = (f32[3,512]{1,0:T(4,128)S(1)}, f32[3,512]{1,0:T(4,128)}, u32[]{:S(2)}) copy-start(f32[3,512]{1,0:T(4,128)} %frac_ref.1) | copy-start | bytes 18436
  16.3 3.4 %copy-start.3 = (f32[16,128]{1,0:T(8,128)S(1)}, f32[16,128]{1,0:T(8,128)}, u32[]{:S(2)}) copy-start(f32[16,128]{1,0:T(8,128)} %get-tuple-element.60) | copy-start | bytes 24580
  19.8 2.2 %collective-permute-start.3 = (f32[64,128]{1,0:T(8,128)S(1)}, f32[64,128]{1,0:T(8,128)S(1)}, u32[]{:S(2)}, u32[]{:S(2)}) collective-permute-start(f32[64,128]{1,0:T(8,128)S(1)} %pad_maximum_fusion.refs_3_), channel_id=1, source_target_pairs={{0,4},{4,0},{8,12},{12,8},{16,20},{20,16},{24,28},{28,24},{1,5},{5... | collective-permute-start | bytes 98312 | tf_op jit(solution)/shard_map/ppermute | solution.py:617
  22.1 7.1 %collective-permute-start.5 = (f32[152,128]{1,0:T(8,128)S(1)}, f32[152,128]{1,0:T(8,128)S(1)}, u32[]{:S(2)}, u32[]{:S(2)}) collective-permute-start(f32[152,128]{1,0:T(8,128)S(1)} %get-tuple-element.67), channel_id=1, source_target_pairs={{4,8},{12,16},{20,24},{28,0},{8,4},{16,12},{24,20},{0,28},{5,9},{1... | collective-permute-start | bytes 233480 | tf_op jit(solution)/shard_map/ppermute | solution.py:683
  24.7 4.5 %collective-permute-start.4 = (f32[120,128]{1,0:T(8,128)S(1)}, f32[120,128]{1,0:T(8,128)S(1)}, u32[]{:S(2)}, u32[]{:S(2)}) collective-permute-start(f32[120,128]{1,0:T(8,128)S(1)} %get-tuple-element.66), channel_id=1, source_target_pairs={{0,4},{4,0},{8,12},{12,8},{16,20},{20,16},{24,28},{28,24},{1,5},{5... | collective-permute-start | bytes 184328 | tf_op jit(solution)/shard_map/ppermute | solution.py:617
  24.7 4.5 %collective-permute-start.6 = (f32[32,128]{1,0:T(8,128)S(1)}, f32[32,128]{1,0:T(8,128)S(1)}, u32[]{:S(2)}, u32[]{:S(2)}) collective-permute-start(f32[32,128]{1,0:T(8,128)S(1)} %get-tuple-element.68), channel_id=1, source_target_pairs={{0,16},{4,20},{8,24},{12,28},{16,0},{20,4},{24,8},{28,12},{1,17},{... | collective-permute-start | bytes 49160 | tf_op jit(solution)/shard_map/ppermute | solution.py:614
  25.3 3.9 %collective-permute-start.7 = (f32[32,128]{1,0:T(8,128)S(1)}, f32[32,128]{1,0:T(8,128)S(1)}, u32[]{:S(2)}, u32[]{:S(2)}) collective-permute-start(f32[32,128]{1,0:T(8,128)S(1)} %get-tuple-element.69), channel_id=1, source_target_pairs={{0,24},{4,12},{8,0},{12,20},{16,8},{20,28},{24,16},{28,4},{1,25},{... | collective-permute-start | bytes 49160 | tf_op jit(solution)/shard_map/ppermute | solution.py:614
  31.5 1.2 %collective-permute-start.8 = (f32[8,512]{1,0:T(8,128)S(1)}, f32[8,512]{1,0:T(8,128)S(1)}, u32[]{:S(2)}, u32[]{:S(2)}) collective-permute-start(f32[8,512]{1,0:T(8,128)S(1)} %get-tuple-element.77.samp_ref), channel_id=1, source_target_pairs={{0,4},{4,0},{8,12},{12,8},{16,20},{20,16},{24,28},{28,24},{1,5},{5... | collective-permute-start | bytes 49160 | tf_op jit(solution)/shard_map/ppermute | solution.py:617
  34.0 6.3 %collective-permute-start.11 = (f32[40,128]{1,0:T(8,128)S(1)}, f32[40,128]{1,0:T(8,128)S(1)}, u32[]{:S(2)}, u32[]{:S(2)}) collective-permute-start(f32[40,128]{1,0:T(8,128)S(1)} %get-tuple-element.85), channel_id=1, source_target_pairs={{0,3},{1,2},{2,1},{3,0},{4,7},{5,6},{6,5},{7,4},{8,11},{9,10},{10,... | collective-permute-start | bytes 61448 | tf_op jit(solution)/shard_map/ppermute | solution.py:633
  36.7 3.8 %collective-permute-start.10 = (f32[40,128]{1,0:T(8,128)S(1)}, f32[40,128]{1,0:T(8,128)S(1)}, u32[]{:S(2)}, u32[]{:S(2)}) collective-permute-start(f32[40,128]{1,0:T(8,128)S(1)} %get-tuple-element.85), channel_id=1, source_target_pairs={{0,1},{1,0},{2,3},{3,2},{4,5},{5,4},{6,7},{7,6},{8,9},{9,8},{10,11... | collective-permute-start | bytes 61448 | tf_op jit(solution)/shard_map/ppermute | solution.py:632
  36.7 5.7 %collective-permute-start.9 = (f32[16,128]{1,0:T(8,128)S(1)}, f32[16,128]{1,0:T(8,128)S(1)}, u32[]{:S(2)}, u32[]{:S(2)}) collective-permute-start(f32[16,128]{1,0:T(8,128)S(1)} %slice.20), channel_id=1, source_target_pairs={{0,2},{1,3},{2,0},{3,1},{4,6},{5,7},{6,4},{7,5},{8,10},{9,11},{10,... | collective-permute-start | bytes 24584 | tf_op jit(solution)/shard_map/ppermute | solution.py:634
  42.5 6.0 %collective-permute-start.14 = (f32[208,128]{1,0:T(8,128)S(1)}, f32[208,128]{1,0:T(8,128)S(1)}, u32[]{:S(2)}, u32[]{:S(2)}) collective-permute-start(f32[208,128]{1,0:T(8,128)S(1)} %get-tuple-element.98), channel_id=1, source_target_pairs={{4,8},{12,16},{20,24},{28,0},{8,4},{16,12},{24,20},{0,28},{5,9},{1... | collective-permute-start | bytes 319496 | tf_op jit(solution)/shard_map/ppermute | solution.py:727
  43.5 3.8 %collective-permute-start.13 = (f32[192,128]{1,0:T(8,128)S(1)}, f32[192,128]{1,0:T(8,128)S(1)}, u32[]{:S(2)}, u32[]{:S(2)}) collective-permute-start(f32[192,128]{1,0:T(8,128)S(1)} %get-tuple-element.97), channel_id=1, source_target_pairs={{0,4},{4,0},{8,12},{12,8},{16,20},{20,16},{24,28},{28,24},{1,5},{5... | collective-permute-start | bytes 294920 | tf_op jit(solution)/shard_map/ppermute | solution.py:617
  45.7 4.5 %collective-permute-start.12 = (f32[16,128]{1,0:T(8,128)S(1)}, f32[16,128]{1,0:T(8,128)S(1)}, u32[]{:S(2)}, u32[]{:S(2)}) collective-permute-start(f32[16,128]{1,0:T(8,128)S(1)} %get-tuple-element.96), channel_id=1, source_target_pairs={{0,16},{4,20},{8,24},{12,28},{16,0},{20,4},{24,8},{28,12},{1,17},{... | collective-permute-start | bytes 24584 | tf_op jit(solution)/shard_map/ppermute | solution.py:728
  48.5 1.8 %collective-permute-start.15 = (f32[16,128]{1,0:T(8,128)S(1)}, f32[16,128]{1,0:T(8,128)S(1)}, u32[]{:S(2)}, u32[]{:S(2)}) collective-permute-start(f32[16,128]{1,0:T(8,128)S(1)} %slice.23), channel_id=1, source_target_pairs={{0,4},{4,0},{8,12},{12,8},{16,20},{20,16},{24,28},{28,24},{1,5},{5... | collective-permute-start | bytes 24584 | tf_op jit(solution)/shard_map/ppermute | solution.py:617

commit v9 on v8

--- a/solution.py
+++ b/solution.py
@@ -86,15 +86,15 @@
 
 
 def pack_body(v_ref, spin_hbm, *rest):
-    params, (pay_c, pay_d, blk_ref, held, held_int, made, spin_ref, sems) = rest[:5], rest[5:]
+    params, (pay_c, pay_d, blk_ref, held, held_int, spin_ref, sems) = rest[:5], rest[5:]
     _, even_y, _, brick, _, _ = place()
 
     def faces(first, second):
-        copies = []
+        made = []
         for k, (ref, y) in enumerate(((pay_c, first), (pay_d, second))):
             for c in range(3):
-                copies.append(pltpu.make_async_copy(v_ref.at[c, :, y], ref.at[pl.ds(c * CX, CX)], sems.at[3 * k + c]))
-        return copies
+                made.append(pltpu.make_async_copy(v_ref.at[c, :, y], ref.at[pl.ds(c * CX, CX)], sems.at[3 * k + c]))
+        return made
 
     @pl.when(even_y)
     def _():
@@ -125,12 +125,11 @@
         jnp.full((1, CZ), spin_ref[0], F32),
         jnp.full((1, CZ), brick.astype(F32), F32),
     ]
-    made[...] = jnp.concatenate(parts, axis=0)
-    targets = (pay_c.at[pl.ds(FACE_Y, ROWS)], pay_d.at[pl.ds(FACE_Y, ROWS)], blk_ref)
-    outward = [pltpu.make_async_copy(made, ref, sems.at[12 + k]) for k, ref in enumerate(targets)]
-    for copy in outward:
-        copy.start()
-    for copy in faces(0, 0) + outward:
+    block = jnp.concatenate(parts, axis=0)
+    blk_ref[...] = block
+    pay_c[FACE_Y:] = block
+    pay_d[FACE_Y:] = block
+    for copy in faces(0, 0):
         copy.wait()
 
 
@@ -142,43 +141,26 @@
     not_last_y, not_first_y = row < CY - 1, row > 0
     not_last_z, not_first_z = lane < CZ - 1, lane > 0
 
-    def plane(x, down, up):
-        at = x * CY if isinstance(x, int) else pl.multiple_of(x * CY, CY)
-        v0, v1, v2 = [v_ref[c, pl.ds(at, CY)] for c in range(3)]
-        a_x, b_x = visc - half * v0, visc + half * v0
+    def step(k, carry):
+        x = start + k
+        up = jnp.minimum(x + 1, CX - 1)
+        down = jnp.maximum(x - 1, 0)
+        v0, v1, v2 = v_ref[0, x], v_ref[1, x], v_ref[2, x]
+        a_x = jnp.where(x < CX - 1, visc - half * v0, 0.0)
+        b_x = jnp.where(x > 0, visc + half * v0, 0.0)
         a_y = jnp.where(not_last_y, visc - half * v1, 0.0)
         b_y = jnp.where(not_first_y, visc + half * v1, 0.0)
         a_z = jnp.where(not_last_z, visc - half * v2, 0.0)
         b_z = jnp.where(not_first_z, visc + half * v2, 0.0)
         for c in range(3):
             mid = (v0, v1, v2)[c]
-            total = (1.0 - 6.0 * visc) * mid
-            total += a_z * pltpu.roll(mid, CZ - 1, 1) + b_z * pltpu.roll(mid, 1, 1)
-            if up is None:
-                y_up = pltpu.roll(mid, CY - 1, 0)
-            else:
-                y_up = v_ref[c, pl.ds(at + 1, CY)]
-                total += a_x * v_ref[c, pl.ds(at + CY, CY)]
-            if down is None:
-                y_down = pltpu.roll(mid, 1, 0)
-            else:
-                y_down = v_ref[c, pl.ds(at - 1, CY)]
-                total += b_x * v_ref[c, pl.ds(at - CY, CY)]
-            out_ref[c, x - start] = total + (a_y * y_up + b_y * y_down)
-
-    first, last = start, start + CX // 2
-    if start == 0:
-        plane(0, None, True)
-        first = 1
-    if last == CX:
-        last = CX - 1
-        plane(last, True, None)
-
-    def step(x, carry):
-        plane(x, True, True)
+            along_x = a_x * v_ref[c, up] + b_x * v_ref[c, down]
+            along_y = a_y * pltpu.roll(mid, CY - 1, 0) + b_y * pltpu.roll(mid, 1, 0)
+            along_z = a_z * pltpu.roll(mid, CZ - 1, 1) + b_z * pltpu.roll(mid, 1, 1)
+            out_ref[c, k] = (1.0 - 6.0 * visc) * mid + along_x + (along_y + along_z)
         return carry
 
-    lax.fori_loop(first, last, step, 0, unroll=2)
+    lax.fori_loop(0, CX // 2, step, 0, unroll=2)
 
 
 def weight(coord, base, frac):
@@ -190,16 +172,19 @@
     fx, fy = [table[:, k : k + 1] for k in range(3, 5)]
     lane = lax.broadcasted_iota(jnp.int32, (HOST, CZ), 1)
     wy = weight(lane % CY, y_col, fy)
-    x_lane = lane // CY + start - x_col
+    x_lane = (lane // CY + start - x_col).astype(F32).astype(BF16)
+    near, far = split((1.0 - fx) * wy), split(fx * wy)
+    zero = jnp.zeros((HOST, CZ), BF16)
     per = 4
     nx = CZ * per // CY
     for j in range(CX // 2 // nx):
-        parts = []
+        highs, lows = [], []
         for i in range(per):
             shift = (CZ // CY) * (j * per + i)
-            wx = jnp.where(x_lane == -shift, 1.0 - fx, jnp.where(x_lane == 1 - shift, fx, 0.0))
-            parts.append(wx * wy)
-        w_high, w_low = split(jnp.concatenate(parts, axis=1))
+            at_base, at_next = x_lane == jnp.bfloat16(-shift), x_lane == jnp.bfloat16(1 - shift)
+            highs.append(jnp.where(at_base, near[0], jnp.where(at_next, far[0], zero)))
+            lows.append(jnp.where(at_base, near[1], jnp.where(at_next, far[1], zero)))
+        w_high, w_low = jnp.concatenate(highs, axis=1), jnp.concatenate(lows, axis=1)
         first = start + j * nx
         field = [v_ref[c, first : first + nx].reshape(nx * CY, CZ) for c in range(3)]
         f_high, f_low = split(jnp.concatenate(field, axis=1))
@@ -410,7 +395,7 @@
             for h in range(2):
                 at = t * P_SIZE + h * CZ
                 pieces.append(force[c][:, at : at + CZ])
-        pieces += [sel_ref[t * ROWS + 15 : t * ROWS + 16]] * 2
+        pieces += [sel_ref[t * ROWS + 15 : t * ROWS + 16] + 1.0] * 2
     blocks = jnp.concatenate(pieces, axis=0)
     pay_ref[0 : 2 * BACK] = blocks
     pay_ref[2 * BACK :] = pos_ref[...]
@@ -498,12 +483,13 @@
         chips = ny * 2
         side = jnp.where(even_x, -chips, chips)
         total = lax.axis_size("gx") * ny
+        closing = jnp.where(b0 < chips, total - chips, chips)
         for ref, at, target in (
             (pay_b, RIM_X, lax.rem(b0 + side + total, total)),
-            (others[0], 0, lax.rem(b0 + 2 * chips, total)),
+            (others[0], 0, lax.rem(b0 + jnp.where(even_x, 2 * chips, closing), total)),
         ):
             for core in range(2):
-                wanted = (target + core * ny).astype(F32)
+                wanted = (target + core * ny + 1).astype(F32)
                 found = jnp.full((BACK, CZ), -1.0, F32)
                 for k in range(back.shape[0] // BACK):
                     value = back[k * BACK : (k + 1) * BACK]
@@ -537,12 +523,25 @@
     return pltpu.make_async_copy(buf.at[:, pl.ds(at, size)], out_ref.at[:, pl.ds(first, size)], sem)
 
 
-def inside_body(main_low, main_high, y_ref, rec_c, rec_d, rim_low, rim_high, out_ref, buf, sems):
+def low_body(lines_ref, gx_ref, gy_ref, base_ref, main_low, y_ref, rec_c, rec_d, rim_low, rim_high, main_ref, out_ref, buf, sems):
     _, even_y, _, _, _, _ = place()
     copies = []
-    for k, (first, size) in enumerate(INNER):
-        face_terms(buf, first - 2, first, size, main_low, main_high, y_ref, rec_c, rec_d, rim_low, rim_high, even_y)
+    for k, (first, size) in enumerate(INNER[: N_CHUNK // 2]):
+        face_terms(buf, first - 2, first, size, main_low, None, y_ref, rec_c, rec_d, rim_low, rim_high, even_y)
         copies.append(chunk_copy(buf, first - 2, out_ref, first, size, sems.at[k]))
+        copies[-1].start()
+    spread_body(CX // 2, lines_ref, gx_ref, gy_ref, base_ref, main_ref)
+    for copy in copies:
+        copy.wait()
+
+
+def high_body(_, main_high, y_ref, rec_c, rec_d, rim_low, rim_high, out_ref, buf, sems):
+    _, even_y, _, _, _, _ = place()
+    copies = []
+    for k, (first, size) in enumerate(INNER[N_CHUNK // 2 :]):
+        at = first - CX // 2
+        face_terms(buf, at, first, size, None, main_high, y_ref, rec_c, rec_d, rim_low, rim_high, even_y)
+        copies.append(chunk_copy(buf, at, out_ref, first, size, sems.at[k]))
         copies[-1].start()
     for copy in copies:
         copy.wait()
@@ -573,7 +572,7 @@
                     buf[c, 2 + i] += jnp.where(even_x, a, b)
         copies.append(chunk_copy(buf, at, out_ref, first, 2, sems.at[k]))
         copies[-1].start()
-    mine = brick.astype(F32)
+    mine = (brick + 1).astype(F32)
     found = jnp.zeros((BACK, CZ), F32)
     for ref, first in [(back_ref, 0), (rim_b, RIM_X)] + [(r, 0) for r in rets]:
         for k in range((ref.shape[0] - first) // BACK):
@@ -610,6 +609,9 @@
     def same_side(n):
         return [(i, (i + (2 if i % 2 else n - 2)) % n) for i in range(n)]
 
+    def opposite(n):
+        return [(i, (i + n // 2) % n) for i in range(0, n, 2)] + [(1, n - 1), (n - 1, 1)]
+
     def across_x(blocks):
         return [lax.ppermute(b, "gx", p) for b, p in zip(blocks, (flip(nx, 4), same_side(nx)))]
 
@@ -651,17 +653,14 @@
         [(FACE_Y + ROWS, CZ)] * 2 + [(ROWS, CZ)],
         7,
         "pack",
-        scratch=[pltpu.VMEM((4, 2, CZ), F32), pltpu.VMEM((2, CZ), jnp.int32), pltpu.VMEM((ROWS, CZ), F32), pltpu.SMEM((1,), F32), dma((15,))],
+        scratch=[pltpu.VMEM((4, 2, CZ), F32), pltpu.VMEM((2, CZ), jnp.int32), pltpu.SMEM((1,), F32), dma((12,))],
         in_specs=[HB] * 7,
-        out_specs=[HB] * 3,
         vmem=56,
     )(velocity, rotor_speed, *[a.reshape(2, CZ) for a in (blade_radius, blade_chord, blade_twist, blade_angle, owner_src)])
     rec_c, rec_d, far = exchange_y(pay_c, pay_d, block)
 
     def stencil(start):
-        return call(lambda *refs: stencil_body(start, *refs), [(3, CX // 2, CY, CZ)], 1, "stencil")(
-            velocity.reshape(3, CX * CY, CZ)
-        )[0]
+        return call(lambda *refs: stencil_body(start, *refs), [(3, CX // 2, CY, CZ)], 1, "stencil")(velocity)[0]
 
     base_low = stencil(0)
     table, sums, x_faces, y_faces = call(
@@ -724,22 +723,32 @@
         3 + len(pieces),
         "rimpack",
     )(xrim, rim_low, rim_high, *pieces)
-    rim_b = lax.ppermute(pay_b, "gx", odd_pairs(nx, ring))
-    rets = [lax.ppermute(across[0], "gx", flip(nx, 4))] if ring else gather_x(back)
+    rim_b = lax.ppermute(pay_b, "gx", odd_pairs(nx))
+    rets = [lax.ppermute(across[0], "gx", opposite(nx))] if ring else gather_x(back)
     rim_a = swap(pay_a)
-    main_high = spread(CX // 2, base_high)
-    (rim_a, rim_b), (main_low, main_high) = after((rim_a, rim_b), (main_low, main_high))
+    faces = (y_faces, rec_c, rec_d, rim_low, rim_high)
+    half_buf = pltpu.VMEM((3, CX // 2 - 2, CY, CZ), F32)
+    main_high, inside = call(
+        low_body,
+        [(3, CX // 2, CY, CZ), velocity.shape],
+        10,
+        "low",
+        scratch=[half_buf, dma((N_CHUNK // 2,))],
+        out_specs=[VM, HB],
+    )(lines, gx, gy, base_high, main_low, *faces)
+    (rim_a, rim_b, rets), inside = after((rim_a, rim_b, rets), inside)
     if ring:
-        rets.append(swap(rim_b[RIM_X:]))
+        rets.append(swap(join([rim_b[RIM_X:]] + rets)))
     inside = call(
-        inside_body,
+        high_body,
         [velocity.shape],
         7,
-        "inside",
-        scratch=[pltpu.VMEM((3, CX - 4, CY, CZ), F32), dma((N_CHUNK,))],
+        "high",
+        scratch=[half_buf, dma((N_CHUNK // 2,))],
+        first=HB,
         out_specs=[HB],
-        vmem=16,
-    )(main_low, main_high, y_faces, rec_c, rec_d, rim_low, rim_high)[0]
+        aliases={0: 0},
+    )(inside, main_high, *faces)[0]
     rets, inside = after(rets, inside)
     return tuple(
         call(

time: 52 us -> 50.2 us (0.965)
  Pallas kernels: 29.6 us -> 24.5 us
  starting transfers between devices: 17.8 us -> 21.9 us
  waiting for transfers between devices: 2.64 us -> 1.55 us
    pallas_call x1, Pallas kernels: 7.21 us -> 1.83 us  [per_device(): call(pack_body, [(FACE_Y + ROWS, CZ)] * 2 + [(ROWS, CZ)], 7, 'pack', scra...]
    pallas_call x1 -> x2, Pallas kernels: 1.73 us -> 4.16 us  [the longest x1 2.92 us: per_device(): call(low_body, [(3, CX // 2, CY, CZ), velocity.shape], 10, 'low', scratch...]
    ppermute x5, starting transfers between devices: 0.55 us -> 2.88 us  [swap(): return lax.ppermute(block, 'gx', flip(nx, 1))]
    pallas_call x2 -> x1, Pallas kernels: 3.63 us -> 1.8 us  [spread(): call(lambda *refs: spread_body(start, *refs), [(3, CX // 2, CY, CZ)], 4,...]
    ppermute x2, starting transfers between devices: 2.51 us -> 4.26 us  [the longest x1 3.59 us: per_device(): lax.ppermute(across[0], 'gx', opposite(nx))]
    ppermute x2, waiting for transfers between devices: 1.26 us -> 0.01 us  [the longest x1 0.01 us: per_device(): rim_b = lax.ppermute(pay_b, 'gx', odd_pairs(nx))]
  transfers between devices with their start and end apart: 16 -> 16, of which waited for: 4 -> 3; matrix products, arithmetic and copies ran while one was open for 0% -> 0% of each run, Pallas kernels for 33% -> 35%
where the time goes in v9:
time: 50.2 us; the launch traced here: 49.9 us
  Pallas kernels  24.5 us (49%)
  starting transfers between devices  21.9 us (44%)
  between operations  1.91 us (4%)
  waiting for transfers between devices  1.55 us (3%)
    ppermute x2, starting transfers between devices, exchange_y(): from_d = lax.ppermute(to_d, 'gy', flip(ny, 3) if short else odd_pairs(ny))  5.18 us
    pallas_call x2, Pallas kernels, stencil(): call(lambda *refs: stencil_body(start, *refs), [(3, CX // 2, CY, CZ)], 1,...  3.9 us
    ppermute x1, starting transfers between devices, per_device(): lax.ppermute(across[0], 'gx', opposite(nx))  3.59 us
    ppermute x2, starting transfers between devices, exchange_y(): from_c = lax.ppermute(to_c, 'gy', flip(ny, 1))  3.09 us
    pallas_call x1, Pallas kernels, per_device(): call(low_body, [(3, CX // 2, CY, CZ), velocity.shape], 10, 'low', scratch...  2.92 us
    ppermute x5, starting transfers between devices, swap(): return lax.ppermute(block, 'gx', flip(nx, 1))  2.88 us
    ppermute x1, starting transfers between devices, per_device(): face_b = lax.ppermute(pay_b, 'gx', odd_pairs(nx, ring))  2.61 us
    pallas_call x1, Pallas kernels, per_device(): call(sample_low_body, [(HOST, CZ), (HOST, 3 * CZ), (6, CY, CZ), (2, CX, C...  2.59 us
  transfers between devices with their start and end apart: 16, of which 3 were waited for; matrix products, arithmetic and copies ran while one was open for 0% of the time, Pallas kernels for 35%

profile of v9, /device:TPU:0, one launch (start us, length us, event | category | flops | bytes accessed | tf_op | source)
XLA Modules:
  0.0 49.9 jit_solution(3095378354763641420)
XLA Ops:
  1.4 1.8 %pack.1 = (f32[208,128]{1,0:T(8,128)}, f32[208,128]{1,0:T(8,128)}, f32[16,128]{1,0:T(8,128)}) custom-call(f32[3,64,32,128]{3,2,1,0:T(8,128)} %v_ref.5, f32[1]{0:T(128)S(6)} %copy.15.spin_hbm, f32[2,128]{1,0:T(2,128)} %bitcast.5, f32[2,128]{1,0:T(2,128)} %bitcast.6, f32[2,128]{1,0:T(2,128)} %bitcast.7, f32[2,128]{1,0:T(2,128)} %bitcast.8, s32[2,128]{1,0:T(2,128)} %bitcast.9), custom_call_target="tpu_custom_call" | custom-call | tf_op jit(solution)/shard_map/pack/pallas_call | solution.py:651
  3.3 3.1 %collective-permute-start = (f32[208,128]{1,0:T(8,128)}, f32[208,128]{1,0:T(8,128)S(1)}, u32[]{:S(2)}, u32[]{:S(2)}) collective-permute-start(f32[208,128]{1,0:T(8,128)} %get-tuple-element.60), channel_id=1, source_target_pairs={{0,1},{1,0},{2,3},{3,2},{4,5},{5,4},{6,7},{7,6},{8,9},{9,8},{10,11... | collective-permute-start | bytes 319496 | tf_op jit(solution)/shard_map/ppermute | solution.py:634
  6.4 2.5 %collective-permute-start.1 = (f32[208,128]{1,0:T(8,128)}, f32[208,128]{1,0:T(8,128)S(1)}, u32[]{:S(2)}, u32[]{:S(2)}) collective-permute-start(f32[208,128]{1,0:T(8,128)} %get-tuple-element.61), channel_id=1, source_target_pairs={{0,3},{1,2},{2,1},{3,0},{4,7},{5,6},{6,5},{7,4},{8,11},{9,10},{10,... | collective-permute-start | bytes 319496 | tf_op jit(solution)/shard_map/ppermute | solution.py:635
  8.9 0.1 collective-permute-start.2
  9.0 1.9 %stencil.2.refs_3_ = f32[3,32,32,128]{3,2,1,0:T(8,128)S(1)} custom-call(f32[3,64,32,128]{3,2,1,0:T(8,128)S(1)} %copy-done), custom_call_target="tpu_custom_call" | custom-call | tf_op jit(solution)/shard_map/stencil/pallas_call | solution.py:663
  11.0 2.6 %sample_low.1 = (f32[512,128]{1,0:T(8,128)S(1)}, f32[512,384]{1,0:T(8,128)S(1)}, f32[6,32,128]{2,1,0:T(8,128)S(1)}, f32[2,64,128]{2,1,0:T(8,128)S(1)}) custom-call(f32[3,64,32,128]{3,2,1,0:T(8,128)S(1)} %copy-done, s32[3,512]{1,0:T(4,128)S(1)} %copy-done.1, f32[3,512]{1,0:T(4,128)S(1)} %copy-done.2), custom_call_target="tpu_custom_call" | custom-call | tf_op jit(solution)/shard_map/sample_low/pallas_call | solution.py:666
  13.5 1.0 %collective-permute-done.2 = f32[16,128]{1,0:T(8,128)S(1)} collective-permute-done((f32[16,128]{1,0:T(8,128)}, f32[16,128]{1,0:T(8,128)S(1)}, u32[]{:S(2)}, u32[]{:S(2)}) %collective-permute-start.2) | collective-permute-done | bytes 8224 | tf_op jit(solution)/shard_map/ppermute | solution.py:636
  14.5 0.1 collective-permute-start.3
  14.6 1.9 %stencil.3.base_ref = f32[3,32,32,128]{3,2,1,0:T(8,128)S(1)} custom-call(f32[3,64,32,128]{3,2,1,0:T(8,128)S(1)} %copy-done), custom_call_target="tpu_custom_call" | custom-call | tf_op jit(solution)/shard_map/stencil/pallas_call | solution.py:663
  16.6 0.1 xpack.1
  16.7 2.6 %collective-permute-start.5 = (f32[152,128]{1,0:T(8,128)S(1)}, f32[152,128]{1,0:T(8,128)S(1)}, u32[]{:S(2)}, u32[]{:S(2)}) collective-permute-start(f32[152,128]{1,0:T(8,128)S(1)} %get-tuple-element.69), channel_id=1, source_target_pairs={{4,8},{12,16},{20,24},{28,0},{8,4},{16,12},{24,20},{0,28},{5,9},{1... | collective-permute-start | bytes 233480 | tf_op jit(solution)/shard_map/ppermute | solution.py:682
  19.3 0.6 %collective-permute-start.6 = (f32[32,128]{1,0:T(8,128)S(1)}, f32[32,128]{1,0:T(8,128)S(1)}, u32[]{:S(2)}, u32[]{:S(2)}) collective-permute-start(f32[32,128]{1,0:T(8,128)S(1)} %get-tuple-element.70), channel_id=1, source_target_pairs={{0,16},{4,20},{8,24},{12,28},{16,0},{20,4},{24,8},{28,12},{1,17},{... | collective-permute-start | bytes 49160 | tf_op jit(solution)/shard_map/ppermute | solution.py:616
  19.9 1.4 %collective-permute-start.7 = (f32[32,128]{1,0:T(8,128)S(1)}, f32[32,128]{1,0:T(8,128)S(1)}, u32[]{:S(2)}, u32[]{:S(2)}) collective-permute-start(f32[32,128]{1,0:T(8,128)S(1)} %get-tuple-element.71), channel_id=1, source_target_pairs={{0,24},{4,12},{8,0},{12,20},{16,8},{20,28},{24,16},{28,4},{1,25},{... | collective-permute-start | bytes 49160 | tf_op jit(solution)/shard_map/ppermute | solution.py:616
  21.3 2.4 %sample_high.1.refs_1_ = f32[512,384]{1,0:T(8,128)S(1)} custom-call(f32[3,64,32,128]{3,2,1,0:T(8,128)S(1)} %copy-done, f32[512,128]{1,0:T(8,128)S(1)} %get-tuple-element.58.tab_ref.refs_0_, f32[512,384]{1,0:T(8,128)S(1)} %get-tuple-element.72.low_ref), custom_call_target="tpu_custom_call" | custom-call | tf_op jit(solution)/shard_map/sample_high/pallas_call | solution.py:685
  23.8 2.3 %select.1 = (f32[8,512]{1,0:T(8,128)S(1)}, f32[32,128]{1,0:T(8,128)S(1)}, f32[512,128]{1,0:T(8,128)S(1)}) custom-call(f32[512,128]{1,0:T(8,128)S(1)} %get-tuple-element.58.tab_ref.refs_0_, f32[512,384]{1,0:T(8,128)S(1)} %sample_high.1.refs_1_, f32[120,128]{1,0:T(8,128)S(1)} %collective-permute-done.4.refs_2_.refs_5_, ...), custom_call_target="tpu_custom_call" | custom-call | tf_op jit(solution)/shard_map/select/pallas_call | solution.py:687
  26.1 0.0 collective-permute-start.8
  26.2 0.8 %weights.1 = (f32[72,512]{1,0:T(8,128)S(1)}, f32[32,512]{1,0:T(8,128)S(1)}, f32[512,128]{1,0:T(8,128)S(1)}, f32[24,128]{1,0:T(8,128)S(1)}, f32[2,256,256]{2,1,0:T(8,128)S(1)}, /*index=5*/f32[128,512]{1,0:T(8,128)S(1)}) custom-call(f32[512,128]{1,0:T(8,128)S(1)} %get-tuple-element.81.pts_ref, f32[32,128]{1,0:T(8,128)S(1)} %get-tuple-element.80.sel_ref), custom_call_target="tpu_custom_call" | custom-call | tf_op jit(solution)/shard_map/weights/pallas_call | solution.py:694
  27.0 0.3 collective-permute-done.8.other_ref
  27.4 1.2 %loads.1 = (f32[512,384]{1,0:T(8,128)S(1)}, f32[40,128]{1,0:T(8,128)S(1)}, f32[384,128]{1,0:T(8,128)S(1)}) custom-call(f32[8,512]{1,0:T(8,128)S(1)} %get-tuple-element.79.samp_ref, f32[8,512]{1,0:T(8,128)S(1)} %collective-permute-done.8.other_ref, f32[32,128]{1,0:T(8,128)S(1)} %get-tuple-element.80.sel_ref, f32[512,128]{1,0:T(8,128)S(1)} %get-tuple-element.82.pz_ref, ...), custom_call_target="tpu_custom_call" | custom-call | tf_op jit(solution)/shard_map/loads/pallas_call | solution.py:700
  28.6 2.7 %collective-permute-start.11 = (f32[40,128]{1,0:T(8,128)S(1)}, f32[40,128]{1,0:T(8,128)S(1)}, u32[]{:S(2)}, u32[]{:S(2)}) collective-permute-start(f32[40,128]{1,0:T(8,128)S(1)} %get-tuple-element.87), channel_id=1, source_target_pairs={{0,3},{1,2},{2,1},{3,0},{4,7},{5,6},{6,5},{7,4},{8,11},{9,10},{10,... | collective-permute-start | bytes 61448 | tf_op jit(solution)/shard_map/ppermute | solution.py:635
  31.3 1.7 %collective-permute-start.9 = (f32[16,128]{1,0:T(8,128)S(1)}, f32[16,128]{1,0:T(8,128)S(1)}, u32[]{:S(2)}, u32[]{:S(2)}) collective-permute-start(f32[16,128]{1,0:T(8,128)S(1)} %slice.20), channel_id=1, source_target_pairs={{0,2},{1,3},{2,0},{3,1},{4,6},{5,7},{6,4},{7,5},{8,10},{9,11},{10,... | collective-permute-start | bytes 24584 | tf_op jit(solution)/shard_map/ppermute | solution.py:636
  33.1 1.8 %spread.1.main_low.refs_1_ = f32[3,32,32,128]{3,2,1,0:T(8,128)S(1)} custom-call(f32[512,384]{1,0:T(8,128)S(1)} %get-tuple-element.88.refs_0_.lines_ref, f32[72,512]{1,0:T(8,128)S(1)} %get-tuple-element.89.refs_1_.gx_ref, f32[32,512]{1,0:T(8,128)S(1)} %get-tuple-element.90.refs_2_.gy_ref, f32[3,32,32,128]{3,2,1,0:T(8,128)S(1)} %stencil.2.refs_3_), custom_call_target="tpu_custom_call" | custom-call | tf_op jit(solution)/shard_map/spread/pallas_call | solution.py:710
  34.9 0.2 collective-permute-done.10.rec_c
  35.1 1.9 %near.1 = (f32[432,128]{1,0:T(8,128)S(1)}, f32[432,128]{1,0:T(8,128)S(1)}) custom-call(f32[40,128]{1,0:T(8,128)S(1)} %collective-permute-done.10.rec_c, f32[40,128]{1,0:T(8,128)S(1)} %collective-permute-done.11.rec_d), custom_call_target="tpu_custom_call" | custom-call | tf_op jit(solution)/shard_map/near/pallas_call | solution.py:715
  37.0 0.1 rimpack.1
  37.1 0.7 %collective-permute-start.13 = (f32[208,128]{1,0:T(8,128)S(1)}, f32[208,128]{1,0:T(8,128)S(1)}, u32[]{:S(2)}, u32[]{:S(2)}) collective-permute-start(f32[208,128]{1,0:T(8,128)S(1)} %get-tuple-element.99), channel_id=1, source_target_pairs={{4,8},{12,16},{20,24},{8,4},{16,12},{24,20},{5,9},{13,17},{21,25},... | collective-permute-start | bytes 319496 | tf_op jit(solution)/shard_map/ppermute | solution.py:726
  37.8 2.7 %collective-permute-start.12 = (f32[192,128]{1,0:T(8,128)S(1)}, f32[192,128]{1,0:T(8,128)S(1)}, u32[]{:S(2)}, u32[]{:S(2)}) collective-permute-start(f32[192,128]{1,0:T(8,128)S(1)} %get-tuple-element.98), channel_id=1, source_target_pairs={{0,4},{4,0},{8,12},{12,8},{16,20},{20,16},{24,28},{28,24},{1,5},{5... | collective-permute-start | bytes 294920 | tf_op jit(solution)/shard_map/ppermute | solution.py:619
  40.5 3.6 %collective-permute-start.14 = (f32[16,128]{1,0:T(8,128)S(1)}, f32[16,128]{1,0:T(8,128)S(1)}, u32[]{:S(2)}, u32[]{:S(2)}) collective-permute-start(f32[16,128]{1,0:T(8,128)S(1)} %get-tuple-element.100), channel_id=1, source_target_pairs={{0,16},{8,24},{16,0},{24,8},{4,28},{28,4},{1,17},{9,25},{17,1},{25... | collective-permute-start | bytes 24584 | tf_op jit(solution)/shard_map/ppermute | solution.py:727
  44.1 2.9 %low.1 = (f32[3,32,32,128]{3,2,1,0:T(8,128)S(1)}, f32[3,64,32,128]{3,2,1,0:T(8,128)}) custom-call(f32[512,384]{1,0:T(8,128)S(1)} %get-tuple-element.88.refs_0_.lines_ref, f32[72,512]{1,0:T(8,128)S(1)} %get-tuple-element.89.refs_1_.gx_ref, f32[32,512]{1,0:T(8,128)S(1)} %get-tuple-element.90.refs_2_.gy_ref, f32[3,32,32,128]{3,2,1,0:T(8,128)S(1)} %stencil.3.base_ref, ...), custom_call_target="tpu_custom_call" | custom-call | tf_op jit(solution)/shard_map/low/pallas_call | solution.py:731
  47.0 0.1 collective-permute-start.15
  47.1 1.2 %high.1.refs_0_ = f32[3,64,32,128]{3,2,1,0:T(8,128)} custom-call(f32[3,64,32,128]{3,2,1,0:T(8,128)} %get-tuple-element.107._, f32[3,32,32,128]{3,2,1,0:T(8,128)S(1)} %get-tuple-element.108.main_high.refs_2_, f32[2,64,128]{2,1,0:T(8,128)S(1)} %get-tuple-element.103.y_ref.refs_4_, ...), custom_call_target="tpu_custom_call", output_to_operand_aliasing={{}: (0, {})} | custom-call | tf_op jit(solution)/shard_map/high/pallas_call | solution.py:742
  48.4 1.4 %final.1 = (f32[3,64,32,128]{3,2,1,0:T(8,128)}, f32[3,256]{1,0:T(4,128)}) custom-call(f32[3,64,32,128]{3,2,1,0:T(8,128)} %high.1.refs_0_, f32[3,32,32,128]{3,2,1,0:T(8,128)S(1)} %spread.1.main_low.refs_1_, f32[3,32,32,128]{3,2,1,0:T(8,128)S(1)} %get-tuple-element.108.main_high.refs_2_, ...), custom_call_target="tpu_custom_call", output_to_operand_aliasing={{0}: (0, {})} | custom-call | tf_op jit(solution)/shard_map/final/pallas_call | solution.py:754
  (32 shorter events, 0.1 us)
Async XLA Ops:
  0.6 8.3 %copy-start = (f32[3,64,32,128]{3,2,1,0:T(8,128)S(1)}, f32[3,64,32,128]{3,2,1,0:T(8,128)}, u32[]{:S(2)}) copy-start(f32[3,64,32,128]{3,2,1,0:T(8,128)} %v_ref.5) | copy-start | bytes 9437188
  3.3 7.7 %copy-start.1 = (s32[3,512]{1,0:T(4,128)S(1)}, s32[3,512]{1,0:T(4,128)}, u32[]{:S(2)}) copy-start(s32[3,512]{1,0:T(4,128)} %cell_ref.1) | copy-start | bytes 18436
  3.3 7.7 %copy-start.2 = (f32[3,512]{1,0:T(4,128)S(1)}, f32[3,512]{1,0:T(4,128)}, u32[]{:S(2)}) copy-start(f32[3,512]{1,0:T(4,128)} %frac_ref.1) | copy-start | bytes 18436
  3.3 11.2 %collective-permute-start = (f32[208,128]{1,0:T(8,128)}, f32[208,128]{1,0:T(8,128)S(1)}, u32[]{:S(2)}, u32[]{:S(2)}) collective-permute-start(f32[208,128]{1,0:T(8,128)} %get-tuple-element.60), channel_id=1, source_target_pairs={{0,1},{1,0},{2,3},{3,2},{4,5},{5,4},{6,7},{7,6},{8,9},{9,8},{10,11... | collective-permute-start | bytes 319496 | tf_op jit(solution)/shard_map/ppermute | solution.py:634
  6.4 8.1 %collective-permute-start.1 = (f32[208,128]{1,0:T(8,128)}, f32[208,128]{1,0:T(8,128)S(1)}, u32[]{:S(2)}, u32[]{:S(2)}) collective-permute-start(f32[208,128]{1,0:T(8,128)} %get-tuple-element.61), channel_id=1, source_target_pairs={{0,3},{1,2},{2,1},{3,0},{4,7},{5,6},{6,5},{7,4},{8,11},{9,10},{10,... | collective-permute-start | bytes 319496 | tf_op jit(solution)/shard_map/ppermute | solution.py:635
  8.9 5.7 %copy-start.3 = (f32[16,128]{1,0:T(8,128)S(1)}, f32[16,128]{1,0:T(8,128)}, u32[]{:S(2)}) copy-start(f32[16,128]{1,0:T(8,128)} %get-tuple-element.62) | copy-start | bytes 24580
  8.9 5.6 %collective-permute-start.2 = (f32[16,128]{1,0:T(8,128)}, f32[16,128]{1,0:T(8,128)S(1)}, u32[]{:S(2)}, u32[]{:S(2)}) collective-permute-start(f32[16,128]{1,0:T(8,128)} %get-tuple-element.62), channel_id=1, source_target_pairs={{0,2},{1,3},{2,0},{3,1},{4,6},{5,7},{6,4},{7,5},{8,10},{9,11},{10,... | collective-permute-start | bytes 24584 | tf_op jit(solution)/shard_map/ppermute | solution.py:636
  14.5 2.0 %collective-permute-start.3 = (f32[64,128]{1,0:T(8,128)S(1)}, f32[64,128]{1,0:T(8,128)S(1)}, u32[]{:S(2)}, u32[]{:S(2)}) collective-permute-start(f32[64,128]{1,0:T(8,128)S(1)} %pad_maximum_fusion.refs_3_), channel_id=1, source_target_pairs={{0,4},{4,0},{8,12},{12,8},{16,20},{20,16},{24,28},{28,24},{1,5},{5... | collective-permute-start | bytes 98312 | tf_op jit(solution)/shard_map/ppermute | solution.py:619
  16.7 7.1 %collective-permute-start.5 = (f32[152,128]{1,0:T(8,128)S(1)}, f32[152,128]{1,0:T(8,128)S(1)}, u32[]{:S(2)}, u32[]{:S(2)}) collective-permute-start(f32[152,128]{1,0:T(8,128)S(1)} %get-tuple-element.69), channel_id=1, source_target_pairs={{4,8},{12,16},{20,24},{28,0},{8,4},{16,12},{24,20},{0,28},{5,9},{1... | collective-permute-start | bytes 233480 | tf_op jit(solution)/shard_map/ppermute | solution.py:682
  19.3 4.5 %collective-permute-start.4 = (f32[120,128]{1,0:T(8,128)S(1)}, f32[120,128]{1,0:T(8,128)S(1)}, u32[]{:S(2)}, u32[]{:S(2)}) collective-permute-start(f32[120,128]{1,0:T(8,128)S(1)} %get-tuple-element.68), channel_id=1, source_target_pairs={{0,4},{4,0},{8,12},{12,8},{16,20},{20,16},{24,28},{28,24},{1,5},{5... | collective-permute-start | bytes 184328 | tf_op jit(solution)/shard_map/ppermute | solution.py:619
  19.3 4.4 %collective-permute-start.6 = (f32[32,128]{1,0:T(8,128)S(1)}, f32[32,128]{1,0:T(8,128)S(1)}, u32[]{:S(2)}, u32[]{:S(2)}) collective-permute-start(f32[32,128]{1,0:T(8,128)S(1)} %get-tuple-element.70), channel_id=1, source_target_pairs={{0,16},{4,20},{8,24},{12,28},{16,0},{20,4},{24,8},{28,12},{1,17},{... | collective-permute-start | bytes 49160 | tf_op jit(solution)/shard_map/ppermute | solution.py:616
  19.9 3.9 %collective-permute-start.7 = (f32[32,128]{1,0:T(8,128)S(1)}, f32[32,128]{1,0:T(8,128)S(1)}, u32[]{:S(2)}, u32[]{:S(2)}) collective-permute-start(f32[32,128]{1,0:T(8,128)S(1)} %get-tuple-element.71), channel_id=1, source_target_pairs={{0,24},{4,12},{8,0},{12,20},{16,8},{20,28},{24,16},{28,4},{1,25},{... | collective-permute-start | bytes 49160 | tf_op jit(solution)/shard_map/ppermute | solution.py:616
  26.1 1.2 %collective-permute-start.8 = (f32[8,512]{1,0:T(8,128)S(1)}, f32[8,512]{1,0:T(8,128)S(1)}, u32[]{:S(2)}, u32[]{:S(2)}) collective-permute-start(f32[8,512]{1,0:T(8,128)S(1)} %get-tuple-element.79.samp_ref), channel_id=1, source_target_pairs={{0,4},{4,0},{8,12},{12,8},{16,20},{20,16},{24,28},{28,24},{1,5},{5... | collective-permute-start | bytes 49160 | tf_op jit(solution)/shard_map/ppermute | solution.py:619
  28.6 6.3 %collective-permute-start.11 = (f32[40,128]{1,0:T(8,128)S(1)}, f32[40,128]{1,0:T(8,128)S(1)}, u32[]{:S(2)}, u32[]{:S(2)}) collective-permute-start(f32[40,128]{1,0:T(8,128)S(1)} %get-tuple-element.87), channel_id=1, source_target_pairs={{0,3},{1,2},{2,1},{3,0},{4,7},{5,6},{6,5},{7,4},{8,11},{9,10},{10,... | collective-permute-start | bytes 61448 | tf_op jit(solution)/shard_map/ppermute | solution.py:635
  31.3 3.8 %collective-permute-start.10 = (f32[40,128]{1,0:T(8,128)S(1)}, f32[40,128]{1,0:T(8,128)S(1)}, u32[]{:S(2)}, u32[]{:S(2)}) collective-permute-start(f32[40,128]{1,0:T(8,128)S(1)} %get-tuple-element.87), channel_id=1, source_target_pairs={{0,1},{1,0},{2,3},{3,2},{4,5},{5,4},{6,7},{7,6},{8,9},{9,8},{10,11... | collective-permute-start | bytes 61448 | tf_op jit(solution)/shard_map/ppermute | solution.py:634
  31.3 5.7 %collective-permute-start.9 = (f32[16,128]{1,0:T(8,128)S(1)}, f32[16,128]{1,0:T(8,128)S(1)}, u32[]{:S(2)}, u32[]{:S(2)}) collective-permute-start(f32[16,128]{1,0:T(8,128)S(1)} %slice.20), channel_id=1, source_target_pairs={{0,2},{1,3},{2,0},{3,1},{4,6},{5,7},{6,4},{7,5},{8,10},{9,11},{10,... | collective-permute-start | bytes 24584 | tf_op jit(solution)/shard_map/ppermute | solution.py:636
  37.1 9.9 %collective-permute-start.13 = (f32[208,128]{1,0:T(8,128)S(1)}, f32[208,128]{1,0:T(8,128)S(1)}, u32[]{:S(2)}, u32[]{:S(2)}) collective-permute-start(f32[208,128]{1,0:T(8,128)S(1)} %get-tuple-element.99), channel_id=1, source_target_pairs={{4,8},{12,16},{20,24},{8,4},{16,12},{24,20},{5,9},{13,17},{21,25},... | collective-permute-start | bytes 319496 | tf_op jit(solution)/shard_map/ppermute | solution.py:726
  37.8 9.2 %collective-permute-start.12 = (f32[192,128]{1,0:T(8,128)S(1)}, f32[192,128]{1,0:T(8,128)S(1)}, u32[]{:S(2)}, u32[]{:S(2)}) collective-permute-start(f32[192,128]{1,0:T(8,128)S(1)} %get-tuple-element.98), channel_id=1, source_target_pairs={{0,4},{4,0},{8,12},{12,8},{16,20},{20,16},{24,28},{28,24},{1,5},{5... | collective-permute-start | bytes 294920 | tf_op jit(solution)/shard_map/ppermute | solution.py:619
  40.5 6.5 %collective-permute-start.14 = (f32[16,128]{1,0:T(8,128)S(1)}, f32[16,128]{1,0:T(8,128)S(1)}, u32[]{:S(2)}, u32[]{:S(2)}) collective-permute-start(f32[16,128]{1,0:T(8,128)S(1)} %get-tuple-element.100), channel_id=1, source_target_pairs={{0,16},{8,24},{16,0},{24,8},{4,28},{28,4},{1,17},{9,25},{17,1},{25... | collective-permute-start | bytes 24584 | tf_op jit(solution)/shard_map/ppermute | solution.py:727
  47.0 1.3 %collective-permute-start.15 = (f32[32,128]{1,0:T(8,128)S(1)}, f32[32,128]{1,0:T(8,128)S(1)}, u32[]{:S(2)}, u32[]{:S(2)}) collective-permute-start(f32[32,128]{1,0:T(8,128)S(1)} %pad_maximum_fusion.2), channel_id=1, source_target_pairs={{0,4},{4,0},{8,12},{12,8},{16,20},{20,16},{24,28},{28,24},{1,5},{5... | collective-permute-start | bytes 49160 | tf_op jit(solution)/shard_map/ppermute | solution.py:619

commit v10 on v9

--- a/solution.py
+++ b/solution.py
@@ -122,7 +122,7 @@
         jnp.cos(angle),
         jnp.sin(angle),
         held_int[...].astype(F32),
-        jnp.full((1, CZ), spin_ref[0], F32),
+        jnp.broadcast_to(spin_ref[...], (1, CZ)),
         jnp.full((1, CZ), brick.astype(F32), F32),
     ]
     block = jnp.concatenate(parts, axis=0)
@@ -395,7 +395,7 @@
             for h in range(2):
                 at = t * P_SIZE + h * CZ
                 pieces.append(force[c][:, at : at + CZ])
-        pieces += [sel_ref[t * ROWS + 15 : t * ROWS + 16] + 1.0] * 2
+        pieces += [sel_ref[t * ROWS + 15 : t * ROWS + 16]] * 2
     blocks = jnp.concatenate(pieces, axis=0)
     pay_ref[0 : 2 * BACK] = blocks
     pay_ref[2 * BACK :] = pos_ref[...]
@@ -483,13 +483,12 @@
         chips = ny * 2
         side = jnp.where(even_x, -chips, chips)
         total = lax.axis_size("gx") * ny
-        closing = jnp.where(b0 < chips, total - chips, chips)
         for ref, at, target in (
             (pay_b, RIM_X, lax.rem(b0 + side + total, total)),
-            (others[0], 0, lax.rem(b0 + jnp.where(even_x, 2 * chips, closing), total)),
+            (others[0], 0, lax.rem(b0 + 2 * chips, total)),
         ):
             for core in range(2):
-                wanted = (target + core * ny + 1).astype(F32)
+                wanted = (target + core * ny).astype(F32)
                 found = jnp.full((BACK, CZ), -1.0, F32)
                 for k in range(back.shape[0] // BACK):
                     value = back[k * BACK : (k + 1) * BACK]
@@ -523,25 +522,12 @@
     return pltpu.make_async_copy(buf.at[:, pl.ds(at, size)], out_ref.at[:, pl.ds(first, size)], sem)
 
 
-def low_body(lines_ref, gx_ref, gy_ref, base_ref, main_low, y_ref, rec_c, rec_d, rim_low, rim_high, main_ref, out_ref, buf, sems):
+def inside_body(main_low, main_high, y_ref, rec_c, rec_d, rim_low, rim_high, out_ref, buf, sems):
     _, even_y, _, _, _, _ = place()
     copies = []
-    for k, (first, size) in enumerate(INNER[: N_CHUNK // 2]):
-        face_terms(buf, first - 2, first, size, main_low, None, y_ref, rec_c, rec_d, rim_low, rim_high, even_y)
+    for k, (first, size) in enumerate(INNER):
+        face_terms(buf, first - 2, first, size, main_low, main_high, y_ref, rec_c, rec_d, rim_low, rim_high, even_y)
         copies.append(chunk_copy(buf, first - 2, out_ref, first, size, sems.at[k]))
-        copies[-1].start()
-    spread_body(CX // 2, lines_ref, gx_ref, gy_ref, base_ref, main_ref)
-    for copy in copies:
-        copy.wait()
-
-
-def high_body(_, main_high, y_ref, rec_c, rec_d, rim_low, rim_high, out_ref, buf, sems):
-    _, even_y, _, _, _, _ = place()
-    copies = []
-    for k, (first, size) in enumerate(INNER[N_CHUNK // 2 :]):
-        at = first - CX // 2
-        face_terms(buf, at, first, size, None, main_high, y_ref, rec_c, rec_d, rim_low, rim_high, even_y)
-        copies.append(chunk_copy(buf, at, out_ref, first, size, sems.at[k]))
         copies[-1].start()
     for copy in copies:
         copy.wait()
@@ -572,7 +558,7 @@
                     buf[c, 2 + i] += jnp.where(even_x, a, b)
         copies.append(chunk_copy(buf, at, out_ref, first, 2, sems.at[k]))
         copies[-1].start()
-    mine = (brick + 1).astype(F32)
+    mine = brick.astype(F32)
     found = jnp.zeros((BACK, CZ), F32)
     for ref, first in [(back_ref, 0), (rim_b, RIM_X)] + [(r, 0) for r in rets]:
         for k in range((ref.shape[0] - first) // BACK):
@@ -609,9 +595,6 @@
     def same_side(n):
         return [(i, (i + (2 if i % 2 else n - 2)) % n) for i in range(n)]
 
-    def opposite(n):
-        return [(i, (i + n // 2) % n) for i in range(0, n, 2)] + [(1, n - 1), (n - 1, 1)]
-
     def across_x(blocks):
         return [lax.ppermute(b, "gx", p) for b, p in zip(blocks, (flip(nx, 4), same_side(nx)))]
 
@@ -653,10 +636,10 @@
         [(FACE_Y + ROWS, CZ)] * 2 + [(ROWS, CZ)],
         7,
         "pack",
-        scratch=[pltpu.VMEM((4, 2, CZ), F32), pltpu.VMEM((2, CZ), jnp.int32), pltpu.SMEM((1,), F32), dma((12,))],
+        scratch=[pltpu.VMEM((4, 2, CZ), F32), pltpu.VMEM((2, CZ), jnp.int32), pltpu.VMEM((1, 1), F32), dma((12,))],
         in_specs=[HB] * 7,
         vmem=56,
-    )(velocity, rotor_speed, *[a.reshape(2, CZ) for a in (blade_radius, blade_chord, blade_twist, blade_angle, owner_src)])
+    )(velocity, rotor_speed.reshape(1, 1), *[a.reshape(2, CZ) for a in (blade_radius, blade_chord, blade_twist, blade_angle, owner_src)])
     rec_c, rec_d, far = exchange_y(pay_c, pay_d, block)
 
     def stencil(start):
@@ -723,32 +706,22 @@
         3 + len(pieces),
         "rimpack",
     )(xrim, rim_low, rim_high, *pieces)
-    rim_b = lax.ppermute(pay_b, "gx", odd_pairs(nx))
-    rets = [lax.ppermute(across[0], "gx", opposite(nx))] if ring else gather_x(back)
+    rim_b = lax.ppermute(pay_b, "gx", odd_pairs(nx, ring))
+    rets = [lax.ppermute(across[0], "gx", flip(nx, 4))] if ring else gather_x(back)
     rim_a = swap(pay_a)
-    faces = (y_faces, rec_c, rec_d, rim_low, rim_high)
-    half_buf = pltpu.VMEM((3, CX // 2 - 2, CY, CZ), F32)
-    main_high, inside = call(
-        low_body,
-        [(3, CX // 2, CY, CZ), velocity.shape],
-        10,
-        "low",
-        scratch=[half_buf, dma((N_CHUNK // 2,))],
-        out_specs=[VM, HB],
-    )(lines, gx, gy, base_high, main_low, *faces)
-    (rim_a, rim_b, rets), inside = after((rim_a, rim_b, rets), inside)
+    main_high = spread(CX // 2, base_high)
+    (rim_a, rim_b), (main_low, main_high) = after((rim_a, rim_b), (main_low, main_high))
     if ring:
-        rets.append(swap(join([rim_b[RIM_X:]] + rets)))
+        rets.append(swap(rim_b[RIM_X:]))
     inside = call(
-        high_body,
+        inside_body,
         [velocity.shape],
         7,
-        "high",
-        scratch=[half_buf, dma((N_CHUNK // 2,))],
-        first=HB,
+        "inside",
+        scratch=[pltpu.VMEM((3, CX - 4, CY, CZ), F32), dma((N_CHUNK,))],
         out_specs=[HB],
-        aliases={0: 0},
-    )(inside, main_high, *faces)[0]
+        vmem=16,
+    )(main_low, main_high, y_faces, rec_c, rec_d, rim_low, rim_high)[0]
     rets, inside = after(rets, inside)
     return tuple(
         call(

time: 50.2 us -> 46.5 us (0.926)
  starting transfers between devices: 21.9 us -> 17.9 us
  waiting for transfers between devices: 1.55 us -> 2.79 us
  Pallas kernels: 24.5 us -> 23.9 us
    pallas_call x2 -> x1, Pallas kernels: 4.16 us -> 1.73 us  [per_device(): call(inside_body, [velocity.shape], 7, 'inside', scratch=[pltpu.VMEM((3,...]
    ppermute x5, starting transfers between devices: 2.88 us -> 0.55 us  [swap(): return lax.ppermute(block, 'gx', flip(nx, 1))]
    pallas_call x1 -> x2, Pallas kernels: 1.8 us -> 3.63 us  [spread(): call(lambda *refs: spread_body(start, *refs), [(3, CX // 2, CY, CZ)], 4,...]
    ppermute x2, starting transfers between devices: 4.26 us -> 2.55 us  [the longest x1 1.54 us: per_device(): lax.ppermute(across[0], 'gx', flip(nx, 4))]
    ppermute x2, waiting for transfers between devices: 0.01 us -> 1.26 us  [the longest x1 1.26 us: per_device(): rim_b = lax.ppermute(pay_b, 'gx', odd_pairs(nx, ring))]
  transfers between devices with their start and end apart: 16 -> 16, of which waited for: 3 -> 4; matrix products, arithmetic and copies ran while one was open for 0% -> 0% of each run, Pallas kernels for 35% -> 37%
where the time goes in v10:
time: 46.5 us; the launch traced here: 46.3 us
  Pallas kernels  23.9 us (51%)
  starting transfers between devices  17.9 us (38%)
  waiting for transfers between devices  2.79 us (6%)
  between operations  1.68 us (4%)
    ppermute x2, starting transfers between devices, exchange_y(): from_d = lax.ppermute(to_d, 'gy', flip(ny, 3) if short else odd_pairs(ny))  5.18 us
    pallas_call x2, Pallas kernels, stencil(): call(lambda *refs: stencil_body(start, *refs), [(3, CX // 2, CY, CZ)], 1,...  3.9 us
    pallas_call x2, Pallas kernels, spread(): call(lambda *refs: spread_body(start, *refs), [(3, CX // 2, CY, CZ)], 4,...  3.63 us
    ppermute x2, starting transfers between devices, exchange_y(): from_c = lax.ppermute(to_c, 'gy', flip(ny, 1))  3.1 us
    ppermute x1, starting transfers between devices, per_device(): face_b = lax.ppermute(pay_b, 'gx', odd_pairs(nx, ring))  2.61 us
    pallas_call x1, Pallas kernels, per_device(): call(sample_low_body, [(HOST, CZ), (HOST, 3 * CZ), (6, CY, CZ), (2, CX, C...  2.59 us
    pallas_call x1, Pallas kernels, per_device(): call(sample_high_body, [(HOST, 3 * CZ)], 3, 'sample_high', vmem=24)  2.41 us
    pallas_call x1, Pallas kernels, per_device(): call(lambda *refs: select_body(len(from_x), *refs), [(8, PTS), (2 * ROWS,...  2.33 us
  transfers between devices with their start and end apart: 16, of which 4 were waited for; matrix products, arithmetic and copies ran while one was open for 0% of the time, Pallas kernels for 37%

profile of v10, /device:TPU:0, one launch (start us, length us, event | category | flops | bytes accessed | tf_op | source)
XLA Modules:
  0.0 46.3 jit_solution(6629324040821058872)
XLA Ops:
  1.3 1.9 %pack.1 = (f32[208,128]{1,0:T(8,128)}, f32[208,128]{1,0:T(8,128)}, f32[16,128]{1,0:T(8,128)}) custom-call(f32[3,64,32,128]{3,2,1,0:T(8,128)} %v_ref.5, f32[1,1]{1,0:T(1,128)} %bitcast.6.spin_hbm, f32[2,128]{1,0:T(2,128)} %bitcast.7, f32[2,128]{1,0:T(2,128)} %bitcast.8, f32[2,128]{1,0:T(2,128)} %bitcast.9, f32[2,128]{1,0:T(2,128)} %bitcast.10, s32[2,128]{1,0:T(2,128)} %bitcast.11), custom_call_target="tpu_custom_call" | custom-call | tf_op jit(solution)/shard_map/pack/pallas_call | solution.py:634
  3.1 3.1 %collective-permute-start = (f32[208,128]{1,0:T(8,128)}, f32[208,128]{1,0:T(8,128)S(1)}, u32[]{:S(2)}, u32[]{:S(2)}) collective-permute-start(f32[208,128]{1,0:T(8,128)} %get-tuple-element.58), channel_id=1, source_target_pairs={{0,1},{1,0},{2,3},{3,2},{4,5},{5,4},{6,7},{7,6},{8,9},{9,8},{10,11... | collective-permute-start | bytes 319496 | tf_op jit(solution)/shard_map/ppermute | solution.py:617
  6.2 2.5 %collective-permute-start.1 = (f32[208,128]{1,0:T(8,128)}, f32[208,128]{1,0:T(8,128)S(1)}, u32[]{:S(2)}, u32[]{:S(2)}) collective-permute-start(f32[208,128]{1,0:T(8,128)} %get-tuple-element.59), channel_id=1, source_target_pairs={{0,3},{1,2},{2,1},{3,0},{4,7},{5,6},{6,5},{7,4},{8,11},{9,10},{10,... | collective-permute-start | bytes 319496 | tf_op jit(solution)/shard_map/ppermute | solution.py:618
  8.7 0.1 collective-permute-start.2
  8.8 1.9 %stencil.2.refs_3_ = f32[3,32,32,128]{3,2,1,0:T(8,128)S(1)} custom-call(f32[3,64,32,128]{3,2,1,0:T(8,128)S(1)} %copy-done), custom_call_target="tpu_custom_call" | custom-call | tf_op jit(solution)/shard_map/stencil/pallas_call | solution.py:646
  10.8 2.6 %sample_low.1 = (f32[512,128]{1,0:T(8,128)S(1)}, f32[512,384]{1,0:T(8,128)S(1)}, f32[6,32,128]{2,1,0:T(8,128)S(1)}, f32[2,64,128]{2,1,0:T(8,128)S(1)}) custom-call(f32[3,64,32,128]{3,2,1,0:T(8,128)S(1)} %copy-done, s32[3,512]{1,0:T(4,128)S(1)} %copy-done.1, f32[3,512]{1,0:T(4,128)S(1)} %copy-done.2), custom_call_target="tpu_custom_call" | custom-call | tf_op jit(solution)/shard_map/sample_low/pallas_call | solution.py:649
  13.4 0.9 %collective-permute-done.2 = f32[16,128]{1,0:T(8,128)S(1)} collective-permute-done((f32[16,128]{1,0:T(8,128)}, f32[16,128]{1,0:T(8,128)S(1)}, u32[]{:S(2)}, u32[]{:S(2)}) %collective-permute-start.2) | collective-permute-done | bytes 8224 | tf_op jit(solution)/shard_map/ppermute | solution.py:619
  14.4 0.1 collective-permute-start.3
  14.5 1.9 %stencil.3.refs_3_ = f32[3,32,32,128]{3,2,1,0:T(8,128)S(1)} custom-call(f32[3,64,32,128]{3,2,1,0:T(8,128)S(1)} %copy-done), custom_call_target="tpu_custom_call" | custom-call | tf_op jit(solution)/shard_map/stencil/pallas_call | solution.py:646
  16.4 0.1 xpack.1
  16.6 2.6 %collective-permute-start.5 = (f32[152,128]{1,0:T(8,128)S(1)}, f32[152,128]{1,0:T(8,128)S(1)}, u32[]{:S(2)}, u32[]{:S(2)}) collective-permute-start(f32[152,128]{1,0:T(8,128)S(1)} %get-tuple-element.67), channel_id=1, source_target_pairs={{4,8},{12,16},{20,24},{28,0},{8,4},{16,12},{24,20},{0,28},{5,9},{1... | collective-permute-start | bytes 233480 | tf_op jit(solution)/shard_map/ppermute | solution.py:665
  19.2 0.6 %collective-permute-start.6 = (f32[32,128]{1,0:T(8,128)S(1)}, f32[32,128]{1,0:T(8,128)S(1)}, u32[]{:S(2)}, u32[]{:S(2)}) collective-permute-start(f32[32,128]{1,0:T(8,128)S(1)} %get-tuple-element.68), channel_id=1, source_target_pairs={{0,16},{4,20},{8,24},{12,28},{16,0},{20,4},{24,8},{28,12},{1,17},{... | collective-permute-start | bytes 49160 | tf_op jit(solution)/shard_map/ppermute | solution.py:599
  19.8 1.4 %collective-permute-start.7 = (f32[32,128]{1,0:T(8,128)S(1)}, f32[32,128]{1,0:T(8,128)S(1)}, u32[]{:S(2)}, u32[]{:S(2)}) collective-permute-start(f32[32,128]{1,0:T(8,128)S(1)} %get-tuple-element.69), channel_id=1, source_target_pairs={{0,24},{4,12},{8,0},{12,20},{16,8},{20,28},{24,16},{28,4},{1,25},{... | collective-permute-start | bytes 49160 | tf_op jit(solution)/shard_map/ppermute | solution.py:599
  21.2 2.4 %sample_high.1.refs_1_ = f32[512,384]{1,0:T(8,128)S(1)} custom-call(f32[3,64,32,128]{3,2,1,0:T(8,128)S(1)} %copy-done, f32[512,128]{1,0:T(8,128)S(1)} %get-tuple-element.56.tab_ref.refs_0_, f32[512,384]{1,0:T(8,128)S(1)} %get-tuple-element.70.low_ref), custom_call_target="tpu_custom_call" | custom-call | tf_op jit(solution)/shard_map/sample_high/pallas_call | solution.py:668
  23.7 2.3 %select.1 = (f32[8,512]{1,0:T(8,128)S(1)}, f32[32,128]{1,0:T(8,128)S(1)}, f32[512,128]{1,0:T(8,128)S(1)}) custom-call(f32[512,128]{1,0:T(8,128)S(1)} %get-tuple-element.56.tab_ref.refs_0_, f32[512,384]{1,0:T(8,128)S(1)} %sample_high.1.refs_1_, f32[120,128]{1,0:T(8,128)S(1)} %collective-permute-done.4.refs_2_.refs_5_, ...), custom_call_target="tpu_custom_call" | custom-call | tf_op jit(solution)/shard_map/select/pallas_call | solution.py:670
  26.0 0.0 collective-permute-start.8
  26.0 0.8 %weights.1 = (f32[72,512]{1,0:T(8,128)S(1)}, f32[32,512]{1,0:T(8,128)S(1)}, f32[512,128]{1,0:T(8,128)S(1)}, f32[24,128]{1,0:T(8,128)S(1)}, f32[2,256,256]{2,1,0:T(8,128)S(1)}, /*index=5*/f32[128,512]{1,0:T(8,128)S(1)}) custom-call(f32[512,128]{1,0:T(8,128)S(1)} %get-tuple-element.79.pts_ref, f32[32,128]{1,0:T(8,128)S(1)} %get-tuple-element.78.sel_ref), custom_call_target="tpu_custom_call" | custom-call | tf_op jit(solution)/shard_map/weights/pallas_call | solution.py:677
  26.9 0.3 collective-permute-done.8.other_ref
  27.2 1.2 %loads.1 = (f32[512,384]{1,0:T(8,128)S(1)}, f32[40,128]{1,0:T(8,128)S(1)}, f32[384,128]{1,0:T(8,128)S(1)}) custom-call(f32[8,512]{1,0:T(8,128)S(1)} %get-tuple-element.77.samp_ref, f32[8,512]{1,0:T(8,128)S(1)} %collective-permute-done.8.other_ref, f32[32,128]{1,0:T(8,128)S(1)} %get-tuple-element.78.sel_ref, f32[512,128]{1,0:T(8,128)S(1)} %get-tuple-element.80.pz_ref, ...), custom_call_target="tpu_custom_call" | custom-call | tf_op jit(solution)/shard_map/loads/pallas_call | solution.py:683
  28.5 2.7 %collective-permute-start.11 = (f32[40,128]{1,0:T(8,128)S(1)}, f32[40,128]{1,0:T(8,128)S(1)}, u32[]{:S(2)}, u32[]{:S(2)}) collective-permute-start(f32[40,128]{1,0:T(8,128)S(1)} %get-tuple-element.85), channel_id=1, source_target_pairs={{0,3},{1,2},{2,1},{3,0},{4,7},{5,6},{6,5},{7,4},{8,11},{9,10},{10,... | collective-permute-start | bytes 61448 | tf_op jit(solution)/shard_map/ppermute | solution.py:618
  31.2 1.7 %collective-permute-start.9 = (f32[16,128]{1,0:T(8,128)S(1)}, f32[16,128]{1,0:T(8,128)S(1)}, u32[]{:S(2)}, u32[]{:S(2)}) collective-permute-start(f32[16,128]{1,0:T(8,128)S(1)} %slice.20), channel_id=1, source_target_pairs={{0,2},{1,3},{2,0},{3,1},{4,6},{5,7},{6,4},{7,5},{8,10},{9,11},{10,... | collective-permute-start | bytes 24584 | tf_op jit(solution)/shard_map/ppermute | solution.py:619
  32.9 1.8 %spread.2.main_low.refs_1_ = f32[3,32,32,128]{3,2,1,0:T(8,128)S(1)} custom-call(f32[512,384]{1,0:T(8,128)S(1)} %get-tuple-element.86.refs_0_, f32[72,512]{1,0:T(8,128)S(1)} %get-tuple-element.87.refs_1_, f32[32,512]{1,0:T(8,128)S(1)} %get-tuple-element.88.refs_2_, f32[3,32,32,128]{3,2,1,0:T(8,128)S(1)} %stencil.2.refs_3_), custom_call_target="tpu_custom_call" | custom-call | tf_op jit(solution)/shard_map/spread/pallas_call | solution.py:693
  34.8 0.2 collective-permute-done.10.rec_c
  35.0 1.9 %near.1 = (f32[432,128]{1,0:T(8,128)S(1)}, f32[432,128]{1,0:T(8,128)S(1)}) custom-call(f32[40,128]{1,0:T(8,128)S(1)} %collective-permute-done.10.rec_c, f32[40,128]{1,0:T(8,128)S(1)} %collective-permute-done.11.rec_d), custom_call_target="tpu_custom_call" | custom-call | tf_op jit(solution)/shard_map/near/pallas_call | solution.py:698
  36.9 0.1 rimpack.1
  37.0 1.0 %collective-permute-start.14 = (f32[208,128]{1,0:T(8,128)S(1)}, f32[208,128]{1,0:T(8,128)S(1)}, u32[]{:S(2)}, u32[]{:S(2)}) collective-permute-start(f32[208,128]{1,0:T(8,128)S(1)} %get-tuple-element.98), channel_id=1, source_target_pairs={{4,8},{12,16},{20,24},{28,0},{8,4},{16,12},{24,20},{0,28},{5,9},{1... | collective-permute-start | bytes 319496 | tf_op jit(solution)/shard_map/ppermute | solution.py:709
  38.0 0.4 collective-permute-start.13
  38.4 1.8 %spread.3.main_high.refs_2_ = f32[3,32,32,128]{3,2,1,0:T(8,128)S(1)} custom-call(f32[512,384]{1,0:T(8,128)S(1)} %get-tuple-element.86.refs_0_, f32[72,512]{1,0:T(8,128)S(1)} %get-tuple-element.87.refs_1_, f32[32,512]{1,0:T(8,128)S(1)} %get-tuple-element.88.refs_2_, f32[3,32,32,128]{3,2,1,0:T(8,128)S(1)} %stencil.3.refs_3_), custom_call_target="tpu_custom_call" | custom-call | tf_op jit(solution)/shard_map/spread/pallas_call | solution.py:693
  40.2 1.5 %collective-permute-start.12 = (f32[16,128]{1,0:T(8,128)S(1)}, f32[16,128]{1,0:T(8,128)S(1)}, u32[]{:S(2)}, u32[]{:S(2)}) collective-permute-start(f32[16,128]{1,0:T(8,128)S(1)} %get-tuple-element.96), channel_id=1, source_target_pairs={{0,16},{4,20},{8,24},{12,28},{16,0},{20,4},{24,8},{28,12},{1,17},{... | collective-permute-start | bytes 24584 | tf_op jit(solution)/shard_map/ppermute | solution.py:710
  41.8 1.3 %collective-permute-done.14.refs_10_ = f32[208,128]{1,0:T(8,128)S(1)} collective-permute-done((f32[208,128]{1,0:T(8,128)S(1)}, f32[208,128]{1,0:T(8,128)S(1)}, u32[]{:S(2)}, u32[]{:S(2)}) %collective-permute-start.14) | collective-permute-done | bytes 106528 | tf_op jit(solution)/shard_map/ppermute | solution.py:709
  43.0 1.7 %inside.1.refs_0_ = f32[3,64,32,128]{3,2,1,0:T(8,128)} custom-call(f32[3,32,32,128]{3,2,1,0:T(8,128)S(1)} %spread.2.main_low.refs_1_, f32[3,32,32,128]{3,2,1,0:T(8,128)S(1)} %spread.3.main_high.refs_2_, f32[2,64,128]{2,1,0:T(8,128)S(1)} %get-tuple-element.104.y_ref.refs_4_, f32[208,128]{1,0:T(8,128)S(1)} %collective-permute-done.refs_1_.refs_4_.rec_c.refs_7_, ...), custom_call_target="tpu_custom_call" | custom-call | tf_op jit(solution)/shard_map/inside/pallas_call | solution.py:716
  44.8 1.4 %final.1 = (f32[3,64,32,128]{3,2,1,0:T(8,128)}, f32[3,256]{1,0:T(4,128)}) custom-call(f32[3,64,32,128]{3,2,1,0:T(8,128)} %inside.1.refs_0_, f32[3,32,32,128]{3,2,1,0:T(8,128)S(1)} %spread.2.main_low.refs_1_, f32[3,32,32,128]{3,2,1,0:T(8,128)S(1)} %spread.3.main_high.refs_2_, ...), custom_call_target="tpu_custom_call", output_to_operand_aliasing={{0}: (0, {})} | custom-call | tf_op jit(solution)/shard_map/final/pallas_call | solution.py:727
  (31 shorter events, 0.1 us)
Async XLA Ops:
  1.3 7.6 %copy-start = (f32[3,64,32,128]{3,2,1,0:T(8,128)S(1)}, f32[3,64,32,128]{3,2,1,0:T(8,128)}, u32[]{:S(2)}) copy-start(f32[3,64,32,128]{3,2,1,0:T(8,128)} %v_ref.5) | copy-start | bytes 9437188
  3.1 11.2 %collective-permute-start = (f32[208,128]{1,0:T(8,128)}, f32[208,128]{1,0:T(8,128)S(1)}, u32[]{:S(2)}, u32[]{:S(2)}) collective-permute-start(f32[208,128]{1,0:T(8,128)} %get-tuple-element.58), channel_id=1, source_target_pairs={{0,1},{1,0},{2,3},{3,2},{4,5},{5,4},{6,7},{7,6},{8,9},{9,8},{10,11... | collective-permute-start | bytes 319496 | tf_op jit(solution)/shard_map/ppermute | solution.py:617
  6.2 8.1 %collective-permute-start.1 = (f32[208,128]{1,0:T(8,128)}, f32[208,128]{1,0:T(8,128)S(1)}, u32[]{:S(2)}, u32[]{:S(2)}) collective-permute-start(f32[208,128]{1,0:T(8,128)} %get-tuple-element.59), channel_id=1, source_target_pairs={{0,3},{1,2},{2,1},{3,0},{4,7},{5,6},{6,5},{7,4},{8,11},{9,10},{10,... | collective-permute-start | bytes 319496 | tf_op jit(solution)/shard_map/ppermute | solution.py:618
  8.7 2.1 %copy-start.1 = (s32[3,512]{1,0:T(4,128)S(1)}, s32[3,512]{1,0:T(4,128)}, u32[]{:S(2)}) copy-start(s32[3,512]{1,0:T(4,128)} %cell_ref.1) | copy-start | bytes 18436
  8.7 2.1 %copy-start.2 = (f32[3,512]{1,0:T(4,128)S(1)}, f32[3,512]{1,0:T(4,128)}, u32[]{:S(2)}) copy-start(f32[3,512]{1,0:T(4,128)} %frac_ref.1) | copy-start | bytes 18436
  8.7 5.6 %collective-permute-start.2 = (f32[16,128]{1,0:T(8,128)}, f32[16,128]{1,0:T(8,128)S(1)}, u32[]{:S(2)}, u32[]{:S(2)}) collective-permute-start(f32[16,128]{1,0:T(8,128)} %get-tuple-element.60), channel_id=1, source_target_pairs={{0,2},{1,3},{2,0},{3,1},{4,6},{5,7},{6,4},{7,5},{8,10},{9,11},{10,... | collective-permute-start | bytes 24584 | tf_op jit(solution)/shard_map/ppermute | solution.py:619
  10.8 3.6 %copy-start.3 = (f32[16,128]{1,0:T(8,128)S(1)}, f32[16,128]{1,0:T(8,128)}, u32[]{:S(2)}) copy-start(f32[16,128]{1,0:T(8,128)} %get-tuple-element.60) | copy-start | bytes 24580
  14.4 2.0 %collective-permute-start.3 = (f32[64,128]{1,0:T(8,128)S(1)}, f32[64,128]{1,0:T(8,128)S(1)}, u32[]{:S(2)}, u32[]{:S(2)}) collective-permute-start(f32[64,128]{1,0:T(8,128)S(1)} %pad_maximum_fusion.refs_3_), channel_id=1, source_target_pairs={{0,4},{4,0},{8,12},{12,8},{16,20},{20,16},{24,28},{28,24},{1,5},{5... | collective-permute-start | bytes 98312 | tf_op jit(solution)/shard_map/ppermute | solution.py:602
  16.6 7.1 %collective-permute-start.5 = (f32[152,128]{1,0:T(8,128)S(1)}, f32[152,128]{1,0:T(8,128)S(1)}, u32[]{:S(2)}, u32[]{:S(2)}) collective-permute-start(f32[152,128]{1,0:T(8,128)S(1)} %get-tuple-element.67), channel_id=1, source_target_pairs={{4,8},{12,16},{20,24},{28,0},{8,4},{16,12},{24,20},{0,28},{5,9},{1... | collective-permute-start | bytes 233480 | tf_op jit(solution)/shard_map/ppermute | solution.py:665
  19.2 4.5 %collective-permute-start.4 = (f32[120,128]{1,0:T(8,128)S(1)}, f32[120,128]{1,0:T(8,128)S(1)}, u32[]{:S(2)}, u32[]{:S(2)}) collective-permute-start(f32[120,128]{1,0:T(8,128)S(1)} %get-tuple-element.66), channel_id=1, source_target_pairs={{0,4},{4,0},{8,12},{12,8},{16,20},{20,16},{24,28},{28,24},{1,5},{5... | collective-permute-start | bytes 184328 | tf_op jit(solution)/shard_map/ppermute | solution.py:602
  19.2 4.4 %collective-permute-start.6 = (f32[32,128]{1,0:T(8,128)S(1)}, f32[32,128]{1,0:T(8,128)S(1)}, u32[]{:S(2)}, u32[]{:S(2)}) collective-permute-start(f32[32,128]{1,0:T(8,128)S(1)} %get-tuple-element.68), channel_id=1, source_target_pairs={{0,16},{4,20},{8,24},{12,28},{16,0},{20,4},{24,8},{28,12},{1,17},{... | collective-permute-start | bytes 49160 | tf_op jit(solution)/shard_map/ppermute | solution.py:599
  19.8 3.9 %collective-permute-start.7 = (f32[32,128]{1,0:T(8,128)S(1)}, f32[32,128]{1,0:T(8,128)S(1)}, u32[]{:S(2)}, u32[]{:S(2)}) collective-permute-start(f32[32,128]{1,0:T(8,128)S(1)} %get-tuple-element.69), channel_id=1, source_target_pairs={{0,24},{4,12},{8,0},{12,20},{16,8},{20,28},{24,16},{28,4},{1,25},{... | collective-permute-start | bytes 49160 | tf_op jit(solution)/shard_map/ppermute | solution.py:599
  26.0 1.2 %collective-permute-start.8 = (f32[8,512]{1,0:T(8,128)S(1)}, f32[8,512]{1,0:T(8,128)S(1)}, u32[]{:S(2)}, u32[]{:S(2)}) collective-permute-start(f32[8,512]{1,0:T(8,128)S(1)} %get-tuple-element.77.samp_ref), channel_id=1, source_target_pairs={{0,4},{4,0},{8,12},{12,8},{16,20},{20,16},{24,28},{28,24},{1,5},{5... | collective-permute-start | bytes 49160 | tf_op jit(solution)/shard_map/ppermute | solution.py:602
  28.5 6.3 %collective-permute-start.11 = (f32[40,128]{1,0:T(8,128)S(1)}, f32[40,128]{1,0:T(8,128)S(1)}, u32[]{:S(2)}, u32[]{:S(2)}) collective-permute-start(f32[40,128]{1,0:T(8,128)S(1)} %get-tuple-element.85), channel_id=1, source_target_pairs={{0,3},{1,2},{2,1},{3,0},{4,7},{5,6},{6,5},{7,4},{8,11},{9,10},{10,... | collective-permute-start | bytes 61448 | tf_op jit(solution)/shard_map/ppermute | solution.py:618
  31.2 3.8 %collective-permute-start.10 = (f32[40,128]{1,0:T(8,128)S(1)}, f32[40,128]{1,0:T(8,128)S(1)}, u32[]{:S(2)}, u32[]{:S(2)}) collective-permute-start(f32[40,128]{1,0:T(8,128)S(1)} %get-tuple-element.85), channel_id=1, source_target_pairs={{0,1},{1,0},{2,3},{3,2},{4,5},{5,4},{6,7},{7,6},{8,9},{9,8},{10,11... | collective-permute-start | bytes 61448 | tf_op jit(solution)/shard_map/ppermute | solution.py:617
  31.2 5.7 %collective-permute-start.9 = (f32[16,128]{1,0:T(8,128)S(1)}, f32[16,128]{1,0:T(8,128)S(1)}, u32[]{:S(2)}, u32[]{:S(2)}) collective-permute-start(f32[16,128]{1,0:T(8,128)S(1)} %slice.20), channel_id=1, source_target_pairs={{0,2},{1,3},{2,0},{3,1},{4,6},{5,7},{6,4},{7,5},{8,10},{9,11},{10,... | collective-permute-start | bytes 24584 | tf_op jit(solution)/shard_map/ppermute | solution.py:619
  37.0 6.1 %collective-permute-start.14 = (f32[208,128]{1,0:T(8,128)S(1)}, f32[208,128]{1,0:T(8,128)S(1)}, u32[]{:S(2)}, u32[]{:S(2)}) collective-permute-start(f32[208,128]{1,0:T(8,128)S(1)} %get-tuple-element.98), channel_id=1, source_target_pairs={{4,8},{12,16},{20,24},{28,0},{8,4},{16,12},{24,20},{0,28},{5,9},{1... | collective-permute-start | bytes 319496 | tf_op jit(solution)/shard_map/ppermute | solution.py:709
  38.0 3.8 %collective-permute-start.13 = (f32[192,128]{1,0:T(8,128)S(1)}, f32[192,128]{1,0:T(8,128)S(1)}, u32[]{:S(2)}, u32[]{:S(2)}) collective-permute-start(f32[192,128]{1,0:T(8,128)S(1)} %get-tuple-element.97), channel_id=1, source_target_pairs={{0,4},{4,0},{8,12},{12,8},{16,20},{20,16},{24,28},{28,24},{1,5},{5... | collective-permute-start | bytes 294920 | tf_op jit(solution)/shard_map/ppermute | solution.py:602
  40.2 4.5 %collective-permute-start.12 = (f32[16,128]{1,0:T(8,128)S(1)}, f32[16,128]{1,0:T(8,128)S(1)}, u32[]{:S(2)}, u32[]{:S(2)}) collective-permute-start(f32[16,128]{1,0:T(8,128)S(1)} %get-tuple-element.96), channel_id=1, source_target_pairs={{0,16},{4,20},{8,24},{12,28},{16,0},{20,4},{24,8},{28,12},{1,17},{... | collective-permute-start | bytes 24584 | tf_op jit(solution)/shard_map/ppermute | solution.py:710
  43.0 1.8 %collective-permute-start.15 = (f32[16,128]{1,0:T(8,128)S(1)}, f32[16,128]{1,0:T(8,128)S(1)}, u32[]{:S(2)}, u32[]{:S(2)}) collective-permute-start(f32[16,128]{1,0:T(8,128)S(1)} %slice.23), channel_id=1, source_target_pairs={{0,4},{4,0},{8,12},{12,8},{16,20},{20,16},{24,28},{28,24},{1,5},{5... | collective-permute-start | bytes 24584 | tf_op jit(solution)/shard_map/ppermute | solution.py:602

commit v11 on v10

--- a/solution.py
+++ b/solution.py
@@ -74,6 +74,13 @@
 def dot3(a_high, a_low, b_high, b_low):
     def one(a, b):
         return jnp.dot(a, b, preferred_element_type=F32)
+
+    return one(a_high, b_high) + (one(a_high, b_low) + one(a_low, b_high))
+
+
+def dot3_last(a_high, a_low, b_high, b_low):
+    def one(a, b):
+        return lax.dot_general(a, b, (((1,), (1,)), ((), ())), preferred_element_type=F32)
 
     return one(a_high, b_high) + (one(a_high, b_low) + one(a_low, b_high))
 
@@ -160,7 +167,7 @@
             out_ref[c, k] = (1.0 - 6.0 * visc) * mid + along_x + (along_y + along_z)
         return carry
 
-    lax.fori_loop(0, CX // 2, step, 0, unroll=2)
+    lax.fori_loop(0, out_ref.shape[1], step, 0, unroll=2)
 
 
 def weight(coord, base, frac):
@@ -326,22 +333,13 @@
     return result
 
 
-def line_profile(base, frac, extra):
-    stack = jnp.concatenate(offsets(frac) + [base] + extra + [jnp.zeros((CZ - 5 - len(extra), PTS), F32)], axis=0).T
-    rel = lax.broadcasted_iota(jnp.int32, (PTS, CZ), 1) - stack[:, 4:5].astype(jnp.int32)
-    result = jnp.zeros((PTS, CZ), F32)
-    for k in range(4):
-        result = jnp.where(rel == k - 1, stack[:, k : k + 1], result)
-    return result, [stack[:, 5 + k : 6 + k] for k in range(len(extra))]
-
-
 def weights_body(pts_ref, sel_ref, gx_ref, gy_ref, pz_ref, pos_ref, pair_ref, edge_ref):
     table = pts_ref[...].T
     gx = profile(YROWS, CX, table[0:1], table[3:4])
     gy = profile(CY, CY, table[1:2], table[4:5])
     gx_ref[...] = gx
     gy_ref[...] = gy
-    pz_ref[...] = line_profile(table[2:3], table[5:6], [])[0] * DT_STEP
+    pz_ref[...] = profile(CZ, CZ, table[2:3], table[5:6]) * DT_STEP
     pos_ref[...] = jnp.concatenate([table[q : q + 1, k * CZ : (k + 1) * CZ] for q in range(6) for k in range(4)], axis=0)
     for t in range(2):
         at = t * ROWS
@@ -399,13 +397,12 @@
     blocks = jnp.concatenate(pieces, axis=0)
     pay_ref[0 : 2 * BACK] = blocks
     pay_ref[2 * BACK :] = pos_ref[...]
-    cols = jnp.concatenate(force + [jnp.zeros((CZ - 3, PTS), F32)], axis=0).T
     pz = pz_ref[...]
-    lines = jnp.concatenate([cols[:, c : c + 1] * pz for c in range(3)], axis=1)
+    lines = jnp.concatenate([f * pz for f in force], axis=0)
     l_high, l_low = split(lines)
     lh_ref[...] = lines
     w_high, w_low = split(edge_ref[...])
-    rim = dot3(w_high, w_low, l_high, l_low)
+    rim = dot3_last(w_high, w_low, l_high, l_low)
     for k in range(4):
         for c in range(3):
             at = (k * 3 + c) * CY
@@ -423,8 +420,8 @@
 
         x, y, z, fx, fy, fz = [wide(2 * BACK + 4 * q, range(4)) for q in range(6)]
         force = [wide(2 * c, (0, 1, BACK, BACK + 1)) * DT_STEP for c in range(3)]
-        pz, columns = line_profile(z, fz, force)
-        l_high, l_low = split(jnp.concatenate([col * pz for col in columns], axis=1))
+        pz = profile(CZ, CZ, z, fz)
+        l_high, l_low = split(jnp.concatenate([f * pz for f in force], axis=0))
         gx = profile(YROWS, CX, x, fx)
         wy = offsets(fy)
         planes = []
@@ -435,7 +432,7 @@
                 gy = jnp.where(rel == k - 1, wy[k], gy)
             planes.append(gx * gy)
         w_high, w_low = split(jnp.concatenate(planes, axis=0))
-        rim = dot3(w_high, w_low, l_high, l_low)
+        rim = dot3_last(w_high, w_low, l_high, l_low)
         for i in range(2):
             for c in range(3):
                 at = (i * 3 + c) * YROWS
@@ -445,18 +442,21 @@
 SPREAD_X = 8
 
 
-def spread_body(start, lines_ref, gx_ref, gy_ref, base_ref, out_ref):
+def spread_body(start, lines_ref, gx_ref, gy_ref, *rest):
+    bases, out_ref = rest[:-1], rest[-1]
     l_high, l_low = split(lines_ref[...])
     gy = gy_ref[0:CY]
+    held = bases[0].shape[1]
     for k in range(out_ref.shape[1] // SPREAD_X):
         at = k * SPREAD_X
         first = start + at
         planes = jnp.concatenate([gx_ref[first + i : first + i + 1] * gy for i in range(SPREAD_X)], axis=0)
         w_high, w_low = split(planes)
-        value = dot3(w_high, w_low, l_high, l_low)
+        value = dot3_last(w_high, w_low, l_high, l_low)
+        base, inner = bases[at // held], at % held
         for c in range(3):
             part = value[:, c * CZ : (c + 1) * CZ].reshape(SPREAD_X, CY, CZ)
-            out_ref[c, at : at + SPREAD_X] = base_ref[c, at : at + SPREAD_X] + part
+            out_ref[c, at : at + SPREAD_X] = base[c, inner : inner + SPREAD_X] + part
 
 
 def rimpack_body(n_blk, xrim_ref, low_ref, high_ref, *rest):
@@ -534,11 +534,20 @@
 
 
 def final_body(n_ret, _, main_low, main_high, x_ref, y_ref, face_a, face_b, rec_c, rec_d, rim_a, rim_b, rim_low, rim_high, back_ref, *rest):
-    rets, (out_ref, pf_ref, buf, sems) = rest[:n_ret], rest[n_ret:]
+    rets, (out_ref, pf_ref, buf, pf_buf, sems) = rest[:n_ret], rest[n_ret:]
     even_x, even_y, inner, brick, _, _ = place()
     half = 0.5 * DT_STEP
     visc = DT_STEP * NU_VISC
-    copies = []
+    mine = brick.astype(F32)
+    found = jnp.zeros((BACK, CZ), F32)
+    for ref, first in [(back_ref, 0), (rim_b, RIM_X)] + [(r, 0) for r in rets]:
+        for k in range((ref.shape[0] - first) // BACK):
+            value = ref[first + BACK * k : first + BACK * k + BACK]
+            found = jnp.where(value[6:7, 0:1] == mine, value, found)
+    for c in range(3):
+        pf_buf[c : c + 1] = jnp.concatenate([found[2 * c : 2 * c + 1], found[2 * c + 1 : 2 * c + 2]], axis=1)
+    copies = [pltpu.make_async_copy(pf_buf, pf_ref, sems.at[2])]
+    copies[0].start()
     for k in range(2):
         first, at = k * (CX - 2), k * 2
         face_terms(buf, at, first, 2, main_low, main_high, y_ref, rec_c, rec_d, rim_low, rim_high, even_y)
@@ -558,14 +567,6 @@
                     buf[c, 2 + i] += jnp.where(even_x, a, b)
         copies.append(chunk_copy(buf, at, out_ref, first, 2, sems.at[k]))
         copies[-1].start()
-    mine = brick.astype(F32)
-    found = jnp.zeros((BACK, CZ), F32)
-    for ref, first in [(back_ref, 0), (rim_b, RIM_X)] + [(r, 0) for r in rets]:
-        for k in range((ref.shape[0] - first) // BACK):
-            value = ref[first + BACK * k : first + BACK * k + BACK]
-            found = jnp.where(value[6:7, 0:1] == mine, value, found)
-    for c in range(3):
-        pf_ref[c : c + 1] = jnp.concatenate([found[2 * c : 2 * c + 1], found[2 * c + 1 : 2 * c + 2]], axis=1)
     for copy in copies:
         copy.wait()
 
@@ -642,17 +643,17 @@
     )(velocity, rotor_speed.reshape(1, 1), *[a.reshape(2, CZ) for a in (blade_radius, blade_chord, blade_twist, blade_angle, owner_src)])
     rec_c, rec_d, far = exchange_y(pay_c, pay_d, block)
 
-    def stencil(start):
-        return call(lambda *refs: stencil_body(start, *refs), [(3, CX // 2, CY, CZ)], 1, "stencil")(velocity)[0]
-
-    base_low = stencil(0)
+    def stencil(start, count):
+        return call(lambda *refs: stencil_body(start, *refs), [(3, count, CY, CZ)], 1, "stencil")(velocity)[0]
+
+    base_low = stencil(0, CX // 2)
     table, sums, x_faces, y_faces = call(
         sample_low_body, [(HOST, CZ), (HOST, 3 * CZ), (6, CY, CZ), (2, CX, CZ)], 3, "sample_low", vmem=24
     )(velocity, host_cell, host_frac)
     (rec_c, rec_d, far), (base_low, sums) = after((rec_c, rec_d, far), (base_low, sums))
     pieces = blocks_y(block, rec_c, rec_d, far, ROWS, FACE_Y)
     beside = [swap(p) for p in pieces]
-    beside, base_high = after(beside, stencil(CX // 2))
+    beside, base_third = after(beside, stencil(CX // 2, CX // 4))
     pieces = pieces + beside
     n_rows = 2 * ny * ROWS
     pair = (2 * ROWS, CZ)
@@ -666,7 +667,8 @@
     from_x = across_x(across) if ring else gather_x(blocks)
     face_a = swap(pay_a)
     sums = call(sample_high_body, [(HOST, 3 * CZ)], 3, "sample_high", vmem=24)(velocity, table, sums)[0]
-    (face_a, face_b, from_x), sums = after((face_a, face_b, from_x), sums)
+    base_last = stencil(3 * CX // 4, CX // 4)
+    (face_a, face_b, from_x), (sums, base_last) = after((face_a, face_b, from_x), (sums, base_last))
     samp, sel, pts = call(
         lambda *refs: select_body(len(from_x), *refs),
         [(8, PTS), (2 * ROWS, CZ), (PTS, CZ)],
@@ -676,23 +678,23 @@
     other = swap(samp)
     gx, gy, pz, pos, pair_kernel, edge = call(
         weights_body,
-        [(YROWS, PTS), (CY, PTS), (PTS, CZ), (24, CZ), (2, P_SIZE, P_SIZE), (4 * CY, PTS)],
+        [(YROWS, PTS), (CY, PTS), (CZ, PTS), (24, CZ), (2, P_SIZE, P_SIZE), (4 * CY, PTS)],
         2,
         "weights",
     )(pts, sel)
     lines, points, xrim = call(
         loads_body,
-        [(PTS, 3 * CZ), (2 * BACK + 24, CZ), (2 * RIM_X, CZ)],
+        [(3 * CZ, PTS), (2 * BACK + 24, CZ), (2 * RIM_X, CZ)],
         7,
         "loads",
     )(samp, other, sel, pz, pos, pair_kernel, edge)
     ret = points[: 2 * BACK]
     near_c, near_d, far = exchange_y(points, points, ret)
 
-    def spread(start, base):
+    def spread(start, *bases):
         return call(
-            lambda *refs: spread_body(start, *refs), [(3, CX // 2, CY, CZ)], 4, "spread"
-        )(lines, gx, gy, base)[0]
+            lambda *refs: spread_body(start, *refs), [(3, CX // 2, CY, CZ)], 3 + len(bases), "spread"
+        )(lines, gx, gy, *bases)[0]
 
     (near_c, near_d), main_low = after((near_c, near_d), spread(0, base_low))
     rim_low, rim_high = call(near_body, [(RIM_Y, CZ)] * 2, 2, "near")(near_c, near_d)
@@ -709,7 +711,7 @@
     rim_b = lax.ppermute(pay_b, "gx", odd_pairs(nx, ring))
     rets = [lax.ppermute(across[0], "gx", flip(nx, 4))] if ring else gather_x(back)
     rim_a = swap(pay_a)
-    main_high = spread(CX // 2, base_high)
+    main_high = spread(CX // 2, base_third, base_last)
     (rim_a, rim_b), (main_low, main_high) = after((rim_a, rim_b), (main_low, main_high))
     if ring:
         rets.append(swap(rim_b[RIM_X:]))
@@ -729,9 +731,9 @@
             [velocity.shape, (3, P_SIZE)],
             14 + len(rets),
             "final",
-            scratch=[pltpu.VMEM((3, 4, CY, CZ), F32), dma((2,))],
+            scratch=[pltpu.VMEM((3, 4, CY, CZ), F32), pltpu.VMEM((3, P_SIZE), F32), dma((3,))],
             first=HB,
-            out_specs=[HB, VM],
+            out_specs=[HB, HB],
             aliases={0: 0},
         )(inside, main_low, main_high, x_faces, y_faces, face_a, face_b, rec_c, rec_d, rim_a, rim_b, rim_low, rim_high, back, *rets)
     )

time: 46.5 us -> 44.4 us (0.955)
  Pallas kernels: 23.9 us -> 22 us
  starting transfers between devices: 17.9 us -> 17 us
  waiting for transfers between devices: 2.79 us -> 3.38 us
    ppermute x1, starting transfers between devices: 1.01 us -> 0.12 us  [per_device(): rim_b = lax.ppermute(pay_b, 'gx', odd_pairs(nx, ring))]
    pallas_call x1, Pallas kernels: 1.88 us -> 1.11 us  [per_device(): call(near_body, [(RIM_Y, CZ)] * 2, 2, 'near')(near_c, near_d)]
    ppermute x5, starting transfers between devices: 0.55 us -> 1.16 us  [swap(): return lax.ppermute(block, 'gx', flip(nx, 1))]
    ppermute x5, waiting for transfers between devices: 0.36 us -> 0.96 us  [swap(): return lax.ppermute(block, 'gx', flip(nx, 1))]
    ppermute x1, starting transfers between devices: 1.54 us -> 0.94 us  [per_device(): lax.ppermute(across[0], 'gx', flip(nx, 4))]
    pallas_call x6 -> x7, Pallas kernels: 9.59 us -> 9 us  [the longest x3 3.9 us: stencil(): call(lambda *refs: stencil_body(start, *refs), [(3, count, CY, CZ)], 1, '...]
    pallas_call x1, Pallas kernels: 1.36 us -> 0.79 us  [per_device(): call(lambda *refs: final_body(len(rets), *refs), [velocity.shape, (3, P_S...]
  transfers between devices with their start and end apart: 16 -> 16, of which waited for: 4 -> 5; matrix products, arithmetic and copies ran while one was open for 0% -> 0% of each run, Pallas kernels for 37% -> 36%
where the time goes in v11:
time: 44.4 us; the launch traced here: 44.2 us
  Pallas kernels  22 us (50%)
  starting transfers between devices  17 us (38%)
  waiting for transfers between devices  3.38 us (8%)
  between operations  1.82 us (4%)
    ppermute x2, starting transfers between devices, exchange_y(): from_d = lax.ppermute(to_d, 'gy', flip(ny, 3) if short else odd_pairs(ny))  5.18 us
    pallas_call x3, Pallas kernels, stencil(): call(lambda *refs: stencil_body(start, *refs), [(3, count, CY, CZ)], 1, '...  3.9 us
    pallas_call x2, Pallas kernels, spread(): call(lambda *refs: spread_body(start, *refs), [(3, CX // 2, CY, CZ)], 3 +...  3.65 us
    ppermute x2, starting transfers between devices, exchange_y(): from_c = lax.ppermute(to_c, 'gy', flip(ny, 1))  3.09 us
    pallas_call x1, Pallas kernels, per_device(): call(sample_low_body, [(HOST, CZ), (HOST, 3 * CZ), (6, CY, CZ), (2, CX, C...  2.59 us
    pallas_call x1, Pallas kernels, per_device(): call(sample_high_body, [(HOST, 3 * CZ)], 3, 'sample_high', vmem=24)  2.42 us
    ppermute x1, starting transfers between devices, per_device(): face_b = lax.ppermute(pay_b, 'gx', odd_pairs(nx, ring))  2.41 us
    pallas_call x1, Pallas kernels, per_device(): call(lambda *refs: select_body(len(from_x), *refs), [(8, PTS), (2 * ROWS,...  2.33 us
  transfers between devices with their start and end apart: 16, of which 5 were waited for; matrix products, arithmetic and copies ran while one was open for 0% of the time, Pallas kernels for 36%

profile of v11, /device:TPU:0, one launch (start us, length us, event | category | flops | bytes accessed | tf_op | source)
XLA Modules:
  0.0 44.2 jit_solution(3695045316495664182)
XLA Ops:
  1.4 1.8 %pack.1 = (f32[208,128]{1,0:T(8,128)}, f32[208,128]{1,0:T(8,128)}, f32[16,128]{1,0:T(8,128)}) custom-call(f32[3,64,32,128]{3,2,1,0:T(8,128)} %refs_0_.5, f32[1,1]{1,0:T(1,128)} %bitcast.6.spin_hbm, f32[2,128]{1,0:T(2,128)} %bitcast.7, f32[2,128]{1,0:T(2,128)} %bitcast.8, f32[2,128]{1,0:T(2,128)} %bitcast.9, f32[2,128]{1,0:T(2,128)} %bitcast.10, ...), custom_call_target="tpu_custom_call" | custom-call | tf_op jit(solution)/shard_map/pack/pallas_call | solution.py:635
  3.3 3.1 %collective-permute-start = (f32[208,128]{1,0:T(8,128)}, f32[208,128]{1,0:T(8,128)S(1)}, u32[]{:S(2)}, u32[]{:S(2)}) collective-permute-start(f32[208,128]{1,0:T(8,128)} %get-tuple-element.59), channel_id=1, source_target_pairs={{0,1},{1,0},{2,3},{3,2},{4,5},{5,4},{6,7},{7,6},{8,9},{9,8},{10,11... | collective-permute-start | bytes 319496 | tf_op jit(solution)/shard_map/ppermute | solution.py:618
  6.4 2.5 %collective-permute-start.1 = (f32[208,128]{1,0:T(8,128)}, f32[208,128]{1,0:T(8,128)S(1)}, u32[]{:S(2)}, u32[]{:S(2)}) collective-permute-start(f32[208,128]{1,0:T(8,128)} %get-tuple-element.60), channel_id=1, source_target_pairs={{0,3},{1,2},{2,1},{3,0},{4,7},{5,6},{6,5},{7,4},{8,11},{9,10},{10,... | collective-permute-start | bytes 319496 | tf_op jit(solution)/shard_map/ppermute | solution.py:619
  8.9 0.1 collective-permute-start.2
  9.0 1.9 %stencil.3.refs_3_ = f32[3,32,32,128]{3,2,1,0:T(8,128)S(1)} custom-call(f32[3,64,32,128]{3,2,1,0:T(8,128)S(1)} %copy-done), custom_call_target="tpu_custom_call" | custom-call | tf_op jit(solution)/shard_map/stencil/pallas_call | solution.py:647
  11.0 2.6 %sample_low.1 = (f32[512,128]{1,0:T(8,128)S(1)}, f32[512,384]{1,0:T(8,128)S(1)}, f32[6,32,128]{2,1,0:T(8,128)S(1)}, f32[2,64,128]{2,1,0:T(8,128)S(1)}) custom-call(f32[3,64,32,128]{3,2,1,0:T(8,128)S(1)} %copy-done, s32[3,512]{1,0:T(4,128)S(1)} %copy-done.1, f32[3,512]{1,0:T(4,128)S(1)} %copy-done.2), custom_call_target="tpu_custom_call" | custom-call | tf_op jit(solution)/shard_map/sample_low/pallas_call | solution.py:650
  13.6 1.0 %collective-permute-done.2 = f32[16,128]{1,0:T(8,128)S(1)} collective-permute-done((f32[16,128]{1,0:T(8,128)}, f32[16,128]{1,0:T(8,128)S(1)}, u32[]{:S(2)}, u32[]{:S(2)}) %collective-permute-start.2) | collective-permute-done | bytes 8224 | tf_op jit(solution)/shard_map/ppermute | solution.py:620
  14.6 1.0 %stencil.4.refs_3_ = f32[3,16,32,128]{3,2,1,0:T(8,128)S(1)} custom-call(f32[3,64,32,128]{3,2,1,0:T(8,128)S(1)} %copy-done), custom_call_target="tpu_custom_call" | custom-call | tf_op jit(solution)/shard_map/stencil/pallas_call | solution.py:647
  15.6 0.2 collective-permute-done.3.refs_4_
  15.8 0.1 xpack.1
  16.0 2.4 %collective-permute-start.5 = (f32[152,128]{1,0:T(8,128)S(1)}, f32[152,128]{1,0:T(8,128)S(1)}, u32[]{:S(2)}, u32[]{:S(2)}) collective-permute-start(f32[152,128]{1,0:T(8,128)S(1)} %get-tuple-element.68), channel_id=1, source_target_pairs={{4,8},{12,16},{20,24},{28,0},{8,4},{16,12},{24,20},{0,28},{5,9},{1... | collective-permute-start | bytes 233480 | tf_op jit(solution)/shard_map/ppermute | solution.py:666
  18.4 0.8 %collective-permute-start.6 = (f32[32,128]{1,0:T(8,128)S(1)}, f32[32,128]{1,0:T(8,128)S(1)}, u32[]{:S(2)}, u32[]{:S(2)}) collective-permute-start(f32[32,128]{1,0:T(8,128)S(1)} %get-tuple-element.69), channel_id=1, source_target_pairs={{0,16},{4,20},{8,24},{12,28},{16,0},{20,4},{24,8},{28,12},{1,17},{... | collective-permute-start | bytes 49160 | tf_op jit(solution)/shard_map/ppermute | solution.py:600
  19.1 1.4 %collective-permute-start.7 = (f32[32,128]{1,0:T(8,128)S(1)}, f32[32,128]{1,0:T(8,128)S(1)}, u32[]{:S(2)}, u32[]{:S(2)}) collective-permute-start(f32[32,128]{1,0:T(8,128)S(1)} %get-tuple-element.70), channel_id=1, source_target_pairs={{0,24},{4,12},{8,0},{12,20},{16,8},{20,28},{24,16},{28,4},{1,25},{... | collective-permute-start | bytes 49160 | tf_op jit(solution)/shard_map/ppermute | solution.py:600
  20.6 1.0 %stencil.5.refs_4_ = f32[3,16,32,128]{3,2,1,0:T(8,128)S(1)} custom-call(f32[3,64,32,128]{3,2,1,0:T(8,128)S(1)} %copy-done), custom_call_target="tpu_custom_call" | custom-call | tf_op jit(solution)/shard_map/stencil/pallas_call | solution.py:647
  21.6 2.4 %sample_high.1.refs_1_ = f32[512,384]{1,0:T(8,128)S(1)} custom-call(f32[3,64,32,128]{3,2,1,0:T(8,128)S(1)} %copy-done, f32[512,128]{1,0:T(8,128)S(1)} %get-tuple-element.57.tab_ref.refs_0_, f32[512,384]{1,0:T(8,128)S(1)} %get-tuple-element.71.low_ref), custom_call_target="tpu_custom_call" | custom-call | tf_op jit(solution)/shard_map/sample_high/pallas_call | solution.py:669
  24.0 2.3 %select.1 = (f32[8,512]{1,0:T(8,128)S(1)}, f32[32,128]{1,0:T(8,128)S(1)}, f32[512,128]{1,0:T(8,128)S(1)}) custom-call(f32[512,128]{1,0:T(8,128)S(1)} %get-tuple-element.57.tab_ref.refs_0_, f32[512,384]{1,0:T(8,128)S(1)} %sample_high.1.refs_1_, f32[120,128]{1,0:T(8,128)S(1)} %collective-permute-done.4.refs_2_.refs_5_, ...), custom_call_target="tpu_custom_call" | custom-call | tf_op jit(solution)/shard_map/select/pallas_call | solution.py:672
  26.4 0.4 weights.1
  26.8 0.7 %collective-permute-done.8.other_ref = f32[8,512]{1,0:T(8,128)S(1)} collective-permute-done((f32[8,512]{1,0:T(8,128)S(1)}, f32[8,512]{1,0:T(8,128)S(1)}, u32[]{:S(2)}, u32[]{:S(2)}) %collective-permute-start.8) | collective-permute-done | bytes 16416 | tf_op jit(solution)/shard_map/ppermute | solution.py:603
  27.6 1.0 %loads.1 = (f32[384,512]{1,0:T(8,128)S(1)}, f32[40,128]{1,0:T(8,128)S(1)}, f32[384,128]{1,0:T(8,128)S(1)}) custom-call(f32[8,512]{1,0:T(8,128)S(1)} %get-tuple-element.78.samp_ref, f32[8,512]{1,0:T(8,128)S(1)} %collective-permute-done.8.other_ref, f32[32,128]{1,0:T(8,128)S(1)} %get-tuple-element.79.sel_ref, f32[128,512]{1,0:T(8,128)S(1)} %get-tuple-element.81.pz_ref, ...), custom_call_target="tpu_custom_call" | custom-call | tf_op jit(solution)/shard_map/loads/pallas_call | solution.py:685
  28.6 2.7 %collective-permute-start.11 = (f32[40,128]{1,0:T(8,128)S(1)}, f32[40,128]{1,0:T(8,128)S(1)}, u32[]{:S(2)}, u32[]{:S(2)}) collective-permute-start(f32[40,128]{1,0:T(8,128)S(1)} %get-tuple-element.86), channel_id=1, source_target_pairs={{0,3},{1,2},{2,1},{3,0},{4,7},{5,6},{6,5},{7,4},{8,11},{9,10},{10,... | collective-permute-start | bytes 61448 | tf_op jit(solution)/shard_map/ppermute | solution.py:619
  31.3 1.7 %collective-permute-start.9 = (f32[16,128]{1,0:T(8,128)S(1)}, f32[16,128]{1,0:T(8,128)S(1)}, u32[]{:S(2)}, u32[]{:S(2)}) collective-permute-start(f32[16,128]{1,0:T(8,128)S(1)} %slice.20), channel_id=1, source_target_pairs={{0,2},{1,3},{2,0},{3,1},{4,6},{5,7},{6,4},{7,5},{8,10},{9,11},{10,... | collective-permute-start | bytes 24584 | tf_op jit(solution)/shard_map/ppermute | solution.py:620
  33.1 1.8 %spread.2.main_low.refs_1_ = f32[3,32,32,128]{3,2,1,0:T(8,128)S(1)} custom-call(f32[384,512]{1,0:T(8,128)S(1)} %get-tuple-element.87.refs_0_, f32[72,512]{1,0:T(8,128)S(1)} %get-tuple-element.88.refs_1_, f32[32,512]{1,0:T(8,128)S(1)} %get-tuple-element.89.refs_2_, f32[3,32,32,128]{3,2,1,0:T(8,128)S(1)} %stencil.3.refs_3_), custom_call_target="tpu_custom_call" | custom-call | tf_op jit(solution)/shard_map/spread/pallas_call | solution.py:695
  34.9 0.2 collective-permute-done.10.rec_c
  35.1 1.1 %near.1 = (f32[432,128]{1,0:T(8,128)S(1)}, f32[432,128]{1,0:T(8,128)S(1)}) custom-call(f32[40,128]{1,0:T(8,128)S(1)} %collective-permute-done.10.rec_c, f32[40,128]{1,0:T(8,128)S(1)} %collective-permute-done.11.rec_d), custom_call_target="tpu_custom_call" | custom-call | tf_op jit(solution)/shard_map/near/pallas_call | solution.py:700
  36.2 0.1 rimpack.1
  36.3 0.1 collective-permute-start.14
  36.4 1.0 %collective-permute-start.13 = (f32[192,128]{1,0:T(8,128)S(1)}, f32[192,128]{1,0:T(8,128)S(1)}, u32[]{:S(2)}, u32[]{:S(2)}) collective-permute-start(f32[192,128]{1,0:T(8,128)S(1)} %get-tuple-element.98), channel_id=1, source_target_pairs={{0,4},{4,0},{8,12},{12,8},{16,20},{20,16},{24,28},{28,24},{1,5},{5... | collective-permute-start | bytes 294920 | tf_op jit(solution)/shard_map/ppermute | solution.py:603
  37.5 1.8 %spread.3.main_high.refs_2_ = f32[3,32,32,128]{3,2,1,0:T(8,128)S(1)} custom-call(f32[384,512]{1,0:T(8,128)S(1)} %get-tuple-element.87.refs_0_, f32[72,512]{1,0:T(8,128)S(1)} %get-tuple-element.88.refs_1_, f32[32,512]{1,0:T(8,128)S(1)} %get-tuple-element.89.refs_2_, f32[3,16,32,128]{3,2,1,0:T(8,128)S(1)} %stencil.4.refs_3_, f32[3,16,32,128]{3,2,1,0:T(8,128)S(1)} %stencil.5.refs_4_), custom_call_target="tpu_custom_call" | custom-call | tf_op jit(solution)/shard_map/spread/pallas_call | solution.py:695
  39.3 0.9 %collective-permute-start.12 = (f32[16,128]{1,0:T(8,128)S(1)}, f32[16,128]{1,0:T(8,128)S(1)}, u32[]{:S(2)}, u32[]{:S(2)}) collective-permute-start(f32[16,128]{1,0:T(8,128)S(1)} %get-tuple-element.97), channel_id=1, source_target_pairs={{0,16},{4,20},{8,24},{12,28},{16,0},{20,4},{24,8},{28,12},{1,17},{... | collective-permute-start | bytes 24584 | tf_op jit(solution)/shard_map/ppermute | solution.py:712
  40.2 1.2 %collective-permute-done.14.refs_10_ = f32[208,128]{1,0:T(8,128)S(1)} collective-permute-done((f32[208,128]{1,0:T(8,128)S(1)}, f32[208,128]{1,0:T(8,128)S(1)}, u32[]{:S(2)}, u32[]{:S(2)}) %collective-permute-start.14) | collective-permute-done | bytes 106528 | tf_op jit(solution)/shard_map/ppermute | solution.py:711
  41.5 1.7 %inside.1.refs_0_ = f32[3,64,32,128]{3,2,1,0:T(8,128)} custom-call(f32[3,32,32,128]{3,2,1,0:T(8,128)S(1)} %spread.2.main_low.refs_1_, f32[3,32,32,128]{3,2,1,0:T(8,128)S(1)} %spread.3.main_high.refs_2_, f32[2,64,128]{2,1,0:T(8,128)S(1)} %get-tuple-element.106.y_ref.refs_4_, f32[208,128]{1,0:T(8,128)S(1)} %collective-permute-done.refs_1_.refs_4_.rec_c.refs_7_, ...), custom_call_target="tpu_custom_call" | custom-call | tf_op jit(solution)/shard_map/inside/pallas_call | solution.py:718
  43.3 0.8 %final.1 = (f32[3,64,32,128]{3,2,1,0:T(8,128)}, f32[3,256]{1,0:T(4,128)}) custom-call(f32[3,64,32,128]{3,2,1,0:T(8,128)} %inside.1.refs_0_, f32[3,32,32,128]{3,2,1,0:T(8,128)S(1)} %spread.2.main_low.refs_1_, f32[3,32,32,128]{3,2,1,0:T(8,128)S(1)} %spread.3.main_high.refs_2_, ...), custom_call_target="tpu_custom_call", output_to_operand_aliasing={{0}: (0, {})} | custom-call | tf_op jit(solution)/shard_map/final/pallas_call | solution.py:729
  (32 shorter events, 0.2 us)
Async XLA Ops:
  0.6 8.4 %copy-start = (f32[3,64,32,128]{3,2,1,0:T(8,128)S(1)}, f32[3,64,32,128]{3,2,1,0:T(8,128)}, u32[]{:S(2)}) copy-start(f32[3,64,32,128]{3,2,1,0:T(8,128)} %refs_0_.5) | copy-start | bytes 9437188
  3.3 7.7 %copy-start.1 = (s32[3,512]{1,0:T(4,128)S(1)}, s32[3,512]{1,0:T(4,128)}, u32[]{:S(2)}) copy-start(s32[3,512]{1,0:T(4,128)} %cell_ref.1) | copy-start | bytes 18436
  3.3 7.7 %copy-start.2 = (f32[3,512]{1,0:T(4,128)S(1)}, f32[3,512]{1,0:T(4,128)}, u32[]{:S(2)}) copy-start(f32[3,512]{1,0:T(4,128)} %frac_ref.1) | copy-start | bytes 18436
  3.3 11.2 %collective-permute-start = (f32[208,128]{1,0:T(8,128)}, f32[208,128]{1,0:T(8,128)S(1)}, u32[]{:S(2)}, u32[]{:S(2)}) collective-permute-start(f32[208,128]{1,0:T(8,128)} %get-tuple-element.59), channel_id=1, source_target_pairs={{0,1},{1,0},{2,3},{3,2},{4,5},{5,4},{6,7},{7,6},{8,9},{9,8},{10,11... | collective-permute-start | bytes 319496 | tf_op jit(solution)/shard_map/ppermute | solution.py:618
  6.4 8.1 %collective-permute-start.1 = (f32[208,128]{1,0:T(8,128)}, f32[208,128]{1,0:T(8,128)S(1)}, u32[]{:S(2)}, u32[]{:S(2)}) collective-permute-start(f32[208,128]{1,0:T(8,128)} %get-tuple-element.60), channel_id=1, source_target_pairs={{0,3},{1,2},{2,1},{3,0},{4,7},{5,6},{6,5},{7,4},{8,11},{9,10},{10,... | collective-permute-start | bytes 319496 | tf_op jit(solution)/shard_map/ppermute | solution.py:619
  8.9 5.7 %copy-start.3 = (f32[16,128]{1,0:T(8,128)S(1)}, f32[16,128]{1,0:T(8,128)}, u32[]{:S(2)}) copy-start(f32[16,128]{1,0:T(8,128)} %get-tuple-element.61) | copy-start | bytes 24580
  8.9 5.6 %collective-permute-start.2 = (f32[16,128]{1,0:T(8,128)}, f32[16,128]{1,0:T(8,128)S(1)}, u32[]{:S(2)}, u32[]{:S(2)}) collective-permute-start(f32[16,128]{1,0:T(8,128)} %get-tuple-element.61), channel_id=1, source_target_pairs={{0,2},{1,3},{2,0},{3,1},{4,6},{5,7},{6,4},{7,5},{8,10},{9,11},{10,... | collective-permute-start | bytes 24584 | tf_op jit(solution)/shard_map/ppermute | solution.py:620
  14.6 1.3 %collective-permute-start.3 = (f32[64,128]{1,0:T(8,128)S(1)}, f32[64,128]{1,0:T(8,128)S(1)}, u32[]{:S(2)}, u32[]{:S(2)}) collective-permute-start(f32[64,128]{1,0:T(8,128)S(1)} %pad_maximum_fusion.refs_3_), channel_id=1, source_target_pairs={{0,4},{4,0},{8,12},{12,8},{16,20},{20,16},{24,28},{28,24},{1,5},{5... | collective-permute-start | bytes 98312 | tf_op jit(solution)/shard_map/ppermute | solution.py:603
  16.0 8.1 %collective-permute-start.5 = (f32[152,128]{1,0:T(8,128)S(1)}, f32[152,128]{1,0:T(8,128)S(1)}, u32[]{:S(2)}, u32[]{:S(2)}) collective-permute-start(f32[152,128]{1,0:T(8,128)S(1)} %get-tuple-element.68), channel_id=1, source_target_pairs={{4,8},{12,16},{20,24},{28,0},{8,4},{16,12},{24,20},{0,28},{5,9},{1... | collective-permute-start | bytes 233480 | tf_op jit(solution)/shard_map/ppermute | solution.py:666
  18.4 5.6 %collective-permute-start.4 = (f32[120,128]{1,0:T(8,128)S(1)}, f32[120,128]{1,0:T(8,128)S(1)}, u32[]{:S(2)}, u32[]{:S(2)}) collective-permute-start(f32[120,128]{1,0:T(8,128)S(1)} %get-tuple-element.67), channel_id=1, source_target_pairs={{0,4},{4,0},{8,12},{12,8},{16,20},{20,16},{24,28},{28,24},{1,5},{5... | collective-permute-start | bytes 184328 | tf_op jit(solution)/shard_map/ppermute | solution.py:603
  18.4 5.6 %collective-permute-start.6 = (f32[32,128]{1,0:T(8,128)S(1)}, f32[32,128]{1,0:T(8,128)S(1)}, u32[]{:S(2)}, u32[]{:S(2)}) collective-permute-start(f32[32,128]{1,0:T(8,128)S(1)} %get-tuple-element.69), channel_id=1, source_target_pairs={{0,16},{4,20},{8,24},{12,28},{16,0},{20,4},{24,8},{28,12},{1,17},{... | collective-permute-start | bytes 49160 | tf_op jit(solution)/shard_map/ppermute | solution.py:600
  19.1 4.9 %collective-permute-start.7 = (f32[32,128]{1,0:T(8,128)S(1)}, f32[32,128]{1,0:T(8,128)S(1)}, u32[]{:S(2)}, u32[]{:S(2)}) collective-permute-start(f32[32,128]{1,0:T(8,128)S(1)} %get-tuple-element.70), channel_id=1, source_target_pairs={{0,24},{4,12},{8,0},{12,20},{16,8},{20,28},{24,16},{28,4},{1,25},{... | collective-permute-start | bytes 49160 | tf_op jit(solution)/shard_map/ppermute | solution.py:600
  26.4 1.2 %collective-permute-start.8 = (f32[8,512]{1,0:T(8,128)S(1)}, f32[8,512]{1,0:T(8,128)S(1)}, u32[]{:S(2)}, u32[]{:S(2)}) collective-permute-start(f32[8,512]{1,0:T(8,128)S(1)} %get-tuple-element.78.samp_ref), channel_id=1, source_target_pairs={{0,4},{4,0},{8,12},{12,8},{16,20},{20,16},{24,28},{28,24},{1,5},{5... | collective-permute-start | bytes 49160 | tf_op jit(solution)/shard_map/ppermute | solution.py:603
  28.6 6.3 %collective-permute-start.11 = (f32[40,128]{1,0:T(8,128)S(1)}, f32[40,128]{1,0:T(8,128)S(1)}, u32[]{:S(2)}, u32[]{:S(2)}) collective-permute-start(f32[40,128]{1,0:T(8,128)S(1)} %get-tuple-element.86), channel_id=1, source_target_pairs={{0,3},{1,2},{2,1},{3,0},{4,7},{5,6},{6,5},{7,4},{8,11},{9,10},{10,... | collective-permute-start | bytes 61448 | tf_op jit(solution)/shard_map/ppermute | solution.py:619
  31.3 3.8 %collective-permute-start.10 = (f32[40,128]{1,0:T(8,128)S(1)}, f32[40,128]{1,0:T(8,128)S(1)}, u32[]{:S(2)}, u32[]{:S(2)}) collective-permute-start(f32[40,128]{1,0:T(8,128)S(1)} %get-tuple-element.86), channel_id=1, source_target_pairs={{0,1},{1,0},{2,3},{3,2},{4,5},{5,4},{6,7},{7,6},{8,9},{9,8},{10,11... | collective-permute-start | bytes 61448 | tf_op jit(solution)/shard_map/ppermute | solution.py:618
  31.3 4.9 %collective-permute-start.9 = (f32[16,128]{1,0:T(8,128)S(1)}, f32[16,128]{1,0:T(8,128)S(1)}, u32[]{:S(2)}, u32[]{:S(2)}) collective-permute-start(f32[16,128]{1,0:T(8,128)S(1)} %slice.20), channel_id=1, source_target_pairs={{0,2},{1,3},{2,0},{3,1},{4,6},{5,7},{6,4},{7,5},{8,10},{9,11},{10,... | collective-permute-start | bytes 24584 | tf_op jit(solution)/shard_map/ppermute | solution.py:620
  36.3 5.2 %collective-permute-start.14 = (f32[208,128]{1,0:T(8,128)S(1)}, f32[208,128]{1,0:T(8,128)S(1)}, u32[]{:S(2)}, u32[]{:S(2)}) collective-permute-start(f32[208,128]{1,0:T(8,128)S(1)} %get-tuple-element.99), channel_id=1, source_target_pairs={{4,8},{12,16},{20,24},{28,0},{8,4},{16,12},{24,20},{0,28},{5,9},{1... | collective-permute-start | bytes 319496 | tf_op jit(solution)/shard_map/ppermute | solution.py:711
  36.4 3.8 %collective-permute-start.13 = (f32[192,128]{1,0:T(8,128)S(1)}, f32[192,128]{1,0:T(8,128)S(1)}, u32[]{:S(2)}, u32[]{:S(2)}) collective-permute-start(f32[192,128]{1,0:T(8,128)S(1)} %get-tuple-element.98), channel_id=1, source_target_pairs={{0,4},{4,0},{8,12},{12,8},{16,20},{20,16},{24,28},{28,24},{1,5},{5... | collective-permute-start | bytes 294920 | tf_op jit(solution)/shard_map/ppermute | solution.py:603
  39.3 3.9 %collective-permute-start.12 = (f32[16,128]{1,0:T(8,128)S(1)}, f32[16,128]{1,0:T(8,128)S(1)}, u32[]{:S(2)}, u32[]{:S(2)}) collective-permute-start(f32[16,128]{1,0:T(8,128)S(1)} %get-tuple-element.97), channel_id=1, source_target_pairs={{0,16},{4,20},{8,24},{12,28},{16,0},{20,4},{24,8},{28,12},{1,17},{... | collective-permute-start | bytes 24584 | tf_op jit(solution)/shard_map/ppermute | solution.py:712
  41.5 1.8 %collective-permute-start.15 = (f32[16,128]{1,0:T(8,128)S(1)}, f32[16,128]{1,0:T(8,128)S(1)}, u32[]{:S(2)}, u32[]{:S(2)}) collective-permute-start(f32[16,128]{1,0:T(8,128)S(1)} %slice.23), channel_id=1, source_target_pairs={{0,4},{4,0},{8,12},{12,8},{16,20},{20,16},{24,28},{28,24},{1,5},{5... | collective-permute-start | bytes 24584 | tf_op jit(solution)/shard_map/ppermute | solution.py:603

commit v12 on v11

--- a/solution.py
+++ b/solution.py
@@ -212,8 +212,18 @@
     acc_ref[...] = sample_part(0, v_ref, table, None)
 
 
-def sample_high_body(v_ref, tab_ref, low_ref, acc_ref):
-    acc_ref[...] = sample_part(CX // 2, v_ref, tab_ref[...], low_ref[...])
+def sample_high_body(v_ref, tab_ref, low_ref, acc_ref, edge_ref, wz_ref):
+    table = tab_ref[...]
+    acc_ref[...] = sample_part(CX // 2, v_ref, table, low_ref[...])
+    lane = lax.broadcasted_iota(jnp.int32, (HOST, CZ), 1)
+    x_col, y_col, z_col = [table[:, k : k + 1].astype(jnp.int32) for k in range(3)]
+    fx, fy, fz = [table[:, k : k + 1] for k in range(3, 6)]
+    on_line = lane >= CX
+    edge_x = jnp.where(on_line, lane - CX, CX)
+    edge_y = jnp.where(on_line, CY, lane)
+    both = weight(edge_x, x_col, fx) * weight(edge_y, y_col, fy)
+    edge_ref[...] = jnp.where(on_line | (lane <= CY), both, 0.0)
+    wz_ref[...] = weight(lane, z_col, fz)
 
 
 def split_blocks(sources):
@@ -267,7 +277,7 @@
     others[0][...] = jnp.concatenate(pick_pair(values, lax.rem(b0 + 2 * chips, total), ny), axis=0)
 
 
-def select_body(n_blk, tab_ref, acc_ref, face_a, face_b, rec_c, rec_d, blk_ref, *rest):
+def select_body(n_blk, tab_ref, acc_ref, edge_ref, wz_ref, face_a, face_b, rec_c, rec_d, blk_ref, *rest):
     others, (samp_ref, sel_ref, pts_ref) = rest[:n_blk], rest[n_blk:]
     even_x, even_y, inner, brick, b0, ny = place()
     sources = [(blk_ref, 0), (face_b, FACE_X)] + [(o, 0) for o in others]
@@ -282,12 +292,6 @@
 
     table = tab_ref[...]
     lane = lax.broadcasted_iota(jnp.int32, (PTS, CZ), 1)
-    x_col, y_col, z_col = [table[:, k : k + 1].astype(jnp.int32) for k in range(3)]
-    fx, fy, fz = [table[:, k : k + 1] for k in range(3, 6)]
-    on_line = lane >= CX
-    edge_x = jnp.where(on_line, lane - CX, CX)
-    edge_y = jnp.where(on_line, CY, lane)
-    edge_w = jnp.where(on_line | (lane <= CY), weight(edge_x, x_col, fx) * weight(edge_y, y_col, fy), 0.0)
     field = []
     for c in range(3):
         at = c * XROWS
@@ -296,10 +300,10 @@
         at = c * CX
         line = jnp.where(even_y, rec_c[at : at + CX], jnp.where(odd_side(), rec_d[at : at + CX], 0.0))
         field.append(jnp.concatenate([plane, jnp.zeros((CX - XROWS, CZ), F32), line], axis=0))
-    w_high, w_low = split(edge_w)
+    w_high, w_low = split(edge_ref[...])
     f_high, f_low = split(jnp.concatenate(field, axis=1))
     acc = acc_ref[...] + dot3(w_high, w_low, f_high, f_low)
-    wz = weight(lane, z_col, fz)
+    wz = wz_ref[...]
     for c in range(3):
         value = jnp.sum(acc[:, c * CZ : (c + 1) * CZ] * wz, axis=1, keepdims=True)
         table = table + jnp.where(lane == 6 + c, value, 0.0)
@@ -446,14 +450,14 @@
     bases, out_ref = rest[:-1], rest[-1]
     l_high, l_low = split(lines_ref[...])
     gy = gy_ref[0:CY]
-    held = bases[0].shape[1]
+    held = [(ref, k) for ref in bases for k in range(0, ref.shape[1], SPREAD_X)]
     for k in range(out_ref.shape[1] // SPREAD_X):
         at = k * SPREAD_X
         first = start + at
         planes = jnp.concatenate([gx_ref[first + i : first + i + 1] * gy for i in range(SPREAD_X)], axis=0)
         w_high, w_low = split(planes)
         value = dot3_last(w_high, w_low, l_high, l_low)
-        base, inner = bases[at // held], at % held
+        base, inner = held[k]
         for c in range(3):
             part = value[:, c * CZ : (c + 1) * CZ].reshape(SPREAD_X, CY, CZ)
             out_ref[c, at : at + SPREAD_X] = base[c, inner : inner + SPREAD_X] + part
@@ -666,15 +670,16 @@
     face_b = lax.ppermute(pay_b, "gx", odd_pairs(nx, ring))
     from_x = across_x(across) if ring else gather_x(blocks)
     face_a = swap(pay_a)
-    sums = call(sample_high_body, [(HOST, 3 * CZ)], 3, "sample_high", vmem=24)(velocity, table, sums)[0]
-    base_last = stencil(3 * CX // 4, CX // 4)
-    (face_a, face_b, from_x), (sums, base_last) = after((face_a, face_b, from_x), (sums, base_last))
+    sums, edge, wz = call(
+        sample_high_body, [(HOST, 3 * CZ), (HOST, CZ), (HOST, CZ)], 3, "sample_high", vmem=24
+    )(velocity, table, sums)
+    (face_a, face_b, from_x), sums = after((face_a, face_b, from_x), sums)
     samp, sel, pts = call(
         lambda *refs: select_body(len(from_x), *refs),
         [(8, PTS), (2 * ROWS, CZ), (PTS, CZ)],
-        7 + len(from_x),
+        9 + len(from_x),
         "select",
-    )(table, sums, face_a, face_b, rec_c, rec_d, blocks, *from_x)
+    )(table, sums, edge, wz, face_a, face_b, rec_c, rec_d, blocks, *from_x)
     other = swap(samp)
     gx, gy, pz, pos, pair_kernel, edge = call(
         weights_body,
@@ -682,6 +687,7 @@
         2,
         "weights",
     )(pts, sel)
+    other, base_next = after(other, stencil(6 * CX // 8, CX // 8))
     lines, points, xrim = call(
         loads_body,
         [(3 * CZ, PTS), (2 * BACK + 24, CZ), (2 * RIM_X, CZ)],
@@ -711,7 +717,7 @@
     rim_b = lax.ppermute(pay_b, "gx", odd_pairs(nx, ring))
     rets = [lax.ppermute(across[0], "gx", flip(nx, 4))] if ring else gather_x(back)
     rim_a = swap(pay_a)
-    main_high = spread(CX // 2, base_third, base_last)
+    main_high = spread(CX // 2, base_third, base_next, stencil(7 * CX // 8, CX // 8))
     (rim_a, rim_b), (main_low, main_high) = after((rim_a, rim_b), (main_low, main_high))
     if ring:
         rets.append(swap(rim_b[RIM_X:]))

time: 44.4 us -> 43.5 us (0.980)
  waiting for transfers between devices: 3.38 us -> 2.42 us
  starting transfers between devices: 17 us -> 17.9 us
  Pallas kernels: 22 us -> 21.2 us
    ppermute x1, starting transfers between devices: 0.12 us -> 1.08 us  [per_device(): rim_b = lax.ppermute(pay_b, 'gx', odd_pairs(nx, ring))]
    pallas_call x1, Pallas kernels: 2.33 us -> 1.51 us  [per_device(): call(lambda *refs: select_body(len(from_x), *refs), [(8, PTS), (2 * ROWS,...]
    ppermute x5, starting transfers between devices: 1.16 us -> 0.42 us  [swap(): return lax.ppermute(block, 'gx', flip(nx, 1))]
    ppermute x1, starting transfers between devices: 0.94 us -> 1.6 us  [per_device(): lax.ppermute(across[0], 'gx', flip(nx, 4))]
    ppermute x1, waiting for transfers between devices: 1.24 us -> 0.75 us  [per_device(): rim_b = lax.ppermute(pay_b, 'gx', odd_pairs(nx, ring))]
    ppermute x5, waiting for transfers between devices: 0.96 us -> 0.48 us  [swap(): return lax.ppermute(block, 'gx', flip(nx, 1))]
    pallas_call x3 -> x4, Pallas kernels: 3.9 us -> 3.91 us  [stencil(): call(lambda *refs: stencil_body(start, *refs), [(3, count, CY, CZ)], 1, '...]
  transfers between devices with their start and end apart: 16 -> 16, of which waited for: 5 -> 5; matrix products, arithmetic and copies ran while one was open for 0% -> 0% of each run, Pallas kernels for 36% -> 37%
where the time goes in v12:
time: 43.5 us; the launch traced here: 43.3 us
  Pallas kernels  21.2 us (49%)
  starting transfers between devices  17.9 us (41%)
  waiting for transfers between devices  2.42 us (6%)
  between operations  1.82 us (4%)
    ppermute x2, starting transfers between devices, exchange_y(): from_d = lax.ppermute(to_d, 'gy', flip(ny, 3) if short else odd_pairs(ny))  5.18 us
    pallas_call x4, Pallas kernels, stencil(): call(lambda *refs: stencil_body(start, *refs), [(3, count, CY, CZ)], 1, '...  3.91 us
    pallas_call x2, Pallas kernels, spread(): call(lambda *refs: spread_body(start, *refs), [(3, CX // 2, CY, CZ)], 3 +...  3.66 us
    ppermute x2, starting transfers between devices, exchange_y(): from_c = lax.ppermute(to_c, 'gy', flip(ny, 1))  3.09 us
    pallas_call x1, Pallas kernels, per_device(): call(sample_low_body, [(HOST, CZ), (HOST, 3 * CZ), (6, CY, CZ), (2, CX, C...  2.59 us
    pallas_call x1, Pallas kernels, per_device(): call(sample_high_body, [(HOST, 3 * CZ), (HOST, CZ), (HOST, CZ)], 3, 'samp...  2.43 us
    ppermute x1, starting transfers between devices, per_device(): face_b = lax.ppermute(pay_b, 'gx', odd_pairs(nx, ring))  2.41 us
    ppermute x2, starting transfers between devices, across_x(): lax.ppermute(b, 'gx', p)  2.21 us
  transfers between devices with their start and end apart: 16, of which 5 were waited for; matrix products, arithmetic and copies ran while one was open for 0% of the time, Pallas kernels for 37%

profile of v12, /device:TPU:0, one launch (start us, length us, event | category | flops | bytes accessed | tf_op | source)
XLA Modules:
  0.0 43.3 jit_solution(7452504800955723067)
XLA Ops:
  1.4 1.8 %pack.1 = (f32[208,128]{1,0:T(8,128)}, f32[208,128]{1,0:T(8,128)}, f32[16,128]{1,0:T(8,128)}) custom-call(f32[3,64,32,128]{3,2,1,0:T(8,128)} %refs_0_.7, f32[1,1]{1,0:T(1,128)} %bitcast.6.spin_hbm, f32[2,128]{1,0:T(2,128)} %bitcast.7, f32[2,128]{1,0:T(2,128)} %bitcast.8, f32[2,128]{1,0:T(2,128)} %bitcast.9, f32[2,128]{1,0:T(2,128)} %bitcast.10, ...), custom_call_target="tpu_custom_call" | custom-call | tf_op jit(solution)/shard_map/pack/pallas_call | solution.py:639
  3.3 3.1 %collective-permute-start = (f32[208,128]{1,0:T(8,128)}, f32[208,128]{1,0:T(8,128)S(1)}, u32[]{:S(2)}, u32[]{:S(2)}) collective-permute-start(f32[208,128]{1,0:T(8,128)} %get-tuple-element.63), channel_id=1, source_target_pairs={{0,1},{1,0},{2,3},{3,2},{4,5},{5,4},{6,7},{7,6},{8,9},{9,8},{10,11... | collective-permute-start | bytes 319496 | tf_op jit(solution)/shard_map/ppermute | solution.py:622
  6.4 2.5 %collective-permute-start.1 = (f32[208,128]{1,0:T(8,128)}, f32[208,128]{1,0:T(8,128)S(1)}, u32[]{:S(2)}, u32[]{:S(2)}) collective-permute-start(f32[208,128]{1,0:T(8,128)} %get-tuple-element.64), channel_id=1, source_target_pairs={{0,3},{1,2},{2,1},{3,0},{4,7},{5,6},{6,5},{7,4},{8,11},{9,10},{10,... | collective-permute-start | bytes 319496 | tf_op jit(solution)/shard_map/ppermute | solution.py:623
  8.9 0.1 collective-permute-start.2
  9.0 1.9 %stencil.4.refs_3_ = f32[3,32,32,128]{3,2,1,0:T(8,128)S(1)} custom-call(f32[3,64,32,128]{3,2,1,0:T(8,128)S(1)} %copy-done), custom_call_target="tpu_custom_call" | custom-call | tf_op jit(solution)/shard_map/stencil/pallas_call | solution.py:651
  11.0 2.6 %sample_low.1 = (f32[512,128]{1,0:T(8,128)S(1)}, f32[512,384]{1,0:T(8,128)S(1)}, f32[6,32,128]{2,1,0:T(8,128)S(1)}, f32[2,64,128]{2,1,0:T(8,128)S(1)}) custom-call(f32[3,64,32,128]{3,2,1,0:T(8,128)S(1)} %copy-done, s32[3,512]{1,0:T(4,128)S(1)} %copy-done.1, f32[3,512]{1,0:T(4,128)S(1)} %copy-done.2), custom_call_target="tpu_custom_call" | custom-call | tf_op jit(solution)/shard_map/sample_low/pallas_call | solution.py:654
  13.6 1.0 %collective-permute-done.2 = f32[16,128]{1,0:T(8,128)S(1)} collective-permute-done((f32[16,128]{1,0:T(8,128)}, f32[16,128]{1,0:T(8,128)S(1)}, u32[]{:S(2)}, u32[]{:S(2)}) %collective-permute-start.2) | collective-permute-done | bytes 8224 | tf_op jit(solution)/shard_map/ppermute | solution.py:624
  14.6 1.0 %stencil.5.refs_3_ = f32[3,16,32,128]{3,2,1,0:T(8,128)S(1)} custom-call(f32[3,64,32,128]{3,2,1,0:T(8,128)S(1)} %copy-done), custom_call_target="tpu_custom_call" | custom-call | tf_op jit(solution)/shard_map/stencil/pallas_call | solution.py:651
  15.6 0.2 collective-permute-done.3.refs_4_
  15.8 0.1 xpack.1
  16.0 2.4 %collective-permute-start.5 = (f32[152,128]{1,0:T(8,128)S(1)}, f32[152,128]{1,0:T(8,128)S(1)}, u32[]{:S(2)}, u32[]{:S(2)}) collective-permute-start(f32[152,128]{1,0:T(8,128)S(1)} %get-tuple-element.72), channel_id=1, source_target_pairs={{4,8},{12,16},{20,24},{28,0},{8,4},{16,12},{24,20},{0,28},{5,9},{1... | collective-permute-start | bytes 233480 | tf_op jit(solution)/shard_map/ppermute | solution.py:670
  18.4 0.8 %collective-permute-start.6 = (f32[32,128]{1,0:T(8,128)S(1)}, f32[32,128]{1,0:T(8,128)S(1)}, u32[]{:S(2)}, u32[]{:S(2)}) collective-permute-start(f32[32,128]{1,0:T(8,128)S(1)} %get-tuple-element.73), channel_id=1, source_target_pairs={{0,16},{4,20},{8,24},{12,28},{16,0},{20,4},{24,8},{28,12},{1,17},{... | collective-permute-start | bytes 49160 | tf_op jit(solution)/shard_map/ppermute | solution.py:604
  19.1 1.4 %collective-permute-start.7 = (f32[32,128]{1,0:T(8,128)S(1)}, f32[32,128]{1,0:T(8,128)S(1)}, u32[]{:S(2)}, u32[]{:S(2)}) collective-permute-start(f32[32,128]{1,0:T(8,128)S(1)} %get-tuple-element.74), channel_id=1, source_target_pairs={{0,24},{4,12},{8,0},{12,20},{16,8},{20,28},{24,16},{28,4},{1,25},{... | collective-permute-start | bytes 49160 | tf_op jit(solution)/shard_map/ppermute | solution.py:604
  20.6 2.4 %sample_high.1 = (f32[512,384]{1,0:T(8,128)S(1)}, f32[512,128]{1,0:T(8,128)S(1)}, f32[512,128]{1,0:T(8,128)S(1)}) custom-call(f32[3,64,32,128]{3,2,1,0:T(8,128)S(1)} %copy-done, f32[512,128]{1,0:T(8,128)S(1)} %get-tuple-element.61.tab_ref.refs_0_, f32[512,384]{1,0:T(8,128)S(1)} %get-tuple-element.75.low_ref), custom_call_target="tpu_custom_call" | custom-call | tf_op jit(solution)/shard_map/sample_high/pallas_call | solution.py:673
  23.1 1.5 %select.1 = (f32[8,512]{1,0:T(8,128)S(1)}, f32[32,128]{1,0:T(8,128)S(1)}, f32[512,128]{1,0:T(8,128)S(1)}) custom-call(f32[512,128]{1,0:T(8,128)S(1)} %get-tuple-element.61.tab_ref.refs_0_, f32[512,384]{1,0:T(8,128)S(1)} %get-tuple-element.77.refs_1_, f32[512,128]{1,0:T(8,128)S(1)} %get-tuple-element.78.refs_2_, f32[512,128]{1,0:T(8,128)S(1)} %get-tuple-element.79.refs_3_, ...), custom_call_target="tpu_custom_call" | custom-call | tf_op jit(solution)/shard_map/select/pallas_call | solution.py:677
  24.6 0.5 %stencil.6.refs_4_ = f32[3,8,32,128]{3,2,1,0:T(8,128)S(1)} custom-call(f32[3,64,32,128]{3,2,1,0:T(8,128)S(1)} %copy-done), custom_call_target="tpu_custom_call" | custom-call | tf_op jit(solution)/shard_map/stencil/pallas_call | solution.py:651
  25.1 0.4 weights.1
  25.5 0.3 collective-permute-done.8.other_ref
  25.8 1.0 %loads.1 = (f32[384,512]{1,0:T(8,128)S(1)}, f32[40,128]{1,0:T(8,128)S(1)}, f32[384,128]{1,0:T(8,128)S(1)}) custom-call(f32[8,512]{1,0:T(8,128)S(1)} %get-tuple-element.85.samp_ref, f32[8,512]{1,0:T(8,128)S(1)} %collective-permute-done.8.other_ref, f32[32,128]{1,0:T(8,128)S(1)} %get-tuple-element.87.sel_ref, f32[128,512]{1,0:T(8,128)S(1)} %get-tuple-element.89.pz_ref, ...), custom_call_target="tpu_custom_call" | custom-call | tf_op jit(solution)/shard_map/loads/pallas_call | solution.py:691
  26.8 2.7 %collective-permute-start.11 = (f32[40,128]{1,0:T(8,128)S(1)}, f32[40,128]{1,0:T(8,128)S(1)}, u32[]{:S(2)}, u32[]{:S(2)}) collective-permute-start(f32[40,128]{1,0:T(8,128)S(1)} %get-tuple-element.94), channel_id=1, source_target_pairs={{0,3},{1,2},{2,1},{3,0},{4,7},{5,6},{6,5},{7,4},{8,11},{9,10},{10,... | collective-permute-start | bytes 61448 | tf_op jit(solution)/shard_map/ppermute | solution.py:623
  29.5 1.7 %collective-permute-start.9 = (f32[16,128]{1,0:T(8,128)S(1)}, f32[16,128]{1,0:T(8,128)S(1)}, u32[]{:S(2)}, u32[]{:S(2)}) collective-permute-start(f32[16,128]{1,0:T(8,128)S(1)} %slice.20), channel_id=1, source_target_pairs={{0,2},{1,3},{2,0},{3,1},{4,6},{5,7},{6,4},{7,5},{8,10},{9,11},{10,... | collective-permute-start | bytes 24584 | tf_op jit(solution)/shard_map/ppermute | solution.py:624
  31.3 1.8 %spread.2.main_low.refs_1_ = f32[3,32,32,128]{3,2,1,0:T(8,128)S(1)} custom-call(f32[384,512]{1,0:T(8,128)S(1)} %get-tuple-element.95.refs_0_, f32[72,512]{1,0:T(8,128)S(1)} %get-tuple-element.96.refs_1_, f32[32,512]{1,0:T(8,128)S(1)} %get-tuple-element.97.refs_2_, f32[3,32,32,128]{3,2,1,0:T(8,128)S(1)} %stencil.4.refs_3_), custom_call_target="tpu_custom_call" | custom-call | tf_op jit(solution)/shard_map/spread/pallas_call | solution.py:701
  33.1 0.2 collective-permute-done.10.rec_c
  33.3 1.1 %near.1 = (f32[432,128]{1,0:T(8,128)S(1)}, f32[432,128]{1,0:T(8,128)S(1)}) custom-call(f32[40,128]{1,0:T(8,128)S(1)} %collective-permute-done.10.rec_c, f32[40,128]{1,0:T(8,128)S(1)} %collective-permute-done.11.rec_d), custom_call_target="tpu_custom_call" | custom-call | tf_op jit(solution)/shard_map/near/pallas_call | solution.py:706
  34.5 1.1 %collective-permute-start.14 = (f32[208,128]{1,0:T(8,128)S(1)}, f32[208,128]{1,0:T(8,128)S(1)}, u32[]{:S(2)}, u32[]{:S(2)}) collective-permute-start(f32[208,128]{1,0:T(8,128)S(1)} %get-tuple-element.107), channel_id=1, source_target_pairs={{4,8},{12,16},{20,24},{28,0},{8,4},{16,12},{24,20},{0,28},{5,9},{1... | collective-permute-start | bytes 319496 | tf_op jit(solution)/shard_map/ppermute | solution.py:717
  35.6 0.3 collective-permute-start.13
  35.9 0.5 %stencil.7.refs_5_ = f32[3,8,32,128]{3,2,1,0:T(8,128)S(1)} custom-call(f32[3,64,32,128]{3,2,1,0:T(8,128)S(1)} %copy-done), custom_call_target="tpu_custom_call" | custom-call | tf_op jit(solution)/shard_map/stencil/pallas_call | solution.py:651
  36.4 1.8 %spread.3.main_high.refs_2_ = f32[3,32,32,128]{3,2,1,0:T(8,128)S(1)} custom-call(f32[384,512]{1,0:T(8,128)S(1)} %get-tuple-element.95.refs_0_, f32[72,512]{1,0:T(8,128)S(1)} %get-tuple-element.96.refs_1_, f32[32,512]{1,0:T(8,128)S(1)} %get-tuple-element.97.refs_2_, f32[3,16,32,128]{3,2,1,0:T(8,128)S(1)} %stencil.5.refs_3_, ...), custom_call_target="tpu_custom_call" | custom-call | tf_op jit(solution)/shard_map/spread/pallas_call | solution.py:701
  38.2 1.6 %collective-permute-start.12 = (f32[16,128]{1,0:T(8,128)S(1)}, f32[16,128]{1,0:T(8,128)S(1)}, u32[]{:S(2)}, u32[]{:S(2)}) collective-permute-start(f32[16,128]{1,0:T(8,128)S(1)} %get-tuple-element.105), channel_id=1, source_target_pairs={{0,16},{4,20},{8,24},{12,28},{16,0},{20,4},{24,8},{28,12},{1,17},{... | collective-permute-start | bytes 24584 | tf_op jit(solution)/shard_map/ppermute | solution.py:718
  39.8 0.8 %collective-permute-done.14.refs_10_ = f32[208,128]{1,0:T(8,128)S(1)} collective-permute-done((f32[208,128]{1,0:T(8,128)S(1)}, f32[208,128]{1,0:T(8,128)S(1)}, u32[]{:S(2)}, u32[]{:S(2)}) %collective-permute-start.14) | collective-permute-done | bytes 106528 | tf_op jit(solution)/shard_map/ppermute | solution.py:717
  40.6 1.7 %inside.1.refs_0_ = f32[3,64,32,128]{3,2,1,0:T(8,128)} custom-call(f32[3,32,32,128]{3,2,1,0:T(8,128)S(1)} %spread.2.main_low.refs_1_, f32[3,32,32,128]{3,2,1,0:T(8,128)S(1)} %spread.3.main_high.refs_2_, f32[2,64,128]{2,1,0:T(8,128)S(1)} %get-tuple-element.114.y_ref.refs_4_, f32[208,128]{1,0:T(8,128)S(1)} %collective-permute-done.refs_1_.refs_6_.rec_c.refs_7_, ...), custom_call_target="tpu_custom_call" | custom-call | tf_op jit(solution)/shard_map/inside/pallas_call | solution.py:724
  42.4 0.8 %final.1 = (f32[3,64,32,128]{3,2,1,0:T(8,128)}, f32[3,256]{1,0:T(4,128)}) custom-call(f32[3,64,32,128]{3,2,1,0:T(8,128)} %inside.1.refs_0_, f32[3,32,32,128]{3,2,1,0:T(8,128)S(1)} %spread.2.main_low.refs_1_, f32[3,32,32,128]{3,2,1,0:T(8,128)S(1)} %spread.3.main_high.refs_2_, ...), custom_call_target="tpu_custom_call", output_to_operand_aliasing={{0}: (0, {})} | custom-call | tf_op jit(solution)/shard_map/final/pallas_call | solution.py:735
  (33 shorter events, 0.3 us)
Async XLA Ops:
  0.6 8.4 %copy-start = (f32[3,64,32,128]{3,2,1,0:T(8,128)S(1)}, f32[3,64,32,128]{3,2,1,0:T(8,128)}, u32[]{:S(2)}) copy-start(f32[3,64,32,128]{3,2,1,0:T(8,128)} %refs_0_.7) | copy-start | bytes 9437188
  3.3 7.7 %copy-start.1 = (s32[3,512]{1,0:T(4,128)S(1)}, s32[3,512]{1,0:T(4,128)}, u32[]{:S(2)}) copy-start(s32[3,512]{1,0:T(4,128)} %cell_ref.1) | copy-start | bytes 18436
  3.3 7.7 %copy-start.2 = (f32[3,512]{1,0:T(4,128)S(1)}, f32[3,512]{1,0:T(4,128)}, u32[]{:S(2)}) copy-start(f32[3,512]{1,0:T(4,128)} %frac_ref.1) | copy-start | bytes 18436
  3.3 11.2 %collective-permute-start = (f32[208,128]{1,0:T(8,128)}, f32[208,128]{1,0:T(8,128)S(1)}, u32[]{:S(2)}, u32[]{:S(2)}) collective-permute-start(f32[208,128]{1,0:T(8,128)} %get-tuple-element.63), channel_id=1, source_target_pairs={{0,1},{1,0},{2,3},{3,2},{4,5},{5,4},{6,7},{7,6},{8,9},{9,8},{10,11... | collective-permute-start | bytes 319496 | tf_op jit(solution)/shard_map/ppermute | solution.py:622
  6.4 8.1 %collective-permute-start.1 = (f32[208,128]{1,0:T(8,128)}, f32[208,128]{1,0:T(8,128)S(1)}, u32[]{:S(2)}, u32[]{:S(2)}) collective-permute-start(f32[208,128]{1,0:T(8,128)} %get-tuple-element.64), channel_id=1, source_target_pairs={{0,3},{1,2},{2,1},{3,0},{4,7},{5,6},{6,5},{7,4},{8,11},{9,10},{10,... | collective-permute-start | bytes 319496 | tf_op jit(solution)/shard_map/ppermute | solution.py:623
  8.9 5.7 %copy-start.3 = (f32[16,128]{1,0:T(8,128)S(1)}, f32[16,128]{1,0:T(8,128)}, u32[]{:S(2)}) copy-start(f32[16,128]{1,0:T(8,128)} %get-tuple-element.65) | copy-start | bytes 24580
  8.9 5.6 %collective-permute-start.2 = (f32[16,128]{1,0:T(8,128)}, f32[16,128]{1,0:T(8,128)S(1)}, u32[]{:S(2)}, u32[]{:S(2)}) collective-permute-start(f32[16,128]{1,0:T(8,128)} %get-tuple-element.65), channel_id=1, source_target_pairs={{0,2},{1,3},{2,0},{3,1},{4,6},{5,7},{6,4},{7,5},{8,10},{9,11},{10,... | collective-permute-start | bytes 24584 | tf_op jit(solution)/shard_map/ppermute | solution.py:624
  14.6 1.3 %collective-permute-start.3 = (f32[64,128]{1,0:T(8,128)S(1)}, f32[64,128]{1,0:T(8,128)S(1)}, u32[]{:S(2)}, u32[]{:S(2)}) collective-permute-start(f32[64,128]{1,0:T(8,128)S(1)} %pad_maximum_fusion.refs_3_), channel_id=1, source_target_pairs={{0,4},{4,0},{8,12},{12,8},{16,20},{20,16},{24,28},{28,24},{1,5},{5... | collective-permute-start | bytes 98312 | tf_op jit(solution)/shard_map/ppermute | solution.py:607
  16.0 7.1 %collective-permute-start.5 = (f32[152,128]{1,0:T(8,128)S(1)}, f32[152,128]{1,0:T(8,128)S(1)}, u32[]{:S(2)}, u32[]{:S(2)}) collective-permute-start(f32[152,128]{1,0:T(8,128)S(1)} %get-tuple-element.72), channel_id=1, source_target_pairs={{4,8},{12,16},{20,24},{28,0},{8,4},{16,12},{24,20},{0,28},{5,9},{1... | collective-permute-start | bytes 233480 | tf_op jit(solution)/shard_map/ppermute | solution.py:670
  18.4 4.7 %collective-permute-start.4 = (f32[120,128]{1,0:T(8,128)S(1)}, f32[120,128]{1,0:T(8,128)S(1)}, u32[]{:S(2)}, u32[]{:S(2)}) collective-permute-start(f32[120,128]{1,0:T(8,128)S(1)} %get-tuple-element.71), channel_id=1, source_target_pairs={{0,4},{4,0},{8,12},{12,8},{16,20},{20,16},{24,28},{28,24},{1,5},{5... | collective-permute-start | bytes 184328 | tf_op jit(solution)/shard_map/ppermute | solution.py:607
  18.4 4.6 %collective-permute-start.6 = (f32[32,128]{1,0:T(8,128)S(1)}, f32[32,128]{1,0:T(8,128)S(1)}, u32[]{:S(2)}, u32[]{:S(2)}) collective-permute-start(f32[32,128]{1,0:T(8,128)S(1)} %get-tuple-element.73), channel_id=1, source_target_pairs={{0,16},{4,20},{8,24},{12,28},{16,0},{20,4},{24,8},{28,12},{1,17},{... | collective-permute-start | bytes 49160 | tf_op jit(solution)/shard_map/ppermute | solution.py:604
  19.1 3.9 %collective-permute-start.7 = (f32[32,128]{1,0:T(8,128)S(1)}, f32[32,128]{1,0:T(8,128)S(1)}, u32[]{:S(2)}, u32[]{:S(2)}) collective-permute-start(f32[32,128]{1,0:T(8,128)S(1)} %get-tuple-element.74), channel_id=1, source_target_pairs={{0,24},{4,12},{8,0},{12,20},{16,8},{20,28},{24,16},{28,4},{1,25},{... | collective-permute-start | bytes 49160 | tf_op jit(solution)/shard_map/ppermute | solution.py:604
  24.6 1.2 %collective-permute-start.8 = (f32[8,512]{1,0:T(8,128)S(1)}, f32[8,512]{1,0:T(8,128)S(1)}, u32[]{:S(2)}, u32[]{:S(2)}) collective-permute-start(f32[8,512]{1,0:T(8,128)S(1)} %get-tuple-element.85.samp_ref), channel_id=1, source_target_pairs={{0,4},{4,0},{8,12},{12,8},{16,20},{20,16},{24,28},{28,24},{1,5},{5... | collective-permute-start | bytes 49160 | tf_op jit(solution)/shard_map/ppermute | solution.py:607
  26.8 6.3 %collective-permute-start.11 = (f32[40,128]{1,0:T(8,128)S(1)}, f32[40,128]{1,0:T(8,128)S(1)}, u32[]{:S(2)}, u32[]{:S(2)}) collective-permute-start(f32[40,128]{1,0:T(8,128)S(1)} %get-tuple-element.94), channel_id=1, source_target_pairs={{0,3},{1,2},{2,1},{3,0},{4,7},{5,6},{6,5},{7,4},{8,11},{9,10},{10,... | collective-permute-start | bytes 61448 | tf_op jit(solution)/shard_map/ppermute | solution.py:623
  29.5 3.8 %collective-permute-start.10 = (f32[40,128]{1,0:T(8,128)S(1)}, f32[40,128]{1,0:T(8,128)S(1)}, u32[]{:S(2)}, u32[]{:S(2)}) collective-permute-start(f32[40,128]{1,0:T(8,128)S(1)} %get-tuple-element.94), channel_id=1, source_target_pairs={{0,1},{1,0},{2,3},{3,2},{4,5},{5,4},{6,7},{7,6},{8,9},{9,8},{10,11... | collective-permute-start | bytes 61448 | tf_op jit(solution)/shard_map/ppermute | solution.py:622
  29.5 4.9 %collective-permute-start.9 = (f32[16,128]{1,0:T(8,128)S(1)}, f32[16,128]{1,0:T(8,128)S(1)}, u32[]{:S(2)}, u32[]{:S(2)}) collective-permute-start(f32[16,128]{1,0:T(8,128)S(1)} %slice.20), channel_id=1, source_target_pairs={{0,2},{1,3},{2,0},{3,1},{4,6},{5,7},{6,4},{7,5},{8,10},{9,11},{10,... | collective-permute-start | bytes 24584 | tf_op jit(solution)/shard_map/ppermute | solution.py:624
  34.5 6.1 %collective-permute-start.14 = (f32[208,128]{1,0:T(8,128)S(1)}, f32[208,128]{1,0:T(8,128)S(1)}, u32[]{:S(2)}, u32[]{:S(2)}) collective-permute-start(f32[208,128]{1,0:T(8,128)S(1)} %get-tuple-element.107), channel_id=1, source_target_pairs={{4,8},{12,16},{20,24},{28,0},{8,4},{16,12},{24,20},{0,28},{5,9},{1... | collective-permute-start | bytes 319496 | tf_op jit(solution)/shard_map/ppermute | solution.py:717
  35.6 4.2 %collective-permute-start.13 = (f32[192,128]{1,0:T(8,128)S(1)}, f32[192,128]{1,0:T(8,128)S(1)}, u32[]{:S(2)}, u32[]{:S(2)}) collective-permute-start(f32[192,128]{1,0:T(8,128)S(1)} %get-tuple-element.106), channel_id=1, source_target_pairs={{0,4},{4,0},{8,12},{12,8},{16,20},{20,16},{24,28},{28,24},{1,5},{5... | collective-permute-start | bytes 294920 | tf_op jit(solution)/shard_map/ppermute | solution.py:607
  38.2 4.1 %collective-permute-start.12 = (f32[16,128]{1,0:T(8,128)S(1)}, f32[16,128]{1,0:T(8,128)S(1)}, u32[]{:S(2)}, u32[]{:S(2)}) collective-permute-start(f32[16,128]{1,0:T(8,128)S(1)} %get-tuple-element.105), channel_id=1, source_target_pairs={{0,16},{4,20},{8,24},{12,28},{16,0},{20,4},{24,8},{28,12},{1,17},{... | collective-permute-start | bytes 24584 | tf_op jit(solution)/shard_map/ppermute | solution.py:718
  40.6 1.8 %collective-permute-start.15 = (f32[16,128]{1,0:T(8,128)S(1)}, f32[16,128]{1,0:T(8,128)S(1)}, u32[]{:S(2)}, u32[]{:S(2)}) collective-permute-start(f32[16,128]{1,0:T(8,128)S(1)} %slice.23), channel_id=1, source_target_pairs={{0,4},{4,0},{8,12},{12,8},{16,20},{20,16},{24,28},{28,24},{1,5},{5... | collective-permute-start | bytes 24584 | tf_op jit(solution)/shard_map/ppermute | solution.py:607

commit v13 on v12

--- a/solution.py
+++ b/solution.py
@@ -635,6 +635,9 @@
             pieces.append(lax.ppermute(join([blocks] + pieces), "gx", flip(nx, bit)))
         return pieces
 
+    def pin(array):
+        return pltpu.with_memory_space_constraint(array, pltpu.MemorySpace.HBM)
+
     dma = pltpu.SemaphoreType.DMA
     pay_c, pay_d, block = call(
         pack_body,
@@ -643,14 +646,13 @@
         "pack",
         scratch=[pltpu.VMEM((4, 2, CZ), F32), pltpu.VMEM((2, CZ), jnp.int32), pltpu.VMEM((1, 1), F32), dma((12,))],
         in_specs=[HB] * 7,
-        vmem=56,
-    )(velocity, rotor_speed.reshape(1, 1), *[a.reshape(2, CZ) for a in (blade_radius, blade_chord, blade_twist, blade_angle, owner_src)])
+    )(pin(velocity), rotor_speed.reshape(1, 1), *[pin(a.reshape(2, CZ)) for a in (blade_radius, blade_chord, blade_twist, blade_angle, owner_src)])
     rec_c, rec_d, far = exchange_y(pay_c, pay_d, block)
 
     def stencil(start, count):
         return call(lambda *refs: stencil_body(start, *refs), [(3, count, CY, CZ)], 1, "stencil")(velocity)[0]
 
-    base_low = stencil(0, CX // 2)
+    base_low = stencil(0, 3 * CX // 8)
     table, sums, x_faces, y_faces = call(
         sample_low_body, [(HOST, CZ), (HOST, 3 * CZ), (6, CY, CZ), (2, CX, CZ)], 3, "sample_low", vmem=24
     )(velocity, host_cell, host_frac)
@@ -673,7 +675,8 @@
     sums, edge, wz = call(
         sample_high_body, [(HOST, 3 * CZ), (HOST, CZ), (HOST, CZ)], 3, "sample_high", vmem=24
     )(velocity, table, sums)
-    (face_a, face_b, from_x), sums = after((face_a, face_b, from_x), sums)
+    base_more = stencil(3 * CX // 8, CX // 8)
+    (face_a, face_b, from_x), (sums, base_more) = after((face_a, face_b, from_x), (sums, base_more))
     samp, sel, pts = call(
         lambda *refs: select_body(len(from_x), *refs),
         [(8, PTS), (2 * ROWS, CZ), (PTS, CZ)],
@@ -702,7 +705,7 @@
             lambda *refs: spread_body(start, *refs), [(3, CX // 2, CY, CZ)], 3 + len(bases), "spread"
         )(lines, gx, gy, *bases)[0]
 
-    (near_c, near_d), main_low = after((near_c, near_d), spread(0, base_low))
+    (near_c, near_d), main_low = after((near_c, near_d), spread(0, base_low, base_more))
     rim_low, rim_high = call(near_body, [(RIM_Y, CZ)] * 2, 2, "near")(near_c, near_d)
     far, rim_low = after(far, rim_low)
     pieces = blocks_y(ret, near_c, near_d, far, 2 * BACK, 0)

time: 43.5 us -> 42.6 us (0.979)
  Pallas kernels: 21.2 us -> 20.5 us
  starting transfers between devices: 17.9 us -> 17.3 us
    pallas_call x1, Pallas kernels: 1.85 us -> 1.16 us  [per_device(): call(pack_body, [(FACE_Y + ROWS, CZ)] * 2 + [(ROWS, CZ)], 7, 'pack', scra...]
    ppermute x1, starting transfers between devices: 1.08 us -> 0.59 us  [per_device(): rim_b = lax.ppermute(pay_b, 'gx', odd_pairs(nx, ring))]
    pallas_call x4 -> x5, Pallas kernels: 3.91 us -> 3.91 us  [stencil(): call(lambda *refs: stencil_body(start, *refs), [(3, count, CY, CZ)], 1, '...]
where the time goes in v13:
time: 42.6 us; the launch traced here: 42.4 us
  Pallas kernels  20.5 us (48%)
  starting transfers between devices  17.3 us (41%)
  waiting for transfers between devices  2.69 us (6%)
  between operations  1.81 us (4%)
    ppermute x2, starting transfers between devices, exchange_y(): from_d = lax.ppermute(to_d, 'gy', flip(ny, 3) if short else odd_pairs(ny))  5.18 us
    pallas_call x5, Pallas kernels, stencil(): call(lambda *refs: stencil_body(start, *refs), [(3, count, CY, CZ)], 1, '...  3.91 us
    pallas_call x2, Pallas kernels, spread(): call(lambda *refs: spread_body(start, *refs), [(3, CX // 2, CY, CZ)], 3 +...  3.65 us
    ppermute x2, starting transfers between devices, exchange_y(): from_c = lax.ppermute(to_c, 'gy', flip(ny, 1))  3.09 us
    pallas_call x1, Pallas kernels, per_device(): call(sample_low_body, [(HOST, CZ), (HOST, 3 * CZ), (6, CY, CZ), (2, CX, C...  2.6 us
    pallas_call x1, Pallas kernels, per_device(): call(sample_high_body, [(HOST, 3 * CZ), (HOST, CZ), (HOST, CZ)], 3, 'samp...  2.43 us
    ppermute x1, starting transfers between devices, per_device(): face_b = lax.ppermute(pay_b, 'gx', odd_pairs(nx, ring))  2.41 us
    ppermute x2, starting transfers between devices, across_x(): lax.ppermute(b, 'gx', p)  2.21 us
  transfers between devices with their start and end apart: 16, of which 5 were waited for; matrix products, arithmetic and copies ran while one was open for 0% of the time, Pallas kernels for 37%

profile of v13, /device:TPU:0, one launch (start us, length us, event | category | flops | bytes accessed | tf_op | source)
XLA Modules:
  0.0 42.4 jit_solution(14272181996845663911)
XLA Ops:
  1.5 1.2 %pack.1 = (f32[208,128]{1,0:T(8,128)S(1)}, f32[208,128]{1,0:T(8,128)S(1)}, f32[16,128]{1,0:T(8,128)S(1)}) custom-call(f32[3,64,32,128]{3,2,1,0:T(8,128)} %refs_0_.9, f32[1,1]{1,0:T(1,128)} %bitcast.6.spin_hbm, f32[2,128]{1,0:T(2,128)} %bitcast.7, f32[2,128]{1,0:T(2,128)} %bitcast.8, f32[2,128]{1,0:T(2,128)} %bitcast.9, f32[2,128]{1,0:T(2,128)} %bitcast.10, ...), custom_call_target="tpu_custom_call" | custom-call | tf_op jit(solution)/shard_map/pack/pallas_call | solution.py:642
  2.6 3.1 %collective-permute-start = (f32[208,128]{1,0:T(8,128)S(1)}, f32[208,128]{1,0:T(8,128)S(1)}, u32[]{:S(2)}, u32[]{:S(2)}) collective-permute-start(f32[208,128]{1,0:T(8,128)S(1)} %get-tuple-element.64), channel_id=1, source_target_pairs={{0,1},{1,0},{2,3},{3,2},{4,5},{5,4},{6,7},{7,6},{8,9},{9,8},{10,11... | collective-permute-start | bytes 319496 | tf_op jit(solution)/shard_map/ppermute | solution.py:622
  5.7 2.5 %collective-permute-start.1 = (f32[208,128]{1,0:T(8,128)S(1)}, f32[208,128]{1,0:T(8,128)S(1)}, u32[]{:S(2)}, u32[]{:S(2)}) collective-permute-start(f32[208,128]{1,0:T(8,128)S(1)} %get-tuple-element.65), channel_id=1, source_target_pairs={{0,3},{1,2},{2,1},{3,0},{4,7},{5,6},{6,5},{7,4},{8,11},{9,10},{10,... | collective-permute-start | bytes 319496 | tf_op jit(solution)/shard_map/ppermute | solution.py:623
  8.2 0.1 collective-permute-start.2
  8.3 1.5 %stencil.5.refs_3_ = f32[3,24,32,128]{3,2,1,0:T(8,128)S(1)} custom-call(f32[3,64,32,128]{3,2,1,0:T(8,128)S(1)} %copy-done), custom_call_target="tpu_custom_call" | custom-call | tf_op jit(solution)/shard_map/stencil/pallas_call | solution.py:653
  9.8 2.6 %sample_low.1 = (f32[512,128]{1,0:T(8,128)S(1)}, f32[512,384]{1,0:T(8,128)S(1)}, f32[6,32,128]{2,1,0:T(8,128)S(1)}, f32[2,64,128]{2,1,0:T(8,128)S(1)}) custom-call(f32[3,64,32,128]{3,2,1,0:T(8,128)S(1)} %copy-done, s32[3,512]{1,0:T(4,128)S(1)} %copy-done.1, f32[3,512]{1,0:T(4,128)S(1)} %copy-done.2), custom_call_target="tpu_custom_call" | custom-call | tf_op jit(solution)/shard_map/sample_low/pallas_call | solution.py:656
  12.4 1.2 %collective-permute-done.2 = f32[16,128]{1,0:T(8,128)S(1)} collective-permute-done((f32[16,128]{1,0:T(8,128)S(1)}, f32[16,128]{1,0:T(8,128)S(1)}, u32[]{:S(2)}, u32[]{:S(2)}) %collective-permute-start.2) | collective-permute-done | bytes 8224 | tf_op jit(solution)/shard_map/ppermute | solution.py:624
  13.7 1.0 %stencil.6.refs_3_ = f32[3,16,32,128]{3,2,1,0:T(8,128)S(1)} custom-call(f32[3,64,32,128]{3,2,1,0:T(8,128)S(1)} %copy-done), custom_call_target="tpu_custom_call" | custom-call | tf_op jit(solution)/shard_map/stencil/pallas_call | solution.py:653
  14.7 0.2 collective-permute-done.3.refs_4_
  15.0 2.4 %collective-permute-start.5 = (f32[152,128]{1,0:T(8,128)S(1)}, f32[152,128]{1,0:T(8,128)S(1)}, u32[]{:S(2)}, u32[]{:S(2)}) collective-permute-start(f32[152,128]{1,0:T(8,128)S(1)} %get-tuple-element.73), channel_id=1, source_target_pairs={{4,8},{12,16},{20,24},{28,0},{8,4},{16,12},{24,20},{0,28},{5,9},{1... | collective-permute-start | bytes 233480 | tf_op jit(solution)/shard_map/ppermute | solution.py:672
  17.5 0.8 %collective-permute-start.6 = (f32[32,128]{1,0:T(8,128)S(1)}, f32[32,128]{1,0:T(8,128)S(1)}, u32[]{:S(2)}, u32[]{:S(2)}) collective-permute-start(f32[32,128]{1,0:T(8,128)S(1)} %get-tuple-element.74), channel_id=1, source_target_pairs={{0,16},{4,20},{8,24},{12,28},{16,0},{20,4},{24,8},{28,12},{1,17},{... | collective-permute-start | bytes 49160 | tf_op jit(solution)/shard_map/ppermute | solution.py:604
  18.2 1.4 %collective-permute-start.7 = (f32[32,128]{1,0:T(8,128)S(1)}, f32[32,128]{1,0:T(8,128)S(1)}, u32[]{:S(2)}, u32[]{:S(2)}) collective-permute-start(f32[32,128]{1,0:T(8,128)S(1)} %get-tuple-element.75), channel_id=1, source_target_pairs={{0,24},{4,12},{8,0},{12,20},{16,8},{20,28},{24,16},{28,4},{1,25},{... | collective-permute-start | bytes 49160 | tf_op jit(solution)/shard_map/ppermute | solution.py:604
  19.7 0.5 %stencil.7.refs_4_ = f32[3,8,32,128]{3,2,1,0:T(8,128)S(1)} custom-call(f32[3,64,32,128]{3,2,1,0:T(8,128)S(1)} %copy-done), custom_call_target="tpu_custom_call" | custom-call | tf_op jit(solution)/shard_map/stencil/pallas_call | solution.py:653
  20.2 2.4 %sample_high.1 = (f32[512,384]{1,0:T(8,128)S(1)}, f32[512,128]{1,0:T(8,128)S(1)}, f32[512,128]{1,0:T(8,128)S(1)}) custom-call(f32[3,64,32,128]{3,2,1,0:T(8,128)S(1)} %copy-done, f32[512,128]{1,0:T(8,128)S(1)} %get-tuple-element.62.tab_ref.refs_0_, f32[512,384]{1,0:T(8,128)S(1)} %get-tuple-element.76.low_ref), custom_call_target="tpu_custom_call" | custom-call | tf_op jit(solution)/shard_map/sample_high/pallas_call | solution.py:675
  22.6 1.5 %select.1 = (f32[8,512]{1,0:T(8,128)S(1)}, f32[32,128]{1,0:T(8,128)S(1)}, f32[512,128]{1,0:T(8,128)S(1)}) custom-call(f32[512,128]{1,0:T(8,128)S(1)} %get-tuple-element.62.tab_ref.refs_0_, f32[512,384]{1,0:T(8,128)S(1)} %get-tuple-element.78.refs_1_, f32[512,128]{1,0:T(8,128)S(1)} %get-tuple-element.79.refs_2_, f32[512,128]{1,0:T(8,128)S(1)} %get-tuple-element.80.refs_3_, ...), custom_call_target="tpu_custom_call" | custom-call | tf_op jit(solution)/shard_map/select/pallas_call | solution.py:680
  24.2 0.5 %stencil.8.refs_4_ = f32[3,8,32,128]{3,2,1,0:T(8,128)S(1)} custom-call(f32[3,64,32,128]{3,2,1,0:T(8,128)S(1)} %copy-done), custom_call_target="tpu_custom_call" | custom-call | tf_op jit(solution)/shard_map/stencil/pallas_call | solution.py:653
  24.7 0.4 weights.1
  25.1 0.3 collective-permute-done.8.other_ref
  25.4 1.0 %loads.1 = (f32[384,512]{1,0:T(8,128)S(1)}, f32[40,128]{1,0:T(8,128)S(1)}, f32[384,128]{1,0:T(8,128)S(1)}) custom-call(f32[8,512]{1,0:T(8,128)S(1)} %get-tuple-element.86.samp_ref, f32[8,512]{1,0:T(8,128)S(1)} %collective-permute-done.8.other_ref, f32[32,128]{1,0:T(8,128)S(1)} %get-tuple-element.88.sel_ref, f32[128,512]{1,0:T(8,128)S(1)} %get-tuple-element.90.pz_ref, ...), custom_call_target="tpu_custom_call" | custom-call | tf_op jit(solution)/shard_map/loads/pallas_call | solution.py:694
  26.4 2.7 %collective-permute-start.11 = (f32[40,128]{1,0:T(8,128)S(1)}, f32[40,128]{1,0:T(8,128)S(1)}, u32[]{:S(2)}, u32[]{:S(2)}) collective-permute-start(f32[40,128]{1,0:T(8,128)S(1)} %get-tuple-element.95), channel_id=1, source_target_pairs={{0,3},{1,2},{2,1},{3,0},{4,7},{5,6},{6,5},{7,4},{8,11},{9,10},{10,... | collective-permute-start | bytes 61448 | tf_op jit(solution)/shard_map/ppermute | solution.py:623
  29.1 1.7 %collective-permute-start.9 = (f32[16,128]{1,0:T(8,128)S(1)}, f32[16,128]{1,0:T(8,128)S(1)}, u32[]{:S(2)}, u32[]{:S(2)}) collective-permute-start(f32[16,128]{1,0:T(8,128)S(1)} %slice.20), channel_id=1, source_target_pairs={{0,2},{1,3},{2,0},{3,1},{4,6},{5,7},{6,4},{7,5},{8,10},{9,11},{10,... | collective-permute-start | bytes 24584 | tf_op jit(solution)/shard_map/ppermute | solution.py:624
  30.9 1.8 %spread.2.main_low.refs_1_ = f32[3,32,32,128]{3,2,1,0:T(8,128)S(1)} custom-call(f32[384,512]{1,0:T(8,128)S(1)} %get-tuple-element.96.refs_0_, f32[72,512]{1,0:T(8,128)S(1)} %get-tuple-element.97.refs_1_, f32[32,512]{1,0:T(8,128)S(1)} %get-tuple-element.98.refs_2_, f32[3,24,32,128]{3,2,1,0:T(8,128)S(1)} %stencil.5.refs_3_, f32[3,8,32,128]{3,2,1,0:T(8,128)S(1)} %stencil.7.refs_4_), custom_call_target="tpu_custom_call" | custom-call | tf_op jit(solution)/shard_map/spread/pallas_call | solution.py:704
  32.7 0.2 collective-permute-done.10.rec_c
  32.9 1.1 %near.1 = (f32[432,128]{1,0:T(8,128)S(1)}, f32[432,128]{1,0:T(8,128)S(1)}) custom-call(f32[40,128]{1,0:T(8,128)S(1)} %collective-permute-done.10.rec_c, f32[40,128]{1,0:T(8,128)S(1)} %collective-permute-done.11.rec_d), custom_call_target="tpu_custom_call" | custom-call | tf_op jit(solution)/shard_map/near/pallas_call | solution.py:709
  34.1 0.6 %collective-permute-start.14 = (f32[208,128]{1,0:T(8,128)S(1)}, f32[208,128]{1,0:T(8,128)S(1)}, u32[]{:S(2)}, u32[]{:S(2)}) collective-permute-start(f32[208,128]{1,0:T(8,128)S(1)} %get-tuple-element.109), channel_id=1, source_target_pairs={{4,8},{12,16},{20,24},{28,0},{8,4},{16,12},{24,20},{0,28},{5,9},{1... | collective-permute-start | bytes 319496 | tf_op jit(solution)/shard_map/ppermute | solution.py:720
  34.7 0.6 %collective-permute-start.13 = (f32[192,128]{1,0:T(8,128)S(1)}, f32[192,128]{1,0:T(8,128)S(1)}, u32[]{:S(2)}, u32[]{:S(2)}) collective-permute-start(f32[192,128]{1,0:T(8,128)S(1)} %get-tuple-element.108), channel_id=1, source_target_pairs={{0,4},{4,0},{8,12},{12,8},{16,20},{20,16},{24,28},{28,24},{1,5},{5... | collective-permute-start | bytes 294920 | tf_op jit(solution)/shard_map/ppermute | solution.py:607
  35.3 0.5 %stencil.9.refs_5_ = f32[3,8,32,128]{3,2,1,0:T(8,128)S(1)} custom-call(f32[3,64,32,128]{3,2,1,0:T(8,128)S(1)} %copy-done), custom_call_target="tpu_custom_call" | custom-call | tf_op jit(solution)/shard_map/stencil/pallas_call | solution.py:653
  35.8 1.8 %spread.3.main_high.refs_2_ = f32[3,32,32,128]{3,2,1,0:T(8,128)S(1)} custom-call(f32[384,512]{1,0:T(8,128)S(1)} %get-tuple-element.96.refs_0_, f32[72,512]{1,0:T(8,128)S(1)} %get-tuple-element.97.refs_1_, f32[32,512]{1,0:T(8,128)S(1)} %get-tuple-element.98.refs_2_, f32[3,16,32,128]{3,2,1,0:T(8,128)S(1)} %stencil.6.refs_3_, ...), custom_call_target="tpu_custom_call" | custom-call | tf_op jit(solution)/shard_map/spread/pallas_call | solution.py:704
  37.6 1.3 %collective-permute-start.12 = (f32[16,128]{1,0:T(8,128)S(1)}, f32[16,128]{1,0:T(8,128)S(1)}, u32[]{:S(2)}, u32[]{:S(2)}) collective-permute-start(f32[16,128]{1,0:T(8,128)S(1)} %get-tuple-element.107), channel_id=1, source_target_pairs={{0,16},{4,20},{8,24},{12,28},{16,0},{20,4},{24,8},{28,12},{1,17},{... | collective-permute-start | bytes 24584 | tf_op jit(solution)/shard_map/ppermute | solution.py:721
  38.9 0.8 %collective-permute-done.14.refs_10_ = f32[208,128]{1,0:T(8,128)S(1)} collective-permute-done((f32[208,128]{1,0:T(8,128)S(1)}, f32[208,128]{1,0:T(8,128)S(1)}, u32[]{:S(2)}, u32[]{:S(2)}) %collective-permute-start.14) | collective-permute-done | bytes 106528 | tf_op jit(solution)/shard_map/ppermute | solution.py:720
  39.7 1.7 %inside.1.refs_0_ = f32[3,64,32,128]{3,2,1,0:T(8,128)} custom-call(f32[3,32,32,128]{3,2,1,0:T(8,128)S(1)} %spread.2.main_low.refs_1_, f32[3,32,32,128]{3,2,1,0:T(8,128)S(1)} %spread.3.main_high.refs_2_, f32[2,64,128]{2,1,0:T(8,128)S(1)} %get-tuple-element.116.y_ref.refs_4_, f32[208,128]{1,0:T(8,128)S(1)} %collective-permute-done.refs_1_.refs_6_.rec_c.refs_7_, ...), custom_call_target="tpu_custom_call" | custom-call | tf_op jit(solution)/shard_map/inside/pallas_call | solution.py:727
  41.5 0.8 %final.1 = (f32[3,64,32,128]{3,2,1,0:T(8,128)}, f32[3,256]{1,0:T(4,128)}) custom-call(f32[3,64,32,128]{3,2,1,0:T(8,128)} %inside.1.refs_0_, f32[3,32,32,128]{3,2,1,0:T(8,128)S(1)} %spread.2.main_low.refs_1_, f32[3,32,32,128]{3,2,1,0:T(8,128)S(1)} %spread.3.main_high.refs_2_, ...), custom_call_target="tpu_custom_call", output_to_operand_aliasing={{0}: (0, {})} | custom-call | tf_op jit(solution)/shard_map/final/pallas_call | solution.py:738
  (32 shorter events, 0.4 us)
Async XLA Ops:
  0.6 7.7 %copy-start = (f32[3,64,32,128]{3,2,1,0:T(8,128)S(1)}, f32[3,64,32,128]{3,2,1,0:T(8,128)}, u32[]{:S(2)}) copy-start(f32[3,64,32,128]{3,2,1,0:T(8,128)} %refs_0_.9) | copy-start | bytes 9437188
  1.4 8.3 %copy-start.1 = (s32[3,512]{1,0:T(4,128)S(1)}, s32[3,512]{1,0:T(4,128)}, u32[]{:S(2)}) copy-start(s32[3,512]{1,0:T(4,128)} %cell_ref.1) | copy-start | bytes 18436
  1.4 8.3 %copy-start.2 = (f32[3,512]{1,0:T(4,128)S(1)}, f32[3,512]{1,0:T(4,128)}, u32[]{:S(2)}) copy-start(f32[3,512]{1,0:T(4,128)} %frac_ref.1) | copy-start | bytes 18436
  2.6 11.0 %collective-permute-start = (f32[208,128]{1,0:T(8,128)S(1)}, f32[208,128]{1,0:T(8,128)S(1)}, u32[]{:S(2)}, u32[]{:S(2)}) collective-permute-start(f32[208,128]{1,0:T(8,128)S(1)} %get-tuple-element.64), channel_id=1, source_target_pairs={{0,1},{1,0},{2,3},{3,2},{4,5},{5,4},{6,7},{7,6},{8,9},{9,8},{10,11... | collective-permute-start | bytes 319496 | tf_op jit(solution)/shard_map/ppermute | solution.py:622
  5.7 7.9 %collective-permute-start.1 = (f32[208,128]{1,0:T(8,128)S(1)}, f32[208,128]{1,0:T(8,128)S(1)}, u32[]{:S(2)}, u32[]{:S(2)}) collective-permute-start(f32[208,128]{1,0:T(8,128)S(1)} %get-tuple-element.65), channel_id=1, source_target_pairs={{0,3},{1,2},{2,1},{3,0},{4,7},{5,6},{6,5},{7,4},{8,11},{9,10},{10,... | collective-permute-start | bytes 319496 | tf_op jit(solution)/shard_map/ppermute | solution.py:623
  8.2 5.4 %collective-permute-start.2 = (f32[16,128]{1,0:T(8,128)S(1)}, f32[16,128]{1,0:T(8,128)S(1)}, u32[]{:S(2)}, u32[]{:S(2)}) collective-permute-start(f32[16,128]{1,0:T(8,128)S(1)} %get-tuple-element.66), channel_id=1, source_target_pairs={{0,2},{1,3},{2,0},{3,1},{4,6},{5,7},{6,4},{7,5},{8,10},{9,11},{10,... | collective-permute-start | bytes 24584 | tf_op jit(solution)/shard_map/ppermute | solution.py:624
  13.7 1.3 %collective-permute-start.3 = (f32[64,128]{1,0:T(8,128)S(1)}, f32[64,128]{1,0:T(8,128)S(1)}, u32[]{:S(2)}, u32[]{:S(2)}) collective-permute-start(f32[64,128]{1,0:T(8,128)S(1)} %pad_maximum_fusion.refs_3_), channel_id=1, source_target_pairs={{0,4},{4,0},{8,12},{12,8},{16,20},{20,16},{24,28},{28,24},{1,5},{5... | collective-permute-start | bytes 98312 | tf_op jit(solution)/shard_map/ppermute | solution.py:607
  15.0 7.6 %collective-permute-start.5 = (f32[152,128]{1,0:T(8,128)S(1)}, f32[152,128]{1,0:T(8,128)S(1)}, u32[]{:S(2)}, u32[]{:S(2)}) collective-permute-start(f32[152,128]{1,0:T(8,128)S(1)} %get-tuple-element.73), channel_id=1, source_target_pairs={{4,8},{12,16},{20,24},{28,0},{8,4},{16,12},{24,20},{0,28},{5,9},{1... | collective-permute-start | bytes 233480 | tf_op jit(solution)/shard_map/ppermute | solution.py:672
  17.5 5.2 %collective-permute-start.4 = (f32[120,128]{1,0:T(8,128)S(1)}, f32[120,128]{1,0:T(8,128)S(1)}, u32[]{:S(2)}, u32[]{:S(2)}) collective-permute-start(f32[120,128]{1,0:T(8,128)S(1)} %get-tuple-element.72), channel_id=1, source_target_pairs={{0,4},{4,0},{8,12},{12,8},{16,20},{20,16},{24,28},{28,24},{1,5},{5... | collective-permute-start | bytes 184328 | tf_op jit(solution)/shard_map/ppermute | solution.py:607
  17.5 5.1 %collective-permute-start.6 = (f32[32,128]{1,0:T(8,128)S(1)}, f32[32,128]{1,0:T(8,128)S(1)}, u32[]{:S(2)}, u32[]{:S(2)}) collective-permute-start(f32[32,128]{1,0:T(8,128)S(1)} %get-tuple-element.74), channel_id=1, source_target_pairs={{0,16},{4,20},{8,24},{12,28},{16,0},{20,4},{24,8},{28,12},{1,17},{... | collective-permute-start | bytes 49160 | tf_op jit(solution)/shard_map/ppermute | solution.py:604
  18.2 4.4 %collective-permute-start.7 = (f32[32,128]{1,0:T(8,128)S(1)}, f32[32,128]{1,0:T(8,128)S(1)}, u32[]{:S(2)}, u32[]{:S(2)}) collective-permute-start(f32[32,128]{1,0:T(8,128)S(1)} %get-tuple-element.75), channel_id=1, source_target_pairs={{0,24},{4,12},{8,0},{12,20},{16,8},{20,28},{24,16},{28,4},{1,25},{... | collective-permute-start | bytes 49160 | tf_op jit(solution)/shard_map/ppermute | solution.py:604
  24.2 1.2 %collective-permute-start.8 = (f32[8,512]{1,0:T(8,128)S(1)}, f32[8,512]{1,0:T(8,128)S(1)}, u32[]{:S(2)}, u32[]{:S(2)}) collective-permute-start(f32[8,512]{1,0:T(8,128)S(1)} %get-tuple-element.86.samp_ref), channel_id=1, source_target_pairs={{0,4},{4,0},{8,12},{12,8},{16,20},{20,16},{24,28},{28,24},{1,5},{5... | collective-permute-start | bytes 49160 | tf_op jit(solution)/shard_map/ppermute | solution.py:607
  26.4 6.3 %collective-permute-start.11 = (f32[40,128]{1,0:T(8,128)S(1)}, f32[40,128]{1,0:T(8,128)S(1)}, u32[]{:S(2)}, u32[]{:S(2)}) collective-permute-start(f32[40,128]{1,0:T(8,128)S(1)} %get-tuple-element.95), channel_id=1, source_target_pairs={{0,3},{1,2},{2,1},{3,0},{4,7},{5,6},{6,5},{7,4},{8,11},{9,10},{10,... | collective-permute-start | bytes 61448 | tf_op jit(solution)/shard_map/ppermute | solution.py:623
  29.1 3.8 %collective-permute-start.10 = (f32[40,128]{1,0:T(8,128)S(1)}, f32[40,128]{1,0:T(8,128)S(1)}, u32[]{:S(2)}, u32[]{:S(2)}) collective-permute-start(f32[40,128]{1,0:T(8,128)S(1)} %get-tuple-element.95), channel_id=1, source_target_pairs={{0,1},{1,0},{2,3},{3,2},{4,5},{5,4},{6,7},{7,6},{8,9},{9,8},{10,11... | collective-permute-start | bytes 61448 | tf_op jit(solution)/shard_map/ppermute | solution.py:622
  29.1 4.9 %collective-permute-start.9 = (f32[16,128]{1,0:T(8,128)S(1)}, f32[16,128]{1,0:T(8,128)S(1)}, u32[]{:S(2)}, u32[]{:S(2)}) collective-permute-start(f32[16,128]{1,0:T(8,128)S(1)} %slice.20), channel_id=1, source_target_pairs={{0,2},{1,3},{2,0},{3,1},{4,6},{5,7},{6,4},{7,5},{8,10},{9,11},{10,... | collective-permute-start | bytes 24584 | tf_op jit(solution)/shard_map/ppermute | solution.py:624
  34.1 5.6 %collective-permute-start.14 = (f32[208,128]{1,0:T(8,128)S(1)}, f32[208,128]{1,0:T(8,128)S(1)}, u32[]{:S(2)}, u32[]{:S(2)}) collective-permute-start(f32[208,128]{1,0:T(8,128)S(1)} %get-tuple-element.109), channel_id=1, source_target_pairs={{4,8},{12,16},{20,24},{28,0},{8,4},{16,12},{24,20},{0,28},{5,9},{1... | collective-permute-start | bytes 319496 | tf_op jit(solution)/shard_map/ppermute | solution.py:720
  34.7 4.2 %collective-permute-start.13 = (f32[192,128]{1,0:T(8,128)S(1)}, f32[192,128]{1,0:T(8,128)S(1)}, u32[]{:S(2)}, u32[]{:S(2)}) collective-permute-start(f32[192,128]{1,0:T(8,128)S(1)} %get-tuple-element.108), channel_id=1, source_target_pairs={{0,4},{4,0},{8,12},{12,8},{16,20},{20,16},{24,28},{28,24},{1,5},{5... | collective-permute-start | bytes 294920 | tf_op jit(solution)/shard_map/ppermute | solution.py:607
  37.6 3.8 %collective-permute-start.12 = (f32[16,128]{1,0:T(8,128)S(1)}, f32[16,128]{1,0:T(8,128)S(1)}, u32[]{:S(2)}, u32[]{:S(2)}) collective-permute-start(f32[16,128]{1,0:T(8,128)S(1)} %get-tuple-element.107), channel_id=1, source_target_pairs={{0,16},{4,20},{8,24},{12,28},{16,0},{20,4},{24,8},{28,12},{1,17},{... | collective-permute-start | bytes 24584 | tf_op jit(solution)/shard_map/ppermute | solution.py:721
  39.7 1.8 %collective-permute-start.15 = (f32[16,128]{1,0:T(8,128)S(1)}, f32[16,128]{1,0:T(8,128)S(1)}, u32[]{:S(2)}, u32[]{:S(2)}) collective-permute-start(f32[16,128]{1,0:T(8,128)S(1)} %slice.23), channel_id=1, source_target_pairs={{0,4},{4,0},{8,12},{12,8},{16,20},{20,16},{24,28},{28,24},{1,5},{5... | collective-permute-start | bytes 24584 | tf_op jit(solution)/shard_map/ppermute | solution.py:607

commit v14 on v13

--- a/solution.py
+++ b/solution.py
@@ -284,12 +284,6 @@
     turbine_a, turbine_b = pick_pair(split_blocks(sources), b0, ny)
     sel = jnp.concatenate([turbine_a, turbine_b], axis=0)
     sel_ref[...] = sel
-    turned = jnp.concatenate([sel, jnp.zeros((CZ - 2 * ROWS, CZ), F32)], axis=0).T
-
-    def column(k):
-        picks = (2 * k, 2 * k + 1, ROWS + 2 * k, ROWS + 2 * k + 1)
-        return jnp.concatenate([turned[:, j : j + 1] for j in picks], axis=0)
-
     table = tab_ref[...]
     lane = lax.broadcasted_iota(jnp.int32, (PTS, CZ), 1)
     field = []
@@ -307,17 +301,18 @@
     for c in range(3):
         value = jnp.sum(acc[:, c * CZ : (c + 1) * CZ] * wz, axis=1, keepdims=True)
         table = table + jnp.where(lane == 6 + c, value, 0.0)
-    slot = column(6).astype(jnp.int32)
+    slot = jnp.concatenate([sel[j : j + 1] for j in (12, 13, ROWS + 12, ROWS + 13)], axis=1).astype(jnp.int32)
     mine = (slot // HOST) == brick
     local = jnp.where(mine, slot % HOST, -1)
-    hit = (lax.broadcasted_iota(jnp.int32, (PTS, HOST), 1) == local).astype(F32).astype(BF16)
-    first, second = split(table)
-    third = (table - first.astype(F32) - second.astype(F32)).astype(BF16)
-    pulled = [jnp.dot(hit, part, preferred_element_type=F32) for part in (first, second, third)]
-    points = pulled[0] + pulled[1] + pulled[2]
-    points = jnp.where(lane == 9, column(0), points)
-    pts_ref[...] = jnp.where((lane == 0) & jnp.logical_not(mine), -100.0, points)
-    samp_ref[...] = points.T[6:14]
+    hit = (lax.broadcasted_iota(jnp.int32, (HOST, PTS), 0) == local).astype(F32).astype(BF16)
+    by_slot = table.T[0:16]
+    first, second = split(by_slot)
+    third = (by_slot - first.astype(F32) - second.astype(F32)).astype(BF16)
+    pulled = jnp.dot(jnp.concatenate([first, second, third], axis=0), hit, preferred_element_type=F32)
+    points = pulled[0:16] + pulled[16:32] + pulled[32:48]
+    row = lax.broadcasted_iota(jnp.int32, (16, PTS), 0)
+    pts_ref[...] = jnp.where((row == 0) & jnp.logical_not(mine), -100.0, points)
+    samp_ref[...] = points[6:14]
 
 
 def offsets(frac):
@@ -338,7 +333,9 @@
 
 
 def weights_body(pts_ref, sel_ref, gx_ref, gy_ref, pz_ref, pos_ref, pair_ref, edge_ref):
-    table = pts_ref[...].T
+    table = pts_ref[...]
+    sel = sel_ref[...]
+    turned = jnp.concatenate([sel, jnp.zeros((CZ - 2 * ROWS, CZ), F32)], axis=0).T
     gx = profile(YROWS, CX, table[0:1], table[3:4])
     gy = profile(CY, CY, table[1:2], table[4:5])
     gx_ref[...] = gx
@@ -348,7 +345,8 @@
     for t in range(2):
         at = t * ROWS
         radius = jnp.concatenate([sel_ref[at : at + 1], sel_ref[at + 1 : at + 2]], axis=1)
-        spacing = radius - pts_ref[t * P_SIZE : (t + 1) * P_SIZE, 9:10]
+        column = jnp.concatenate([turned[:, at : at + 1], turned[:, at + 1 : at + 2]], axis=0)
+        spacing = radius - column
         pair_ref[t] = spacing / (spacing * spacing + CORE_SQ)
     for k in range(4):
         edge_ref[k * CY : (k + 1) * CY] = gx[CX + k : CX + k + 1] * gy
@@ -679,7 +677,7 @@
     (face_a, face_b, from_x), (sums, base_more) = after((face_a, face_b, from_x), (sums, base_more))
     samp, sel, pts = call(
         lambda *refs: select_body(len(from_x), *refs),
-        [(8, PTS), (2 * ROWS, CZ), (PTS, CZ)],
+        [(8, PTS), (2 * ROWS, CZ), (16, PTS)],
         9 + len(from_x),
         "select",
     )(table, sums, edge, wz, face_a, face_b, rec_c, rec_d, blocks, *from_x)

time: 42.6 us -> 42.1 us (0.988)
    pallas_call x1, Pallas kernels: 1.52 us -> 0.96 us  [per_device(): call(lambda *refs: select_body(len(from_x), *refs), [(8, PTS), (2 * ROWS,...]
  transfers between devices with their start and end apart: 16 -> 16, of which waited for: 5 -> 5; matrix products, arithmetic and copies ran while one was open for 0% -> 0% of each run, Pallas kernels for 37% -> 38%
where the time goes in v14:
time: 42.1 us; the launch traced here: 41.9 us
  Pallas kernels  20.1 us (48%)
  starting transfers between devices  17.3 us (41%)
  waiting for transfers between devices  2.68 us (6%)
  between operations  1.81 us (4%)
    ppermute x2, starting transfers between devices, exchange_y(): from_d = lax.ppermute(to_d, 'gy', flip(ny, 3) if short else odd_pairs(ny))  5.18 us
    pallas_call x5, Pallas kernels, stencil(): call(lambda *refs: stencil_body(start, *refs), [(3, count, CY, CZ)], 1, '...  3.92 us
    pallas_call x2, Pallas kernels, spread(): call(lambda *refs: spread_body(start, *refs), [(3, CX // 2, CY, CZ)], 3 +...  3.66 us
    ppermute x2, starting transfers between devices, exchange_y(): from_c = lax.ppermute(to_c, 'gy', flip(ny, 1))  3.09 us
    pallas_call x1, Pallas kernels, per_device(): call(sample_low_body, [(HOST, CZ), (HOST, 3 * CZ), (6, CY, CZ), (2, CX, C...  2.6 us
    pallas_call x1, Pallas kernels, per_device(): call(sample_high_body, [(HOST, 3 * CZ), (HOST, CZ), (HOST, CZ)], 3, 'samp...  2.43 us
    ppermute x1, starting transfers between devices, per_device(): face_b = lax.ppermute(pay_b, 'gx', odd_pairs(nx, ring))  2.41 us
    ppermute x2, starting transfers between devices, across_x(): lax.ppermute(b, 'gx', p)  2.21 us
  transfers between devices with their start and end apart: 16, of which 5 were waited for; matrix products, arithmetic and copies ran while one was open for 0% of the time, Pallas kernels for 38%

profile of v14, /device:TPU:0, one launch (start us, length us, event | category | flops | bytes accessed | tf_op | source)
XLA Modules:
  0.0 41.9 jit_solution(11907725084748996697)
XLA Ops:
  1.5 1.2 %pack.1 = (f32[208,128]{1,0:T(8,128)S(1)}, f32[208,128]{1,0:T(8,128)S(1)}, f32[16,128]{1,0:T(8,128)S(1)}) custom-call(f32[3,64,32,128]{3,2,1,0:T(8,128)} %refs_0_.9, f32[1,1]{1,0:T(1,128)} %bitcast.6.spin_hbm, f32[2,128]{1,0:T(2,128)} %bitcast.7, f32[2,128]{1,0:T(2,128)} %bitcast.8, f32[2,128]{1,0:T(2,128)} %bitcast.9, f32[2,128]{1,0:T(2,128)} %bitcast.10, ...), custom_call_target="tpu_custom_call" | custom-call | tf_op jit(solution)/shard_map/pack/pallas_call | solution.py:640
  2.6 3.1 %collective-permute-start = (f32[208,128]{1,0:T(8,128)S(1)}, f32[208,128]{1,0:T(8,128)S(1)}, u32[]{:S(2)}, u32[]{:S(2)}) collective-permute-start(f32[208,128]{1,0:T(8,128)S(1)} %get-tuple-element.64), channel_id=1, source_target_pairs={{0,1},{1,0},{2,3},{3,2},{4,5},{5,4},{6,7},{7,6},{8,9},{9,8},{10,11... | collective-permute-start | bytes 319496 | tf_op jit(solution)/shard_map/ppermute | solution.py:620
  5.7 2.5 %collective-permute-start.1 = (f32[208,128]{1,0:T(8,128)S(1)}, f32[208,128]{1,0:T(8,128)S(1)}, u32[]{:S(2)}, u32[]{:S(2)}) collective-permute-start(f32[208,128]{1,0:T(8,128)S(1)} %get-tuple-element.65), channel_id=1, source_target_pairs={{0,3},{1,2},{2,1},{3,0},{4,7},{5,6},{6,5},{7,4},{8,11},{9,10},{10,... | collective-permute-start | bytes 319496 | tf_op jit(solution)/shard_map/ppermute | solution.py:621
  8.2 0.1 collective-permute-start.2
  8.3 1.5 %stencil.5.refs_3_ = f32[3,24,32,128]{3,2,1,0:T(8,128)S(1)} custom-call(f32[3,64,32,128]{3,2,1,0:T(8,128)S(1)} %copy-done), custom_call_target="tpu_custom_call" | custom-call | tf_op jit(solution)/shard_map/stencil/pallas_call | solution.py:651
  9.8 2.6 %sample_low.1 = (f32[512,128]{1,0:T(8,128)S(1)}, f32[512,384]{1,0:T(8,128)S(1)}, f32[6,32,128]{2,1,0:T(8,128)S(1)}, f32[2,64,128]{2,1,0:T(8,128)S(1)}) custom-call(f32[3,64,32,128]{3,2,1,0:T(8,128)S(1)} %copy-done, s32[3,512]{1,0:T(4,128)S(1)} %copy-done.1, f32[3,512]{1,0:T(4,128)S(1)} %copy-done.2), custom_call_target="tpu_custom_call" | custom-call | tf_op jit(solution)/shard_map/sample_low/pallas_call | solution.py:654
  12.4 1.2 %collective-permute-done.2 = f32[16,128]{1,0:T(8,128)S(1)} collective-permute-done((f32[16,128]{1,0:T(8,128)S(1)}, f32[16,128]{1,0:T(8,128)S(1)}, u32[]{:S(2)}, u32[]{:S(2)}) %collective-permute-start.2) | collective-permute-done | bytes 8224 | tf_op jit(solution)/shard_map/ppermute | solution.py:622
  13.7 1.0 %stencil.6.refs_3_ = f32[3,16,32,128]{3,2,1,0:T(8,128)S(1)} custom-call(f32[3,64,32,128]{3,2,1,0:T(8,128)S(1)} %copy-done), custom_call_target="tpu_custom_call" | custom-call | tf_op jit(solution)/shard_map/stencil/pallas_call | solution.py:651
  14.7 0.2 collective-permute-done.3.refs_4_
  15.0 2.4 %collective-permute-start.5 = (f32[152,128]{1,0:T(8,128)S(1)}, f32[152,128]{1,0:T(8,128)S(1)}, u32[]{:S(2)}, u32[]{:S(2)}) collective-permute-start(f32[152,128]{1,0:T(8,128)S(1)} %get-tuple-element.73), channel_id=1, source_target_pairs={{4,8},{12,16},{20,24},{28,0},{8,4},{16,12},{24,20},{0,28},{5,9},{1... | collective-permute-start | bytes 233480 | tf_op jit(solution)/shard_map/ppermute | solution.py:670
  17.5 0.8 %collective-permute-start.6 = (f32[32,128]{1,0:T(8,128)S(1)}, f32[32,128]{1,0:T(8,128)S(1)}, u32[]{:S(2)}, u32[]{:S(2)}) collective-permute-start(f32[32,128]{1,0:T(8,128)S(1)} %get-tuple-element.74), channel_id=1, source_target_pairs={{0,16},{4,20},{8,24},{12,28},{16,0},{20,4},{24,8},{28,12},{1,17},{... | collective-permute-start | bytes 49160 | tf_op jit(solution)/shard_map/ppermute | solution.py:602
  18.2 1.4 %collective-permute-start.7 = (f32[32,128]{1,0:T(8,128)S(1)}, f32[32,128]{1,0:T(8,128)S(1)}, u32[]{:S(2)}, u32[]{:S(2)}) collective-permute-start(f32[32,128]{1,0:T(8,128)S(1)} %get-tuple-element.75), channel_id=1, source_target_pairs={{0,24},{4,12},{8,0},{12,20},{16,8},{20,28},{24,16},{28,4},{1,25},{... | collective-permute-start | bytes 49160 | tf_op jit(solution)/shard_map/ppermute | solution.py:602
  19.7 0.5 %stencil.7.refs_4_ = f32[3,8,32,128]{3,2,1,0:T(8,128)S(1)} custom-call(f32[3,64,32,128]{3,2,1,0:T(8,128)S(1)} %copy-done), custom_call_target="tpu_custom_call" | custom-call | tf_op jit(solution)/shard_map/stencil/pallas_call | solution.py:651
  20.2 2.4 %sample_high.1 = (f32[512,384]{1,0:T(8,128)S(1)}, f32[512,128]{1,0:T(8,128)S(1)}, f32[512,128]{1,0:T(8,128)S(1)}) custom-call(f32[3,64,32,128]{3,2,1,0:T(8,128)S(1)} %copy-done, f32[512,128]{1,0:T(8,128)S(1)} %get-tuple-element.62.tab_ref.refs_0_, f32[512,384]{1,0:T(8,128)S(1)} %get-tuple-element.76.low_ref), custom_call_target="tpu_custom_call" | custom-call | tf_op jit(solution)/shard_map/sample_high/pallas_call | solution.py:673
  22.6 1.0 %select.1 = (f32[8,512]{1,0:T(8,128)S(1)}, f32[32,128]{1,0:T(8,128)S(1)}, f32[16,512]{1,0:T(8,128)S(1)}) custom-call(f32[512,128]{1,0:T(8,128)S(1)} %get-tuple-element.62.tab_ref.refs_0_, f32[512,384]{1,0:T(8,128)S(1)} %get-tuple-element.78.refs_1_, f32[512,128]{1,0:T(8,128)S(1)} %get-tuple-element.79.refs_2_, f32[512,128]{1,0:T(8,128)S(1)} %get-tuple-element.80.refs_3_, ...), custom_call_target="tpu_custom_call" | custom-call | tf_op jit(solution)/shard_map/select/pallas_call | solution.py:678
  23.6 0.5 %stencil.8.refs_4_ = f32[3,8,32,128]{3,2,1,0:T(8,128)S(1)} custom-call(f32[3,64,32,128]{3,2,1,0:T(8,128)S(1)} %copy-done), custom_call_target="tpu_custom_call" | custom-call | tf_op jit(solution)/shard_map/stencil/pallas_call | solution.py:651
  24.1 0.5 %weights.1 = (f32[72,512]{1,0:T(8,128)S(1)}, f32[32,512]{1,0:T(8,128)S(1)}, f32[128,512]{1,0:T(8,128)S(1)}, f32[24,128]{1,0:T(8,128)S(1)}, f32[2,256,256]{2,1,0:T(8,128)S(1)}, /*index=5*/f32[128,512]{1,0:T(8,128)S(1)}) custom-call(f32[16,512]{1,0:T(8,128)S(1)} %get-tuple-element.89.pts_ref, f32[32,128]{1,0:T(8,128)S(1)} %get-tuple-element.88.sel_ref), custom_call_target="tpu_custom_call" | custom-call | tf_op jit(solution)/shard_map/weights/pallas_call | solution.py:685
  24.6 0.2 collective-permute-done.8.other_ref
  24.8 1.0 %loads.1 = (f32[384,512]{1,0:T(8,128)S(1)}, f32[40,128]{1,0:T(8,128)S(1)}, f32[384,128]{1,0:T(8,128)S(1)}) custom-call(f32[8,512]{1,0:T(8,128)S(1)} %get-tuple-element.86.samp_ref, f32[8,512]{1,0:T(8,128)S(1)} %collective-permute-done.8.other_ref, f32[32,128]{1,0:T(8,128)S(1)} %get-tuple-element.88.sel_ref, f32[128,512]{1,0:T(8,128)S(1)} %get-tuple-element.90.pz_ref, ...), custom_call_target="tpu_custom_call" | custom-call | tf_op jit(solution)/shard_map/loads/pallas_call | solution.py:692
  25.8 2.7 %collective-permute-start.11 = (f32[40,128]{1,0:T(8,128)S(1)}, f32[40,128]{1,0:T(8,128)S(1)}, u32[]{:S(2)}, u32[]{:S(2)}) collective-permute-start(f32[40,128]{1,0:T(8,128)S(1)} %get-tuple-element.95), channel_id=1, source_target_pairs={{0,3},{1,2},{2,1},{3,0},{4,7},{5,6},{6,5},{7,4},{8,11},{9,10},{10,... | collective-permute-start | bytes 61448 | tf_op jit(solution)/shard_map/ppermute | solution.py:621
  28.5 1.7 %collective-permute-start.9 = (f32[16,128]{1,0:T(8,128)S(1)}, f32[16,128]{1,0:T(8,128)S(1)}, u32[]{:S(2)}, u32[]{:S(2)}) collective-permute-start(f32[16,128]{1,0:T(8,128)S(1)} %slice.20), channel_id=1, source_target_pairs={{0,2},{1,3},{2,0},{3,1},{4,6},{5,7},{6,4},{7,5},{8,10},{9,11},{10,... | collective-permute-start | bytes 24584 | tf_op jit(solution)/shard_map/ppermute | solution.py:622
  30.3 1.8 %spread.2.main_low.refs_1_ = f32[3,32,32,128]{3,2,1,0:T(8,128)S(1)} custom-call(f32[384,512]{1,0:T(8,128)S(1)} %get-tuple-element.96.refs_0_, f32[72,512]{1,0:T(8,128)S(1)} %get-tuple-element.97.refs_1_, f32[32,512]{1,0:T(8,128)S(1)} %get-tuple-element.98.refs_2_, f32[3,24,32,128]{3,2,1,0:T(8,128)S(1)} %stencil.5.refs_3_, f32[3,8,32,128]{3,2,1,0:T(8,128)S(1)} %stencil.7.refs_4_), custom_call_target="tpu_custom_call" | custom-call | tf_op jit(solution)/shard_map/spread/pallas_call | solution.py:702
  32.1 0.3 collective-permute-done.10.rec_c
  32.4 1.1 %near.1 = (f32[432,128]{1,0:T(8,128)S(1)}, f32[432,128]{1,0:T(8,128)S(1)}) custom-call(f32[40,128]{1,0:T(8,128)S(1)} %collective-permute-done.10.rec_c, f32[40,128]{1,0:T(8,128)S(1)} %collective-permute-done.11.rec_d), custom_call_target="tpu_custom_call" | custom-call | tf_op jit(solution)/shard_map/near/pallas_call | solution.py:707
  33.6 0.6 %collective-permute-start.14 = (f32[208,128]{1,0:T(8,128)S(1)}, f32[208,128]{1,0:T(8,128)S(1)}, u32[]{:S(2)}, u32[]{:S(2)}) collective-permute-start(f32[208,128]{1,0:T(8,128)S(1)} %get-tuple-element.109), channel_id=1, source_target_pairs={{4,8},{12,16},{20,24},{28,0},{8,4},{16,12},{24,20},{0,28},{5,9},{1... | collective-permute-start | bytes 319496 | tf_op jit(solution)/shard_map/ppermute | solution.py:718
  34.2 0.6 %collective-permute-start.13 = (f32[192,128]{1,0:T(8,128)S(1)}, f32[192,128]{1,0:T(8,128)S(1)}, u32[]{:S(2)}, u32[]{:S(2)}) collective-permute-start(f32[192,128]{1,0:T(8,128)S(1)} %get-tuple-element.108), channel_id=1, source_target_pairs={{0,4},{4,0},{8,12},{12,8},{16,20},{20,16},{24,28},{28,24},{1,5},{5... | collective-permute-start | bytes 294920 | tf_op jit(solution)/shard_map/ppermute | solution.py:605
  34.8 0.5 %stencil.9.refs_5_ = f32[3,8,32,128]{3,2,1,0:T(8,128)S(1)} custom-call(f32[3,64,32,128]{3,2,1,0:T(8,128)S(1)} %copy-done), custom_call_target="tpu_custom_call" | custom-call | tf_op jit(solution)/shard_map/stencil/pallas_call | solution.py:651
  35.3 1.8 %spread.3.main_high.refs_2_ = f32[3,32,32,128]{3,2,1,0:T(8,128)S(1)} custom-call(f32[384,512]{1,0:T(8,128)S(1)} %get-tuple-element.96.refs_0_, f32[72,512]{1,0:T(8,128)S(1)} %get-tuple-element.97.refs_1_, f32[32,512]{1,0:T(8,128)S(1)} %get-tuple-element.98.refs_2_, f32[3,16,32,128]{3,2,1,0:T(8,128)S(1)} %stencil.6.refs_3_, ...), custom_call_target="tpu_custom_call" | custom-call | tf_op jit(solution)/shard_map/spread/pallas_call | solution.py:702
  37.1 1.3 %collective-permute-start.12 = (f32[16,128]{1,0:T(8,128)S(1)}, f32[16,128]{1,0:T(8,128)S(1)}, u32[]{:S(2)}, u32[]{:S(2)}) collective-permute-start(f32[16,128]{1,0:T(8,128)S(1)} %get-tuple-element.107), channel_id=1, source_target_pairs={{0,16},{4,20},{8,24},{12,28},{16,0},{20,4},{24,8},{28,12},{1,17},{... | collective-permute-start | bytes 24584 | tf_op jit(solution)/shard_map/ppermute | solution.py:719
  38.4 0.7 %collective-permute-done.14.refs_10_ = f32[208,128]{1,0:T(8,128)S(1)} collective-permute-done((f32[208,128]{1,0:T(8,128)S(1)}, f32[208,128]{1,0:T(8,128)S(1)}, u32[]{:S(2)}, u32[]{:S(2)}) %collective-permute-start.14) | collective-permute-done | bytes 106528 | tf_op jit(solution)/shard_map/ppermute | solution.py:718
  39.2 1.7 %inside.1.refs_0_ = f32[3,64,32,128]{3,2,1,0:T(8,128)} custom-call(f32[3,32,32,128]{3,2,1,0:T(8,128)S(1)} %spread.2.main_low.refs_1_, f32[3,32,32,128]{3,2,1,0:T(8,128)S(1)} %spread.3.main_high.refs_2_, f32[2,64,128]{2,1,0:T(8,128)S(1)} %get-tuple-element.116.y_ref.refs_4_, f32[208,128]{1,0:T(8,128)S(1)} %collective-permute-done.refs_1_.refs_6_.rec_c.refs_7_, ...), custom_call_target="tpu_custom_call" | custom-call | tf_op jit(solution)/shard_map/inside/pallas_call | solution.py:725
  40.9 0.8 %final.1 = (f32[3,64,32,128]{3,2,1,0:T(8,128)}, f32[3,256]{1,0:T(4,128)}) custom-call(f32[3,64,32,128]{3,2,1,0:T(8,128)} %inside.1.refs_0_, f32[3,32,32,128]{3,2,1,0:T(8,128)S(1)} %spread.2.main_low.refs_1_, f32[3,32,32,128]{3,2,1,0:T(8,128)S(1)} %spread.3.main_high.refs_2_, ...), custom_call_target="tpu_custom_call", output_to_operand_aliasing={{0}: (0, {})} | custom-call | tf_op jit(solution)/shard_map/final/pallas_call | solution.py:736
  (32 shorter events, 0.3 us)
Async XLA Ops:
  0.6 7.7 %copy-start = (f32[3,64,32,128]{3,2,1,0:T(8,128)S(1)}, f32[3,64,32,128]{3,2,1,0:T(8,128)}, u32[]{:S(2)}) copy-start(f32[3,64,32,128]{3,2,1,0:T(8,128)} %refs_0_.9) | copy-start | bytes 9437188
  1.4 8.3 %copy-start.1 = (s32[3,512]{1,0:T(4,128)S(1)}, s32[3,512]{1,0:T(4,128)}, u32[]{:S(2)}) copy-start(s32[3,512]{1,0:T(4,128)} %cell_ref.1) | copy-start | bytes 18436
  1.4 8.3 %copy-start.2 = (f32[3,512]{1,0:T(4,128)S(1)}, f32[3,512]{1,0:T(4,128)}, u32[]{:S(2)}) copy-start(f32[3,512]{1,0:T(4,128)} %frac_ref.1) | copy-start | bytes 18436
  2.6 11.0 %collective-permute-start = (f32[208,128]{1,0:T(8,128)S(1)}, f32[208,128]{1,0:T(8,128)S(1)}, u32[]{:S(2)}, u32[]{:S(2)}) collective-permute-start(f32[208,128]{1,0:T(8,128)S(1)} %get-tuple-element.64), channel_id=1, source_target_pairs={{0,1},{1,0},{2,3},{3,2},{4,5},{5,4},{6,7},{7,6},{8,9},{9,8},{10,11... | collective-permute-start | bytes 319496 | tf_op jit(solution)/shard_map/ppermute | solution.py:620
  5.7 7.9 %collective-permute-start.1 = (f32[208,128]{1,0:T(8,128)S(1)}, f32[208,128]{1,0:T(8,128)S(1)}, u32[]{:S(2)}, u32[]{:S(2)}) collective-permute-start(f32[208,128]{1,0:T(8,128)S(1)} %get-tuple-element.65), channel_id=1, source_target_pairs={{0,3},{1,2},{2,1},{3,0},{4,7},{5,6},{6,5},{7,4},{8,11},{9,10},{10,... | collective-permute-start | bytes 319496 | tf_op jit(solution)/shard_map/ppermute | solution.py:621
  8.2 5.4 %collective-permute-start.2 = (f32[16,128]{1,0:T(8,128)S(1)}, f32[16,128]{1,0:T(8,128)S(1)}, u32[]{:S(2)}, u32[]{:S(2)}) collective-permute-start(f32[16,128]{1,0:T(8,128)S(1)} %get-tuple-element.66), channel_id=1, source_target_pairs={{0,2},{1,3},{2,0},{3,1},{4,6},{5,7},{6,4},{7,5},{8,10},{9,11},{10,... | collective-permute-start | bytes 24584 | tf_op jit(solution)/shard_map/ppermute | solution.py:622
  13.7 1.3 %collective-permute-start.3 = (f32[64,128]{1,0:T(8,128)S(1)}, f32[64,128]{1,0:T(8,128)S(1)}, u32[]{:S(2)}, u32[]{:S(2)}) collective-permute-start(f32[64,128]{1,0:T(8,128)S(1)} %pad_maximum_fusion.refs_3_), channel_id=1, source_target_pairs={{0,4},{4,0},{8,12},{12,8},{16,20},{20,16},{24,28},{28,24},{1,5},{5... | collective-permute-start | bytes 98312 | tf_op jit(solution)/shard_map/ppermute | solution.py:605
  15.0 7.6 %collective-permute-start.5 = (f32[152,128]{1,0:T(8,128)S(1)}, f32[152,128]{1,0:T(8,128)S(1)}, u32[]{:S(2)}, u32[]{:S(2)}) collective-permute-start(f32[152,128]{1,0:T(8,128)S(1)} %get-tuple-element.73), channel_id=1, source_target_pairs={{4,8},{12,16},{20,24},{28,0},{8,4},{16,12},{24,20},{0,28},{5,9},{1... | collective-permute-start | bytes 233480 | tf_op jit(solution)/shard_map/ppermute | solution.py:670
  17.5 5.2 %collective-permute-start.4 = (f32[120,128]{1,0:T(8,128)S(1)}, f32[120,128]{1,0:T(8,128)S(1)}, u32[]{:S(2)}, u32[]{:S(2)}) collective-permute-start(f32[120,128]{1,0:T(8,128)S(1)} %get-tuple-element.72), channel_id=1, source_target_pairs={{0,4},{4,0},{8,12},{12,8},{16,20},{20,16},{24,28},{28,24},{1,5},{5... | collective-permute-start | bytes 184328 | tf_op jit(solution)/shard_map/ppermute | solution.py:605
  17.5 5.1 %collective-permute-start.6 = (f32[32,128]{1,0:T(8,128)S(1)}, f32[32,128]{1,0:T(8,128)S(1)}, u32[]{:S(2)}, u32[]{:S(2)}) collective-permute-start(f32[32,128]{1,0:T(8,128)S(1)} %get-tuple-element.74), channel_id=1, source_target_pairs={{0,16},{4,20},{8,24},{12,28},{16,0},{20,4},{24,8},{28,12},{1,17},{... | collective-permute-start | bytes 49160 | tf_op jit(solution)/shard_map/ppermute | solution.py:602
  18.2 4.4 %collective-permute-start.7 = (f32[32,128]{1,0:T(8,128)S(1)}, f32[32,128]{1,0:T(8,128)S(1)}, u32[]{:S(2)}, u32[]{:S(2)}) collective-permute-start(f32[32,128]{1,0:T(8,128)S(1)} %get-tuple-element.75), channel_id=1, source_target_pairs={{0,24},{4,12},{8,0},{12,20},{16,8},{20,28},{24,16},{28,4},{1,25},{... | collective-permute-start | bytes 49160 | tf_op jit(solution)/shard_map/ppermute | solution.py:602
  23.6 1.2 %collective-permute-start.8 = (f32[8,512]{1,0:T(8,128)S(1)}, f32[8,512]{1,0:T(8,128)S(1)}, u32[]{:S(2)}, u32[]{:S(2)}) collective-permute-start(f32[8,512]{1,0:T(8,128)S(1)} %get-tuple-element.86.samp_ref), channel_id=1, source_target_pairs={{0,4},{4,0},{8,12},{12,8},{16,20},{20,16},{24,28},{28,24},{1,5},{5... | collective-permute-start | bytes 49160 | tf_op jit(solution)/shard_map/ppermute | solution.py:605
  25.8 6.3 %collective-permute-start.11 = (f32[40,128]{1,0:T(8,128)S(1)}, f32[40,128]{1,0:T(8,128)S(1)}, u32[]{:S(2)}, u32[]{:S(2)}) collective-permute-start(f32[40,128]{1,0:T(8,128)S(1)} %get-tuple-element.95), channel_id=1, source_target_pairs={{0,3},{1,2},{2,1},{3,0},{4,7},{5,6},{6,5},{7,4},{8,11},{9,10},{10,... | collective-permute-start | bytes 61448 | tf_op jit(solution)/shard_map/ppermute | solution.py:621
  28.5 3.9 %collective-permute-start.10 = (f32[40,128]{1,0:T(8,128)S(1)}, f32[40,128]{1,0:T(8,128)S(1)}, u32[]{:S(2)}, u32[]{:S(2)}) collective-permute-start(f32[40,128]{1,0:T(8,128)S(1)} %get-tuple-element.95), channel_id=1, source_target_pairs={{0,1},{1,0},{2,3},{3,2},{4,5},{5,4},{6,7},{7,6},{8,9},{9,8},{10,11... | collective-permute-start | bytes 61448 | tf_op jit(solution)/shard_map/ppermute | solution.py:620
  28.5 5.0 %collective-permute-start.9 = (f32[16,128]{1,0:T(8,128)S(1)}, f32[16,128]{1,0:T(8,128)S(1)}, u32[]{:S(2)}, u32[]{:S(2)}) collective-permute-start(f32[16,128]{1,0:T(8,128)S(1)} %slice.20), channel_id=1, source_target_pairs={{0,2},{1,3},{2,0},{3,1},{4,6},{5,7},{6,4},{7,5},{8,10},{9,11},{10,... | collective-permute-start | bytes 24584 | tf_op jit(solution)/shard_map/ppermute | solution.py:622
  33.6 5.6 %collective-permute-start.14 = (f32[208,128]{1,0:T(8,128)S(1)}, f32[208,128]{1,0:T(8,128)S(1)}, u32[]{:S(2)}, u32[]{:S(2)}) collective-permute-start(f32[208,128]{1,0:T(8,128)S(1)} %get-tuple-element.109), channel_id=1, source_target_pairs={{4,8},{12,16},{20,24},{28,0},{8,4},{16,12},{24,20},{0,28},{5,9},{1... | collective-permute-start | bytes 319496 | tf_op jit(solution)/shard_map/ppermute | solution.py:718
  34.2 4.2 %collective-permute-start.13 = (f32[192,128]{1,0:T(8,128)S(1)}, f32[192,128]{1,0:T(8,128)S(1)}, u32[]{:S(2)}, u32[]{:S(2)}) collective-permute-start(f32[192,128]{1,0:T(8,128)S(1)} %get-tuple-element.108), channel_id=1, source_target_pairs={{0,4},{4,0},{8,12},{12,8},{16,20},{20,16},{24,28},{28,24},{1,5},{5... | collective-permute-start | bytes 294920 | tf_op jit(solution)/shard_map/ppermute | solution.py:605
  37.1 3.8 %collective-permute-start.12 = (f32[16,128]{1,0:T(8,128)S(1)}, f32[16,128]{1,0:T(8,128)S(1)}, u32[]{:S(2)}, u32[]{:S(2)}) collective-permute-start(f32[16,128]{1,0:T(8,128)S(1)} %get-tuple-element.107), channel_id=1, source_target_pairs={{0,16},{4,20},{8,24},{12,28},{16,0},{20,4},{24,8},{28,12},{1,17},{... | collective-permute-start | bytes 24584 | tf_op jit(solution)/shard_map/ppermute | solution.py:719
  39.2 1.8 %collective-permute-start.15 = (f32[16,128]{1,0:T(8,128)S(1)}, f32[16,128]{1,0:T(8,128)S(1)}, u32[]{:S(2)}, u32[]{:S(2)}) collective-permute-start(f32[16,128]{1,0:T(8,128)S(1)} %slice.23), channel_id=1, source_target_pairs={{0,4},{4,0},{8,12},{12,8},{16,20},{20,16},{24,28},{28,24},{1,5},{5... | collective-permute-start | bytes 24584 | tf_op jit(solution)/shard_map/ppermute | solution.py:605

commit v15 on v14

--- a/solution.py
+++ b/solution.py
@@ -524,10 +524,11 @@
     return pltpu.make_async_copy(buf.at[:, pl.ds(at, size)], out_ref.at[:, pl.ds(first, size)], sem)
 
 
-def inside_body(main_low, main_high, y_ref, rec_c, rec_d, rim_low, rim_high, out_ref, buf, sems):
+def inside_body(chunks, *refs):
+    main_low, main_high, y_ref, rec_c, rec_d, rim_low, rim_high, out_ref, buf, sems = refs[-10:]
     _, even_y, _, _, _, _ = place()
     copies = []
-    for k, (first, size) in enumerate(INNER):
+    for k, (first, size) in enumerate(chunks):
         face_terms(buf, first - 2, first, size, main_low, main_high, y_ref, rec_c, rec_d, rim_low, rim_high, even_y)
         copies.append(chunk_copy(buf, first - 2, out_ref, first, size, sems.at[k]))
         copies[-1].start()
@@ -719,18 +720,25 @@
     rets = [lax.ppermute(across[0], "gx", flip(nx, 4))] if ring else gather_x(back)
     rim_a = swap(pay_a)
     main_high = spread(CX // 2, base_third, base_next, stencil(7 * CX // 8, CX // 8))
-    (rim_a, rim_b), (main_low, main_high) = after((rim_a, rim_b), (main_low, main_high))
+    faces = (main_low, main_high, y_faces, rec_c, rec_d, rim_low, rim_high)
+    room = [pltpu.VMEM((3, CX - 4, CY, CZ), F32), dma((N_CHUNK,))]
+    inside = call(
+        lambda *refs: inside_body(INNER[:2], *refs), [velocity.shape], 7, "inside", scratch=room, out_specs=[HB], vmem=16
+    )(*faces)[0]
+    (rim_a, rim_b), inside = after((rim_a, rim_b), inside)
     if ring:
         rets.append(swap(rim_b[RIM_X:]))
     inside = call(
-        inside_body,
+        lambda *refs: inside_body(INNER[2:], *refs),
         [velocity.shape],
-        7,
+        8,
         "inside",
-        scratch=[pltpu.VMEM((3, CX - 4, CY, CZ), F32), dma((N_CHUNK,))],
+        scratch=room,
+        first=HB,
         out_specs=[HB],
         vmem=16,
-    )(main_low, main_high, y_faces, rec_c, rec_d, rim_low, rim_high)[0]
+        aliases={0: 0},
+    )(inside, *faces)[0]
     rets, inside = after(rets, inside)
     return tuple(
         call(

time: 42.1 us -> 42.2 us (level)
  waiting for transfers between devices: 2.68 us -> 1.94 us
  Pallas kernels: 20.1 us -> 20.8 us
    pallas_call x1 -> x2, Pallas kernels: 1.73 us -> 2.52 us  [the longest x1 1.53 us: per_device(): call(lambda *refs: inside_body(INNER[2:], *refs), [velocity.shape], 8, 'i...]
    ppermute x1, waiting for transfers between devices: 0.75 us -> 0.01 us  [per_device(): rim_b = lax.ppermute(pay_b, 'gx', odd_pairs(nx, ring))]
  transfers between devices with their start and end apart: 16 -> 16, of which waited for: 5 -> 4; matrix products, arithmetic and copies ran while one was open for 0% -> 0% of each run, Pallas kernels for 38% -> 40%
where the time goes in v15:
time: 42.2 us; the launch traced here: 42 us
  Pallas kernels  20.8 us (49%)
  starting transfers between devices  17.4 us (41%)
  waiting for transfers between devices  1.94 us (5%)
  between operations  1.85 us (4%)
    ppermute x2, starting transfers between devices, exchange_y(): from_d = lax.ppermute(to_d, 'gy', flip(ny, 3) if short else odd_pairs(ny))  5.18 us
    pallas_call x5, Pallas kernels, stencil(): call(lambda *refs: stencil_body(start, *refs), [(3, count, CY, CZ)], 1, '...  3.92 us
    pallas_call x2, Pallas kernels, spread(): call(lambda *refs: spread_body(start, *refs), [(3, CX // 2, CY, CZ)], 3 +...  3.66 us
    ppermute x2, starting transfers between devices, exchange_y(): from_c = lax.ppermute(to_c, 'gy', flip(ny, 1))  3.09 us
    pallas_call x1, Pallas kernels, per_device(): call(sample_low_body, [(HOST, CZ), (HOST, 3 * CZ), (6, CY, CZ), (2, CX, C...  2.59 us
    pallas_call x1, Pallas kernels, per_device(): call(sample_high_body, [(HOST, 3 * CZ), (HOST, CZ), (HOST, CZ)], 3, 'samp...  2.43 us
    ppermute x1, starting transfers between devices, per_device(): face_b = lax.ppermute(pay_b, 'gx', odd_pairs(nx, ring))  2.41 us
    ppermute x2, starting transfers between devices, across_x(): lax.ppermute(b, 'gx', p)  2.21 us
  transfers between devices with their start and end apart: 16, of which 4 were waited for; matrix products, arithmetic and copies ran while one was open for 0% of the time, Pallas kernels for 40%

profile of v15, /device:TPU:0, one launch (start us, length us, event | category | flops | bytes accessed | tf_op | source)
XLA Modules:
  0.0 42.0 jit_solution(3353506928988233121)
XLA Ops:
  1.5 1.2 %pack.1 = (f32[208,128]{1,0:T(8,128)S(1)}, f32[208,128]{1,0:T(8,128)S(1)}, f32[16,128]{1,0:T(8,128)S(1)}) custom-call(f32[3,64,32,128]{3,2,1,0:T(8,128)} %refs_0_.9, f32[1,1]{1,0:T(1,128)} %bitcast.6.spin_hbm, f32[2,128]{1,0:T(2,128)} %bitcast.7, f32[2,128]{1,0:T(2,128)} %bitcast.8, f32[2,128]{1,0:T(2,128)} %bitcast.9, f32[2,128]{1,0:T(2,128)} %bitcast.10, ...), custom_call_target="tpu_custom_call" | custom-call | tf_op jit(solution)/shard_map/pack/pallas_call | solution.py:641
  2.6 3.1 %collective-permute-start = (f32[208,128]{1,0:T(8,128)S(1)}, f32[208,128]{1,0:T(8,128)S(1)}, u32[]{:S(2)}, u32[]{:S(2)}) collective-permute-start(f32[208,128]{1,0:T(8,128)S(1)} %get-tuple-element.63), channel_id=1, source_target_pairs={{0,1},{1,0},{2,3},{3,2},{4,5},{5,4},{6,7},{7,6},{8,9},{9,8},{10,11... | collective-permute-start | bytes 319496 | tf_op jit(solution)/shard_map/ppermute | solution.py:621
  5.7 2.5 %collective-permute-start.1 = (f32[208,128]{1,0:T(8,128)S(1)}, f32[208,128]{1,0:T(8,128)S(1)}, u32[]{:S(2)}, u32[]{:S(2)}) collective-permute-start(f32[208,128]{1,0:T(8,128)S(1)} %get-tuple-element.64), channel_id=1, source_target_pairs={{0,3},{1,2},{2,1},{3,0},{4,7},{5,6},{6,5},{7,4},{8,11},{9,10},{10,... | collective-permute-start | bytes 319496 | tf_op jit(solution)/shard_map/ppermute | solution.py:622
  8.2 0.1 collective-permute-start.2
  8.3 1.5 %stencil.5.refs_3_ = f32[3,24,32,128]{3,2,1,0:T(8,128)S(1)} custom-call(f32[3,64,32,128]{3,2,1,0:T(8,128)S(1)} %copy-done), custom_call_target="tpu_custom_call" | custom-call | tf_op jit(solution)/shard_map/stencil/pallas_call | solution.py:652
  9.8 2.6 %sample_low.1 = (f32[512,128]{1,0:T(8,128)S(1)}, f32[512,384]{1,0:T(8,128)S(1)}, f32[6,32,128]{2,1,0:T(8,128)S(1)}, f32[2,64,128]{2,1,0:T(8,128)S(1)}) custom-call(f32[3,64,32,128]{3,2,1,0:T(8,128)S(1)} %copy-done, s32[3,512]{1,0:T(4,128)S(1)} %copy-done.1, f32[3,512]{1,0:T(4,128)S(1)} %copy-done.2), custom_call_target="tpu_custom_call" | custom-call | tf_op jit(solution)/shard_map/sample_low/pallas_call | solution.py:655
  12.4 1.2 %collective-permute-done.2 = f32[16,128]{1,0:T(8,128)S(1)} collective-permute-done((f32[16,128]{1,0:T(8,128)S(1)}, f32[16,128]{1,0:T(8,128)S(1)}, u32[]{:S(2)}, u32[]{:S(2)}) %collective-permute-start.2) | collective-permute-done | bytes 8224 | tf_op jit(solution)/shard_map/ppermute | solution.py:623
  13.7 1.0 %stencil.6.refs_3_ = f32[3,16,32,128]{3,2,1,0:T(8,128)S(1)} custom-call(f32[3,64,32,128]{3,2,1,0:T(8,128)S(1)} %copy-done), custom_call_target="tpu_custom_call" | custom-call | tf_op jit(solution)/shard_map/stencil/pallas_call | solution.py:652
  14.7 0.2 collective-permute-done.3.refs_4_
  15.0 2.4 %collective-permute-start.5 = (f32[152,128]{1,0:T(8,128)S(1)}, f32[152,128]{1,0:T(8,128)S(1)}, u32[]{:S(2)}, u32[]{:S(2)}) collective-permute-start(f32[152,128]{1,0:T(8,128)S(1)} %get-tuple-element.72), channel_id=1, source_target_pairs={{4,8},{12,16},{20,24},{28,0},{8,4},{16,12},{24,20},{0,28},{5,9},{1... | collective-permute-start | bytes 233480 | tf_op jit(solution)/shard_map/ppermute | solution.py:671
  17.5 0.8 %collective-permute-start.6 = (f32[32,128]{1,0:T(8,128)S(1)}, f32[32,128]{1,0:T(8,128)S(1)}, u32[]{:S(2)}, u32[]{:S(2)}) collective-permute-start(f32[32,128]{1,0:T(8,128)S(1)} %get-tuple-element.73), channel_id=1, source_target_pairs={{0,16},{4,20},{8,24},{12,28},{16,0},{20,4},{24,8},{28,12},{1,17},{... | collective-permute-start | bytes 49160 | tf_op jit(solution)/shard_map/ppermute | solution.py:603
  18.2 1.4 %collective-permute-start.7 = (f32[32,128]{1,0:T(8,128)S(1)}, f32[32,128]{1,0:T(8,128)S(1)}, u32[]{:S(2)}, u32[]{:S(2)}) collective-permute-start(f32[32,128]{1,0:T(8,128)S(1)} %get-tuple-element.74), channel_id=1, source_target_pairs={{0,24},{4,12},{8,0},{12,20},{16,8},{20,28},{24,16},{28,4},{1,25},{... | collective-permute-start | bytes 49160 | tf_op jit(solution)/shard_map/ppermute | solution.py:603
  19.7 0.5 %stencil.7.refs_4_ = f32[3,8,32,128]{3,2,1,0:T(8,128)S(1)} custom-call(f32[3,64,32,128]{3,2,1,0:T(8,128)S(1)} %copy-done), custom_call_target="tpu_custom_call" | custom-call | tf_op jit(solution)/shard_map/stencil/pallas_call | solution.py:652
  20.2 2.4 %sample_high.1 = (f32[512,384]{1,0:T(8,128)S(1)}, f32[512,128]{1,0:T(8,128)S(1)}, f32[512,128]{1,0:T(8,128)S(1)}) custom-call(f32[3,64,32,128]{3,2,1,0:T(8,128)S(1)} %copy-done, f32[512,128]{1,0:T(8,128)S(1)} %get-tuple-element.61.tab_ref.refs_0_, f32[512,384]{1,0:T(8,128)S(1)} %get-tuple-element.75.low_ref), custom_call_target="tpu_custom_call" | custom-call | tf_op jit(solution)/shard_map/sample_high/pallas_call | solution.py:674
  22.6 1.0 %select.1 = (f32[8,512]{1,0:T(8,128)S(1)}, f32[32,128]{1,0:T(8,128)S(1)}, f32[16,512]{1,0:T(8,128)S(1)}) custom-call(f32[512,128]{1,0:T(8,128)S(1)} %get-tuple-element.61.tab_ref.refs_0_, f32[512,384]{1,0:T(8,128)S(1)} %get-tuple-element.77.refs_1_, f32[512,128]{1,0:T(8,128)S(1)} %get-tuple-element.78.refs_2_, f32[512,128]{1,0:T(8,128)S(1)} %get-tuple-element.79.refs_3_, ...), custom_call_target="tpu_custom_call" | custom-call | tf_op jit(solution)/shard_map/select/pallas_call | solution.py:679
  23.6 0.5 %stencil.8.refs_4_ = f32[3,8,32,128]{3,2,1,0:T(8,128)S(1)} custom-call(f32[3,64,32,128]{3,2,1,0:T(8,128)S(1)} %copy-done), custom_call_target="tpu_custom_call" | custom-call | tf_op jit(solution)/shard_map/stencil/pallas_call | solution.py:652
  24.1 0.5 %weights.1 = (f32[72,512]{1,0:T(8,128)S(1)}, f32[32,512]{1,0:T(8,128)S(1)}, f32[128,512]{1,0:T(8,128)S(1)}, f32[24,128]{1,0:T(8,128)S(1)}, f32[2,256,256]{2,1,0:T(8,128)S(1)}, /*index=5*/f32[128,512]{1,0:T(8,128)S(1)}) custom-call(f32[16,512]{1,0:T(8,128)S(1)} %get-tuple-element.88.pts_ref, f32[32,128]{1,0:T(8,128)S(1)} %get-tuple-element.87.sel_ref), custom_call_target="tpu_custom_call" | custom-call | tf_op jit(solution)/shard_map/weights/pallas_call | solution.py:686
  24.6 0.2 collective-permute-done.8.other_ref
  24.8 1.0 %loads.1 = (f32[384,512]{1,0:T(8,128)S(1)}, f32[40,128]{1,0:T(8,128)S(1)}, f32[384,128]{1,0:T(8,128)S(1)}) custom-call(f32[8,512]{1,0:T(8,128)S(1)} %get-tuple-element.85.samp_ref, f32[8,512]{1,0:T(8,128)S(1)} %collective-permute-done.8.other_ref, f32[32,128]{1,0:T(8,128)S(1)} %get-tuple-element.87.sel_ref, f32[128,512]{1,0:T(8,128)S(1)} %get-tuple-element.89.pz_ref, ...), custom_call_target="tpu_custom_call" | custom-call | tf_op jit(solution)/shard_map/loads/pallas_call | solution.py:693
  25.8 2.7 %collective-permute-start.11 = (f32[40,128]{1,0:T(8,128)S(1)}, f32[40,128]{1,0:T(8,128)S(1)}, u32[]{:S(2)}, u32[]{:S(2)}) collective-permute-start(f32[40,128]{1,0:T(8,128)S(1)} %get-tuple-element.94), channel_id=1, source_target_pairs={{0,3},{1,2},{2,1},{3,0},{4,7},{5,6},{6,5},{7,4},{8,11},{9,10},{10,... | collective-permute-start | bytes 61448 | tf_op jit(solution)/shard_map/ppermute | solution.py:622
  28.5 1.7 %collective-permute-start.9 = (f32[16,128]{1,0:T(8,128)S(1)}, f32[16,128]{1,0:T(8,128)S(1)}, u32[]{:S(2)}, u32[]{:S(2)}) collective-permute-start(f32[16,128]{1,0:T(8,128)S(1)} %slice.20), channel_id=1, source_target_pairs={{0,2},{1,3},{2,0},{3,1},{4,6},{5,7},{6,4},{7,5},{8,10},{9,11},{10,... | collective-permute-start | bytes 24584 | tf_op jit(solution)/shard_map/ppermute | solution.py:623
  30.3 1.8 %spread.2.refs_0_.refs_1_ = f32[3,32,32,128]{3,2,1,0:T(8,128)S(1)} custom-call(f32[384,512]{1,0:T(8,128)S(1)} %get-tuple-element.95.refs_0_, f32[72,512]{1,0:T(8,128)S(1)} %get-tuple-element.96.refs_1_, f32[32,512]{1,0:T(8,128)S(1)} %get-tuple-element.97.refs_2_, f32[3,24,32,128]{3,2,1,0:T(8,128)S(1)} %stencil.5.refs_3_, f32[3,8,32,128]{3,2,1,0:T(8,128)S(1)} %stencil.7.refs_4_), custom_call_target="tpu_custom_call" | custom-call | tf_op jit(solution)/shard_map/spread/pallas_call | solution.py:703
  32.1 0.3 collective-permute-done.10.rec_c
  32.4 1.1 %near.1 = (f32[432,128]{1,0:T(8,128)S(1)}, f32[432,128]{1,0:T(8,128)S(1)}) custom-call(f32[40,128]{1,0:T(8,128)S(1)} %collective-permute-done.10.rec_c, f32[40,128]{1,0:T(8,128)S(1)} %collective-permute-done.11.rec_d), custom_call_target="tpu_custom_call" | custom-call | tf_op jit(solution)/shard_map/near/pallas_call | solution.py:708
  33.6 0.6 %collective-permute-start.14 = (f32[208,128]{1,0:T(8,128)S(1)}, f32[208,128]{1,0:T(8,128)S(1)}, u32[]{:S(2)}, u32[]{:S(2)}) collective-permute-start(f32[208,128]{1,0:T(8,128)S(1)} %get-tuple-element.108), channel_id=1, source_target_pairs={{4,8},{12,16},{20,24},{28,0},{8,4},{16,12},{24,20},{0,28},{5,9},{1... | collective-permute-start | bytes 319496 | tf_op jit(solution)/shard_map/ppermute | solution.py:719
  34.2 0.6 %collective-permute-start.13 = (f32[192,128]{1,0:T(8,128)S(1)}, f32[192,128]{1,0:T(8,128)S(1)}, u32[]{:S(2)}, u32[]{:S(2)}) collective-permute-start(f32[192,128]{1,0:T(8,128)S(1)} %get-tuple-element.107), channel_id=1, source_target_pairs={{0,4},{4,0},{8,12},{12,8},{16,20},{20,16},{24,28},{28,24},{1,5},{5... | collective-permute-start | bytes 294920 | tf_op jit(solution)/shard_map/ppermute | solution.py:606
  34.8 0.5 %stencil.9.refs_5_ = f32[3,8,32,128]{3,2,1,0:T(8,128)S(1)} custom-call(f32[3,64,32,128]{3,2,1,0:T(8,128)S(1)} %copy-done), custom_call_target="tpu_custom_call" | custom-call | tf_op jit(solution)/shard_map/stencil/pallas_call | solution.py:652
  35.3 1.8 %spread.3.refs_1_.refs_2_ = f32[3,32,32,128]{3,2,1,0:T(8,128)S(1)} custom-call(f32[384,512]{1,0:T(8,128)S(1)} %get-tuple-element.95.refs_0_, f32[72,512]{1,0:T(8,128)S(1)} %get-tuple-element.96.refs_1_, f32[32,512]{1,0:T(8,128)S(1)} %get-tuple-element.97.refs_2_, f32[3,16,32,128]{3,2,1,0:T(8,128)S(1)} %stencil.6.refs_3_, ...), custom_call_target="tpu_custom_call" | custom-call | tf_op jit(solution)/shard_map/spread/pallas_call | solution.py:703
  37.1 1.3 %collective-permute-start.12 = (f32[16,128]{1,0:T(8,128)S(1)}, f32[16,128]{1,0:T(8,128)S(1)}, u32[]{:S(2)}, u32[]{:S(2)}) collective-permute-start(f32[16,128]{1,0:T(8,128)S(1)} %get-tuple-element.106), channel_id=1, source_target_pairs={{0,16},{4,20},{8,24},{12,28},{16,0},{20,4},{24,8},{28,12},{1,17},{... | collective-permute-start | bytes 24584 | tf_op jit(solution)/shard_map/ppermute | solution.py:720
  38.4 1.0 %inside.2.refs_0_ = f32[3,64,32,128]{3,2,1,0:T(8,128)} custom-call(f32[3,32,32,128]{3,2,1,0:T(8,128)S(1)} %spread.2.refs_0_.refs_1_, f32[3,32,32,128]{3,2,1,0:T(8,128)S(1)} %spread.3.refs_1_.refs_2_, f32[2,64,128]{2,1,0:T(8,128)S(1)} %get-tuple-element.112.refs_2_.refs_3_.refs_4_, ...), custom_call_target="tpu_custom_call" | custom-call | tf_op jit(solution)/shard_map/inside/pallas_call | solution.py:725
  39.5 1.5 %inside.3.refs_0_ = f32[3,64,32,128]{3,2,1,0:T(8,128)} custom-call(f32[3,64,32,128]{3,2,1,0:T(8,128)} %inside.2.refs_0_, f32[3,32,32,128]{3,2,1,0:T(8,128)S(1)} %spread.2.refs_0_.refs_1_, f32[3,32,32,128]{3,2,1,0:T(8,128)S(1)} %spread.3.refs_1_.refs_2_, f32[2,64,128]{2,1,0:T(8,128)S(1)} %get-tuple-element.112.refs_2_.refs_3_.refs_4_, ...), custom_call_target="tpu_custom_call", output_to_operand_aliasing={{}: (0, {})} | custom-call | tf_op jit(solution)/shard_map/inside/pallas_call | solution.py:731
  41.1 0.8 %final.1 = (f32[3,64,32,128]{3,2,1,0:T(8,128)}, f32[3,256]{1,0:T(4,128)}) custom-call(f32[3,64,32,128]{3,2,1,0:T(8,128)} %inside.3.refs_0_, f32[3,32,32,128]{3,2,1,0:T(8,128)S(1)} %spread.2.refs_0_.refs_1_, f32[3,32,32,128]{3,2,1,0:T(8,128)S(1)} %spread.3.refs_1_.refs_2_, ...), custom_call_target="tpu_custom_call", output_to_operand_aliasing={{0}: (0, {})} | custom-call | tf_op jit(solution)/shard_map/final/pallas_call | solution.py:744
  (33 shorter events, 0.4 us)
Async XLA Ops:
  0.6 7.7 %copy-start = (f32[3,64,32,128]{3,2,1,0:T(8,128)S(1)}, f32[3,64,32,128]{3,2,1,0:T(8,128)}, u32[]{:S(2)}) copy-start(f32[3,64,32,128]{3,2,1,0:T(8,128)} %refs_0_.9) | copy-start | bytes 9437188
  1.4 8.3 %copy-start.1 = (s32[3,512]{1,0:T(4,128)S(1)}, s32[3,512]{1,0:T(4,128)}, u32[]{:S(2)}) copy-start(s32[3,512]{1,0:T(4,128)} %cell_ref.1) | copy-start | bytes 18436
  1.4 8.3 %copy-start.2 = (f32[3,512]{1,0:T(4,128)S(1)}, f32[3,512]{1,0:T(4,128)}, u32[]{:S(2)}) copy-start(f32[3,512]{1,0:T(4,128)} %frac_ref.1) | copy-start | bytes 18436
  2.6 11.0 %collective-permute-start = (f32[208,128]{1,0:T(8,128)S(1)}, f32[208,128]{1,0:T(8,128)S(1)}, u32[]{:S(2)}, u32[]{:S(2)}) collective-permute-start(f32[208,128]{1,0:T(8,128)S(1)} %get-tuple-element.63), channel_id=1, source_target_pairs={{0,1},{1,0},{2,3},{3,2},{4,5},{5,4},{6,7},{7,6},{8,9},{9,8},{10,11... | collective-permute-start | bytes 319496 | tf_op jit(solution)/shard_map/ppermute | solution.py:621
  5.7 7.9 %collective-permute-start.1 = (f32[208,128]{1,0:T(8,128)S(1)}, f32[208,128]{1,0:T(8,128)S(1)}, u32[]{:S(2)}, u32[]{:S(2)}) collective-permute-start(f32[208,128]{1,0:T(8,128)S(1)} %get-tuple-element.64), channel_id=1, source_target_pairs={{0,3},{1,2},{2,1},{3,0},{4,7},{5,6},{6,5},{7,4},{8,11},{9,10},{10,... | collective-permute-start | bytes 319496 | tf_op jit(solution)/shard_map/ppermute | solution.py:622
  8.2 5.4 %collective-permute-start.2 = (f32[16,128]{1,0:T(8,128)S(1)}, f32[16,128]{1,0:T(8,128)S(1)}, u32[]{:S(2)}, u32[]{:S(2)}) collective-permute-start(f32[16,128]{1,0:T(8,128)S(1)} %get-tuple-element.65), channel_id=1, source_target_pairs={{0,2},{1,3},{2,0},{3,1},{4,6},{5,7},{6,4},{7,5},{8,10},{9,11},{10,... | collective-permute-start | bytes 24584 | tf_op jit(solution)/shard_map/ppermute | solution.py:623
  13.7 1.3 %collective-permute-start.3 = (f32[64,128]{1,0:T(8,128)S(1)}, f32[64,128]{1,0:T(8,128)S(1)}, u32[]{:S(2)}, u32[]{:S(2)}) collective-permute-start(f32[64,128]{1,0:T(8,128)S(1)} %pad_maximum_fusion.refs_3_), channel_id=1, source_target_pairs={{0,4},{4,0},{8,12},{12,8},{16,20},{20,16},{24,28},{28,24},{1,5},{5... | collective-permute-start | bytes 98312 | tf_op jit(solution)/shard_map/ppermute | solution.py:606
  15.0 7.6 %collective-permute-start.5 = (f32[152,128]{1,0:T(8,128)S(1)}, f32[152,128]{1,0:T(8,128)S(1)}, u32[]{:S(2)}, u32[]{:S(2)}) collective-permute-start(f32[152,128]{1,0:T(8,128)S(1)} %get-tuple-element.72), channel_id=1, source_target_pairs={{4,8},{12,16},{20,24},{28,0},{8,4},{16,12},{24,20},{0,28},{5,9},{1... | collective-permute-start | bytes 233480 | tf_op jit(solution)/shard_map/ppermute | solution.py:671
  17.5 5.2 %collective-permute-start.4 = (f32[120,128]{1,0:T(8,128)S(1)}, f32[120,128]{1,0:T(8,128)S(1)}, u32[]{:S(2)}, u32[]{:S(2)}) collective-permute-start(f32[120,128]{1,0:T(8,128)S(1)} %get-tuple-element.71), channel_id=1, source_target_pairs={{0,4},{4,0},{8,12},{12,8},{16,20},{20,16},{24,28},{28,24},{1,5},{5... | collective-permute-start | bytes 184328 | tf_op jit(solution)/shard_map/ppermute | solution.py:606
  17.5 5.1 %collective-permute-start.6 = (f32[32,128]{1,0:T(8,128)S(1)}, f32[32,128]{1,0:T(8,128)S(1)}, u32[]{:S(2)}, u32[]{:S(2)}) collective-permute-start(f32[32,128]{1,0:T(8,128)S(1)} %get-tuple-element.73), channel_id=1, source_target_pairs={{0,16},{4,20},{8,24},{12,28},{16,0},{20,4},{24,8},{28,12},{1,17},{... | collective-permute-start | bytes 49160 | tf_op jit(solution)/shard_map/ppermute | solution.py:603
  18.2 4.4 %collective-permute-start.7 = (f32[32,128]{1,0:T(8,128)S(1)}, f32[32,128]{1,0:T(8,128)S(1)}, u32[]{:S(2)}, u32[]{:S(2)}) collective-permute-start(f32[32,128]{1,0:T(8,128)S(1)} %get-tuple-element.74), channel_id=1, source_target_pairs={{0,24},{4,12},{8,0},{12,20},{16,8},{20,28},{24,16},{28,4},{1,25},{... | collective-permute-start | bytes 49160 | tf_op jit(solution)/shard_map/ppermute | solution.py:603
  23.6 1.2 %collective-permute-start.8 = (f32[8,512]{1,0:T(8,128)S(1)}, f32[8,512]{1,0:T(8,128)S(1)}, u32[]{:S(2)}, u32[]{:S(2)}) collective-permute-start(f32[8,512]{1,0:T(8,128)S(1)} %get-tuple-element.85.samp_ref), channel_id=1, source_target_pairs={{0,4},{4,0},{8,12},{12,8},{16,20},{20,16},{24,28},{28,24},{1,5},{5... | collective-permute-start | bytes 49160 | tf_op jit(solution)/shard_map/ppermute | solution.py:606
  25.8 6.3 %collective-permute-start.11 = (f32[40,128]{1,0:T(8,128)S(1)}, f32[40,128]{1,0:T(8,128)S(1)}, u32[]{:S(2)}, u32[]{:S(2)}) collective-permute-start(f32[40,128]{1,0:T(8,128)S(1)} %get-tuple-element.94), channel_id=1, source_target_pairs={{0,3},{1,2},{2,1},{3,0},{4,7},{5,6},{6,5},{7,4},{8,11},{9,10},{10,... | collective-permute-start | bytes 61448 | tf_op jit(solution)/shard_map/ppermute | solution.py:622
  28.5 3.9 %collective-permute-start.10 = (f32[40,128]{1,0:T(8,128)S(1)}, f32[40,128]{1,0:T(8,128)S(1)}, u32[]{:S(2)}, u32[]{:S(2)}) collective-permute-start(f32[40,128]{1,0:T(8,128)S(1)} %get-tuple-element.94), channel_id=1, source_target_pairs={{0,1},{1,0},{2,3},{3,2},{4,5},{5,4},{6,7},{7,6},{8,9},{9,8},{10,11... | collective-permute-start | bytes 61448 | tf_op jit(solution)/shard_map/ppermute | solution.py:621
  28.5 5.0 %collective-permute-start.9 = (f32[16,128]{1,0:T(8,128)S(1)}, f32[16,128]{1,0:T(8,128)S(1)}, u32[]{:S(2)}, u32[]{:S(2)}) collective-permute-start(f32[16,128]{1,0:T(8,128)S(1)} %slice.20), channel_id=1, source_target_pairs={{0,2},{1,3},{2,0},{3,1},{4,6},{5,7},{6,4},{7,5},{8,10},{9,11},{10,... | collective-permute-start | bytes 24584 | tf_op jit(solution)/shard_map/ppermute | solution.py:623
  33.6 5.8 %collective-permute-start.14 = (f32[208,128]{1,0:T(8,128)S(1)}, f32[208,128]{1,0:T(8,128)S(1)}, u32[]{:S(2)}, u32[]{:S(2)}) collective-permute-start(f32[208,128]{1,0:T(8,128)S(1)} %get-tuple-element.108), channel_id=1, source_target_pairs={{4,8},{12,16},{20,24},{28,0},{8,4},{16,12},{24,20},{0,28},{5,9},{1... | collective-permute-start | bytes 319496 | tf_op jit(solution)/shard_map/ppermute | solution.py:719
  34.2 5.2 %collective-permute-start.13 = (f32[192,128]{1,0:T(8,128)S(1)}, f32[192,128]{1,0:T(8,128)S(1)}, u32[]{:S(2)}, u32[]{:S(2)}) collective-permute-start(f32[192,128]{1,0:T(8,128)S(1)} %get-tuple-element.107), channel_id=1, source_target_pairs={{0,4},{4,0},{8,12},{12,8},{16,20},{20,16},{24,28},{28,24},{1,5},{5... | collective-permute-start | bytes 294920 | tf_op jit(solution)/shard_map/ppermute | solution.py:606
  37.1 4.0 %collective-permute-start.12 = (f32[16,128]{1,0:T(8,128)S(1)}, f32[16,128]{1,0:T(8,128)S(1)}, u32[]{:S(2)}, u32[]{:S(2)}) collective-permute-start(f32[16,128]{1,0:T(8,128)S(1)} %get-tuple-element.106), channel_id=1, source_target_pairs={{0,16},{4,20},{8,24},{12,28},{16,0},{20,4},{24,8},{28,12},{1,17},{... | collective-permute-start | bytes 24584 | tf_op jit(solution)/shard_map/ppermute | solution.py:720
  39.4 1.6 %collective-permute-start.15 = (f32[16,128]{1,0:T(8,128)S(1)}, f32[16,128]{1,0:T(8,128)S(1)}, u32[]{:S(2)}, u32[]{:S(2)}) collective-permute-start(f32[16,128]{1,0:T(8,128)S(1)} %slice.23), channel_id=1, source_target_pairs={{0,4},{4,0},{8,12},{12,8},{16,20},{20,16},{24,28},{28,24},{1,5},{5... | collective-permute-start | bytes 24584 | tf_op jit(solution)/shard_map/ppermute | solution.py:606

commit v16 on v14

--- a/solution.py
+++ b/solution.py
@@ -379,7 +379,7 @@
     for t in range(2):
         seg = slice(t * P_SIZE, (t + 1) * P_SIZE)
         lhs = jnp.concatenate([cos_a[:, seg] * circ[:, seg], sin_a[:, seg] * circ[:, seg], jnp.zeros((6, P_SIZE), F32)], axis=0)
-        both = jnp.dot(lhs, pair_ref[t], preferred_element_type=F32, precision=lax.Precision.HIGHEST)
+        both = dot3(*split(lhs), *split(pair_ref[t]))
         parts.append((cos_a[:, seg] * both[0:1] + sin_a[:, seg] * both[1:2]) / (4.0 * math.pi))
     induced = jnp.concatenate(parts, axis=1)
     rel_speed, cos_phi, sin_phi, lift_coef, drag_coef = attack(axial + induced, tangent, cos_t, sin_t)

time: 42.1 us -> 42 us (level)
  no operation moved by 1% of the time
where the time goes in v16:
time: 42 us; the launch traced here: 41.8 us
  Pallas kernels  19.9 us (47%)
  starting transfers between devices  17.3 us (41%)
  waiting for transfers between devices  2.68 us (6%)
  between operations  1.81 us (4%)
    ppermute x2, starting transfers between devices, exchange_y(): from_d = lax.ppermute(to_d, 'gy', flip(ny, 3) if short else odd_pairs(ny))  5.18 us
    pallas_call x5, Pallas kernels, stencil(): call(lambda *refs: stencil_body(start, *refs), [(3, count, CY, CZ)], 1, '...  3.92 us
    pallas_call x2, Pallas kernels, spread(): call(lambda *refs: spread_body(start, *refs), [(3, CX // 2, CY, CZ)], 3 +...  3.66 us
    ppermute x2, starting transfers between devices, exchange_y(): from_c = lax.ppermute(to_c, 'gy', flip(ny, 1))  3.09 us
    pallas_call x1, Pallas kernels, per_device(): call(sample_low_body, [(HOST, CZ), (HOST, 3 * CZ), (6, CY, CZ), (2, CX, C...  2.6 us
    pallas_call x1, Pallas kernels, per_device(): call(sample_high_body, [(HOST, 3 * CZ), (HOST, CZ), (HOST, CZ)], 3, 'samp...  2.43 us
    ppermute x1, starting transfers between devices, per_device(): face_b = lax.ppermute(pay_b, 'gx', odd_pairs(nx, ring))  2.41 us
    ppermute x2, starting transfers between devices, across_x(): lax.ppermute(b, 'gx', p)  2.21 us
  transfers between devices with their start and end apart: 16, of which 5 were waited for; matrix products, arithmetic and copies ran while one was open for 0% of the time, Pallas kernels for 38%

profile of v16, /device:TPU:0, one launch (start us, length us, event | category | flops | bytes accessed | tf_op | source)
XLA Modules:
  0.0 41.8 jit_solution(14222802150299394336)
XLA Ops:
  1.5 1.2 %pack.1 = (f32[208,128]{1,0:T(8,128)S(1)}, f32[208,128]{1,0:T(8,128)S(1)}, f32[16,128]{1,0:T(8,128)S(1)}) custom-call(f32[3,64,32,128]{3,2,1,0:T(8,128)} %refs_0_.9, f32[1,1]{1,0:T(1,128)} %bitcast.6.spin_hbm, f32[2,128]{1,0:T(2,128)} %bitcast.7, f32[2,128]{1,0:T(2,128)} %bitcast.8, f32[2,128]{1,0:T(2,128)} %bitcast.9, f32[2,128]{1,0:T(2,128)} %bitcast.10, ...), custom_call_target="tpu_custom_call" | custom-call | tf_op jit(solution)/shard_map/pack/pallas_call | solution.py:640
  2.6 3.1 %collective-permute-start = (f32[208,128]{1,0:T(8,128)S(1)}, f32[208,128]{1,0:T(8,128)S(1)}, u32[]{:S(2)}, u32[]{:S(2)}) collective-permute-start(f32[208,128]{1,0:T(8,128)S(1)} %get-tuple-element.64), channel_id=1, source_target_pairs={{0,1},{1,0},{2,3},{3,2},{4,5},{5,4},{6,7},{7,6},{8,9},{9,8},{10,11... | collective-permute-start | bytes 319496 | tf_op jit(solution)/shard_map/ppermute | solution.py:620
  5.7 2.5 %collective-permute-start.1 = (f32[208,128]{1,0:T(8,128)S(1)}, f32[208,128]{1,0:T(8,128)S(1)}, u32[]{:S(2)}, u32[]{:S(2)}) collective-permute-start(f32[208,128]{1,0:T(8,128)S(1)} %get-tuple-element.65), channel_id=1, source_target_pairs={{0,3},{1,2},{2,1},{3,0},{4,7},{5,6},{6,5},{7,4},{8,11},{9,10},{10,... | collective-permute-start | bytes 319496 | tf_op jit(solution)/shard_map/ppermute | solution.py:621
  8.2 0.1 collective-permute-start.2
  8.3 1.5 %stencil.5.refs_3_ = f32[3,24,32,128]{3,2,1,0:T(8,128)S(1)} custom-call(f32[3,64,32,128]{3,2,1,0:T(8,128)S(1)} %copy-done), custom_call_target="tpu_custom_call" | custom-call | tf_op jit(solution)/shard_map/stencil/pallas_call | solution.py:651
  9.8 2.6 %sample_low.1 = (f32[512,128]{1,0:T(8,128)S(1)}, f32[512,384]{1,0:T(8,128)S(1)}, f32[6,32,128]{2,1,0:T(8,128)S(1)}, f32[2,64,128]{2,1,0:T(8,128)S(1)}) custom-call(f32[3,64,32,128]{3,2,1,0:T(8,128)S(1)} %copy-done, s32[3,512]{1,0:T(4,128)S(1)} %copy-done.1, f32[3,512]{1,0:T(4,128)S(1)} %copy-done.2), custom_call_target="tpu_custom_call" | custom-call | tf_op jit(solution)/shard_map/sample_low/pallas_call | solution.py:654
  12.4 1.2 %collective-permute-done.2 = f32[16,128]{1,0:T(8,128)S(1)} collective-permute-done((f32[16,128]{1,0:T(8,128)S(1)}, f32[16,128]{1,0:T(8,128)S(1)}, u32[]{:S(2)}, u32[]{:S(2)}) %collective-permute-start.2) | collective-permute-done | bytes 8224 | tf_op jit(solution)/shard_map/ppermute | solution.py:622
  13.7 1.0 %stencil.6.refs_3_ = f32[3,16,32,128]{3,2,1,0:T(8,128)S(1)} custom-call(f32[3,64,32,128]{3,2,1,0:T(8,128)S(1)} %copy-done), custom_call_target="tpu_custom_call" | custom-call | tf_op jit(solution)/shard_map/stencil/pallas_call | solution.py:651
  14.7 0.2 collective-permute-done.3.refs_4_
  15.0 2.4 %collective-permute-start.5 = (f32[152,128]{1,0:T(8,128)S(1)}, f32[152,128]{1,0:T(8,128)S(1)}, u32[]{:S(2)}, u32[]{:S(2)}) collective-permute-start(f32[152,128]{1,0:T(8,128)S(1)} %get-tuple-element.73), channel_id=1, source_target_pairs={{4,8},{12,16},{20,24},{28,0},{8,4},{16,12},{24,20},{0,28},{5,9},{1... | collective-permute-start | bytes 233480 | tf_op jit(solution)/shard_map/ppermute | solution.py:670
  17.5 0.8 %collective-permute-start.6 = (f32[32,128]{1,0:T(8,128)S(1)}, f32[32,128]{1,0:T(8,128)S(1)}, u32[]{:S(2)}, u32[]{:S(2)}) collective-permute-start(f32[32,128]{1,0:T(8,128)S(1)} %get-tuple-element.74), channel_id=1, source_target_pairs={{0,16},{4,20},{8,24},{12,28},{16,0},{20,4},{24,8},{28,12},{1,17},{... | collective-permute-start | bytes 49160 | tf_op jit(solution)/shard_map/ppermute | solution.py:602
  18.2 1.4 %collective-permute-start.7 = (f32[32,128]{1,0:T(8,128)S(1)}, f32[32,128]{1,0:T(8,128)S(1)}, u32[]{:S(2)}, u32[]{:S(2)}) collective-permute-start(f32[32,128]{1,0:T(8,128)S(1)} %get-tuple-element.75), channel_id=1, source_target_pairs={{0,24},{4,12},{8,0},{12,20},{16,8},{20,28},{24,16},{28,4},{1,25},{... | collective-permute-start | bytes 49160 | tf_op jit(solution)/shard_map/ppermute | solution.py:602
  19.7 0.5 %stencil.7.refs_4_ = f32[3,8,32,128]{3,2,1,0:T(8,128)S(1)} custom-call(f32[3,64,32,128]{3,2,1,0:T(8,128)S(1)} %copy-done), custom_call_target="tpu_custom_call" | custom-call | tf_op jit(solution)/shard_map/stencil/pallas_call | solution.py:651
  20.2 2.4 %sample_high.1 = (f32[512,384]{1,0:T(8,128)S(1)}, f32[512,128]{1,0:T(8,128)S(1)}, f32[512,128]{1,0:T(8,128)S(1)}) custom-call(f32[3,64,32,128]{3,2,1,0:T(8,128)S(1)} %copy-done, f32[512,128]{1,0:T(8,128)S(1)} %get-tuple-element.62.tab_ref.refs_0_, f32[512,384]{1,0:T(8,128)S(1)} %get-tuple-element.76.low_ref), custom_call_target="tpu_custom_call" | custom-call | tf_op jit(solution)/shard_map/sample_high/pallas_call | solution.py:673
  22.6 1.0 %select.1 = (f32[8,512]{1,0:T(8,128)S(1)}, f32[32,128]{1,0:T(8,128)S(1)}, f32[16,512]{1,0:T(8,128)S(1)}) custom-call(f32[512,128]{1,0:T(8,128)S(1)} %get-tuple-element.62.tab_ref.refs_0_, f32[512,384]{1,0:T(8,128)S(1)} %get-tuple-element.78.refs_1_, f32[512,128]{1,0:T(8,128)S(1)} %get-tuple-element.79.refs_2_, f32[512,128]{1,0:T(8,128)S(1)} %get-tuple-element.80.refs_3_, ...), custom_call_target="tpu_custom_call" | custom-call | tf_op jit(solution)/shard_map/select/pallas_call | solution.py:678
  23.6 0.5 %stencil.8.refs_4_ = f32[3,8,32,128]{3,2,1,0:T(8,128)S(1)} custom-call(f32[3,64,32,128]{3,2,1,0:T(8,128)S(1)} %copy-done), custom_call_target="tpu_custom_call" | custom-call | tf_op jit(solution)/shard_map/stencil/pallas_call | solution.py:651
  24.1 0.5 %weights.1 = (f32[72,512]{1,0:T(8,128)S(1)}, f32[32,512]{1,0:T(8,128)S(1)}, f32[128,512]{1,0:T(8,128)S(1)}, f32[24,128]{1,0:T(8,128)S(1)}, f32[2,256,256]{2,1,0:T(8,128)S(1)}, /*index=5*/f32[128,512]{1,0:T(8,128)S(1)}) custom-call(f32[16,512]{1,0:T(8,128)S(1)} %get-tuple-element.89.pts_ref, f32[32,128]{1,0:T(8,128)S(1)} %get-tuple-element.88.sel_ref), custom_call_target="tpu_custom_call" | custom-call | tf_op jit(solution)/shard_map/weights/pallas_call | solution.py:685
  24.6 0.2 collective-permute-done.8.other_ref
  24.8 0.9 %loads.1 = (f32[384,512]{1,0:T(8,128)S(1)}, f32[40,128]{1,0:T(8,128)S(1)}, f32[384,128]{1,0:T(8,128)S(1)}) custom-call(f32[8,512]{1,0:T(8,128)S(1)} %get-tuple-element.86.samp_ref, f32[8,512]{1,0:T(8,128)S(1)} %collective-permute-done.8.other_ref, f32[32,128]{1,0:T(8,128)S(1)} %get-tuple-element.88.sel_ref, f32[128,512]{1,0:T(8,128)S(1)} %get-tuple-element.90.pz_ref, ...), custom_call_target="tpu_custom_call" | custom-call | tf_op jit(solution)/shard_map/loads/pallas_call | solution.py:692
  25.7 2.7 %collective-permute-start.11 = (f32[40,128]{1,0:T(8,128)S(1)}, f32[40,128]{1,0:T(8,128)S(1)}, u32[]{:S(2)}, u32[]{:S(2)}) collective-permute-start(f32[40,128]{1,0:T(8,128)S(1)} %get-tuple-element.95), channel_id=1, source_target_pairs={{0,3},{1,2},{2,1},{3,0},{4,7},{5,6},{6,5},{7,4},{8,11},{9,10},{10,... | collective-permute-start | bytes 61448 | tf_op jit(solution)/shard_map/ppermute | solution.py:621
  28.4 1.7 %collective-permute-start.9 = (f32[16,128]{1,0:T(8,128)S(1)}, f32[16,128]{1,0:T(8,128)S(1)}, u32[]{:S(2)}, u32[]{:S(2)}) collective-permute-start(f32[16,128]{1,0:T(8,128)S(1)} %slice.20), channel_id=1, source_target_pairs={{0,2},{1,3},{2,0},{3,1},{4,6},{5,7},{6,4},{7,5},{8,10},{9,11},{10,... | collective-permute-start | bytes 24584 | tf_op jit(solution)/shard_map/ppermute | solution.py:622
  30.1 1.8 %spread.2.main_low.refs_1_ = f32[3,32,32,128]{3,2,1,0:T(8,128)S(1)} custom-call(f32[384,512]{1,0:T(8,128)S(1)} %get-tuple-element.96.refs_0_, f32[72,512]{1,0:T(8,128)S(1)} %get-tuple-element.97.refs_1_, f32[32,512]{1,0:T(8,128)S(1)} %get-tuple-element.98.refs_2_, f32[3,24,32,128]{3,2,1,0:T(8,128)S(1)} %stencil.5.refs_3_, f32[3,8,32,128]{3,2,1,0:T(8,128)S(1)} %stencil.7.refs_4_), custom_call_target="tpu_custom_call" | custom-call | tf_op jit(solution)/shard_map/spread/pallas_call | solution.py:702
  32.0 0.3 collective-permute-done.10.rec_c
  32.3 1.1 %near.1 = (f32[432,128]{1,0:T(8,128)S(1)}, f32[432,128]{1,0:T(8,128)S(1)}) custom-call(f32[40,128]{1,0:T(8,128)S(1)} %collective-permute-done.10.rec_c, f32[40,128]{1,0:T(8,128)S(1)} %collective-permute-done.11.rec_d), custom_call_target="tpu_custom_call" | custom-call | tf_op jit(solution)/shard_map/near/pallas_call | solution.py:707
  33.5 0.6 %collective-permute-start.14 = (f32[208,128]{1,0:T(8,128)S(1)}, f32[208,128]{1,0:T(8,128)S(1)}, u32[]{:S(2)}, u32[]{:S(2)}) collective-permute-start(f32[208,128]{1,0:T(8,128)S(1)} %get-tuple-element.109), channel_id=1, source_target_pairs={{4,8},{12,16},{20,24},{28,0},{8,4},{16,12},{24,20},{0,28},{5,9},{1... | collective-permute-start | bytes 319496 | tf_op jit(solution)/shard_map/ppermute | solution.py:718
  34.1 0.6 %collective-permute-start.13 = (f32[192,128]{1,0:T(8,128)S(1)}, f32[192,128]{1,0:T(8,128)S(1)}, u32[]{:S(2)}, u32[]{:S(2)}) collective-permute-start(f32[192,128]{1,0:T(8,128)S(1)} %get-tuple-element.108), channel_id=1, source_target_pairs={{0,4},{4,0},{8,12},{12,8},{16,20},{20,16},{24,28},{28,24},{1,5},{5... | collective-permute-start | bytes 294920 | tf_op jit(solution)/shard_map/ppermute | solution.py:605
  34.6 0.5 %stencil.9.refs_5_ = f32[3,8,32,128]{3,2,1,0:T(8,128)S(1)} custom-call(f32[3,64,32,128]{3,2,1,0:T(8,128)S(1)} %copy-done), custom_call_target="tpu_custom_call" | custom-call | tf_op jit(solution)/shard_map/stencil/pallas_call | solution.py:651
  35.1 1.8 %spread.3.main_high.refs_2_ = f32[3,32,32,128]{3,2,1,0:T(8,128)S(1)} custom-call(f32[384,512]{1,0:T(8,128)S(1)} %get-tuple-element.96.refs_0_, f32[72,512]{1,0:T(8,128)S(1)} %get-tuple-element.97.refs_1_, f32[32,512]{1,0:T(8,128)S(1)} %get-tuple-element.98.refs_2_, f32[3,16,32,128]{3,2,1,0:T(8,128)S(1)} %stencil.6.refs_3_, ...), custom_call_target="tpu_custom_call" | custom-call | tf_op jit(solution)/shard_map/spread/pallas_call | solution.py:702
  37.0 1.3 %collective-permute-start.12 = (f32[16,128]{1,0:T(8,128)S(1)}, f32[16,128]{1,0:T(8,128)S(1)}, u32[]{:S(2)}, u32[]{:S(2)}) collective-permute-start(f32[16,128]{1,0:T(8,128)S(1)} %get-tuple-element.107), channel_id=1, source_target_pairs={{0,16},{4,20},{8,24},{12,28},{16,0},{20,4},{24,8},{28,12},{1,17},{... | collective-permute-start | bytes 24584 | tf_op jit(solution)/shard_map/ppermute | solution.py:719
  38.3 0.7 %collective-permute-done.14.refs_10_ = f32[208,128]{1,0:T(8,128)S(1)} collective-permute-done((f32[208,128]{1,0:T(8,128)S(1)}, f32[208,128]{1,0:T(8,128)S(1)}, u32[]{:S(2)}, u32[]{:S(2)}) %collective-permute-start.14) | collective-permute-done | bytes 106528 | tf_op jit(solution)/shard_map/ppermute | solution.py:718
  39.0 1.7 %inside.1.refs_0_ = f32[3,64,32,128]{3,2,1,0:T(8,128)} custom-call(f32[3,32,32,128]{3,2,1,0:T(8,128)S(1)} %spread.2.main_low.refs_1_, f32[3,32,32,128]{3,2,1,0:T(8,128)S(1)} %spread.3.main_high.refs_2_, f32[2,64,128]{2,1,0:T(8,128)S(1)} %get-tuple-element.116.y_ref.refs_4_, f32[208,128]{1,0:T(8,128)S(1)} %collective-permute-done.refs_1_.refs_6_.rec_c.refs_7_, ...), custom_call_target="tpu_custom_call" | custom-call | tf_op jit(solution)/shard_map/inside/pallas_call | solution.py:725
  40.8 0.8 %final.1 = (f32[3,64,32,128]{3,2,1,0:T(8,128)}, f32[3,256]{1,0:T(4,128)}) custom-call(f32[3,64,32,128]{3,2,1,0:T(8,128)} %inside.1.refs_0_, f32[3,32,32,128]{3,2,1,0:T(8,128)S(1)} %spread.2.main_low.refs_1_, f32[3,32,32,128]{3,2,1,0:T(8,128)S(1)} %spread.3.main_high.refs_2_, ...), custom_call_target="tpu_custom_call", output_to_operand_aliasing={{0}: (0, {})} | custom-call | tf_op jit(solution)/shard_map/final/pallas_call | solution.py:736
  (32 shorter events, 0.3 us)
Async XLA Ops:
  0.6 7.7 %copy-start = (f32[3,64,32,128]{3,2,1,0:T(8,128)S(1)}, f32[3,64,32,128]{3,2,1,0:T(8,128)}, u32[]{:S(2)}) copy-start(f32[3,64,32,128]{3,2,1,0:T(8,128)} %refs_0_.9) | copy-start | bytes 9437188
  1.4 8.3 %copy-start.1 = (s32[3,512]{1,0:T(4,128)S(1)}, s32[3,512]{1,0:T(4,128)}, u32[]{:S(2)}) copy-start(s32[3,512]{1,0:T(4,128)} %cell_ref.1) | copy-start | bytes 18436
  1.4 8.3 %copy-start.2 = (f32[3,512]{1,0:T(4,128)S(1)}, f32[3,512]{1,0:T(4,128)}, u32[]{:S(2)}) copy-start(f32[3,512]{1,0:T(4,128)} %frac_ref.1) | copy-start | bytes 18436
  2.6 11.0 %collective-permute-start = (f32[208,128]{1,0:T(8,128)S(1)}, f32[208,128]{1,0:T(8,128)S(1)}, u32[]{:S(2)}, u32[]{:S(2)}) collective-permute-start(f32[208,128]{1,0:T(8,128)S(1)} %get-tuple-element.64), channel_id=1, source_target_pairs={{0,1},{1,0},{2,3},{3,2},{4,5},{5,4},{6,7},{7,6},{8,9},{9,8},{10,11... | collective-permute-start | bytes 319496 | tf_op jit(solution)/shard_map/ppermute | solution.py:620
  5.7 7.9 %collective-permute-start.1 = (f32[208,128]{1,0:T(8,128)S(1)}, f32[208,128]{1,0:T(8,128)S(1)}, u32[]{:S(2)}, u32[]{:S(2)}) collective-permute-start(f32[208,128]{1,0:T(8,128)S(1)} %get-tuple-element.65), channel_id=1, source_target_pairs={{0,3},{1,2},{2,1},{3,0},{4,7},{5,6},{6,5},{7,4},{8,11},{9,10},{10,... | collective-permute-start | bytes 319496 | tf_op jit(solution)/shard_map/ppermute | solution.py:621
  8.2 5.4 %collective-permute-start.2 = (f32[16,128]{1,0:T(8,128)S(1)}, f32[16,128]{1,0:T(8,128)S(1)}, u32[]{:S(2)}, u32[]{:S(2)}) collective-permute-start(f32[16,128]{1,0:T(8,128)S(1)} %get-tuple-element.66), channel_id=1, source_target_pairs={{0,2},{1,3},{2,0},{3,1},{4,6},{5,7},{6,4},{7,5},{8,10},{9,11},{10,... | collective-permute-start | bytes 24584 | tf_op jit(solution)/shard_map/ppermute | solution.py:622
  13.7 1.3 %collective-permute-start.3 = (f32[64,128]{1,0:T(8,128)S(1)}, f32[64,128]{1,0:T(8,128)S(1)}, u32[]{:S(2)}, u32[]{:S(2)}) collective-permute-start(f32[64,128]{1,0:T(8,128)S(1)} %pad_maximum_fusion.refs_3_), channel_id=1, source_target_pairs={{0,4},{4,0},{8,12},{12,8},{16,20},{20,16},{24,28},{28,24},{1,5},{5... | collective-permute-start | bytes 98312 | tf_op jit(solution)/shard_map/ppermute | solution.py:605
  15.0 7.6 %collective-permute-start.5 = (f32[152,128]{1,0:T(8,128)S(1)}, f32[152,128]{1,0:T(8,128)S(1)}, u32[]{:S(2)}, u32[]{:S(2)}) collective-permute-start(f32[152,128]{1,0:T(8,128)S(1)} %get-tuple-element.73), channel_id=1, source_target_pairs={{4,8},{12,16},{20,24},{28,0},{8,4},{16,12},{24,20},{0,28},{5,9},{1... | collective-permute-start | bytes 233480 | tf_op jit(solution)/shard_map/ppermute | solution.py:670
  17.5 5.2 %collective-permute-start.4 = (f32[120,128]{1,0:T(8,128)S(1)}, f32[120,128]{1,0:T(8,128)S(1)}, u32[]{:S(2)}, u32[]{:S(2)}) collective-permute-start(f32[120,128]{1,0:T(8,128)S(1)} %get-tuple-element.72), channel_id=1, source_target_pairs={{0,4},{4,0},{8,12},{12,8},{16,20},{20,16},{24,28},{28,24},{1,5},{5... | collective-permute-start | bytes 184328 | tf_op jit(solution)/shard_map/ppermute | solution.py:605
  17.5 5.1 %collective-permute-start.6 = (f32[32,128]{1,0:T(8,128)S(1)}, f32[32,128]{1,0:T(8,128)S(1)}, u32[]{:S(2)}, u32[]{:S(2)}) collective-permute-start(f32[32,128]{1,0:T(8,128)S(1)} %get-tuple-element.74), channel_id=1, source_target_pairs={{0,16},{4,20},{8,24},{12,28},{16,0},{20,4},{24,8},{28,12},{1,17},{... | collective-permute-start | bytes 49160 | tf_op jit(solution)/shard_map/ppermute | solution.py:602
  18.2 4.4 %collective-permute-start.7 = (f32[32,128]{1,0:T(8,128)S(1)}, f32[32,128]{1,0:T(8,128)S(1)}, u32[]{:S(2)}, u32[]{:S(2)}) collective-permute-start(f32[32,128]{1,0:T(8,128)S(1)} %get-tuple-element.75), channel_id=1, source_target_pairs={{0,24},{4,12},{8,0},{12,20},{16,8},{20,28},{24,16},{28,4},{1,25},{... | collective-permute-start | bytes 49160 | tf_op jit(solution)/shard_map/ppermute | solution.py:602
  23.6 1.2 %collective-permute-start.8 = (f32[8,512]{1,0:T(8,128)S(1)}, f32[8,512]{1,0:T(8,128)S(1)}, u32[]{:S(2)}, u32[]{:S(2)}) collective-permute-start(f32[8,512]{1,0:T(8,128)S(1)} %get-tuple-element.86.samp_ref), channel_id=1, source_target_pairs={{0,4},{4,0},{8,12},{12,8},{16,20},{20,16},{24,28},{28,24},{1,5},{5... | collective-permute-start | bytes 49160 | tf_op jit(solution)/shard_map/ppermute | solution.py:605
  25.7 6.3 %collective-permute-start.11 = (f32[40,128]{1,0:T(8,128)S(1)}, f32[40,128]{1,0:T(8,128)S(1)}, u32[]{:S(2)}, u32[]{:S(2)}) collective-permute-start(f32[40,128]{1,0:T(8,128)S(1)} %get-tuple-element.95), channel_id=1, source_target_pairs={{0,3},{1,2},{2,1},{3,0},{4,7},{5,6},{6,5},{7,4},{8,11},{9,10},{10,... | collective-permute-start | bytes 61448 | tf_op jit(solution)/shard_map/ppermute | solution.py:621
  28.4 3.9 %collective-permute-start.10 = (f32[40,128]{1,0:T(8,128)S(1)}, f32[40,128]{1,0:T(8,128)S(1)}, u32[]{:S(2)}, u32[]{:S(2)}) collective-permute-start(f32[40,128]{1,0:T(8,128)S(1)} %get-tuple-element.95), channel_id=1, source_target_pairs={{0,1},{1,0},{2,3},{3,2},{4,5},{5,4},{6,7},{7,6},{8,9},{9,8},{10,11... | collective-permute-start | bytes 61448 | tf_op jit(solution)/shard_map/ppermute | solution.py:620
  28.4 5.0 %collective-permute-start.9 = (f32[16,128]{1,0:T(8,128)S(1)}, f32[16,128]{1,0:T(8,128)S(1)}, u32[]{:S(2)}, u32[]{:S(2)}) collective-permute-start(f32[16,128]{1,0:T(8,128)S(1)} %slice.20), channel_id=1, source_target_pairs={{0,2},{1,3},{2,0},{3,1},{4,6},{5,7},{6,4},{7,5},{8,10},{9,11},{10,... | collective-permute-start | bytes 24584 | tf_op jit(solution)/shard_map/ppermute | solution.py:622
  33.5 5.6 %collective-permute-start.14 = (f32[208,128]{1,0:T(8,128)S(1)}, f32[208,128]{1,0:T(8,128)S(1)}, u32[]{:S(2)}, u32[]{:S(2)}) collective-permute-start(f32[208,128]{1,0:T(8,128)S(1)} %get-tuple-element.109), channel_id=1, source_target_pairs={{4,8},{12,16},{20,24},{28,0},{8,4},{16,12},{24,20},{0,28},{5,9},{1... | collective-permute-start | bytes 319496 | tf_op jit(solution)/shard_map/ppermute | solution.py:718
  34.1 4.2 %collective-permute-start.13 = (f32[192,128]{1,0:T(8,128)S(1)}, f32[192,128]{1,0:T(8,128)S(1)}, u32[]{:S(2)}, u32[]{:S(2)}) collective-permute-start(f32[192,128]{1,0:T(8,128)S(1)} %get-tuple-element.108), channel_id=1, source_target_pairs={{0,4},{4,0},{8,12},{12,8},{16,20},{20,16},{24,28},{28,24},{1,5},{5... | collective-permute-start | bytes 294920 | tf_op jit(solution)/shard_map/ppermute | solution.py:605
  37.0 3.8 %collective-permute-start.12 = (f32[16,128]{1,0:T(8,128)S(1)}, f32[16,128]{1,0:T(8,128)S(1)}, u32[]{:S(2)}, u32[]{:S(2)}) collective-permute-start(f32[16,128]{1,0:T(8,128)S(1)} %get-tuple-element.107), channel_id=1, source_target_pairs={{0,16},{4,20},{8,24},{12,28},{16,0},{20,4},{24,8},{28,12},{1,17},{... | collective-permute-start | bytes 24584 | tf_op jit(solution)/shard_map/ppermute | solution.py:719
  39.0 1.8 %collective-permute-start.15 = (f32[16,128]{1,0:T(8,128)S(1)}, f32[16,128]{1,0:T(8,128)S(1)}, u32[]{:S(2)}, u32[]{:S(2)}) collective-permute-start(f32[16,128]{1,0:T(8,128)S(1)} %slice.23), channel_id=1, source_target_pairs={{0,4},{4,0},{8,12},{12,8},{16,20},{20,16},{24,28},{28,24},{1,5},{5... | collective-permute-start | bytes 24584 | tf_op jit(solution)/shard_map/ppermute | solution.py:605
